TPU v7x, 32 devices: a whole 2x2x4 slice. The times are simulated.
32 devices in a mesh: fsdp: 8 (over y, x, core), sp: 4 (over z).
Axes of the slice: x: 2, y: 2, z: 4, core: 2. Of those that a mesh axis runs over, the one named last changes fastest.
Arguments:
- tokens: bfloat16 [16384, 1024], P(('fsdp', 'sp')), may hold values from -6 to 6
- query_weight: float32 [1024, 1024], P('fsdp'), may hold values from -0.1875 to 0.1875
- key_projection_weight: float32 [1024, 512], P('fsdp'), may hold values from -0.1875 to 0.1875
- value_projection_weight: float32 [1024, 512], P('fsdp'), may hold values from -0.1875 to 0.1875
- output_weight: float32 [1024, 1024], P('fsdp'), may hold values from -1.5 to 1.5
- router_weight: float32 [1024, 32], P('fsdp'), may hold values from -0.09375 to 0.09375
- first_gain: float32 [1024], P('fsdp'), may hold values from 0.5 to 1.5
- second_gain: float32 [1024], P('fsdp'), may hold values from 0.5 to 1.5
- expert_gate: float32 [32, 1024, 512], P('fsdp', 'sp'), may hold values from -0.1875 to 0.1875
- expert_up: float32 [32, 1024, 512], P('fsdp', 'sp'), may hold values from -0.1875 to 0.1875
- expert_down: float32 [32, 512, 1024], P('fsdp', None, 'sp'), may hold values from -1 to 1
- routes: int32 [16384, 8], P(('fsdp', 'sp')), may hold values from 0 to 31, all different within a row; in each aligned block of 512 rows (0 to 511, 512 to 1023, ...) at most 192 rows name the same one
- dealing: int32 [8, 2048], P('fsdp'), may hold values from 0 to 2047, each once within a row
- lengths: int32 [8, 3], P('fsdp'), may hold values from 1 to 1024, 2048 in all within a row
- cotangent: bfloat16 [16384, 1024], P(('fsdp', 'sp')), may hold values from -6 to 6
Outputs:
- layer_out: bfloat16 [16384, 1024], P(('fsdp', 'sp'))
- tokens_grad: bfloat16 [16384, 1024], P(('fsdp', 'sp'))
- grad_query_weight: float32 [1024, 1024], P('fsdp')
- grad_key_weight: float32 [1024, 512], P('fsdp')
- grad_value_weight: float32 [1024, 512], P('fsdp')
- grad_output_weight: float32 [1024, 1024], P('fsdp')
- grad_router_weight: float32 [1024, 32], P('fsdp')
- grad_first_gain: float32 [1024], P('fsdp')
- grad_second_gain: float32 [1024], P('fsdp')
- grad_expert_gate: float32 [32, 1024, 512], P('fsdp', 'sp')
- grad_expert_up: float32 [32, 1024, 512], P('fsdp', 'sp')
- grad_expert_down: float32 [32, 512, 1024], P('fsdp', None, 'sp')
Inputs may be any that keep to these rules, and one draw needn't show every extreme that they name: `routes`: each token names 8 different experts; among the 512 rows of one device no expert is named more than 192 times, and in some devices' rows an expert is named exactly 192 times. `dealing`: each row names every place of its group once. `lengths`: each row sums to 2048, and its largest entry is exactly 1024.
All inputs are finite; a program needn't handle non-finite values.
Results may differ from a plain program's by a relative error of at most 0.02.
Values may be sent and summed in bfloat16 or wider, within the bound.
No kernel may reach another device: no remote copies, remote signals or barrier semaphores. Data moves between devices by JAX's collectives and lax.ppermute only.
A program may use at most 256 MiB of HBM per device.

v0:
```python
import math

import jax
import jax.numpy as jnp
from jax import lax
from jax.sharding import PartitionSpec as P

MODEL_WIDTH = 1024
QUERY_HEADS = 16
KEY_VALUE_HEADS = 8
HEAD_SIZE = 64
EXPERTS = 32
TOPK = 8
BLOCK = 512
CAP = 192


NORM_EPS = 1e-06
ROPE_BASE = 10000.0
MASKED = -1e30


def apply_rotary(values, places, direction):
    half_dim = HEAD_SIZE // 2
    frequency = ROPE_BASE ** (-(jnp.arange(half_dim, dtype=jnp.float32) * 2.0 / HEAD_SIZE))
    angles = places[:, None] * frequency[None, :]
    cosine = jnp.cos(angles)[:, None, :]
    sine_part = direction * jnp.sin(angles)[:, None, :]
    first_half = values[..., :half_dim]
    second_half = values[..., half_dim:]
    return jnp.concatenate(
        [
            first_half * cosine - second_half * sine_part,
            second_half * cosine + first_half * sine_part,
        ],
        axis=-1,
    )


def sequence_info(length_row, places):
    seq_ends = jnp.cumsum(length_row)
    starts = seq_ends - length_row
    within = starts[None, :] <= places[:, None]
    first_place = jnp.max(jnp.where(within, starts[None, :], 0), axis=1)
    seq_index = jnp.sum(within.astype(jnp.int32), axis=1) - 1
    return (first_place, seq_index)


def block_scores(q_block, k_block, q_first, k_first, seq_ids, score_scale):
    span = q_block.shape[0]
    raw_scores = (
        jnp.einsum("qlgd,kld->lgqk", q_block, k_block, preferred_element_type=jnp.float32)
        * score_scale
    )
    q_places = q_first + jnp.arange(span, dtype=jnp.int32)
    k_places = k_first + jnp.arange(span, dtype=jnp.int32)
    q_seqs = lax.dynamic_slice_in_dim(seq_ids, q_first, span)
    k_seqs = lax.dynamic_slice_in_dim(seq_ids, k_first, span)
    allowed = (k_places[None, :] <= q_places[:, None]) & (k_seqs[None, :] == q_seqs[:, None])
    return jnp.where(allowed, raw_scores, MASKED)


def body(
    tokens,
    query_weight,
    key_projection_weight,
    value_projection_weight,
    output_weight,
    router_weight,
    first_gain,
    second_gain,
    expert_gate,
    expert_up,
    expert_down,
    routes,
    dealing,
    lengths,
    cotangent,
):
    token_row_block = tokens.shape[0]
    sequence_parallel_count = lax.axis_size("sp")
    sp_index = lax.axis_index("sp")
    fsdp_count = lax.axis_size("fsdp")
    grouped_row_count = token_row_block * sequence_parallel_count
    local_experts = EXPERTS // fsdp_count
    key_value_resident = KEY_VALUE_HEADS // sequence_parallel_count
    query_per_key_ratio = QUERY_HEADS // KEY_VALUE_HEADS
    score_scale = 1.0 / math.sqrt(HEAD_SIZE)
    block_count = grouped_row_count // BLOCK
    pair_count = token_row_block * TOPK
    query_full, key_full, value_full, output_full, router_full, gain_attend, gain_mixer = (
        lax.all_gather(query_weight.astype(jnp.bfloat16), "fsdp", axis=0, tiled=True),
        lax.all_gather(key_projection_weight.astype(jnp.bfloat16), "fsdp", axis=0, tiled=True),
        lax.all_gather(value_projection_weight.astype(jnp.bfloat16), "fsdp", axis=0, tiled=True),
        lax.all_gather(output_weight.astype(jnp.bfloat16), "fsdp", axis=0, tiled=True),
        lax.all_gather(router_weight.astype(jnp.bfloat16), "fsdp", axis=0, tiled=True),
        lax.all_gather(first_gain.astype(jnp.bfloat16), "fsdp", axis=0, tiled=True),
        lax.all_gather(second_gain.astype(jnp.bfloat16), "fsdp", axis=0, tiled=True),
    )
    gain_attend = gain_attend.astype(jnp.float32)
    gain_mixer = gain_mixer.astype(jnp.float32)
    tokens_value = tokens.astype(jnp.float32)
    inv_one = lax.rsqrt(jnp.mean(tokens_value * tokens_value, axis=1, keepdims=True) + NORM_EPS)
    normed_one = tokens_value * inv_one
    first_activation = (normed_one * gain_attend).astype(jnp.bfloat16)
    query_pre = jnp.dot(first_activation, query_full, preferred_element_type=jnp.float32)
    key_projected = jnp.dot(first_activation, key_full, preferred_element_type=jnp.float32)
    value_projected = jnp.dot(first_activation, value_full, preferred_element_type=jnp.float32)
    order_row = dealing[0]
    length_row = lengths[0]
    mine_places = lax.dynamic_slice_in_dim(order_row, sp_index * token_row_block, token_row_block)
    mine_start = sequence_info(length_row, mine_places)[0]
    resident_positions = (mine_places - mine_start).astype(jnp.float32)
    query_rot = apply_rotary(
        query_pre.reshape(token_row_block, QUERY_HEADS, HEAD_SIZE), resident_positions, 1.0
    ).astype(jnp.bfloat16)
    key_rotated = apply_rotary(
        key_projected.reshape(token_row_block, KEY_VALUE_HEADS, HEAD_SIZE), resident_positions, 1.0
    ).astype(jnp.bfloat16)
    value_second_part = value_projected.reshape(token_row_block, KEY_VALUE_HEADS, HEAD_SIZE).astype(
        jnp.bfloat16
    )
    key_value_packed = jnp.stack([key_rotated, value_second_part], axis=2).reshape(
        token_row_block, KEY_VALUE_HEADS * 2 * HEAD_SIZE
    )
    query_heads, kv_heads, token_cols = (
        lax.all_to_all(
            query_rot.reshape(token_row_block, QUERY_HEADS * HEAD_SIZE),
            "sp",
            split_axis=1,
            concat_axis=0,
            tiled=True,
        ),
        lax.all_to_all(key_value_packed, "sp", split_axis=1, concat_axis=0, tiled=True),
        lax.all_to_all(tokens, "sp", split_axis=1, concat_axis=0, tiled=True),
    )
    inverse_row = (
        jnp.zeros((grouped_row_count,), jnp.int32)
        .at[order_row]
        .set(jnp.arange(grouped_row_count, dtype=jnp.int32))
    )
    query_orig = jnp.take(query_heads, inverse_row, axis=0).reshape(
        grouped_row_count, key_value_resident, query_per_key_ratio, HEAD_SIZE
    )
    kv_orig = jnp.take(kv_heads, inverse_row, axis=0).reshape(
        grouped_row_count, key_value_resident, 2, HEAD_SIZE
    )
    keys_orig = kv_orig[:, :, 0]
    values_orig = kv_orig[:, :, 1]
    resid_cols = jnp.take(token_cols, inverse_row, axis=0)
    every_place = jnp.arange(grouped_row_count, dtype=jnp.int32)
    seq_start, seq_ids = sequence_info(length_row, every_place)
    seq_pos = (every_place - seq_start).astype(jnp.float32)
    first_block = seq_start[::BLOCK] // BLOCK

    def attend_block(block_index):
        q_first = block_index * BLOCK
        q_block = lax.dynamic_slice_in_dim(query_orig, q_first, BLOCK)
        lowest = first_block[block_index]

        def stat_step(k_index, carry):
            running_max, running_sum = carry
            k_first = k_index * BLOCK
            scores = block_scores(
                q_block,
                lax.dynamic_slice_in_dim(keys_orig, k_first, BLOCK),
                q_first,
                k_first,
                seq_ids,
                score_scale,
            )
            new_max = jnp.maximum(running_max, jnp.max(scores, axis=-1))
            terms = jnp.where(scores > MASKED, jnp.exp(scores - new_max[..., None]), 0.0)
            running_sum = running_sum * jnp.exp(running_max - new_max) + jnp.sum(terms, axis=-1)
            return (new_max, running_sum)

        start_stats = (
            jnp.full((key_value_resident, query_per_key_ratio, BLOCK), MASKED, jnp.float32),
            jnp.zeros((key_value_resident, query_per_key_ratio, BLOCK), jnp.float32),
        )
        top_value, total_value = lax.fori_loop(lowest, block_index + 1, stat_step, start_stats)
        log_total = top_value + jnp.log(total_value)

        def value_step(k_index, accum):
            k_first = k_index * BLOCK
            scores = block_scores(
                q_block,
                lax.dynamic_slice_in_dim(keys_orig, k_first, BLOCK),
                q_first,
                k_first,
                seq_ids,
                score_scale,
            )
            probs = jnp.exp(scores - log_total[..., None]).astype(jnp.bfloat16)
            v_block = lax.dynamic_slice_in_dim(values_orig, k_first, BLOCK)
            return accum + jnp.einsum(
                "lgqk,kld->qlgd", probs, v_block, preferred_element_type=jnp.float32
            )

        attended_block = lax.fori_loop(
            lowest,
            block_index + 1,
            value_step,
            jnp.zeros((BLOCK, key_value_resident, query_per_key_ratio, HEAD_SIZE), jnp.float32),
        )
        return (attended_block.astype(jnp.bfloat16), log_total)

    attended, log_totals = lax.map(attend_block, jnp.arange(block_count, dtype=jnp.int32))
    attended_rows = attended.reshape(
        grouped_row_count, key_value_resident * query_per_key_ratio * HEAD_SIZE
    )
    attn_back, resid_back = (
        lax.all_to_all(attended_rows, "sp", split_axis=0, concat_axis=1, tiled=True),
        lax.all_to_all(resid_cols, "sp", split_axis=0, concat_axis=1, tiled=True),
    )
    branch = jnp.dot(attn_back, output_full, preferred_element_type=jnp.float32)
    middle = resid_back.astype(jnp.float32) + branch
    inv_two = lax.rsqrt(jnp.mean(middle * middle, axis=1, keepdims=True) + NORM_EPS)
    normed_two = middle * inv_two
    act_two = (normed_two * gain_mixer).astype(jnp.bfloat16)
    logits = jnp.dot(act_two, router_full, preferred_element_type=jnp.float32)
    expert_range = jnp.arange(EXPERTS, dtype=jnp.int32)
    route_match = routes[:, :, None] == expert_range[None, None, :]
    picked = jnp.sum(jnp.where(route_match, logits[:, None, :], 0.0), axis=-1)
    gate_probs = jax.nn.softmax(picked, axis=-1)
    pair_experts = routes.reshape(-1)
    pair_hot = (pair_experts[:, None] == expert_range[None, :]).astype(jnp.int32)
    pair_slot = jnp.sum((jnp.cumsum(pair_hot, axis=0) - 1) * pair_hot, axis=1)
    destination = pair_experts * CAP + pair_slot
    source_pair = (
        jnp.full((EXPERTS * CAP,), pair_count, jnp.int32)
        .at[destination]
        .set(jnp.arange(pair_count, dtype=jnp.int32))
    )
    source_token = jnp.where(source_pair < pair_count, source_pair // TOPK, token_row_block)
    padded_act = jnp.concatenate([act_two, jnp.zeros((1, MODEL_WIDTH), jnp.bfloat16)], axis=0)
    outgoing = jnp.take(padded_act, source_token, axis=0).reshape(
        fsdp_count, local_experts, CAP, MODEL_WIDTH
    )
    gate_full, up_full, down_full = (
        lax.all_gather(expert_gate.astype(jnp.bfloat16), "sp", axis=1, tiled=True),
        lax.all_gather(expert_up.astype(jnp.bfloat16), "sp", axis=1, tiled=True),
        lax.all_gather(expert_down.astype(jnp.bfloat16), "sp", axis=2, tiled=True),
    )
    arrived_rows = lax.all_to_all(outgoing, "fsdp", split_axis=0, concat_axis=0, tiled=True)
    gate_part = jnp.einsum(
        "secd,edf->secf", arrived_rows, gate_full, preferred_element_type=jnp.float32
    )
    up_part = jnp.einsum(
        "secd,edf->secf", arrived_rows, up_full, preferred_element_type=jnp.float32
    )
    hidden = (jax.nn.silu(gate_part) * up_part).astype(jnp.bfloat16)
    produced = jnp.einsum(
        "secf,efd->secd", hidden, down_full, preferred_element_type=jnp.float32
    ).astype(jnp.bfloat16)
    coming_back = lax.all_to_all(produced, "fsdp", split_axis=0, concat_axis=0, tiled=True)
    pair_rows = jnp.take(
        coming_back.reshape(EXPERTS * CAP, MODEL_WIDTH), destination, axis=0
    ).reshape(token_row_block, TOPK, MODEL_WIDTH)
    mixture = jnp.sum(gate_probs[:, :, None] * pair_rows.astype(jnp.float32), axis=1)
    layer_out = (middle + mixture).astype(jnp.bfloat16)
    upstream = cotangent.astype(jnp.float32)
    gate_grad = jnp.sum(pair_rows.astype(jnp.float32) * upstream[:, None, :], axis=-1)
    pair_grad = (
        (gate_probs[:, :, None] * upstream[:, None, :])
        .astype(jnp.bfloat16)
        .reshape(pair_count, MODEL_WIDTH)
    )
    padded_pair = jnp.concatenate([pair_grad, jnp.zeros((1, MODEL_WIDTH), jnp.bfloat16)], axis=0)
    grad_outgoing = jnp.take(padded_pair, source_pair, axis=0).reshape(
        fsdp_count, local_experts, CAP, MODEL_WIDTH
    )
    grad_arrived = lax.all_to_all(grad_outgoing, "fsdp", split_axis=0, concat_axis=0, tiled=True)
    hidden_grad = jnp.einsum(
        "secd,efd->secf", grad_arrived, down_full, preferred_element_type=jnp.float32
    )
    sigmoid_gate = jax.nn.sigmoid(gate_part)
    silu_gate = gate_part * sigmoid_gate
    hidden_again = (silu_gate * up_part).astype(jnp.bfloat16)
    grad_down = jnp.einsum(
        "secf,secd->efd", hidden_again, grad_arrived, preferred_element_type=jnp.float32
    )
    grad_gate_pre = (
        hidden_grad * up_part * sigmoid_gate * (1.0 + gate_part * (1.0 - sigmoid_gate))
    ).astype(jnp.bfloat16)
    grad_up_pre = (hidden_grad * silu_gate).astype(jnp.bfloat16)
    grad_gate_w = jnp.einsum(
        "secd,secf->edf", arrived_rows, grad_gate_pre, preferred_element_type=jnp.float32
    )
    grad_up_w = jnp.einsum(
        "secd,secf->edf", arrived_rows, grad_up_pre, preferred_element_type=jnp.float32
    )
    grad_rows = (
        jnp.einsum("secf,edf->secd", grad_gate_pre, gate_full, preferred_element_type=jnp.float32)
        + jnp.einsum("secf,edf->secd", grad_up_pre, up_full, preferred_element_type=jnp.float32)
    ).astype(jnp.bfloat16)
    grad_back = lax.all_to_all(grad_rows, "fsdp", split_axis=0, concat_axis=0, tiled=True)
    grad_pairs = jnp.take(
        grad_back.reshape(EXPERTS * CAP, MODEL_WIDTH), destination, axis=0
    ).reshape(token_row_block, TOPK, MODEL_WIDTH)
    grad_act_moe = jnp.sum(grad_pairs.astype(jnp.float32), axis=1)
    weighted = jnp.sum(gate_probs * gate_grad, axis=1, keepdims=True)
    picked_grad = gate_probs * (gate_grad - weighted)
    logit_grad = jnp.sum(jnp.where(route_match, picked_grad[:, :, None], 0.0), axis=1).astype(
        jnp.bfloat16
    )
    grad_router_w = jnp.einsum("td,te->de", act_two, logit_grad, preferred_element_type=jnp.float32)
    grad_act_two = grad_act_moe + jnp.dot(
        logit_grad, router_full.T, preferred_element_type=jnp.float32
    )
    grad_gain_two = jnp.sum(grad_act_two * normed_two, axis=0)
    scaled_two = grad_act_two * gain_mixer
    grad_middle = upstream + inv_two * (
        scaled_two - normed_two * jnp.mean(scaled_two * normed_two, axis=1, keepdims=True)
    )
    middle_low = grad_middle.astype(jnp.bfloat16)
    grad_output_w = jnp.einsum(
        "tc,td->cd", attn_back, middle_low, preferred_element_type=jnp.float32
    )
    grad_attn = jnp.dot(middle_low, output_full.T, preferred_element_type=jnp.float32).astype(
        jnp.bfloat16
    )
    grad_heads, grad_resid = (
        lax.all_to_all(grad_attn, "sp", split_axis=1, concat_axis=0, tiled=True),
        lax.all_to_all(middle_low, "sp", split_axis=1, concat_axis=0, tiled=True),
    )
    grad_heads_four = grad_heads.reshape(
        grouped_row_count, key_value_resident, query_per_key_ratio, HEAD_SIZE
    )

    def backward_block(block_index, carry):
        grad_query_all, grad_key_all, grad_value_all = carry
        q_first = block_index * BLOCK
        q_block = lax.dynamic_slice_in_dim(query_orig, q_first, BLOCK)
        dout_block = lax.dynamic_slice_in_dim(grad_heads_four, q_first, BLOCK)
        log_block = log_totals[block_index]
        lowest = first_block[block_index]

        def dot_step(k_index, accum):
            k_first = k_index * BLOCK
            scores = block_scores(
                q_block,
                lax.dynamic_slice_in_dim(keys_orig, k_first, BLOCK),
                q_first,
                k_first,
                seq_ids,
                score_scale,
            )
            probs = jnp.exp(scores - log_block[..., None])
            prob_grad = jnp.einsum(
                "qlgd,kld->lgqk",
                dout_block,
                lax.dynamic_slice_in_dim(values_orig, k_first, BLOCK),
                preferred_element_type=jnp.float32,
            )
            return accum + jnp.sum(probs * prob_grad, axis=-1)

        row_dots = lax.fori_loop(
            lowest,
            block_index + 1,
            dot_step,
            jnp.zeros((key_value_resident, query_per_key_ratio, BLOCK), jnp.float32),
        )

        def grad_step(k_index, inner):
            query_grad, key_grad_all, value_grad_all = inner
            k_first = k_index * BLOCK
            k_block = lax.dynamic_slice_in_dim(keys_orig, k_first, BLOCK)
            v_block = lax.dynamic_slice_in_dim(values_orig, k_first, BLOCK)
            scores = block_scores(q_block, k_block, q_first, k_first, seq_ids, score_scale)
            probs = jnp.exp(scores - log_block[..., None])
            prob_grad = jnp.einsum(
                "qlgd,kld->lgqk", dout_block, v_block, preferred_element_type=jnp.float32
            )
            score_grad = (probs * (prob_grad - row_dots[..., None]) * score_scale).astype(
                jnp.bfloat16
            )
            query_grad = query_grad + jnp.einsum(
                "lgqk,kld->qlgd", score_grad, k_block, preferred_element_type=jnp.float32
            )
            key_add = jnp.einsum(
                "lgqk,qlgd->kld", score_grad, q_block, preferred_element_type=jnp.float32
            )
            value_add = jnp.einsum(
                "lgqk,qlgd->kld",
                probs.astype(jnp.bfloat16),
                dout_block,
                preferred_element_type=jnp.float32,
            )
            key_grad_all = lax.dynamic_update_slice_in_dim(
                key_grad_all,
                lax.dynamic_slice_in_dim(key_grad_all, k_first, BLOCK) + key_add,
                k_first,
                0,
            )
            value_grad_all = lax.dynamic_update_slice_in_dim(
                value_grad_all,
                lax.dynamic_slice_in_dim(value_grad_all, k_first, BLOCK) + value_add,
                k_first,
                0,
            )
            return (query_grad, key_grad_all, value_grad_all)

        start_inner = (
            jnp.zeros((BLOCK, key_value_resident, query_per_key_ratio, HEAD_SIZE), jnp.float32),
            grad_key_all,
            grad_value_all,
        )
        query_grad, grad_key_all, grad_value_all = lax.fori_loop(
            lowest, block_index + 1, grad_step, start_inner
        )
        grad_query_all = lax.dynamic_update_slice_in_dim(grad_query_all, query_grad, q_first, 0)
        return (grad_query_all, grad_key_all, grad_value_all)

    start_grads = (
        jnp.zeros(
            (grouped_row_count, key_value_resident, query_per_key_ratio, HEAD_SIZE), jnp.float32
        ),
        jnp.zeros((grouped_row_count, key_value_resident, HEAD_SIZE), jnp.float32),
        jnp.zeros((grouped_row_count, key_value_resident, HEAD_SIZE), jnp.float32),
    )
    grad_query_all, grad_key_all, grad_value_all = lax.fori_loop(
        0, block_count, backward_block, start_grads
    )
    grad_query_rows = apply_rotary(
        grad_query_all.reshape(
            grouped_row_count, key_value_resident * query_per_key_ratio, HEAD_SIZE
        ),
        seq_pos,
        -1.0,
    ).astype(jnp.bfloat16)
    grad_key_rows = apply_rotary(grad_key_all, seq_pos, -1.0).astype(jnp.bfloat16)
    grad_value_rows = grad_value_all.astype(jnp.bfloat16)
    grad_kv_rows = jnp.stack([grad_key_rows, grad_value_rows], axis=2).reshape(
        grouped_row_count, key_value_resident * 2 * HEAD_SIZE
    )
    grad_query_dealt, key_value_gradient_shared, grad_resid_dealt = (
        lax.all_to_all(
            jnp.take(
                grad_query_rows.reshape(
                    grouped_row_count, key_value_resident * query_per_key_ratio * HEAD_SIZE
                ),
                order_row,
                axis=0,
            ),
            "sp",
            split_axis=0,
            concat_axis=1,
            tiled=True,
        ),
        lax.all_to_all(
            jnp.take(grad_kv_rows, order_row, axis=0), "sp", split_axis=0, concat_axis=1, tiled=True
        ),
        lax.all_to_all(
            jnp.take(grad_resid, order_row, axis=0), "sp", split_axis=0, concat_axis=1, tiled=True
        ),
    )
    key_value_gradient_split = key_value_gradient_shared.reshape(
        token_row_block, KEY_VALUE_HEADS, 2, HEAD_SIZE
    )
    key_gradient_shared = key_value_gradient_split[:, :, 0].reshape(
        token_row_block, KEY_VALUE_HEADS * HEAD_SIZE
    )
    value_gradient_shared = key_value_gradient_split[:, :, 1].reshape(
        token_row_block, KEY_VALUE_HEADS * HEAD_SIZE
    )
    grad_act_one = (
        jnp.dot(grad_query_dealt, query_full.T, preferred_element_type=jnp.float32)
        + jnp.dot(key_gradient_shared, key_full.T, preferred_element_type=jnp.float32)
        + jnp.dot(value_gradient_shared, value_full.T, preferred_element_type=jnp.float32)
    )
    grad_query_w = jnp.einsum(
        "td,tc->dc", first_activation, grad_query_dealt, preferred_element_type=jnp.float32
    )
    grad_key_w = jnp.einsum(
        "td,tc->dc", first_activation, key_gradient_shared, preferred_element_type=jnp.float32
    )
    grad_value_w = jnp.einsum(
        "td,tc->dc", first_activation, value_gradient_shared, preferred_element_type=jnp.float32
    )
    grad_gain_one = jnp.sum(grad_act_one * normed_one, axis=0)
    scaled_one = grad_act_one * gain_attend
    tokens_grad = (
        grad_resid_dealt.astype(jnp.float32)
        + inv_one
        * (scaled_one - normed_one * jnp.mean(scaled_one * normed_one, axis=1, keepdims=True))
    ).astype(jnp.bfloat16)
    expert_sums = (
        lax.psum_scatter(
            grad_gate_w.astype(jnp.bfloat16), "sp", scatter_dimension=1, tiled=True
        ).astype(jnp.float32),
        lax.psum_scatter(
            grad_up_w.astype(jnp.bfloat16), "sp", scatter_dimension=1, tiled=True
        ).astype(jnp.float32),
        lax.psum_scatter(
            grad_down.astype(jnp.bfloat16), "sp", scatter_dimension=2, tiled=True
        ).astype(jnp.float32),
    )
    shard_sums = (
        lax.psum_scatter(
            grad_query_w.astype(jnp.bfloat16), "fsdp", scatter_dimension=0, tiled=True
        ).astype(jnp.float32),
        lax.psum_scatter(
            grad_key_w.astype(jnp.bfloat16), "fsdp", scatter_dimension=0, tiled=True
        ).astype(jnp.float32),
        lax.psum_scatter(
            grad_value_w.astype(jnp.bfloat16), "fsdp", scatter_dimension=0, tiled=True
        ).astype(jnp.float32),
        lax.psum_scatter(
            grad_output_w.astype(jnp.bfloat16), "fsdp", scatter_dimension=0, tiled=True
        ).astype(jnp.float32),
        lax.psum_scatter(
            grad_router_w.astype(jnp.bfloat16), "fsdp", scatter_dimension=0, tiled=True
        ).astype(jnp.float32),
        lax.psum_scatter(
            grad_gain_one.astype(jnp.bfloat16), "fsdp", scatter_dimension=0, tiled=True
        ).astype(jnp.float32),
        lax.psum_scatter(
            grad_gain_two.astype(jnp.bfloat16), "fsdp", scatter_dimension=0, tiled=True
        ).astype(jnp.float32),
    )
    summed = (
        lax.psum(shard_sums[0].astype(jnp.bfloat16), "sp").astype(jnp.float32),
        lax.psum(shard_sums[1].astype(jnp.bfloat16), "sp").astype(jnp.float32),
        lax.psum(shard_sums[2].astype(jnp.bfloat16), "sp").astype(jnp.float32),
        lax.psum(shard_sums[3].astype(jnp.bfloat16), "sp").astype(jnp.float32),
        lax.psum(shard_sums[4].astype(jnp.bfloat16), "sp").astype(jnp.float32),
        lax.psum(shard_sums[5].astype(jnp.bfloat16), "sp").astype(jnp.float32),
        lax.psum(shard_sums[6].astype(jnp.bfloat16), "sp").astype(jnp.float32),
    )
    return (
        layer_out,
        tokens_grad,
        summed[0],
        summed[1],
        summed[2],
        summed[3],
        summed[4],
        summed[5],
        summed[6],
        expert_sums[0],
        expert_sums[1],
        expert_sums[2],
    )


def solution(mesh):
    return jax.shard_map(
        body,
        mesh=mesh,
        in_specs=(
            P(("fsdp", "sp"), None),
            P("fsdp", None),
            P("fsdp", None),
            P("fsdp", None),
            P("fsdp", None),
            P("fsdp", None),
            P("fsdp"),
            P("fsdp"),
            P("fsdp", "sp", None),
            P("fsdp", "sp", None),
            P("fsdp", None, "sp"),
            P(("fsdp", "sp"), None),
            P("fsdp", None),
            P("fsdp", None),
            P(("fsdp", "sp"), None),
        ),
        out_specs=(
            P(("fsdp", "sp"), None),
            P(("fsdp", "sp"), None),
            P("fsdp", None),
            P("fsdp", None),
            P("fsdp", None),
            P("fsdp", None),
            P("fsdp", None),
            P("fsdp"),
            P("fsdp"),
            P("fsdp", "sp", None),
            P("fsdp", "sp", None),
            P("fsdp", None, "sp"),
        ),
        check_vma=False,
    )
```

profile of v0, /device:TPU:0, one launch (start us, length us, event | category | flops | bytes accessed | tf_op | source)
XLA Modules:
  0.0 1582.5 jit_solution(1844198928008344579)
XLA Ops:
  39.0 23.7 %all-gather.14.cloned.1.call-done = bf16[1024,512]{1,0:T(8,128)(2,1)} async-done(((bf16[128,512]{1,0:T(8,128)(2,1)}), bf16[1024,512]{1,0:T(8,128)(2,1)}) %all-gather.14.cloned.1.call-update) | async-done | bytes 1048592 | tf_op jit(solution)/shard_map/all_gather | solution.py:94
  151.7 76.6 %while.113 = (s32[]{:T(128)}, bf16[4,512,2,2,64]{1,4,3,2,0:T(8,128)(2,1)}, f32[4,2,2,512]{3,2,1,0:T(2,128)}, s32[4]{0:T(128)S(1)}, s32[4]{0:T(128)S(1)}, /*index...) while((s32[]{:T(128)}, ...), condition=%wide.region_13.15_spmd, body=%wide.region_6.14_spmd.sunk | while | flops 418127872 | bytes 13703111 | solution.py:208
  177.8 11.4 while.118
  233.5 15.5 scatter_custom_fusion.1
  264.0 26.9 %gather_fusion = bf16[6144,1024]{1,0:T(8,128)(2,1)} fusion(bf16[513,1024]{1,0:T(8,128)(2,1)S(1)} %concatenate.48, s32[6144]{0:T(1024)S(1)} %get-tuple-element.1006), kind=kCustom, calls=%fused_computation.8 | custom fusion | bytes 25190400 | tf_op jit(solution)/shard_map/jit(_take)/gather | solution.py:237
  316.8 134.9 %all-to-all-done.5 = bf16[8,4,192,1024]{3,2,1,0:T(8,128)(2,1)} async-done(((bf16[8,4,192,1024]{3,2,1,0:T(8,128)(2,1)}), bf16[8,4,192,1024]{3,2,1,0:T(8,128)(2,1)}, u32[]{:S(2)}, u32[]{:S(2)}) %all-to-all-start.5) | async-done | bytes 12582944 | tf_op jit(solution)/shard_map/all_to_all | solution.py:245
  451.7 13.5 fusion.84
  465.3 17.2 %fusion.73 = (bf16[8,4,192,512]{3,2,0,1:T(8,128)(2,1)}, f32[4,8,192,512]{3,2,1,0:T(8,128)}) fusion(f32[4,8,192,512]{3,2,1,0:T(8,128)} %fusion.84, bf16[4,1024,512]{2,1,0:T(8,128)(2,1)} %all-gather.20.cloned.1.call-done, bf16[8,4,192,1024]{3,2,1,0:T(8,128)(2,1)} %all-to-all-done.5), kind=kOutput, calls=%fused_computation.113 | convolution fusion | flops 6461325312 | bytes 48234496 | tf_op jit(solution)/shard_map/secd,edf->secf/dot_general | solution.py:249
  504.8 140.4 %all_gather.36 = bf16[1024,32]{0,1:T(8,128)(2,1)S(1)} all-gather(bf16[128,32]{0,1:T(8,128)(2,1)S(1)} %convert_element_type.299), channel_id=1, replica_groups=mesh['fsdp'=8,'sp'=4] {'fsdp'}, dimensions={0}, use_global_device_ids=true | all-gather | bytes 73728 | tf_op jit(solution)/shard_map/all_gather | solution.py:96
  646.5 27.1 %gather_fusion.5 = bf16[4096,1024]{1,0:T(8,128)(2,1)} fusion(bf16[6144,1024]{1,0:T(8,128)(2,1)} %bitcast.81, s32[4096]{0:T(1024)S(1)} %broadcast_clamp_fusion.1), kind=kCustom, calls=%fused_computation.1.clone | custom fusion | bytes 16793600 | tf_op jit(solution)/shard_map/jit(_take)/gather | solution.py:257
  691.4 35.2 %gather_fusion.1 = bf16[6144,1024]{1,0:T(8,128)(2,1)} fusion(bf16[4097,1024]{1,0:T(8,128)(2,1)} %concatenate.49, s32[6144]{0:T(1024)S(1)} %get-tuple-element.1005), kind=kCustom, calls=%fused_computation.9 | custom fusion | bytes 25190400 | tf_op jit(solution)/shard_map/jit(_take)/gather | solution.py:270
  744.7 138.1 %all-to-all-done.7 = bf16[8,4,192,1024]{3,2,1,0:T(8,128)(2,1)} async-done(((bf16[8,4,192,1024]{3,2,1,0:T(8,128)(2,1)}), bf16[8,4,192,1024]{3,2,1,0:T(8,128)(2,1)}, u32[]{:S(2)}, u32[]{:S(2)}) %all-to-all-start.7) | async-done | bytes 12582944 | tf_op jit(solution)/shard_map/all_to_all | solution.py:273
  882.8 13.8 bitcast_convert_fusion
  896.8 23.2 %fusion.72 = (bf16[8,4,192,512]{3,2,0,1:T(8,128)(2,1)}, bf16[8,4,192,512]{3,2,0,1:T(8,128)(2,1)}) fusion(f32[4,8,192,512]{3,2,1,0:T(8,128)} %fusion.84, f32[4,8,192,512]{3,2,1,0:T(8,128)} %get-tuple-element.1020, bf16[4,512,1024]{2,1,0:T(8,128)(2,1)} %all-gather.22.cloned.1.call-done, bf16[8,4,192,1024]{3,2,1,0:T(8,128)(2,1)} %all-to-all-done.7), kind=kOutput, calls=%fused_computation.111 | convolution fusion | flops 6483345408 | bytes 54525952 | tf_op jit(solution)/shard_map/secd,efd->secf/dot_general | solution.py:274
  920.0 13.0 bitcast_convert_fusion.1
  933.0 15.1 fusion.92
  948.1 17.0 %fusion.68 = bf16[8,4,192,1024]{3,2,0,1:T(8,128)(2,1)} fusion(f32[4,8,192,1024]{3,2,1,0:T(8,128)} %fusion.92, bf16[8,4,192,512]{3,2,0,1:T(8,128)(2,1)} %get-tuple-element.987, bf16[4,1024,512]{2,1,0:T(8,128)(2,1)S(1)} %copy-done.10), kind=kOutput, calls=%fused_computation.105 | convolution fusion | flops 6455033856 | bytes 48234496 | tf_op jit(solution)/shard_map/secf,edf->secd/dot_general | solution.py:295
  981.7 13.0 bitcast_convert_fusion.2
  994.7 125.5 %all-to-all-done.8 = bf16[8,4,192,1024]{3,2,1,0:T(8,128)(2,1)} async-done(((bf16[8,4,192,1024]{3,2,1,0:T(8,128)(2,1)}), bf16[8,4,192,1024]{3,2,1,0:T(8,128)(2,1)}, u32[]{:S(2)}, u32[]{:S(2)}) %all-to-all-start.8) | async-done | bytes 12582944 | tf_op jit(solution)/shard_map/all_to_all | solution.py:297
  1120.2 27.1 %gather_fusion.6 = bf16[4096,1024]{1,0:T(8,128)(2,1)} fusion(bf16[6144,1024]{1,0:T(8,128)(2,1)} %bitcast.91, s32[4096]{0:T(1024)S(1)} %copy-done.38), kind=kCustom, calls=%fused_computation.7.clone | custom fusion | bytes 16793600 | tf_op jit(solution)/shard_map/jit(_take)/gather | solution.py:298
  1147.4 13.7 convert_reduce_fusion
  1178.0 16.2 %all-to-all-done.11 = bf16[512,4,256]{2,0,1:T(8,128)(2,1)S(1)} async-done(((bf16[512,4,256]{2,0,1:T(8,128)(2,1)}), bf16[512,4,256]{2,0,1:T(8,128)(2,1)S(1)}, u32[]{:S(2)}, u32[]{:S(2)}) %all-to-all-start.11) | async-done | bytes 1048608 | tf_op jit(solution)/shard_map/all_to_all | solution.py:324
  1204.1 101.7 %while.116 = (s32[]{:T(128)}, f32[2048,2,2,64]{0,3,2,1:T(8,128)}, f32[2048,2,64]{0,2,1:T(8,128)S(1)}, f32[2048,2,64]{0,2,1:T(8,128)}, s32[4]{0:T(128)S(1)}, /*in...) while((s32[]{:T(128)}, f32[2048,2,2,64]{0,3,2,1:T(8,128)}, ...), condition=%wide.region_34.37_spmd, body=%wide.region_28.36_spmd.sunk | while | flops 958138368 | bytes 35648528 | solution.py:422
  1232.9 21.2 %while.120 = (s32[]{:T(128)}, f32[512,2,2,64]{0,3,2,1:T(8,128)S(1)}, f32[2048,2,64]{0,2,1:T(8,128)S(1)}, f32[2048,2,64]{0,2,1:T(8,128)}, s32[]{:T(128)}, /*index...) while((s32[]{:T(128)}, f32[512,2,2,64]{0,3,2,1:T(8,128)S(1)}, ...), condition=%wide.region_33.35_spmd, body=%wide.region_32.34_spmd.sunk | while | flops 683672576 | bytes 23240948 | solution.py:409
  1283.7 21.2 %while.120 = (s32[]{:T(128)}, f32[512,2,2,64]{0,3,2,1:T(8,128)S(1)}, f32[2048,2,64]{0,2,1:T(8,128)S(1)}, f32[2048,2,64]{0,2,1:T(8,128)}, s32[]{:T(128)}, /*index...) while((s32[]{:T(128)}, f32[512,2,2,64]{0,3,2,1:T(8,128)S(1)}, ...), condition=%wide.region_33.35_spmd, body=%wide.region_32.34_spmd.sunk | while | flops 683672576 | bytes 23240948 | solution.py:409
  1343.7 29.0 %all_to_all.189 = bf16[4,512,256]{1,2,0:T(8,128)(2,1)S(1)} all-to-all(bf16[4,512,256]{1,2,0:T(8,128)(2,1)S(1)} %copy.189), channel_id=1, replica_groups=mesh['fsdp'=8,'sp'=4] {'sp'}, dimensions={0} | all-to-all | bytes 2097152 | tf_op jit(solution)/shard_map/all_to_all | solution.py:451
  1381.9 22.5 %all-to-all-done.12 = bf16[4,512,256]{1,2,0:T(8,128)(2,1)S(1)} async-done(((bf16[4,512,256]{1,2,0:T(8,128)(2,1)}), bf16[4,512,256]{1,2,0:T(8,128)(2,1)S(1)}, u32[]{:S(2)}, u32[]{:S(2)}) %all-to-all-start.12) | async-done | bytes 1048608 | tf_op jit(solution)/shard_map/all_to_all | solution.py:438
  1436.7 39.4 %reduce-scatter.15.cloned.1.call-done = bf16[128,512]{1,0:T(8,128)(2,1)} async-done(((bf16[1024,512]{1,0:T(8,128)(2,1)}), bf16[128,512]{1,0:T(8,128)(2,1)}) %reduce-scatter.15.cloned.1.call-update) | async-done | bytes 131088 | tf_op jit(solution)/shard_map/reduce_scatter | solution.py:506
  1476.1 44.8 %reduce-scatter.11.cloned.1.call-done = bf16[128,1024]{1,0:T(8,128)(2,1)} async-done(((bf16[1024,1024]{1,0:T(8,128)(2,1)}), bf16[128,1024]{1,0:T(8,128)(2,1)}) %reduce-scatter.11.cloned.1.call-update) | async-done | bytes 262160 | tf_op jit(solution)/shard_map/reduce_scatter | solution.py:500
  1521.4 12.7 all-reduce.4
  1534.2 12.7 all-reduce.5
  1551.7 17.2 %all-reduce.9.cloned.1.call-done = (bf16[128,1024]{1,0:T(8,128)(2,1)}, bf16[128,512]{1,0:T(8,128)(2,1)}, bf16[128,512]{1,0:T(8,128)(2,1)}, bf16[128,1024]{1,0:T(8,128)(2,1)}) async-done(((bf16[128,1024]{1,0:T(8,128)(2,1)}, bf16[128,512]{1,0:T(8,128)(2,1)}, bf16[128,512]{1,0:T(8,128)(2,1)}, bf16[128,1024]{1,0:T(8,128)(2,1)}), (bf16[128,1024]{1,0:T(8,128)(2,1)}, bf16[128,512]{1,0:T(8,128)(2,1)}, ...) | async-done | bytes 786448 | tf_op jit(solution)/shard_map/psum | solution.py:523
  (583 shorter events, 565.4 us)
Async XLA Ops:
  7.2 29.6 %all-gather.12.cloned.1.call-start = ((), (), s32[]{:S(2)}) async-start(), calls=%async_computation.23 | async-start | bytes 1179648 | tf_op jit(solution)/shard_map/all_gather | solution.py:93
  8.9 53.8 %all-gather.14.cloned.1.call-start = ((), (), s32[]{:S(2)}) async-start(), calls=%async_computation.24 | async-start | bytes 1179648 | tf_op jit(solution)/shard_map/all_gather | solution.py:94
  10.6 82.5 %all-gather.10.cloned.1.call-start = ((), (), s32[]{:S(2)}) async-start(), calls=%async_computation.22 | async-start | bytes 2359296 | tf_op jit(solution)/shard_map/all_gather | solution.py:92
  12.4 239.8 %all-gather.16.cloned.1.call-start = ((), (), s32[]{:S(2)}) async-start(), calls=%async_computation.25 | async-start | bytes 2359296 | tf_op jit(solution)/shard_map/all_gather | solution.py:95
  16.7 49.2 %all-to-all-start = ((bf16[512,4,256]{2,0,1:T(8,128)(2,1)}), bf16[512,4,256]{2,0,1:T(8,128)(2,1)S(1)}, u32[]{:S(2)}, u32[]{:S(2)}) async-start(bf16[512,4,256]{2,0,1:T(8,128)(2,1)} %bitcast.374), calls=%async_computation | async-start | bytes 2097152 | tf_op jit(solution)/shard_map/all_to_all | solution.py:135
  23.1 293.7 %all-gather.18.cloned.1.call-start = ((), (), s32[]{:S(2)}) async-start(), calls=%async_computation.26 | async-start | bytes 5242880 | tf_op jit(solution)/shard_map/all_gather | solution.py:241
  65.9 31.7 %all-to-all-start.3 = ((bf16[512,4,256]{0,2,1:T(8,128)(2,1)}), bf16[512,4,256]{0,2,1:T(8,128)(2,1)}, u32[]{:S(2)}, u32[]{:S(2)}) async-start(bf16[512,4,256]{0,2,1:T(8,128)(2,1)} %bitcast.57), calls=%async_computation.3 | async-start | bytes 2097152 | tf_op jit(solution)/shard_map/all_to_all | solution.py:134
  79.6 182.8 %copy-start.42 = (f32[8,1,128]{2,1,0:T(1,128)}, f32[8,1,128]{2,1,0:T(1,128)S(1)}, u32[]{:S(2)}) copy-start(f32[8,1,128]{2,1,0:T(1,128)S(1)} %convert_element_type.356) | copy-start | bytes 12292
  97.5 33.5 %all-to-all-start.2 = ((bf16[512,4,256]{0,2,1:T(8,128)(2,1)}), bf16[512,4,256]{0,2,1:T(8,128)(2,1)S(1)}, u32[]{:S(2)}, u32[]{:S(2)}) async-start(bf16[512,4,256]{0,2,1:T(8,128)(2,1)} %bitcast.47), calls=%async_computation.2 | async-start | bytes 2097152 | tf_op jit(solution)/shard_map/all_to_all | solution.py:127
  145.8 82.6 %all-to-all-start.1 = ((bf16[4,512,256]{2,1,0:T(8,128)(2,1)}), bf16[4,512,256]{2,1,0:T(8,128)(2,1)}, u32[]{:S(2)}, u32[]{:S(2)}) async-start(bf16[4,512,256]{2,1,0:T(8,128)(2,1)} %bitcast.40), calls=%async_computation.1 | async-start | bytes 2097152 | tf_op jit(solution)/shard_map/all_to_all | solution.py:214
  228.3 30.1 %all-to-all-start.4 = ((bf16[4,512,256]{1,2,0:T(8,128)(2,1)}), bf16[4,512,256]{1,2,0:T(8,128)(2,1)S(1)}, u32[]{:S(2)}, u32[]{:S(2)}) async-start(bf16[4,512,256]{1,2,0:T(8,128)(2,1)} %bitcast.479), calls=%async_computation.4 | async-start | bytes 2097152 | tf_op jit(solution)/shard_map/all_to_all | solution.py:213
  301.7 150.0 %all-to-all-start.5 = ((bf16[8,4,192,1024]{3,2,1,0:T(8,128)(2,1)}), bf16[8,4,192,1024]{3,2,1,0:T(8,128)(2,1)}, u32[]{:S(2)}, u32[]{:S(2)}) async-start(bf16[8,4,192,1024]{3,2,1,0:T(8,128)(2,1)} %broadcast_select_fusion.1), calls=%async_computation.5 | async-start | bytes 25165824 | tf_op jit(solution)/shard_map/all_to_all | solution.py:245
  312.6 152.7 %all-gather.20.cloned.1.call-start = ((), (), s32[]{:S(2)}) async-start(), calls=%async_computation.27 | async-start | bytes 5242880 | tf_op jit(solution)/shard_map/all_gather | solution.py:242
  313.8 168.7 %all-gather.22.cloned.1.call-start = ((), (), s32[]{:S(2)}) async-start(), calls=%async_computation.28 | async-start | bytes 5242880 | tf_op jit(solution)/shard_map/all_gather | solution.py:243
  497.8 147.5 %copy-start.34 = (s32[4096]{0:T(1024)S(1)}, s32[4096]{0:T(1024)}, u32[]{:S(2)}) copy-start(s32[4096]{0:T(1024)} %copy-done.33) | copy-start | bytes 49156
  497.8 148.7 %all-to-all-start.6 = ((bf16[8,4,192,1024]{3,2,1,0:T(8,128)(2,1)}), bf16[8,4,192,1024]{3,2,1,0:T(8,128)(2,1)}, u32[]{:S(2)}, u32[]{:S(2)}) async-start(bf16[8,4,192,1024]{3,2,1,0:T(8,128)(2,1)} %copy.175), calls=%async_computation.6 | async-start | bytes 25165824 | tf_op jit(solution)/shard_map/all_to_all | solution.py:256
  503.2 143.1 %copy-start.36 = (s32[512,8]{0,1:T(8,128)S(1)}, s32[512,8]{0,1:T(8,128)}, u32[]{:S(2)}) copy-start(s32[512,8]{0,1:T(8,128)} %param.42) | copy-start | bytes 49156
  737.4 145.4 %all-to-all-start.7 = ((bf16[8,4,192,1024]{3,2,1,0:T(8,128)(2,1)}), bf16[8,4,192,1024]{3,2,1,0:T(8,128)(2,1)}, u32[]{:S(2)}, u32[]{:S(2)}) async-start(bf16[8,4,192,1024]{3,2,1,0:T(8,128)(2,1)} %broadcast_select_fusion), calls=%async_computation.7 | async-start | bytes 25165824 | tf_op jit(solution)/shard_map/all_to_all | solution.py:273
  742.7 669.4 %reduce-scatter.25.cloned.1.call-start = ((), (), s32[]{:S(2)}) async-start(), calls=%async_computation.36 | async-start | bytes 294912
  744.6 668.4 %reduce-scatter.23.cloned.1.call-start = ((), (), s32[]{:S(2)}) async-start(), calls=%async_computation.35 | async-start | bytes 5242880 | tf_op jit(solution)/shard_map/reduce_scatter | solution.py:495
  896.6 519.2 %reduce-scatter.21.cloned.1.call-start = ((), (), s32[]{:S(2)}) async-start(), calls=%async_computation.34 | async-start | bytes 5242880 | tf_op jit(solution)/shard_map/reduce_scatter | solution.py:492
  975.8 144.4 %all-to-all-start.8 = ((bf16[8,4,192,1024]{3,2,1,0:T(8,128)(2,1)}), bf16[8,4,192,1024]{3,2,1,0:T(8,128)(2,1)}, u32[]{:S(2)}, u32[]{:S(2)}) async-start(bf16[8,4,192,1024]{3,2,1,0:T(8,128)(2,1)} %copy.178), calls=%async_computation.8 | async-start | bytes 25165824 | tf_op jit(solution)/shard_map/all_to_all | solution.py:297
  981.2 437.4 %reduce-scatter.19.cloned.1.call-start = ((), (), s32[]{:S(2)}) async-start(), calls=%async_computation.33 | async-start | bytes 5242880 | tf_op jit(solution)/shard_map/reduce_scatter | solution.py:489
  1166.7 27.5 %all-to-all-start.11 = ((bf16[512,4,256]{2,0,1:T(8,128)(2,1)}), bf16[512,4,256]{2,0,1:T(8,128)(2,1)S(1)}, u32[]{:S(2)}, u32[]{:S(2)}) async-start(bf16[512,4,256]{2,0,1:T(8,128)(2,1)} %bitcast.372), calls=%async_computation.11 | async-start | bytes 2097152 | tf_op jit(solution)/shard_map/all_to_all | solution.py:324
  1171.4 256.3 %reduce-scatter.17.cloned.1.call-start = ((), (), s32[]{:S(2)}) async-start(), calls=%async_computation.32 | async-start | bytes 2359296 | tf_op jit(solution)/shard_map/reduce_scatter | solution.py:509
  1194.2 135.3 %all-to-all-start.9 = ((bf16[512,4,256]{2,0,1:T(8,128)(2,1)}), bf16[512,4,256]{2,0,1:T(8,128)(2,1)}, u32[]{:S(2)}, u32[]{:S(2)}) async-start(bf16[512,4,256]{2,0,1:T(8,128)(2,1)} %bitcast.373), calls=%async_computation.9 | async-start | bytes 2097152 | tf_op jit(solution)/shard_map/all_to_all | solution.py:325
  1198.5 238.3 %reduce-scatter.13.cloned.1.call-start = ((), (), s32[]{:S(2)}) async-start(), calls=%async_computation.30 | async-start | bytes 1179648 | tf_op jit(solution)/shard_map/reduce_scatter | solution.py:503
  1376.1 28.3 %all-to-all-start.12 = ((bf16[4,512,256]{1,2,0:T(8,128)(2,1)}), bf16[4,512,256]{1,2,0:T(8,128)(2,1)S(1)}, u32[]{:S(2)}, u32[]{:S(2)}) async-start(bf16[4,512,256]{1,2,0:T(8,128)(2,1)} %copy.186), calls=%async_computation.12 | async-start | bytes 2097152 | tf_op jit(solution)/shard_map/all_to_all | solution.py:438
  1379.8 96.3 %reduce-scatter.15.cloned.1.call-start = ((), (), s32[]{:S(2)}) async-start(), calls=%async_computation.31 | async-start | bytes 1179648 | tf_op jit(solution)/shard_map/reduce_scatter | solution.py:506
  1381.9 139.0 %reduce-scatter.11.cloned.1.call-start = ((), (), s32[]{:S(2)}) async-start(), calls=%async_computation.29 | async-start | bytes 2359296 | tf_op jit(solution)/shard_map/reduce_scatter | solution.py:500
  1407.3 113.7 %all-to-all-start.10 = ((bf16[4,512,256]{2,1,0:T(8,128)(2,1)}), bf16[4,512,256]{2,1,0:T(8,128)(2,1)S(1)}, u32[]{:S(2)}, u32[]{:S(2)}) async-start(bf16[4,512,256]{2,1,0:T(8,128)(2,1)} %bitcast.95), calls=%async_computation.10 | async-start | bytes 2097152 | tf_op jit(solution)/shard_map/all_to_all | solution.py:454
  1410.8 158.1 %all-reduce.9.cloned.1.call-start = ((), (), s32[]{:S(2)}) async-start(), calls=%async_computation.37 | async-start | bytes 1572864 | tf_op jit(solution)/shard_map/psum | solution.py:523
  (63 other events, 1299.3 us)
Sparse Core Ops, SparseCore 0:
  10.5 26.2 all-gather.11
  39.2 23.4 all-gather.13
  65.2 27.8 all-gather.9
  95.4 27.9 all-gather.15
  125.4 103.0 all-gather.17
  315.3 83.5 all-gather.19
  401.0 79.0 all-gather.21
  746.6 70.0 reduce-scatter.24
  896.7 76.0 reduce-scatter.22
  975.0 77.2 reduce-scatter.20
  1054.6 77.2 reduce-scatter.18
  1178.1 40.8 reduce-scatter.16
  1374.9 61.7 reduce-scatter.12
  1440.1 36.0 reduce-scatter.14
  1479.6 41.2 reduce-scatter.10
  1523.4 45.4 all-reduce.8
where the time goes:
time: 1590 us; the launch traced here: 1580 us
  waiting for transfers between devices  582 us (37%)
  local copies, waits for them, and re-layouts  268 us (17%)
  matrix products  249 us (16%)
  blocking collectives  212 us (13%)
  other arithmetic  130 us (8%)
  starting transfers between devices  70.9 us (4%)
  loops' own time  54.3 us (3%)
  between operations  16 us (1%)
    all_gather x1, blocking collectives, body(): lax.all_gather(router_weight.astype(jnp.bfloat16), 'fsdp', axis=0, tiled=...  140 us
    all_to_all x1, waiting for transfers between devices, body(): lax.all_to_all(grad_outgoing, 'fsdp', split_axis=0, concat_axis=0, tiled=...  138 us
    all_to_all x1, waiting for transfers between devices, body(): lax.all_to_all(outgoing, 'fsdp', split_axis=0, concat_axis=0, tiled=True)  135 us
    all_to_all x1, waiting for transfers between devices, body(): lax.all_to_all(grad_rows, 'fsdp', split_axis=0, concat_axis=0, tiled=True)  126 us
    reduce_scatter x1, waiting for transfers between devices, body(): lax.psum_scatter(grad_query_w.astype(jnp.bfloat16), 'fsdp', scatter_dimen...  44.8 us
    reduce_scatter x1, waiting for transfers between devices, body(): lax.psum_scatter(grad_value_w.astype(jnp.bfloat16), 'fsdp', scatter_dimen...  39.4 us
    gather x1, local copies, waits for them, and re-layouts, body(): jnp.take(padded_pair, source_pair, axis=0)  35.2 us
  transfers between devices with their start and end apart: 29, of which 13 were waited for; matrix products, arithmetic and copies ran while one was open for 33% of the time, Pallas kernels for 0%

commit v1 on v0

--- a/solution.py
+++ b/solution.py
@@ -3,6 +3,8 @@
 import jax
 import jax.numpy as jnp
 from jax import lax
+from jax.experimental import pallas as pl
+from jax.experimental.pallas import tpu as pltpu
 from jax.sharding import PartitionSpec as P
 
 MODEL_WIDTH = 1024
@@ -18,6 +20,7 @@
 NORM_EPS = 1e-06
 ROPE_BASE = 10000.0
 MASKED = -1e30
+VMEM_LIMIT = 60 * 1024 * 1024
 
 
 def apply_rotary(values, places, direction):
@@ -58,6 +61,246 @@
     k_seqs = lax.dynamic_slice_in_dim(seq_ids, k_first, span)
     allowed = (k_places[None, :] <= q_places[:, None]) & (k_seqs[None, :] == q_seqs[:, None])
     return jnp.where(allowed, raw_scores, MASKED)
+
+
+def contract(left, right, left_dim, right_dim):
+    return lax.dot_general(
+        left, right, (((left_dim,), (right_dim,)), ((), ())), preferred_element_type=jnp.float32
+    )
+
+
+def axis_bits(count):
+    bits = [1 << place for place in range(count.bit_length() - 1)]
+    return bits[::-1]
+
+
+def flip(values, axis_name, bit):
+    count = lax.axis_size(axis_name)
+    return lax.ppermute(values, axis_name, [(place, place ^ bit) for place in range(count)])
+
+
+def gather_rows(values, axis_name):
+    count = lax.axis_size(axis_name)
+    high, low = axis_bits(count), []
+    if count > 2:
+        low = high[1:2] + high[:1] + high[2:]
+        orders = (high, low)
+    else:
+        orders = (high, high)
+    half = values.shape[1] // 2
+    halves = []
+    for order, part in zip(orders, (values[:, :half], values[:, half:])):
+        pieces = {0: part}
+        for bit in order:
+            pieces.update({r ^ bit: flip(piece, axis_name, bit) for r, piece in list(pieces.items())})
+        halves.append(jnp.stack([pieces[r] for r in range(count)]))
+    return jnp.concatenate(halves, axis=2)
+
+
+def reduce_rows(values, axis_name):
+    count = lax.axis_size(axis_name)
+    high = axis_bits(count)
+    if count > 2:
+        orders = (high[::-1], high[2:][::-1] + high[:1] + high[1:2])
+    else:
+        orders = (high, high)
+    half = values.shape[2] // 2
+    sums = []
+    for order, part in zip(orders, (values[:, :, :half], values[:, :, half:])):
+        kept, pieces = list(range(count)), part
+        for bit in order:
+            stay = [i for i, r in enumerate(kept) if not r & bit]
+            leave = [kept.index(kept[i] ^ bit) for i in stay]
+            arrived = flip(jnp.stack([pieces[i] for i in leave]), axis_name, bit)
+            pieces = (
+                jnp.stack([pieces[i] for i in stay]).astype(jnp.float32) + arrived.astype(jnp.float32)
+            ).astype(jnp.bfloat16)
+            kept = [kept[i] for i in stay]
+        sums.append(pieces[0])
+    return jnp.concatenate(sums, axis=1).astype(jnp.float32)
+
+
+def expert_step(
+    slot_ref,
+    share_ref,
+    act_ref,
+    cot_ref,
+    gate_ref,
+    up_ref,
+    down_ref,
+    mixed_ref,
+    back_ref,
+    share_grad_ref,
+    gate_grad_ref,
+    up_grad_ref,
+    down_grad_ref,
+    act_rows,
+    hidden_rows,
+    down_rows,
+    gate_rows,
+    up_rows,
+):
+    sources, rows, width = act_ref.shape
+    shards, shard_width = down_ref.shape[0], down_ref.shape[3]
+    hidden_width = gate_ref.shape[3]
+    gate_w = gate_ref[...].reshape(width, hidden_width)
+    up_w = up_ref[...].reshape(width, hidden_width)
+    picked, cots, shares, masks = [], [], [], []
+    for source in range(sources):
+        mask = lax.broadcasted_iota(jnp.int32, (CAP, rows), 0) == slot_ref[0, source]
+        choose = jnp.where(mask, 1.0, 0.0).astype(jnp.bfloat16)
+        picked.append(contract(choose, act_ref[source], 1, 0).astype(jnp.bfloat16))
+        cots.append(contract(choose, cot_ref[source], 1, 0))
+        shares.append(
+            jnp.sum(jnp.where(mask, share_ref[0, source], 0.0), axis=1, keepdims=True)
+        )
+        masks.append(mask)
+    act = jnp.concatenate(picked, 0)
+    cot = jnp.concatenate(cots, 0)
+    share = jnp.concatenate(shares, 0)
+    gate_pre = contract(act, gate_w, 1, 0)
+    up_pre = contract(act, up_w, 1, 0)
+    sigmoid = 1.0 / (1.0 + jnp.exp(-gate_pre))
+    silu = gate_pre * sigmoid
+    hidden = (silu * up_pre).astype(jnp.bfloat16)
+    made = jnp.concatenate(
+        [contract(hidden, down_ref[shard, 0], 1, 0) for shard in range(shards)], axis=1
+    )
+    made = made.astype(jnp.bfloat16).astype(jnp.float32)
+    share_grad = jnp.sum(made * cot, axis=1, keepdims=True)
+    mixed = (made * share).astype(jnp.bfloat16)
+    made_grad = (share * cot).astype(jnp.bfloat16)
+    hidden_grad = sum(
+        contract(
+            made_grad[:, shard * shard_width : (shard + 1) * shard_width], down_ref[shard, 0], 1, 1
+        )
+        for shard in range(shards)
+    )
+    up_grad = (hidden_grad * silu).astype(jnp.bfloat16)
+    gate_grad = (
+        hidden_grad * up_pre * sigmoid * (1.0 + gate_pre * (1.0 - sigmoid))
+    ).astype(jnp.bfloat16)
+    back = (contract(gate_grad, gate_w, 1, 1) + contract(up_grad, up_w, 1, 1)).astype(jnp.bfloat16)
+    for source in range(sources):
+        part = slice(source * CAP, (source + 1) * CAP)
+        mixed_ref[0, source] = mixed[part]
+        back_ref[0, source] = back[part]
+        share_grad_ref[0, source] = jnp.sum(
+            jnp.where(masks[source], share_grad[part], 0.0), axis=0, keepdims=True
+        )
+    step = pl.program_id(1)
+    here = pl.ds(pl.multiple_of(step * sources * CAP, sources * CAP), sources * CAP)
+    act_rows[here, :] = act
+    hidden_rows[here, :] = hidden
+    down_rows[here, :] = made_grad
+    gate_rows[here, :] = gate_grad
+    up_rows[here, :] = up_grad
+
+    @pl.when(step == pl.num_programs(1) - 1)
+    def _():
+        gate_sum = contract(act_rows[...], gate_rows[...], 0, 0)
+        gate_grad_ref[...] = gate_sum.astype(jnp.bfloat16).reshape(gate_grad_ref.shape)
+        up_sum = contract(act_rows[...], up_rows[...], 0, 0)
+        up_grad_ref[...] = up_sum.astype(jnp.bfloat16).reshape(up_grad_ref.shape)
+        for shard in range(shards):
+            cols = slice(shard * shard_width, (shard + 1) * shard_width)
+            down_grad_ref[shard, 0] = contract(
+                hidden_rows[...], down_rows[:, cols], 0, 0
+            ).astype(jnp.bfloat16)
+
+
+def run_experts(slots, shares, act_all, cot_all, gate_all, up_all, down_all):
+    experts, sources, rows = slots.shape
+    width = act_all.shape[2]
+    shards, _, gate_shard, hidden_width = gate_all.shape
+    down_shard = down_all.shape[3]
+    pair = 2
+    listed = sources * CAP
+
+    def by_source(*shape):
+        return pl.BlockSpec((1, pair) + shape, lambda e, s: (e, s) + (0,) * len(shape))
+
+    def rows_of(*shape):
+        return pl.BlockSpec((pair,) + shape, lambda e, s: (s,) + (0,) * len(shape))
+
+    def weight_of(*shape):
+        return pl.BlockSpec((shards, 1) + shape, lambda e, s: (0, e) + (0,) * len(shape))
+
+    low = jnp.bfloat16
+    outs = pl.pallas_call(
+        expert_step,
+        grid=(experts, sources // pair),
+        in_specs=[
+            by_source(1, rows),
+            by_source(1, rows),
+            rows_of(rows, width),
+            rows_of(rows, width),
+            weight_of(gate_shard, hidden_width),
+            weight_of(gate_shard, hidden_width),
+            weight_of(hidden_width, down_shard),
+        ],
+        out_specs=[
+            by_source(CAP, width),
+            by_source(CAP, width),
+            by_source(1, rows),
+            weight_of(gate_shard, hidden_width),
+            weight_of(gate_shard, hidden_width),
+            weight_of(hidden_width, down_shard),
+        ],
+        out_shape=[
+            jax.ShapeDtypeStruct((experts, sources, CAP, width), low),
+            jax.ShapeDtypeStruct((experts, sources, CAP, width), low),
+            jax.ShapeDtypeStruct((experts, sources, 1, rows), jnp.float32),
+            jax.ShapeDtypeStruct(gate_all.shape, low),
+            jax.ShapeDtypeStruct(up_all.shape, low),
+            jax.ShapeDtypeStruct(down_all.shape, low),
+        ],
+        scratch_shapes=[
+            pltpu.VMEM((listed, width), low),
+            pltpu.VMEM((listed, hidden_width), low),
+            pltpu.VMEM((listed, width), low),
+            pltpu.VMEM((listed, hidden_width), low),
+            pltpu.VMEM((listed, hidden_width), low),
+        ],
+        compiler_params=pltpu.CompilerParams(
+            dimension_semantics=("arbitrary", "arbitrary"), vmem_limit_bytes=VMEM_LIMIT
+        ),
+        name="experts",
+    )(slots[:, :, None], shares[:, :, None], act_all, cot_all, gate_all, up_all, down_all)
+    return (outs[0], outs[1], outs[2][:, :, 0], outs[3], outs[4], outs[5])
+
+
+def combine_step(slot_ref, mixed_ref, back_ref, mixture_ref, act_grad_ref):
+    experts, _, _, width = mixed_ref.shape
+    rows = mixture_ref.shape[1]
+    place = lax.broadcasted_iota(jnp.int32, (rows, experts * CAP), 1)
+    hit = None
+    for expert in range(experts):
+        slot = slot_ref[0, :, expert : expert + 1]
+        match = place == jnp.where(slot >= 0, slot + expert * CAP, -1)
+        hit = match if hit is None else hit | match
+    choose = jnp.where(hit, 1.0, 0.0).astype(jnp.bfloat16)
+    for source, target in ((mixed_ref, mixture_ref), (back_ref, act_grad_ref)):
+        listed = source[:, 0].reshape(experts * CAP, width)
+        target[0] = contract(choose, listed, 1, 0).astype(jnp.bfloat16)
+
+
+def combine_rows(slots_by_row, mixed_rows, back_rows):
+    sources, rows, experts = slots_by_row.shape
+    width = mixed_rows.shape[3]
+    listed = pl.BlockSpec((experts, 1, CAP, width), lambda s: (0, s, 0, 0))
+    dense = pl.BlockSpec((1, rows, width), lambda s: (s, 0, 0))
+    return pl.pallas_call(
+        combine_step,
+        grid=(sources,),
+        in_specs=[pl.BlockSpec((1, rows, experts), lambda s: (s, 0, 0)), listed, listed],
+        out_specs=[dense, dense],
+        out_shape=[jax.ShapeDtypeStruct((sources, rows, width), jnp.bfloat16)] * 2,
+        compiler_params=pltpu.CompilerParams(
+            dimension_semantics=("arbitrary",), vmem_limit_bytes=VMEM_LIMIT
+        ),
+        name="combine",
+    )(slots_by_row, mixed_rows, back_rows)
 
 
 def body(
@@ -220,90 +463,54 @@
     act_two = (normed_two * gain_mixer).astype(jnp.bfloat16)
     logits = jnp.dot(act_two, router_full, preferred_element_type=jnp.float32)
     expert_range = jnp.arange(EXPERTS, dtype=jnp.int32)
-    route_match = routes[:, :, None] == expert_range[None, None, :]
-    picked = jnp.sum(jnp.where(route_match, logits[:, None, :], 0.0), axis=-1)
-    gate_probs = jax.nn.softmax(picked, axis=-1)
-    pair_experts = routes.reshape(-1)
-    pair_hot = (pair_experts[:, None] == expert_range[None, :]).astype(jnp.int32)
-    pair_slot = jnp.sum((jnp.cumsum(pair_hot, axis=0) - 1) * pair_hot, axis=1)
-    destination = pair_experts * CAP + pair_slot
-    source_pair = (
-        jnp.full((EXPERTS * CAP,), pair_count, jnp.int32)
-        .at[destination]
-        .set(jnp.arange(pair_count, dtype=jnp.int32))
-    )
-    source_token = jnp.where(source_pair < pair_count, source_pair // TOPK, token_row_block)
-    padded_act = jnp.concatenate([act_two, jnp.zeros((1, MODEL_WIDTH), jnp.bfloat16)], axis=0)
-    outgoing = jnp.take(padded_act, source_token, axis=0).reshape(
-        fsdp_count, local_experts, CAP, MODEL_WIDTH
-    )
-    gate_full, up_full, down_full = (
-        lax.all_gather(expert_gate.astype(jnp.bfloat16), "sp", axis=1, tiled=True),
-        lax.all_gather(expert_up.astype(jnp.bfloat16), "sp", axis=1, tiled=True),
-        lax.all_gather(expert_down.astype(jnp.bfloat16), "sp", axis=2, tiled=True),
-    )
-    arrived_rows = lax.all_to_all(outgoing, "fsdp", split_axis=0, concat_axis=0, tiled=True)
-    gate_part = jnp.einsum(
-        "secd,edf->secf", arrived_rows, gate_full, preferred_element_type=jnp.float32
-    )
-    up_part = jnp.einsum(
-        "secd,edf->secf", arrived_rows, up_full, preferred_element_type=jnp.float32
-    )
-    hidden = (jax.nn.silu(gate_part) * up_part).astype(jnp.bfloat16)
-    produced = jnp.einsum(
-        "secf,efd->secd", hidden, down_full, preferred_element_type=jnp.float32
-    ).astype(jnp.bfloat16)
-    coming_back = lax.all_to_all(produced, "fsdp", split_axis=0, concat_axis=0, tiled=True)
-    pair_rows = jnp.take(
-        coming_back.reshape(EXPERTS * CAP, MODEL_WIDTH), destination, axis=0
-    ).reshape(token_row_block, TOPK, MODEL_WIDTH)
-    mixture = jnp.sum(gate_probs[:, :, None] * pair_rows.astype(jnp.float32), axis=1)
+    member = jnp.any(routes[:, :, None] == expert_range[None, None, :], axis=1)
+    row_range = jnp.arange(token_row_block, dtype=jnp.int32)
+    upto = (row_range[:, None] <= row_range[None, :]).astype(jnp.bfloat16)
+    member_rows = member.T.astype(jnp.bfloat16)
+    rank = jnp.dot(member_rows, upto, preferred_element_type=jnp.float32).astype(jnp.int32) - 1
+    slots = jnp.where(member.T, rank, -1)
+    relative = lax.axis_index("fsdp") ^ jnp.arange(fsdp_count, dtype=jnp.int32)
+
+    def to_experts(by_expert):
+        arrived = lax.all_to_all(
+            by_expert.reshape(fsdp_count, local_experts, token_row_block),
+            "fsdp",
+            split_axis=0,
+            concat_axis=0,
+            tiled=True,
+        )
+        return jnp.swapaxes(jnp.take(arrived, relative, axis=0), 0, 1)
+
+    slots_here = to_experts(slots)
+    gate_dense = jax.nn.softmax(jnp.where(member, logits, -jnp.inf), axis=-1)
+    gates_here = to_experts(gate_dense.T)
+    gate_all, up_all, down_all = (
+        lax.all_gather(expert_gate.astype(jnp.bfloat16), "sp", axis=0, tiled=False),
+        lax.all_gather(expert_up.astype(jnp.bfloat16), "sp", axis=0, tiled=False),
+        lax.all_gather(expert_down.astype(jnp.bfloat16), "sp", axis=0, tiled=False),
+    )
+    cotangent_all = gather_rows(cotangent, "fsdp")
+    act_all = gather_rows(act_two, "fsdp")
+    mixed_rows, back_rows, gate_grads, grad_gate_w, grad_up_w, grad_down = run_experts(
+        slots_here, gates_here, act_all, cotangent_all, gate_all, up_all, down_all
+    )
+    mixture_parts, act_grad_parts = combine_rows(
+        jnp.transpose(slots_here, (1, 2, 0)), mixed_rows, back_rows
+    )
+    grad_act_moe = reduce_rows(act_grad_parts, "fsdp")
+    mixture = reduce_rows(mixture_parts, "fsdp")
     layer_out = (middle + mixture).astype(jnp.bfloat16)
     upstream = cotangent.astype(jnp.float32)
-    gate_grad = jnp.sum(pair_rows.astype(jnp.float32) * upstream[:, None, :], axis=-1)
-    pair_grad = (
-        (gate_probs[:, :, None] * upstream[:, None, :])
-        .astype(jnp.bfloat16)
-        .reshape(pair_count, MODEL_WIDTH)
-    )
-    padded_pair = jnp.concatenate([pair_grad, jnp.zeros((1, MODEL_WIDTH), jnp.bfloat16)], axis=0)
-    grad_outgoing = jnp.take(padded_pair, source_pair, axis=0).reshape(
-        fsdp_count, local_experts, CAP, MODEL_WIDTH
-    )
-    grad_arrived = lax.all_to_all(grad_outgoing, "fsdp", split_axis=0, concat_axis=0, tiled=True)
-    hidden_grad = jnp.einsum(
-        "secd,efd->secf", grad_arrived, down_full, preferred_element_type=jnp.float32
-    )
-    sigmoid_gate = jax.nn.sigmoid(gate_part)
-    silu_gate = gate_part * sigmoid_gate
-    hidden_again = (silu_gate * up_part).astype(jnp.bfloat16)
-    grad_down = jnp.einsum(
-        "secf,secd->efd", hidden_again, grad_arrived, preferred_element_type=jnp.float32
-    )
-    grad_gate_pre = (
-        hidden_grad * up_part * sigmoid_gate * (1.0 + gate_part * (1.0 - sigmoid_gate))
-    ).astype(jnp.bfloat16)
-    grad_up_pre = (hidden_grad * silu_gate).astype(jnp.bfloat16)
-    grad_gate_w = jnp.einsum(
-        "secd,secf->edf", arrived_rows, grad_gate_pre, preferred_element_type=jnp.float32
-    )
-    grad_up_w = jnp.einsum(
-        "secd,secf->edf", arrived_rows, grad_up_pre, preferred_element_type=jnp.float32
-    )
-    grad_rows = (
-        jnp.einsum("secf,edf->secd", grad_gate_pre, gate_full, preferred_element_type=jnp.float32)
-        + jnp.einsum("secf,edf->secd", grad_up_pre, up_full, preferred_element_type=jnp.float32)
-    ).astype(jnp.bfloat16)
-    grad_back = lax.all_to_all(grad_rows, "fsdp", split_axis=0, concat_axis=0, tiled=True)
-    grad_pairs = jnp.take(
-        grad_back.reshape(EXPERTS * CAP, MODEL_WIDTH), destination, axis=0
-    ).reshape(token_row_block, TOPK, MODEL_WIDTH)
-    grad_act_moe = jnp.sum(grad_pairs.astype(jnp.float32), axis=1)
-    weighted = jnp.sum(gate_probs * gate_grad, axis=1, keepdims=True)
-    picked_grad = gate_probs * (gate_grad - weighted)
-    logit_grad = jnp.sum(jnp.where(route_match, picked_grad[:, :, None], 0.0), axis=1).astype(
-        jnp.bfloat16
-    )
+    gate_grad_back = lax.all_to_all(
+        jnp.take(jnp.swapaxes(gate_grads, 0, 1), relative, axis=0),
+        "fsdp",
+        split_axis=0,
+        concat_axis=0,
+        tiled=True,
+    )
+    gate_grad = gate_grad_back.reshape(EXPERTS, token_row_block).T
+    weighted = jnp.sum(gate_dense * gate_grad, axis=1, keepdims=True)
+    logit_grad = (gate_dense * (gate_grad - weighted)).astype(jnp.bfloat16)
     grad_router_w = jnp.einsum("td,te->de", act_two, logit_grad, preferred_element_type=jnp.float32)
     grad_act_two = grad_act_moe + jnp.dot(
         logit_grad, router_full.T, preferred_element_type=jnp.float32
@@ -485,16 +692,9 @@
         + inv_one
         * (scaled_one - normed_one * jnp.mean(scaled_one * normed_one, axis=1, keepdims=True))
     ).astype(jnp.bfloat16)
-    expert_sums = (
-        lax.psum_scatter(
-            grad_gate_w.astype(jnp.bfloat16), "sp", scatter_dimension=1, tiled=True
-        ).astype(jnp.float32),
-        lax.psum_scatter(
-            grad_up_w.astype(jnp.bfloat16), "sp", scatter_dimension=1, tiled=True
-        ).astype(jnp.float32),
-        lax.psum_scatter(
-            grad_down.astype(jnp.bfloat16), "sp", scatter_dimension=2, tiled=True
-        ).astype(jnp.float32),
+    expert_sums = tuple(
+        lax.psum_scatter(grads, "sp", scatter_dimension=0, tiled=False).astype(jnp.float32)
+        for grads in (grad_gate_w, grad_up_w, grad_down)
     )
     shard_sums = (
         lax.psum_scatter(

time: 1590 us -> 1330 us (0.84)
  matrix products: 249 us -> 115 us
  Pallas kernels: 0 us -> 111 us
  blocking collectives: 212 us -> 107 us
  local copies, waits for them, and re-layouts: 268 us -> 175 us
  waiting for transfers between devices: 582 us -> 538 us
  other arithmetic: 130 us -> 114 us
    all_to_all x4 -> x3, waiting for transfers between devices: 399 us -> 7.59 us  [the longest x2 6.17 us: to_experts(): lax.all_to_all(by_expert.reshape(fsdp_count, local_experts, token_row_blo...]
    reduce_scatter x3, waiting for transfers between devices: 0.03 us -> 233 us  [body(): lax.psum_scatter(grads, 'sp', scatter_dimension=0, tiled=False)]
    dot_general x9 -> x1, matrix products: 136 us -> 0.2 us  [body(): jnp.dot(member_rows, upto, preferred_element_type=jnp.float32)]
    all_gather x1, blocking collectives: 140 us -> 9.75 us  [body(): lax.all_gather(router_weight.astype(jnp.bfloat16), 'fsdp', axis=0, tiled=...]
    gather x4, local copies, waits for them, and re-layouts: 116 us -> 3.98 us  [the longest x3 3.27 us: to_experts(): return jnp.swapaxes(jnp.take(arrived, relative, axis=0), 0, 1)]
    pallas_call x0 -> x2, Pallas kernels: none -> 111 us  [the longest x1 87.6 us: run_experts(): pl.pallas_call(expert_step, grid=(experts, sources // pair), in_specs=[by...]
    ppermute x0 -> x40, waiting for transfers between devices: none -> 71.5 us  [flip(): lax.ppermute(values, axis_name, [(place, place ^ bit) for place in range(...]
    unnamed x138 -> x166, local copies, waits for them, and re-layouts: 5.63 us -> 47.5 us
  transfers between devices with their start and end apart: 29 -> 68, of which waited for: 13 -> 21; matrix products, arithmetic and copies ran while one was open for 33% -> 29% of each run, Pallas kernels for 0% -> 0%
where the time goes in v1:
time: 1330 us; the launch traced here: 1320 us
  waiting for transfers between devices  538 us (40%)
  local copies, waits for them, and re-layouts  175 us (13%)
  matrix products  115 us (9%)
  other arithmetic  114 us (9%)
  Pallas kernels  111 us (8%)
  blocking collectives  107 us (8%)
  starting transfers between devices  84.5 us (6%)
  loops' own time  54.3 us (4%)
  between operations  16.3 us (1%)
    reduce_scatter x3, waiting for transfers between devices, body(): lax.psum_scatter(grads, 'sp', scatter_dimension=0, tiled=False)  233 us
    pallas_call x1, Pallas kernels, run_experts(): pl.pallas_call(expert_step, grid=(experts, sources // pair), in_specs=[by...  87.6 us
    ppermute x40, waiting for transfers between devices, flip(): lax.ppermute(values, axis_name, [(place, place ^ bit) for place in range(...  71.5 us
    unnamed x166, local copies, waits for them, and re-layouts  47.5 us
    psum x1, waiting for transfers between devices, body(): lax.psum(shard_sums[0].astype(jnp.bfloat16), 'sp').astype(jnp.float32)  44.9 us
    reduce_scatter x1, waiting for transfers between devices, body(): lax.psum_scatter(grad_query_w.astype(jnp.bfloat16), 'fsdp', scatter_dimen...  43.5 us
    unnamed x1, blocking collectives  36.8 us
    all_to_all x1, waiting for transfers between devices, body(): lax.all_to_all(attended_rows, 'sp', split_axis=0, concat_axis=1, tiled=True)  33.3 us
  transfers between devices with their start and end apart: 68, of which 21 were waited for; matrix products, arithmetic and copies ran while one was open for 29% of the time, Pallas kernels for 0%

profile of v1, /device:TPU:0, one launch (start us, length us, event | category | flops | bytes accessed | tf_op | source)
XLA Modules:
  0.0 1315.5 jit_solution(10298653007255196979)
XLA Ops:
  43.1 10.2 all-gather.3
  63.9 9.7 all_gather.45
  122.3 11.1 all-to-all-done.3
  160.5 9.1 gather_fusion.3
  169.6 20.7 %all-to-all-done.2 = bf16[512,4,256]{0,2,1:T(8,128)(2,1)S(1)} async-done(((bf16[512,4,256]{0,2,1:T(8,128)(2,1)}), bf16[512,4,256]{0,2,1:T(8,128)(2,1)S(1)}, u32[]{:S(2)}, u32[]{:S(2)}) %all-to-all-start.2) | async-done | bytes 1048608 | tf_op jit(solution)/shard_map/all_to_all | solution.py:370
  209.9 74.3 %while.113 = (s32[]{:T(128)}, bf16[4,512,2,2,64]{1,4,3,2,0:T(8,128)(2,1)}, f32[4,2,2,512]{3,2,1,0:T(2,128)S(1)}, s32[4]{0:T(128)S(1)}, s32[4]{0:T(128)S(1)}, /*i...) while((s32[]{:T(128)}, ...), condition=%wide.region_13.15_spmd, body=%wide.region_6.14_spmd.sunk | while | flops 418127872 | bytes 13703611 | solution.py:451
  234.9 11.4 while.118
  272.0 11.4 while.118
  305.7 33.3 %all-to-all-done.4 = bf16[4,512,256]{1,2,0:T(8,128)(2,1)S(1)} async-done(((bf16[4,512,256]{1,2,0:T(8,128)(2,1)}), bf16[4,512,256]{1,2,0:T(8,128)(2,1)S(1)}, u32[]{:S(2)}, u32[]{:S(2)}) %all-to-all-start.4) | async-done | bytes 1048608 | tf_op jit(solution)/shard_map/all_to_all | solution.py:456
  346.0 13.7 %all-to-all-start.6 = ((f32[8,4,512]{2,1,0:T(4,128)}), f32[8,4,512]{2,1,0:T(4,128)S(1)}, u32[]{:S(2)}, u32[]{:S(2)}) async-start(f32[8,4,512]{2,1,0:T(4,128)} %reshape.449), calls=%async_computation.6 | async-start | bytes 131072 | tf_op jit(solution)/shard_map/all_to_all | solution.py:475
  411.9 24.3 %all-gather.25.cloned.1.call-done = bf16[16,512,256]{2,1,0:T(8,128)(2,1)} async-done(((bf16[4,512,256]{2,1,0:T(8,128)(2,1)}), bf16[16,512,256]{2,1,0:T(8,128)(2,1)}) %all-gather.25.cloned.1.call-update) | async-done | bytes 4194320 | tf_op jit(solution)/shard_map/all_gather | solution.py:490
  436.3 87.6 %experts.1 = (bf16[4,8,192,1024]{3,2,1,0:T(8,128)(2,1)}, bf16[4,8,192,1024]{3,2,1,0:T(8,128)(2,1)}, f32[4,8,1,512]{3,2,1,0:T(1,128)}, bf16[4,4,256,512]{3,2,1,0:...) custom-call(s32[4,8,1,512]{3,2,1,0:T(1,128)} %copy.149.slot_ref, ...), custom_call_target="tpu_custom_call" | custom-call | tf_op jit(solution)/shard_map/experts/pallas_call | solution.py:230
  523.9 23.5 %combine.1 = (bf16[8,512,1024]{2,1,0:T(8,128)(2,1)}, bf16[8,512,1024]{2,1,0:T(8,128)(2,1)}) custom-call(s32[8,512,4]{2,1,0:T(8,128)} %get-tuple-element.1036.slot_ref, bf16[4,8,192,1024]{3,2,1,0:T(8,128)(2,1)} %get-tuple-element.772.mixed_ref, bf16[4,8,192,1024]{3,2,1,0:T(8,128)(2,1)} %get-tuple-element.773.back_ref), custom_call_target="tpu_custom_call" | custom-call | tf_op jit(solution)/shard_map/combine/pallas_call | solution.py:293
  587.3 14.1 %collective-permute-done.29 = bf16[2,512,512]{2,1,0:T(8,128)(2,1)S(1)} collective-permute-done((bf16[2,512,512]{2,1,0:T(8,128)(2,1)S(1)}, bf16[2,512,512]{2,1,0:T(8,128)(2,1)S(1)}, u32[]{:S(2)}, u32[]{:S(2)}) %collective-permute-start.29) | collective-permute-done | bytes 1048608 | tf_op jit(solution)/shard_map/ppermute | solution.py:79
  602.4 20.2 %collective-permute-done.35 = bf16[2,512,512]{2,1,0:T(8,128)(2,1)S(1)} collective-permute-done((bf16[2,512,512]{2,1,0:T(8,128)(2,1)S(1)}, bf16[2,512,512]{2,1,0:T(8,128)(2,1)S(1)}, u32[]{:S(2)}, u32[]{:S(2)}) %collective-permute-start.35) | collective-permute-done | bytes 1048608 | tf_op jit(solution)/shard_map/ppermute | solution.py:79
  632.6 20.0 %collective-permute-done.36 = bf16[1,512,512]{2,1,0:T(8,128)(2,1)S(1)} collective-permute-done((bf16[1,512,512]{2,1,0:T(8,128)(2,1)S(1)}, bf16[1,512,512]{2,1,0:T(8,128)(2,1)S(1)}, u32[]{:S(2)}, u32[]{:S(2)}) %collective-permute-start.36) | collective-permute-done | bytes 524320 | tf_op jit(solution)/shard_map/ppermute | solution.py:79
  673.4 15.4 %all-to-all-done.10 = bf16[512,4,256]{2,0,1:T(8,128)(2,1)} async-done(((bf16[512,4,256]{2,0,1:T(8,128)(2,1)}), bf16[512,4,256]{2,0,1:T(8,128)(2,1)}, u32[]{:S(2)}, u32[]{:S(2)}) %all-to-all-start.10) | async-done | bytes 1048608 | tf_op jit(solution)/shard_map/all_to_all | solution.py:531
  699.5 103.5 %while.116 = (s32[]{:T(128)}, f32[2048,2,2,64]{0,3,2,1:T(8,128)}, f32[2048,2,64]{0,2,1:T(8,128)S(1)}, f32[2048,2,64]{0,2,1:T(8,128)}, s32[4]{0:T(128)S(1)}, /*in...) while((s32[]{:T(128)}, f32[2048,2,2,64]{0,3,2,1:T(8,128)}, ...), condition=%wide.region_26.29_spmd, body=%wide.region_20.28_spmd.sunk | while | flops 958138368 | bytes 35648504 | solution.py:629
  706.3 11.2 while.120
  728.8 21.7 %while.120 = (s32[]{:T(128)}, f32[512,2,2,64]{0,3,2,1:T(8,128)S(1)}, f32[2048,2,64]{0,2,1:T(8,128)S(1)}, f32[2048,2,64]{0,2,1:T(8,128)}, s32[]{:T(128)}, /*index...) while((s32[]{:T(128)}, f32[512,2,2,64]{0,3,2,1:T(8,128)S(1)}, ...), condition=%wide.region_25.27_spmd, body=%wide.region_24.26_spmd.sunk | while | flops 683672576 | bytes 23240948 | solution.py:616
  758.1 11.2 while.120
  780.5 21.7 %while.120 = (s32[]{:T(128)}, f32[512,2,2,64]{0,3,2,1:T(8,128)S(1)}, f32[2048,2,64]{0,2,1:T(8,128)S(1)}, f32[2048,2,64]{0,2,1:T(8,128)}, s32[]{:T(128)}, /*index...) while((s32[]{:T(128)}, f32[512,2,2,64]{0,3,2,1:T(8,128)S(1)}, ...), condition=%wide.region_25.27_spmd, body=%wide.region_24.26_spmd.sunk | while | flops 683672576 | bytes 23240948 | solution.py:616
  827.9 10.0 gather_fusion.6
  841.0 29.6 %all_to_all.184 = bf16[4,512,256]{1,2,0:T(8,128)(2,1)S(1)} all-to-all(bf16[4,512,256]{1,2,0:T(8,128)(2,1)S(1)} %copy.159), channel_id=1, replica_groups=mesh['fsdp'=8,'sp'=4] {'sp'}, dimensions={0} | all-to-all | bytes 2097152 | tf_op jit(solution)/shard_map/all_to_all | solution.py:658
  879.8 22.5 %all-to-all-done.11 = bf16[4,512,256]{1,2,0:T(8,128)(2,1)S(1)} async-done(((bf16[4,512,256]{1,2,0:T(8,128)(2,1)}), bf16[4,512,256]{1,2,0:T(8,128)(2,1)S(1)}, u32[]{:S(2)}, u32[]{:S(2)}) %all-to-all-start.11) | async-done | bytes 1048608 | tf_op jit(solution)/shard_map/all_to_all | solution.py:645
  918.3 36.8 %all-reduce.2 = (bf16[1024]{0:T(1024)(128)(2,1)S(1)}, bf16[1024]{0:T(1024)(128)(2,1)S(1)}) all-reduce(bf16[1024]{0:T(1024)(128)(2,1)S(1)} %get-tuple-element.844, bf16[1024]{0:T(1024)(128)(2,1)S(1)} %copy-done.53), channel_id=10, replica_groups=mesh['fsdp'=8,'sp'=4] {'fsdp'}, use_global_device_ids=true, to_apply=%region_39.42.clone | all-reduce | flops 2048 | bytes 8192
  955.3 12.1 all-reduce.3
  972.3 43.5 %reduce-scatter.11.cloned.1.call-done = bf16[128,1024]{1,0:T(8,128)(2,1)} async-done(((bf16[1024,1024]{1,0:T(8,128)(2,1)}), bf16[128,1024]{1,0:T(8,128)(2,1)}) %reduce-scatter.11.cloned.1.call-update) | async-done | bytes 262160 | tf_op jit(solution)/shard_map/reduce_scatter | solution.py:700
  1015.8 79.2 %reduce-scatter.23.cloned.1.call-done = bf16[1,4,512,256]{3,2,1,0:T(8,128)(2,1)} async-done(((bf16[4,4,512,256]{3,2,1,0:T(8,128)(2,1)}), bf16[1,4,512,256]{3,2,1,0:T(8,128)(2,1)}) %reduce-scatter.23.cloned.1.call-update) | async-done | bytes 1048592 | tf_op jit(solution)/shard_map/reduce_scatter | solution.py:696
  1097.7 76.7 %reduce-scatter.21.cloned.1.call-done = bf16[1,4,256,512]{3,2,1,0:T(8,128)(2,1)} async-done(((bf16[4,4,256,512]{3,2,1,0:T(8,128)(2,1)}), bf16[1,4,256,512]{3,2,1,0:T(8,128)(2,1)}) %reduce-scatter.21.cloned.1.call-update) | async-done | bytes 1048592 | tf_op jit(solution)/shard_map/reduce_scatter | solution.py:696
  1177.3 76.7 %reduce-scatter.19.cloned.1.call-done = bf16[1,4,256,512]{3,2,1,0:T(8,128)(2,1)} async-done(((bf16[4,4,256,512]{3,2,1,0:T(8,128)(2,1)}), bf16[1,4,256,512]{3,2,1,0:T(8,128)(2,1)}) %reduce-scatter.19.cloned.1.call-update) | async-done | bytes 1048592 | tf_op jit(solution)/shard_map/reduce_scatter | solution.py:696
  1256.8 44.9 %all-reduce.7.cloned.1.call-done = (bf16[128,1024]{1,0:T(8,128)(2,1)}, bf16[128,512]{1,0:T(8,128)(2,1)}, bf16[128,512]{1,0:T(8,128)(2,1)}, bf16[128,1024]{1,0:T(8,128)(2,1)}) async-done(((bf16[128,1024]{1,0:T(8,128)(2,1)}, bf16[128,512]{1,0:T(8,128)(2,1)}, bf16[128,512]{1,0:T(8,128)(2,1)}, bf16[128,1024]{1,0:T(8,128)(2,1)}), (bf16[128,1024]{1,0:T(8,128)(2,1)}, bf16[128,512]{1,0:T(8,128)(2,1)}, ...) | async-done | bytes 786448 | tf_op jit(solution)/shard_map/psum | solution.py:723
  (698 shorter events, 549.1 us)
Async XLA Ops:
  7.2 81.7 %all-gather.15.cloned.1.call-start = ((), (), s32[]{:S(2)}) async-start(), calls=%async_computation.22 | async-start | bytes 1179648 | tf_op jit(solution)/shard_map/all_gather | solution.py:336
  9.0 82.8 %all-gather.17.cloned.1.call-start = ((), (), s32[]{:S(2)}) async-start(), calls=%async_computation.23 | async-start | bytes 1179648 | tf_op jit(solution)/shard_map/all_gather | solution.py:337
  10.7 105.5 %all-gather.13.cloned.1.call-start = ((), (), s32[]{:S(2)}) async-start(), calls=%async_computation.21 | async-start | bytes 2359296 | tf_op jit(solution)/shard_map/all_gather | solution.py:335
  12.6 293.1 %all-gather.19.cloned.1.call-start = ((), (), s32[]{:S(2)}) async-start(), calls=%async_computation.24 | async-start | bytes 2359296 | tf_op jit(solution)/shard_map/all_gather | solution.py:338
  13.4 398.5 %all-gather.21.cloned.1.call-start = ((), (), s32[]{:S(2)}) async-start(), calls=%async_computation.32 | async-start | bytes 5242880 | tf_op jit(solution)/shard_map/all_gather | solution.py:488
  14.7 397.2 %all-gather.23.cloned.1.call-start = ((), (), s32[]{:S(2)}) async-start(), calls=%async_computation.33 | async-start | bytes 5242880 | tf_op jit(solution)/shard_map/all_gather | solution.py:489
  18.6 76.4 %collective-permute-start.14 = (bf16[512,512]{1,0:T(8,128)(2,1)}, bf16[512,512]{1,0:T(8,128)(2,1)}, u32[]{:S(2)}, u32[]{:S(2)}) collective-permute-start(bf16[512,512]{1,0:T(8,128)(2,1)} %get-tuple-element.1053), channel_id=1, source_target_pairs={{0,4},{4,0},{8,12},{12,8},{16,20},{20,16},{24,28},{28,24},{1,5},{5... | collective-permute-start | bytes 1572872 | tf_op jit(solution)/shard_map/ppermute | solution.py:79
  19.1 76.7 %collective-permute-start.15 = (bf16[512,512]{1,0:T(8,128)(2,1)}, bf16[512,512]{1,0:T(8,128)(2,1)}, u32[]{:S(2)}, u32[]{:S(2)}) collective-permute-start(bf16[512,512]{1,0:T(8,128)(2,1)} %get-tuple-element.1053), channel_id=1, source_target_pairs={{0,8},{4,12},{8,0},{12,4},{16,24},{20,28},{24,16},{28,20},{1,9},{5... | collective-permute-start | bytes 1572872 | tf_op jit(solution)/shard_map/ppermute | solution.py:79
  21.6 74.2 %collective-permute-start.17 = (bf16[512,512]{1,0:T(8,128)(2,1)}, bf16[512,512]{1,0:T(8,128)(2,1)}, u32[]{:S(2)}, u32[]{:S(2)}) collective-permute-start(bf16[512,512]{1,0:T(8,128)(2,1)} %get-tuple-element.1053), channel_id=1, source_target_pairs={{0,16},{4,20},{8,24},{12,28},{16,0},{20,4},{24,8},{28,12},{1,17},{... | collective-permute-start | bytes 1572872 | tf_op jit(solution)/shard_map/ppermute | solution.py:79
  23.1 88.7 %collective-permute-start.22 = (bf16[512,512]{1,0:T(8,128)(2,1)}, bf16[512,512]{1,0:T(8,128)(2,1)}, u32[]{:S(2)}, u32[]{:S(2)}) collective-permute-start(bf16[512,512]{1,0:T(8,128)(2,1)} %get-tuple-element.1054), channel_id=1, source_target_pairs={{0,8},{4,12},{8,0},{12,4},{16,24},{20,28},{24,16},{28,20},{1,9},{5... | collective-permute-start | bytes 1572872 | tf_op jit(solution)/shard_map/ppermute | solution.py:79
  23.6 88.9 %collective-permute-start.21 = (bf16[512,512]{1,0:T(8,128)(2,1)}, bf16[512,512]{1,0:T(8,128)(2,1)}, u32[]{:S(2)}, u32[]{:S(2)}) collective-permute-start(bf16[512,512]{1,0:T(8,128)(2,1)} %get-tuple-element.1054), channel_id=1, source_target_pairs={{0,4},{4,0},{8,12},{12,8},{16,20},{20,16},{24,28},{28,24},{1,5},{5... | collective-permute-start | bytes 1572872 | tf_op jit(solution)/shard_map/ppermute | solution.py:79
  25.2 48.5 %all-to-all-start.5 = ((s32[8,4,512]{2,1,0:T(4,128)}), s32[8,4,512]{2,1,0:T(4,128)S(1)}, u32[]{:S(2)}, u32[]{:S(2)}) async-start(s32[8,4,512]{2,1,0:T(4,128)} %reshape.448), calls=%async_computation.5 | async-start | bytes 131072 | tf_op jit(solution)/shard_map/all_to_all | solution.py:475
  28.6 407.7 %all-gather.25.cloned.1.call-start = ((), (), s32[]{:S(2)}) async-start(), calls=%async_computation.34 | async-start | bytes 5242880 | tf_op jit(solution)/shard_map/all_gather | solution.py:490
  95.7 45.2 %collective-permute-start.18 = (bf16[512,512]{1,0:T(8,128)(2,1)}, bf16[512,512]{1,0:T(8,128)(2,1)}, u32[]{:S(2)}, u32[]{:S(2)}) collective-permute-start(bf16[512,512]{1,0:T(8,128)(2,1)} %collective-permute-done.17), channel_id=1, source_target_pairs={{0,4},{4,0},{8,12},{12,8},{16,20},{20,16},{24,28},{28,24},{1,5},{5... | collective-permute-start | bytes 1572872 | tf_op jit(solution)/shard_map/ppermute | solution.py:79
  133.4 56.8 %all-to-all-start.2 = ((bf16[512,4,256]{0,2,1:T(8,128)(2,1)}), bf16[512,4,256]{0,2,1:T(8,128)(2,1)S(1)}, u32[]{:S(2)}, u32[]{:S(2)}) async-start(bf16[512,4,256]{0,2,1:T(8,128)(2,1)} %bitcast.47), calls=%async_computation.2 | async-start | bytes 2097152 | tf_op jit(solution)/shard_map/all_to_all | solution.py:370
  141.0 150.1 %collective-permute-start.20 = (bf16[512,512]{1,0:T(8,128)(2,1)}, bf16[512,512]{1,0:T(8,128)(2,1)}, u32[]{:S(2)}, u32[]{:S(2)}) collective-permute-start(bf16[512,512]{1,0:T(8,128)(2,1)} %collective-permute-done.19), channel_id=1, source_target_pairs={{0,4},{4,0},{8,12},{12,8},{16,20},{20,16},{24,28},{28,24},{1,5},{5... | collective-permute-start | bytes 1572872 | tf_op jit(solution)/shard_map/ppermute | solution.py:79
  144.8 148.1 %collective-permute-start.27 = (bf16[512,512]{1,0:T(8,128)(2,1)}, bf16[512,512]{1,0:T(8,128)(2,1)}, u32[]{:S(2)}, u32[]{:S(2)}) collective-permute-start(bf16[512,512]{1,0:T(8,128)(2,1)} %collective-permute-done.26), channel_id=1, source_target_pairs={{0,4},{4,0},{8,12},{12,8},{16,20},{20,16},{24,28},{28,24},{1,5},{5... | collective-permute-start | bytes 1572872 | tf_op jit(solution)/shard_map/ppermute | solution.py:79
  205.6 78.6 %all-to-all-start.1 = ((bf16[4,512,256]{2,1,0:T(8,128)(2,1)}), bf16[4,512,256]{2,1,0:T(8,128)(2,1)}, u32[]{:S(2)}, u32[]{:S(2)}) async-start(bf16[4,512,256]{2,1,0:T(8,128)(2,1)} %bitcast.40), calls=%async_computation.1 | async-start | bytes 2097152 | tf_op jit(solution)/shard_map/all_to_all | solution.py:457
  284.2 54.7 %all-to-all-start.4 = ((bf16[4,512,256]{1,2,0:T(8,128)(2,1)}), bf16[4,512,256]{1,2,0:T(8,128)(2,1)S(1)}, u32[]{:S(2)}, u32[]{:S(2)}) async-start(bf16[4,512,256]{1,2,0:T(8,128)(2,1)} %bitcast.484), calls=%async_computation.4 | async-start | bytes 2097152 | tf_op jit(solution)/shard_map/all_to_all | solution.py:456
  586.4 45.1 %collective-permute-start.32 = (bf16[2,512,512]{2,1,0:T(8,128)(2,1)S(1)}, bf16[2,512,512]{2,1,0:T(8,128)(2,1)S(1)}, u32[]{:S(2)}, u32[]{:S(2)}) collective-permute-start(bf16[2,512,512]{2,1,0:T(8,128)(2,1)S(1)} %stack.224), channel_id=1, source_target_pairs={{0,16},{4,20},{8,24},{12,28},{16,0},{20,4},{24,8},{28,12},{1,17},{... | collective-permute-start | bytes 3145736 | tf_op jit(solution)/shard_map/ppermute | solution.py:79
  601.8 52.5 %collective-permute-start.30 = (bf16[1,512,512]{2,1,0:T(8,128)(2,1)S(1)}, bf16[1,512,512]{2,1,0:T(8,128)(2,1)S(1)}, u32[]{:S(2)}, u32[]{:S(2)}) collective-permute-start(bf16[1,512,512]{2,1,0:T(8,128)(2,1)S(1)} %slice.339), channel_id=1, source_target_pairs={{0,16},{4,20},{8,24},{12,28},{16,0},{20,4},{24,8},{28,12},{1,17},{... | collective-permute-start | bytes 1572872 | tf_op jit(solution)/shard_map/ppermute | solution.py:79
  663.8 248.9 %reduce-scatter.25.cloned.1.call-start = ((), (), s32[]{:S(2)}) async-start(), calls=%async_computation.35 | async-start | bytes 294912
  668.1 304.2 %reduce-scatter.17.cloned.1.call-start = ((), (), s32[]{:S(2)}) async-start(), calls=%async_computation.28 | async-start | bytes 2359296 | tf_op jit(solution)/shard_map/reduce_scatter | solution.py:709
  688.8 139.1 %all-to-all-start.8 = ((bf16[512,4,256]{2,0,1:T(8,128)(2,1)}), bf16[512,4,256]{2,0,1:T(8,128)(2,1)}, u32[]{:S(2)}, u32[]{:S(2)}) async-start(bf16[512,4,256]{2,0,1:T(8,128)(2,1)} %bitcast.377), calls=%async_computation.8 | async-start | bytes 2097152 | tf_op jit(solution)/shard_map/all_to_all | solution.py:532
  693.1 279.3 %reduce-scatter.13.cloned.1.call-start = ((), (), s32[]{:S(2)}) async-start(), calls=%async_computation.26 | async-start | bytes 1179648 | tf_op jit(solution)/shard_map/reduce_scatter | solution.py:703
  877.5 94.8 %reduce-scatter.15.cloned.1.call-start = ((), (), s32[]{:S(2)}) async-start(), calls=%async_computation.27 | async-start | bytes 1179648 | tf_op jit(solution)/shard_map/reduce_scatter | solution.py:706
  879.7 136.1 %reduce-scatter.11.cloned.1.call-start = ((), (), s32[]{:S(2)}) async-start(), calls=%async_computation.25 | async-start | bytes 2359296 | tf_op jit(solution)/shard_map/reduce_scatter | solution.py:700
  905.1 189.9 %reduce-scatter.23.cloned.1.call-start = ((), (), s32[]{:S(2)}) async-start(), calls=%async_computation.31 | async-start | bytes 5242880 | tf_op jit(solution)/shard_map/reduce_scatter | solution.py:696
  905.9 268.6 %reduce-scatter.21.cloned.1.call-start = ((), (), s32[]{:S(2)}) async-start(), calls=%async_computation.30 | async-start | bytes 5242880 | tf_op jit(solution)/shard_map/reduce_scatter | solution.py:696
  906.4 347.6 %reduce-scatter.19.cloned.1.call-start = ((), (), s32[]{:S(2)}) async-start(), calls=%async_computation.29 | async-start | bytes 5242880 | tf_op jit(solution)/shard_map/reduce_scatter | solution.py:696
  907.0 62.0 %all-to-all-start.9 = ((bf16[4,512,256]{2,1,0:T(8,128)(2,1)}), bf16[4,512,256]{2,1,0:T(8,128)(2,1)}, u32[]{:S(2)}, u32[]{:S(2)}) async-start(bf16[4,512,256]{2,1,0:T(8,128)(2,1)} %bitcast.119), calls=%async_computation.9 | async-start | bytes 2097152 | tf_op jit(solution)/shard_map/all_to_all | solution.py:661
  911.5 390.2 %all-reduce.7.cloned.1.call-start = ((), (), s32[]{:S(2)}) async-start(), calls=%async_computation.36 | async-start | bytes 1572864 | tf_op jit(solution)/shard_map/psum | solution.py:723
  (103 other events, 1370.4 us)
Sparse Core Ops, SparseCore 0:
  10.5 30.3 all-gather.14
  43.3 23.4 all-gather.16
  69.3 28.4 all-gather.12
  99.5 31.9 all-gather.18
  133.0 119.8 all-gather.20
  254.3 101.0 all-gather.22
  357.0 79.1 all-gather.24
  668.2 34.3 reduce-scatter.24
  706.8 41.2 reduce-scatter.16
  872.8 58.8 reduce-scatter.12
  934.8 35.9 reduce-scatter.14
  974.6 41.1 reduce-scatter.10
  1018.2 76.7 reduce-scatter.22
  1097.2 77.2 reduce-scatter.20
  1176.7 77.2 reduce-scatter.18
  1256.5 45.1 all-reduce.6

commit v2 on v1

v2 whole, which is shorter than its diff:
```python
import functools
import math

import jax
import jax.numpy as jnp
from jax import lax
from jax.experimental import pallas as pl
from jax.experimental.pallas import tpu as pltpu
from jax.sharding import PartitionSpec as P

MODEL_WIDTH = 1024
QUERY_HEADS = 16
KEY_VALUE_HEADS = 8
HEAD_SIZE = 64
EXPERTS = 32
SPAN = 256
CAP = 192


NORM_EPS = 1e-06
ROPE_BASE = 10000.0
MASKED = -1e30
VMEM_LIMIT = 60 * 1024 * 1024


def contract(left, right, left_dim, right_dim):
    return lax.dot_general(
        left, right, (((left_dim,), (right_dim,)), ((), ())), preferred_element_type=jnp.float32
    )


def axis_bits(count):
    bits = [1 << place for place in range(count.bit_length() - 1)]
    return bits[::-1]


def flip(values, axis_name, bit):
    count = lax.axis_size(axis_name)
    return lax.ppermute(values, axis_name, [(place, place ^ bit) for place in range(count)])


def stage_orders(count):
    high = axis_bits(count)
    if count <= 2:
        return (high, high)
    return (high, high[1:2] + high[:1] + high[2:])


def gather_pieces(values, axis_name):
    count = lax.axis_size(axis_name)
    half = values.shape[1] // 2
    lists = []
    for order, part in zip(stage_orders(count), (values[:, :half], values[:, half:])):
        pieces = {0: part}
        for bit in order:
            pieces.update({r ^ bit: flip(piece, axis_name, bit) for r, piece in list(pieces.items())})
        lists.append([pieces[r] for r in range(count)])
    return lists


def chunk_place(index, order):
    place = 0
    for bit in order:
        place = place * 2 + (index * 2 // bit) % 2
    return place


def reduce_halves(leave, stay, axis_name):
    count = lax.axis_size(axis_name)
    sums = []
    for order, gone, kept in zip(stage_orders(count), leave, stay):
        for bit in order[::-1]:
            arrived = flip(gone, axis_name, bit).astype(jnp.float32)
            middle = kept.shape[0] // 2
            if middle:
                gone = (kept[middle:].astype(jnp.float32) + arrived[middle:]).astype(jnp.bfloat16)
                kept = (kept[:middle].astype(jnp.float32) + arrived[:middle]).astype(jnp.bfloat16)
            else:
                kept = kept[0].astype(jnp.float32) + arrived[0]
        sums.append(kept)
    return jnp.concatenate(sums, axis=1)


def reduce_rows(values, axis_name):
    count = lax.axis_size(axis_name)
    half = values.shape[2] // 2
    leave, stay = [], []
    for order, part in zip(stage_orders(count), (values[:, :, :half], values[:, :, half:])):
        later = order[:-1][::-1]
        evens = sorted(range(count // 2), key=lambda i: chunk_place(i, later))
        leave.append(jnp.stack([part[2 * i + 1] for i in evens]))
        stay.append(jnp.stack([part[2 * i] for i in evens]))
    return reduce_halves(leave, stay, axis_name)


def pack_expert(gate, up, down):
    rows = gate.shape[0]
    blocks = [down[k * rows : (k + 1) * rows] for k in range(down.shape[0] // rows)]
    return jnp.concatenate([gate, up, jnp.concatenate(blocks, axis=1)], axis=0)


def expert_step(slot_ref, share_ref, weight_ref, *refs, count):
    acts, cots = refs[: 2 * count], refs[2 * count : 4 * count]
    mixed_ref, back_ref, share_grad_ref, weight_grad_ref = refs[4 * count : 4 * count + 4]
    act_buf, cot_buf, arrive, act_rows, hidden_rows, down_rows, gate_rows, up_rows = refs[
        4 * count + 4 :
    ]
    pair, rows = act_buf.shape[1], act_buf.shape[3]
    shards, packed_rows, hidden_width = weight_ref.shape
    deep = packed_rows // 3
    width = shards * deep
    step, steps = pl.program_id(0), pl.num_programs(0)

    def copies(first, slot):
        made = []
        for source in range(pair):
            for half in range(2):
                lane = 2 * source + half
                index = half * count + first + source
                made.append(
                    pltpu.make_async_copy(
                        acts[index], act_buf.at[slot, source, half], arrive.at[slot, 0, lane]
                    )
                )
                made.append(
                    pltpu.make_async_copy(
                        cots[index], cot_buf.at[slot, source, half], arrive.at[slot, 1, lane]
                    )
                )
        return made

    def fetch(target, slot):
        for known in range(count // pair):

            @pl.when(target == known)
            def _():
                for copy in copies(known * pair, slot):
                    copy.start()

    @pl.when(step == 0)
    def _():
        fetch(0, 0)

    @pl.when(step + 1 < steps)
    def _():
        fetch(step + 1, (step + 1) % 2)

    slot = step % 2
    for copy in copies(0, slot):
        copy.wait()

    gate_w = weight_ref[:, :deep, :].reshape(width, hidden_width)
    up_w = weight_ref[:, deep : 2 * deep, :].reshape(width, hidden_width)

    def down_w(shard):
        part = weight_ref[shard, 2 * deep :, :]
        blocks = [part[:, k * deep : (k + 1) * deep] for k in range(hidden_width // deep)]
        return jnp.concatenate(blocks, axis=0)

    picked, cots_here, shares, masks = [], [], [], []
    for source in range(pair):
        mask = lax.broadcasted_iota(jnp.int32, (CAP, rows), 0) == slot_ref[source]
        choose = jnp.where(mask, 1.0, 0.0).astype(jnp.bfloat16)
        picked.append(
            jnp.concatenate(
                [contract(choose, act_buf[slot, source, half], 1, 0) for half in range(2)], axis=1
            )
        )
        cots_here.append(
            jnp.concatenate(
                [contract(choose, cot_buf[slot, source, half], 1, 0) for half in range(2)], axis=1
            )
        )
        shares.append(jnp.sum(jnp.where(mask, share_ref[source], 0.0), axis=1, keepdims=True))
        masks.append(mask)
    act = jnp.concatenate(picked, 0).astype(jnp.bfloat16)
    cot = jnp.concatenate(cots_here, 0)
    share = jnp.concatenate(shares, 0)
    gate_pre = contract(act, gate_w, 1, 0)
    up_pre = contract(act, up_w, 1, 0)
    sigmoid = 1.0 / (1.0 + jnp.exp(-gate_pre))
    silu = gate_pre * sigmoid
    hidden = (silu * up_pre).astype(jnp.bfloat16)
    made = jnp.concatenate(
        [contract(hidden, down_w(shard), 1, 0) for shard in range(shards)], axis=1
    )
    made = made.astype(jnp.bfloat16).astype(jnp.float32)
    share_grad = jnp.sum(made * cot, axis=1, keepdims=True)
    mixed = (made * share).astype(jnp.bfloat16)
    made_grad = (share * cot).astype(jnp.bfloat16)
    hidden_grad = sum(
        contract(made_grad[:, shard * deep : (shard + 1) * deep], down_w(shard), 1, 1)
        for shard in range(shards)
    )
    up_grad = (hidden_grad * silu).astype(jnp.bfloat16)
    gate_grad = (
        hidden_grad * up_pre * sigmoid * (1.0 + gate_pre * (1.0 - sigmoid))
    ).astype(jnp.bfloat16)
    back = (contract(gate_grad, gate_w, 1, 1) + contract(up_grad, up_w, 1, 1)).astype(jnp.bfloat16)
    for source in range(pair):
        part = slice(source * CAP, (source + 1) * CAP)
        mixed_ref[source] = mixed[part]
        back_ref[source] = back[part]
        share_grad_ref[source] = jnp.sum(
            jnp.where(masks[source], share_grad[part], 0.0), axis=0, keepdims=True
        )
    here = pl.ds(pl.multiple_of(step * pair * CAP, pair * CAP), pair * CAP)
    act_rows[here, :] = act
    hidden_rows[here, :] = hidden
    down_rows[here, :] = made_grad
    gate_rows[here, :] = gate_grad
    up_rows[here, :] = up_grad

    @pl.when(step == steps - 1)
    def _():
        gate_sum = contract(act_rows[...], gate_rows[...], 0, 0).astype(jnp.bfloat16)
        weight_grad_ref[:, :deep, :] = gate_sum.reshape(shards, deep, hidden_width)
        up_sum = contract(act_rows[...], up_rows[...], 0, 0).astype(jnp.bfloat16)
        weight_grad_ref[:, deep : 2 * deep, :] = up_sum.reshape(shards, deep, hidden_width)
        for shard in range(shards):
            cols = slice(shard * deep, (shard + 1) * deep)
            down_sum = contract(hidden_rows[...], down_rows[:, cols], 0, 0).astype(jnp.bfloat16)
            for k in range(hidden_width // deep):
                weight_grad_ref[shard, 2 * deep :, k * deep : (k + 1) * deep] = down_sum[
                    k * deep : (k + 1) * deep
                ]


def run_expert(slots, shares, weights, acts, cots):
    count, rows = slots.shape
    half = acts[0].shape[1]
    hidden_width = weights.shape[2]
    pair = 2
    listed = count * CAP
    low = jnp.bfloat16

    def by_source(*shape):
        return pl.BlockSpec((pair,) + shape, lambda s: (s,) + (0,) * len(shape))

    anywhere = pl.BlockSpec(memory_space=pl.ANY)
    outs = pl.pallas_call(
        functools.partial(expert_step, count=count),
        grid=(count // pair,),
        in_specs=[by_source(1, rows), by_source(1, rows), whole_block(weights)]
        + [anywhere] * (4 * count),
        out_specs=[
            by_source(CAP, 2 * half),
            by_source(CAP, 2 * half),
            by_source(1, rows),
            pl.BlockSpec(weights.shape, lambda s: (0, 0, 0)),
        ],
        out_shape=[
            jax.ShapeDtypeStruct((count, CAP, 2 * half), low),
            jax.ShapeDtypeStruct((count, CAP, 2 * half), low),
            jax.ShapeDtypeStruct((count, 1, rows), jnp.float32),
            jax.ShapeDtypeStruct(weights.shape, low),
        ],
        scratch_shapes=[
            pltpu.VMEM((2, pair, 2, rows, half), low),
            pltpu.VMEM((2, pair, 2, rows, half), low),
            pltpu.SemaphoreType.DMA((2, 2, 2 * pair)),
            pltpu.VMEM((listed, 2 * half), low),
            pltpu.VMEM((listed, hidden_width), low),
            pltpu.VMEM((listed, 2 * half), low),
            pltpu.VMEM((listed, hidden_width), low),
            pltpu.VMEM((listed, hidden_width), low),
        ],
        compiler_params=pltpu.CompilerParams(
            dimension_semantics=("arbitrary",), vmem_limit_bytes=VMEM_LIMIT
        ),
        name="expert",
    )(slots[:, None], shares[:, None], weights, *acts, *cots)
    return (outs[0], outs[1], outs[2][:, 0], outs[3])


def combine_step(slot_ref, *refs):
    parts, (left_ref, right_ref) = refs[:-2], refs[-2:]
    experts = len(parts)
    rows, half = left_ref.shape[1:]
    place = lax.broadcasted_iota(jnp.int32, (rows, experts * CAP), 1)
    hit = None
    for expert in range(experts):
        slot = slot_ref[0, :, expert : expert + 1]
        match = place == jnp.where(slot >= 0, slot + expert * CAP, -1)
        hit = match if hit is None else hit | match
    choose = jnp.where(hit, 1.0, 0.0).astype(jnp.bfloat16)
    listed = jnp.concatenate([part[0] for part in parts], axis=0)
    total = contract(choose, listed, 1, 0).astype(jnp.bfloat16)
    left_ref[0] = total[:, :half]
    right_ref[0] = total[:, half:]


def combine_rows(slots_by_row, parts, odd):
    sources, rows, experts = slots_by_row.shape
    width = parts[0].shape[2]
    orders = [order[:-1][::-1] for order in stage_orders(sources)]

    def half_of(order):
        return pl.BlockSpec((1, rows, width // 2), lambda i: (chunk_place(i, order), 0, 0))

    return pl.pallas_call(
        combine_step,
        grid=(sources // 2,),
        in_specs=[pl.BlockSpec((1, rows, experts), lambda i: (2 * i + odd, 0, 0))]
        + [pl.BlockSpec((1, CAP, width), lambda i: (2 * i + odd, 0, 0))] * experts,
        out_specs=[half_of(order) for order in orders],
        out_shape=[jax.ShapeDtypeStruct((sources // 2, rows, width // 2), jnp.bfloat16)] * 2,
        compiler_params=pltpu.CompilerParams(
            dimension_semantics=("arbitrary",), vmem_limit_bytes=VMEM_LIMIT
        ),
        name="combine",
    )(slots_by_row, *parts)


def ring_pieces(values, axis_name):
    count = lax.axis_size(axis_name)
    ahead = [(place, (place + 1) % count) for place in range(count)]
    behind = [(place, (place - 1) % count) for place in range(count)]
    half = values.shape[1] // 2
    lists = []
    for pairs, part in ((ahead, values[:, :half]), (behind, values[:, half:])):
        pieces = [part]
        for _ in range(count - 1):
            pieces.append(lax.ppermute(pieces[-1], axis_name, pairs))
        lists.append(pieces)
    return lists


def ring_reduce(values, axis_name):
    count = lax.axis_size(axis_name)
    ahead = [(place, (place + 1) % count) for place in range(count)]
    behind = [(place, (place - 1) % count) for place in range(count)]
    half = values.shape[2] // 2
    sums = []
    for pairs, turn, part in ((ahead, -1, values[:, :, :half]), (behind, 1, values[:, :, half:])):
        moving = part[turn % count]
        for step in range(1, count):
            moving = lax.ppermute(moving, axis_name, pairs)
            own = part[(turn * (step + 1)) % count]
            moving = moving.astype(jnp.float32) + own.astype(jnp.float32)
            if step < count - 1:
                moving = moving.astype(jnp.bfloat16)
        sums.append(moving)
    return jnp.concatenate(sums, axis=1)


def sequence_starts(length_row, places):
    count = length_row.shape[0]
    ends = [length_row[0]]
    for index in range(1, count):
        ends.append(ends[-1] + length_row[index])
    first = jnp.zeros_like(places)
    for index in range(count - 1):
        first = jnp.where(places >= ends[index], ends[index], first)
    return first


def turn_halves(values, cosine, sine, turned_lanes):
    groups = []
    for first in range(0, values.shape[1], 128):
        group = values[:, first : first + 128]
        lane = lax.broadcasted_iota(jnp.int32, group.shape, 1)
        partner = jnp.where(
            lane % HEAD_SIZE < HEAD_SIZE // 2,
            pltpu.roll(group, 128 - HEAD_SIZE // 2, 1),
            pltpu.roll(group, HEAD_SIZE // 2, 1),
        )
        turned = group * cosine + partner * sine
        groups.append(jnp.where(lane + first < turned_lanes, turned, group))
    return jnp.concatenate(groups, axis=1)


def scale_rows(values):
    return lax.rsqrt(jnp.mean(values * values, axis=1, keepdims=True) + NORM_EPS)


def project_step(order_ref, gain_ref, weight_ref, cos_ref, sin_ref, *refs):
    pieces, (rows_ref, query_ref, key_ref, value_ref) = refs[:-4], refs[-4:]
    count = len(pieces) // 2
    span, width = rows_ref.shape
    token_rows = pieces[0].shape[0]
    first = pl.program_id(0) * span
    places = first + lax.broadcasted_iota(jnp.int32, (span, token_rows), 0)
    left, right = 0.0, 0.0
    for index in range(count):
        part = order_ref[:, index * token_rows : (index + 1) * token_rows]
        choose = jnp.where(part == places, 1.0, 0.0).astype(jnp.bfloat16)
        left = left + contract(choose, pieces[index][...], 1, 0)
        right = right + contract(choose, pieces[count + index][...], 1, 0)
    values = jnp.concatenate([left, right], axis=1)
    rows_ref[...] = values.astype(jnp.bfloat16)
    act = (values * scale_rows(values) * gain_ref[...]).astype(jnp.bfloat16)
    made = contract(act, weight_ref[...], 1, 0)
    share = made.shape[1] // 4
    made = turn_halves(made, cos_ref[...], sin_ref[...], 3 * share).astype(jnp.bfloat16)
    query_ref[...] = made[:, : 2 * share]
    key_ref[...] = made[:, 2 * share : 3 * share]
    value_ref[...] = made[:, 3 * share :]


def whole_block(array):
    return pl.BlockSpec(
        array.shape, lambda *_: (0,) * array.ndim, pipeline_mode=pl.Buffered(1)
    )


def row_block(width):
    return pl.BlockSpec((SPAN, width), lambda i, *_: (i, 0))


def project(order_row, gain, weight, cosine, sine, pieces):
    rows = order_row.shape[1]
    width, columns = weight.shape
    share = columns // 4
    low = jnp.bfloat16
    return pl.pallas_call(
        project_step,
        grid=(rows // SPAN,),
        in_specs=[
            whole_block(order_row),
            whole_block(gain),
            whole_block(weight),
            row_block(128),
            row_block(128),
        ]
        + [whole_block(piece) for piece in pieces],
        out_specs=[row_block(width), row_block(2 * share), row_block(share), row_block(share)],
        out_shape=[
            jax.ShapeDtypeStruct((rows, width), low),
            jax.ShapeDtypeStruct((rows, 2 * share), low),
            jax.ShapeDtypeStruct((rows, share), low),
            jax.ShapeDtypeStruct((rows, share), low),
        ],
        compiler_params=pltpu.CompilerParams(
            dimension_semantics=("arbitrary",), vmem_limit_bytes=VMEM_LIMIT
        ),
        name="project",
    )(order_row, gain, weight, cosine, sine, *pieces)


def stack_heads(values, lanes):
    lane = lax.broadcasted_iota(jnp.int32, (values.shape[0], lanes), 1)
    blocks = []
    for member in range(values.shape[1] // lanes):
        part = values[:, member * lanes : (member + 1) * lanes]
        for head in range(lanes // HEAD_SIZE):
            blocks.append(jnp.where(lane // HEAD_SIZE == head, part, jnp.zeros_like(part)))
    return jnp.concatenate(blocks, axis=0)


def unstack_heads(values, lanes, span):
    lane = lax.broadcasted_iota(jnp.int32, (span, lanes), 1)
    heads = lanes // HEAD_SIZE
    members = []
    for member in range(values.shape[0] // span // heads):
        merged = None
        for head in range(heads):
            first = (member * heads + head) * span
            part = values[first : first + span]
            merged = part if merged is None else jnp.where(lane // HEAD_SIZE == head, part, merged)
        members.append(merged)
    return jnp.concatenate(members, axis=1)


def allowed_pairs(start_ref, block, key_block, span):
    query_place = block * span + lax.broadcasted_iota(jnp.int32, (span, span), 0)
    key_place = key_block * span + lax.broadcasted_iota(jnp.int32, (span, span), 1)
    return (key_place <= query_place) & (key_place >= start_ref[...])


def mask_scores(scores, allowed):
    span = allowed.shape[0]
    heads = scores.shape[0] // span
    stacked = scores.reshape(heads, span, span)
    return jnp.where(allowed[None], stacked, MASKED).reshape(scores.shape)


def attend_step(lowest_ref, start_ref, query_ref, key_ref, value_ref, out_ref, log_ref, best, accum):
    block = pl.program_id(0)
    span = query_ref.shape[0]
    lanes = key_ref.shape[1]
    query = stack_heads(query_ref[...], lanes) * jnp.bfloat16(1.0 / math.sqrt(HEAD_SIZE))
    lowest = lowest_ref[block]

    def scores_of(key_block):
        here = pl.ds(pl.multiple_of(key_block * span, span), span)
        scores = contract(query, key_ref[here, :], 1, 1)
        return mask_scores(scores, allowed_pairs(start_ref, block, key_block, span))

    best[...] = scores_of(block)

    def look(key_block, _):
        best[...] = jnp.maximum(best[...], scores_of(key_block))
        return 0

    lax.fori_loop(lowest, block, look, 0)
    top = jnp.max(best[...], axis=1, keepdims=True)
    accum[...] = jnp.zeros_like(accum)

    def visit(key_block, _):
        here = pl.ds(pl.multiple_of(key_block * span, span), span)
        terms = jnp.exp(scores_of(key_block) - top).astype(jnp.bfloat16)
        values = value_ref[here, :]
        values = jnp.concatenate([values, jnp.ones((span, 128), jnp.bfloat16)], axis=1)
        accum[...] += contract(terms, values, 1, 0)
        return 0

    lax.fori_loop(lowest, block + 1, visit, 0)
    total = accum[:, lanes : lanes + 1]
    out_ref[...] = unstack_heads(accum[:, :lanes] / total, lanes, span).astype(jnp.bfloat16)
    logs = top + jnp.log(total)
    heads = logs.shape[0] // span
    log_ref[...] = jnp.concatenate(
        [logs[head * span : (head + 1) * span] for head in range(heads)], axis=1
    )


def attend(lowest, start, query, key, value):
    rows, columns = query.shape
    lanes = key.shape[1]
    heads = columns // HEAD_SIZE
    return pl.pallas_call(
        attend_step,
        grid_spec=pltpu.PrefetchScalarGridSpec(
            num_scalar_prefetch=1,
            grid=(rows // SPAN,),
            in_specs=[row_block(1), row_block(columns), whole_block(key), whole_block(value)],
            out_specs=[row_block(columns), row_block(heads)],
            scratch_shapes=[
                pltpu.VMEM((heads * SPAN, SPAN), jnp.float32),
                pltpu.VMEM((heads * SPAN, lanes + 128), jnp.float32),
            ],
        ),
        out_shape=[
            jax.ShapeDtypeStruct((rows, columns), jnp.bfloat16),
            jax.ShapeDtypeStruct((rows, heads), jnp.float32),
        ],
        compiler_params=pltpu.CompilerParams(
            dimension_semantics=("arbitrary",), vmem_limit_bytes=VMEM_LIMIT
        ),
        name="attend",
    )(lowest, start, query, key, value)


def attend_back_step(
    lowest_ref,
    start_ref,
    log_ref,
    query_ref,
    out_ref,
    cot_ref,
    key_ref,
    value_ref,
    query_grad_ref,
    key_grad_ref,
    value_grad_ref,
    accum,
):
    block = pl.program_id(0)
    span = query_ref.shape[0]
    lanes = key_ref.shape[1]
    scale = 1.0 / math.sqrt(HEAD_SIZE)

    @pl.when(block == 0)
    def _():
        key_grad_ref[...] = jnp.zeros_like(key_grad_ref)
        value_grad_ref[...] = jnp.zeros_like(value_grad_ref)

    query = stack_heads(query_ref[...], lanes) * jnp.bfloat16(scale)
    cot = stack_heads(cot_ref[...], lanes)
    out = stack_heads(out_ref[...], lanes)
    dots = jnp.sum(cot.astype(jnp.float32) * out.astype(jnp.float32), axis=1, keepdims=True)
    heads = log_ref.shape[1]
    logs = jnp.concatenate([log_ref[:, head : head + 1] for head in range(heads)], axis=0)
    accum[...] = jnp.zeros_like(accum)

    def visit(key_block, _):
        here = pl.ds(pl.multiple_of(key_block * span, span), span)
        keys = key_ref[here, :]
        scores = contract(query, keys, 1, 1)
        scores = mask_scores(scores, allowed_pairs(start_ref, block, key_block, span))
        probs = jnp.exp(scores - logs)
        prob_grad = contract(cot, value_ref[here, :], 1, 1)
        score_grad = (probs * (prob_grad - dots)).astype(jnp.bfloat16)
        accum[...] += contract(score_grad, keys, 1, 0)
        key_grad_ref[here, :] += contract(score_grad, query, 0, 0)
        value_grad_ref[here, :] += contract(probs.astype(jnp.bfloat16), cot, 0, 0)
        return 0

    lax.fori_loop(lowest_ref[block], block + 1, visit, 0)
    query_grad_ref[...] = unstack_heads(accum[...] * scale, lanes, span)


def attend_back(lowest, start, logs, query, out, cot, key, value):
    rows, columns = query.shape
    lanes = key.shape[1]
    heads = columns // HEAD_SIZE
    return pl.pallas_call(
        attend_back_step,
        grid_spec=pltpu.PrefetchScalarGridSpec(
            num_scalar_prefetch=1,
            grid=(rows // SPAN,),
            in_specs=[
                row_block(1),
                row_block(heads),
                row_block(columns),
                row_block(columns),
                row_block(columns),
                whole_block(key),
                whole_block(value),
            ],
            out_specs=[
                row_block(columns),
                pl.BlockSpec((rows, lanes), lambda *_: (0, 0)),
                pl.BlockSpec((rows, lanes), lambda *_: (0, 0)),
            ],
            scratch_shapes=[pltpu.VMEM((heads * SPAN, lanes), jnp.float32)],
        ),
        out_shape=[
            jax.ShapeDtypeStruct((rows, columns), jnp.float32),
            jax.ShapeDtypeStruct((rows, lanes), jnp.float32),
            jax.ShapeDtypeStruct((rows, lanes), jnp.float32),
        ],
        compiler_params=pltpu.CompilerParams(
            dimension_semantics=("arbitrary",), vmem_limit_bytes=VMEM_LIMIT
        ),
        name="attend_back",
    )(lowest, start, logs, query, out, cot, key, value)


def project_back_step(
    own_ref,
    order_ref,
    gain_ref,
    weight_ref,
    cos_ref,
    sin_ref,
    query_ref,
    key_ref,
    value_ref,
    rows_ref,
    residual_ref,
    out_ref,
    weight_grad_ref,
    gain_grad_ref,
    act_rows,
    grad_rows,
    token_rows,
    gain_sum,
):
    phase, block = pl.program_id(0), pl.program_id(1)
    blocks = pl.num_programs(1)
    span, width = rows_ref.shape
    here = pl.ds(pl.multiple_of(block * span, span), span)

    @pl.when(phase == 0)
    def _():
        grads = jnp.concatenate([query_ref[...], key_ref[...], value_ref[...]], axis=1)
        share = grads.shape[1] // 4
        grads = turn_halves(grads, cos_ref[...], -sin_ref[...], 3 * share).astype(jnp.bfloat16)
        values = rows_ref[...].astype(jnp.float32)
        scale = scale_rows(values)
        normed = values * scale
        gain = gain_ref[...]
        act_grad = contract(grads, weight_ref[...], 1, 1)
        scaled = act_grad * gain
        token_grad = scale * (scaled - normed * jnp.mean(scaled * normed, axis=1, keepdims=True))
        per_device = residual_ref.shape[0]
        offset = block * span - own_ref[0] * per_device
        owned = (offset >= 0) & (offset < per_device)
        at = pl.ds(pl.multiple_of(jnp.where(owned, offset, 0), span), span)
        residual = jnp.where(owned, residual_ref[at, :].astype(jnp.float32), 0.0)
        token_rows[here, :] = (token_grad + residual).astype(jnp.bfloat16)
        act_rows[here, :] = (normed * gain).astype(jnp.bfloat16)
        grad_rows[here, :] = grads
        part = jnp.sum(act_grad * normed, axis=0, keepdims=True)

        @pl.when(block == 0)
        def _():
            gain_sum[...] = part

        @pl.when(block > 0)
        def _():
            gain_sum[...] += part

        @pl.when(block == blocks - 1)
        def _():
            weight_grad_ref[...] = contract(act_rows[...], grad_rows[...], 0, 0).astype(
                jnp.bfloat16
            )
            gain_grad_ref[...] = gain_sum[...]

    @pl.when(phase == 1)
    def _():
        total = token_rows.shape[0]
        places = lax.broadcasted_iota(jnp.int32, (span, total), 1)
        choose = jnp.where(order_ref[...] == places, 1.0, 0.0).astype(jnp.bfloat16)
        out_ref[...] = contract(choose, token_rows[...], 1, 0).astype(jnp.bfloat16)


def project_back(own, order_column, gain, weight, cosine, sine, query_grad, key_grad, value_grad, rows_in, residual):
    rows, width = rows_in.shape
    columns = weight.shape[1]
    share = columns // 4
    blocks = rows // SPAN
    low = jnp.bfloat16

    def early(columns):
        return pl.BlockSpec((SPAN, columns), lambda p, i, *_: (jnp.where(p == 0, i, blocks - 1), 0))

    def late(columns):
        return pl.BlockSpec((SPAN, columns), lambda p, i, *_: (jnp.where(p == 0, 0, i), 0))

    return pl.pallas_call(
        project_back_step,
        grid_spec=pltpu.PrefetchScalarGridSpec(
            num_scalar_prefetch=1,
            grid=(2, blocks),
            in_specs=[
                late(1),
                whole_block(gain),
                whole_block(weight),
                early(128),
                early(128),
                early(2 * share),
                early(share),
                early(share),
                early(width),
                whole_block(residual),
            ],
            out_specs=[
                late(width),
                pl.BlockSpec((width, columns), lambda *_: (0, 0)),
                pl.BlockSpec((1, width), lambda *_: (0, 0)),
            ],
            scratch_shapes=[
                pltpu.VMEM((rows, width), low),
                pltpu.VMEM((rows, columns), low),
                pltpu.VMEM((rows, width), low),
                pltpu.VMEM((1, width), jnp.float32),
            ],
        ),
        out_shape=[
            jax.ShapeDtypeStruct((rows, width), low),
            jax.ShapeDtypeStruct((width, columns), low),
            jax.ShapeDtypeStruct((1, width), jnp.float32),
        ],
        compiler_params=pltpu.CompilerParams(
            dimension_semantics=("arbitrary", "arbitrary"), vmem_limit_bytes=VMEM_LIMIT
        ),
        name="project_back",
    )(own, order_column, gain, weight, cosine, sine, query_grad, key_grad, value_grad, rows_in, residual)


def body(
    tokens,
    query_weight,
    key_projection_weight,
    value_projection_weight,
    output_weight,
    router_weight,
    first_gain,
    second_gain,
    expert_gate,
    expert_up,
    expert_down,
    routes,
    dealing,
    lengths,
    cotangent,
):
    low = jnp.bfloat16
    token_rows = tokens.shape[0]
    sp_count = lax.axis_size("sp")
    sp_index = lax.axis_index("sp")
    fsdp_count = lax.axis_size("fsdp")
    fsdp_index = lax.axis_index("fsdp")
    group_rows = token_rows * sp_count
    local_experts = EXPERTS // fsdp_count
    kept_heads = KEY_VALUE_HEADS // sp_count
    ratio = QUERY_HEADS // KEY_VALUE_HEADS
    share = kept_heads * HEAD_SIZE
    shard_rows = query_weight.shape[0]
    relative = fsdp_index ^ jnp.arange(fsdp_count, dtype=jnp.int32)

    def own_columns(weight, heads):
        part = lax.dynamic_slice_in_dim(weight, sp_index * heads * HEAD_SIZE, heads * HEAD_SIZE, 1)
        return part.astype(low)

    query_part = own_columns(query_weight, kept_heads * ratio)
    query_part = query_part.reshape(shard_rows, kept_heads, ratio, HEAD_SIZE)
    query_part = jnp.swapaxes(query_part, 1, 2).reshape(shard_rows, ratio * share)
    packed = jnp.concatenate(
        [
            query_part,
            own_columns(key_projection_weight, kept_heads),
            own_columns(value_projection_weight, kept_heads),
            output_weight.astype(low),
            router_weight.astype(low),
            first_gain.astype(low)[:, None],
            second_gain.astype(low)[:, None],
            jnp.zeros((shard_rows, 128 - EXPERTS - 2), low),
        ],
        axis=1,
    )
    packed_all = lax.all_gather(packed, "fsdp", axis=0, tiled=True)
    qkv_columns = (ratio + 2) * share
    qkv_weight = packed_all[:, :qkv_columns]
    output_full = packed_all[:, qkv_columns : qkv_columns + MODEL_WIDTH]
    output_full = output_full.reshape(sp_count, kept_heads, ratio, HEAD_SIZE, MODEL_WIDTH)
    output_full = jnp.swapaxes(output_full, 1, 2).reshape(sp_count, ratio * share, MODEL_WIDTH)
    rest = packed_all[:, qkv_columns + MODEL_WIDTH :]
    router_full = rest[:, :EXPERTS]
    gain_attend = rest[:, EXPERTS].astype(jnp.float32)[None, :]
    gain_mixer = rest[:, EXPERTS + 1].astype(jnp.float32)[None, :]

    left, right = ring_pieces(tokens, "sp")
    pieces = [left[-k % sp_count] for k in range(sp_count)] + right
    expert_parts = [
        pack_expert(expert_gate[e].astype(low), expert_up[e].astype(low), expert_down[e].astype(low))
        for e in range(local_experts)
    ]
    *expert_parts, routes, _, _ = lax.optimization_barrier(
        (*expert_parts, routes, left[-1], right[-1])
    )
    cot_source, _, _ = lax.optimization_barrier((cotangent, left[1], right[1]))
    expert_weights = [lax.all_gather(part, "sp", axis=0, tiled=False) for part in expert_parts]
    order_row = dealing[0]
    order_here = lax.dynamic_slice_in_dim(
        jnp.concatenate([order_row, order_row]), sp_index * token_rows, group_rows
    )
    places = jnp.arange(group_rows, dtype=jnp.int32)
    starts = sequence_starts(lengths[0], places)
    lowest = starts[::SPAN] // SPAN
    start_column = starts[:, None]
    half_dim = HEAD_SIZE // 2
    frequency = ROPE_BASE ** (-(jnp.arange(half_dim, dtype=jnp.float32) * 2.0 / HEAD_SIZE))
    angles = (places - starts).astype(jnp.float32)[:, None] * frequency[None, :]
    cosine = jnp.tile(jnp.cos(angles), (1, 4))
    sine = jnp.sin(angles)
    sine = jnp.concatenate([-sine, sine, -sine, sine], axis=1)

    rows_initial, query, key, value = project(
        order_here[None, :], gain_attend, qkv_weight, cosine, sine, pieces
    )
    attended, logs = attend(lowest, start_column, query, key, value)
    attn_back = lax.all_to_all(
        attended.reshape(sp_count, token_rows, ratio * share),
        "sp",
        split_axis=0,
        concat_axis=0,
        tiled=True,
    )
    resid = lax.dynamic_slice_in_dim(rows_initial, sp_index * token_rows, token_rows)
    branch = jnp.einsum("stc,scd->td", attn_back, output_full, preferred_element_type=jnp.float32)
    middle = resid.astype(jnp.float32) + branch
    inv_two = lax.rsqrt(jnp.mean(middle * middle, axis=1, keepdims=True) + NORM_EPS)
    normed_two = middle * inv_two
    act_two = (normed_two * gain_mixer).astype(low)
    logits = jnp.dot(act_two, router_full, preferred_element_type=jnp.float32)
    expert_range = jnp.arange(EXPERTS, dtype=jnp.int32)
    member = jnp.any(routes[:, :, None] == expert_range[None, None, :], axis=1)
    row_range = jnp.arange(token_rows, dtype=jnp.int32)
    upto = (row_range[:, None] <= row_range[None, :]).astype(low)
    rank = jnp.dot(member.T.astype(low), upto, preferred_element_type=jnp.float32)
    slots = jnp.where(member.T, rank.astype(jnp.int32) - 1, -1)

    def to_experts(by_expert):
        arrived = lax.all_to_all(
            by_expert.reshape(fsdp_count, local_experts, token_rows),
            "fsdp",
            split_axis=0,
            concat_axis=0,
            tiled=True,
        )
        return jnp.swapaxes(jnp.take(arrived, relative, axis=0), 0, 1)

    slots_here = to_experts(slots)
    gate_dense = jax.nn.softmax(jnp.where(member, logits, -jnp.inf), axis=-1)
    gates_here = to_experts(gate_dense.T)
    cot_left, cot_right = gather_pieces(cot_source, "fsdp")
    act_left, act_right = gather_pieces(act_two, "fsdp")
    mixed_rows, back_rows, gate_grads, expert_sums = [], [], [], []
    for e in range(local_experts):
        mixed, back, gate_grad, weight_grad = run_expert(
            slots_here[e], gates_here[e], expert_weights[e], act_left + act_right, cot_left + cot_right
        )
        mixed_rows.append(mixed)
        back_rows.append(back)
        gate_grads.append(gate_grad)
        expert_sums.append(lax.psum_scatter(weight_grad, "sp", scatter_dimension=0, tiled=False))
    gate_grads = jnp.stack(gate_grads, axis=1)
    slots_by_row = jnp.transpose(slots_here, (1, 2, 0))
    leave = combine_rows(slots_by_row, back_rows, 1)
    stay = combine_rows(slots_by_row, back_rows, 0)
    grad_act_moe = reduce_halves(leave, stay, "fsdp")
    upstream = cotangent.astype(jnp.float32)
    gate_grad_back = lax.all_to_all(
        jnp.take(gate_grads, relative, axis=0),
        "fsdp",
        split_axis=0,
        concat_axis=0,
        tiled=True,
    )
    gate_grad = gate_grad_back.reshape(EXPERTS, token_rows).T
    weighted = jnp.sum(gate_dense * gate_grad, axis=1, keepdims=True)
    logit_grad = (gate_dense * (gate_grad - weighted)).astype(low)
    grad_router_w = jnp.einsum("td,te->de", act_two, logit_grad, preferred_element_type=jnp.float32)
    grad_act_two = grad_act_moe + jnp.dot(
        logit_grad, router_full.T, preferred_element_type=jnp.float32
    )
    grad_gain_two = jnp.sum(grad_act_two * normed_two, axis=0)
    scaled_two = grad_act_two * gain_mixer
    grad_middle = upstream + inv_two * (
        scaled_two - normed_two * jnp.mean(scaled_two * normed_two, axis=1, keepdims=True)
    )
    middle_low = grad_middle.astype(low)
    grad_attn = jnp.einsum(
        "td,scd->stc", middle_low, output_full, preferred_element_type=jnp.float32
    ).astype(low)
    grad_heads = lax.all_to_all(
        grad_attn, "sp", split_axis=0, concat_axis=0, tiled=True
    ).reshape(group_rows, ratio * share)
    leave = combine_rows(slots_by_row, mixed_rows, 1)
    stay = combine_rows(slots_by_row, mixed_rows, 0)
    *leave, grad_heads = lax.optimization_barrier((*leave, grad_heads))
    mixture = reduce_halves(leave, stay, "fsdp")
    layer_out = (middle + mixture).astype(low)
    grad_output_w = jnp.einsum(
        "stc,td->scd", attn_back, middle_low, preferred_element_type=jnp.float32
    ).astype(low)
    grad_output_w = grad_output_w.reshape(sp_count, ratio, kept_heads, HEAD_SIZE, MODEL_WIDTH)
    grad_output_w = jnp.swapaxes(grad_output_w, 1, 2).reshape(MODEL_WIDTH, MODEL_WIDTH)
    early_grads = jnp.concatenate(
        [
            grad_output_w,
            grad_router_w.astype(low),
            grad_gain_two.astype(low)[:, None],
            jnp.zeros((MODEL_WIDTH, 256 - EXPERTS - 1), low),
        ],
        axis=1,
    ).reshape(fsdp_count, shard_rows, MODEL_WIDTH + 256)
    early_sum = reduce_rows(jnp.take(early_grads, relative, axis=0), "fsdp").astype(low)
    early_left, early_right = ring_pieces(early_sum, "sp")
    early_sum = jnp.concatenate(
        [sum(part.astype(jnp.float32) for part in parts) for parts in (early_left, early_right)],
        axis=1,
    )

    grad_query, grad_key, grad_value = attend_back(
        lowest, start_column, logs, query, attended, grad_heads, key, value
    )
    token_grads, grad_qkv, grad_gain_one = project_back(
        sp_index[None],
        order_here[:, None],
        gain_attend,
        qkv_weight,
        cosine,
        sine,
        grad_query,
        grad_key,
        grad_value,
        rows_initial,
        middle_low,
    )
    tokens_grad = ring_reduce(
        token_grads.reshape(sp_count, token_rows, MODEL_WIDTH), "sp"
    ).astype(low)
    late_grads = jnp.concatenate(
        [
            grad_qkv,
            grad_gain_one.astype(low).T,
            jnp.zeros((MODEL_WIDTH, 255), low),
        ],
        axis=1,
    ).reshape(fsdp_count, shard_rows, qkv_columns + 256)
    late_sum = reduce_rows(jnp.take(late_grads, relative, axis=0), "fsdp").astype(low)
    late_left, late_right = ring_pieces(late_sum, "sp")
    late_left = [late_left[-k % sp_count] for k in range(sp_count)]
    late_all = jnp.concatenate([jnp.stack(late_left), jnp.stack(late_right)], axis=2)
    late_all = jnp.take(late_all, (jnp.arange(sp_count) - sp_index) % sp_count, axis=0)
    late_all = late_all.astype(jnp.float32)
    query_sum = late_all[:, :, : ratio * share]
    query_sum = query_sum.reshape(sp_count, shard_rows, ratio, kept_heads, HEAD_SIZE)
    query_sum = jnp.transpose(query_sum, (1, 0, 3, 2, 4)).reshape(shard_rows, MODEL_WIDTH)
    key_sum = jnp.swapaxes(late_all[:, :, ratio * share : (ratio + 1) * share], 0, 1)
    deep = expert_gate.shape[1]

    def unpack_down(part):
        blocks = [part[:, k * deep : (k + 1) * deep] for k in range(part.shape[1] // deep)]
        return jnp.concatenate(blocks, axis=0)

    value_sum = jnp.swapaxes(late_all[:, :, (ratio + 1) * share : qkv_columns], 0, 1)
    return (
        layer_out,
        tokens_grad,
        query_sum,
        key_sum.reshape(shard_rows, KEY_VALUE_HEADS * HEAD_SIZE),
        value_sum.reshape(shard_rows, KEY_VALUE_HEADS * HEAD_SIZE),
        early_sum[:, :MODEL_WIDTH],
        early_sum[:, MODEL_WIDTH : MODEL_WIDTH + EXPERTS],
        jnp.sum(late_all[:, :, qkv_columns], axis=0),
        early_sum[:, MODEL_WIDTH + EXPERTS],
        jnp.stack([part[:deep] for part in expert_sums]).astype(jnp.float32),
        jnp.stack([part[deep : 2 * deep] for part in expert_sums]).astype(jnp.float32),
        jnp.stack([unpack_down(part[2 * deep :]) for part in expert_sums]).astype(jnp.float32),
    )


def solution(mesh):
    return jax.shard_map(
        body,
        mesh=mesh,
        in_specs=(
            P(("fsdp", "sp"), None),
            P("fsdp", None),
            P("fsdp", None),
            P("fsdp", None),
            P("fsdp", None),
            P("fsdp", None),
            P("fsdp"),
            P("fsdp"),
            P("fsdp", "sp", None),
            P("fsdp", "sp", None),
            P("fsdp", None, "sp"),
            P(("fsdp", "sp"), None),
            P("fsdp", None),
            P("fsdp", None),
            P(("fsdp", "sp"), None),
        ),
        out_specs=(
            P(("fsdp", "sp"), None),
            P(("fsdp", "sp"), None),
            P("fsdp", None),
            P("fsdp", None),
            P("fsdp", None),
            P("fsdp", None),
            P("fsdp", None),
            P("fsdp"),
            P("fsdp"),
            P("fsdp", "sp", None),
            P("fsdp", "sp", None),
            P("fsdp", None, "sp"),
        ),
        check_vma=False,
    )
```

time: 1330 us -> 799 us (0.60)
  waiting for transfers between devices: 538 us -> 246 us
  Pallas kernels: 111 us -> 246 us
  blocking collectives: 107 us -> 0 us
  local copies, waits for them, and re-layouts: 175 us -> 71.2 us
  matrix products: 115 us -> 11.7 us
  loops' own time: 54.3 us -> 0 us
  other arithmetic: 114 us -> 83.1 us
  starting transfers between devices: 84.5 us -> 113 us
    reduce_scatter x7 -> x4, waiting for transfers between devices: 276 us -> 0.03 us  [body(): lax.psum_scatter(weight_grad, 'sp', scatter_dimension=0, tiled=False)]
    pallas_call x2 -> x12, Pallas kernels: 111 us -> 246 us  [the longest x4 108 us: run_expert(): pl.pallas_call(functools.partial(expert_step, count=count), grid=(count /...]
    dot_general x67 -> x4, matrix products: 113 us -> 9.03 us  [the longest x1 3.58 us: body(): jnp.einsum('stc,scd->td', attn_back, output_full, preferred_element_type=...]
    ppermute x0 -> x24, waiting for transfers between devices: none -> 99.2 us  [the longest x18 89.8 us: ring_pieces(): pieces.append(lax.ppermute(pieces[-1], axis_name, pairs))]
    ppermute x0 -> x24, starting transfers between devices: none -> 63.1 us  [the longest x18 51.6 us: ring_pieces(): pieces.append(lax.ppermute(pieces[-1], axis_name, pairs))]
    all_to_all x12 -> x5, waiting for transfers between devices: 119 us -> 58.6 us  [the longest x1 22.8 us: body(): lax.all_to_all(attended.reshape(sp_count, token_rows, ratio * share), 'sp...]
    another operation x18 -> x0, loops' own time: 54.3 us -> none  [the longest x4 17.6 us: backward_block(): lax.fori_loop(lowest, block_index + 1, grad_step, start_inner)]
    gather x7 -> x4, local copies, waits for them, and re-layouts: 55.9 us -> 9.47 us  [the longest x1 3.96 us: body(): jnp.take(early_grads, relative, axis=0)]
  transfers between devices with their start and end apart: 68 -> 90, of which waited for: 21 -> 36; matrix products, arithmetic and copies ran while one was open for 29% -> 19% of each run, Pallas kernels for 0% -> 31%
where the time goes in v2:
time: 799 us; the launch traced here: 788 us
  waiting for transfers between devices  246 us (31%)
  Pallas kernels  246 us (31%)
  starting transfers between devices  113 us (14%)
  other arithmetic  83.1 us (10%)
  local copies, waits for them, and re-layouts  71.2 us (9%)
  between operations  16.9 us (2%)
  matrix products  11.7 us (1%)
    pallas_call x4, Pallas kernels, run_expert(): pl.pallas_call(functools.partial(expert_step, count=count), grid=(count /...  108 us
    ppermute x18, waiting for transfers between devices, ring_pieces(): pieces.append(lax.ppermute(pieces[-1], axis_name, pairs))  89.8 us
    ppermute x52, waiting for transfers between devices, flip(): lax.ppermute(values, axis_name, [(place, place ^ bit) for place in range(...  82 us
    ppermute x18, starting transfers between devices, ring_pieces(): pieces.append(lax.ppermute(pieces[-1], axis_name, pairs))  51.6 us
    pallas_call x4, Pallas kernels, combine_rows(): pl.pallas_call(combine_step, grid=(sources // 2,), in_specs=[pl.BlockSpec...  36.9 us
    ppermute x52, starting transfers between devices, flip(): lax.ppermute(values, axis_name, [(place, place ^ bit) for place in range(...  29.9 us
    pallas_call x1, Pallas kernels, attend_back(): pl.pallas_call(attend_back_step, grid_spec=pltpu.PrefetchScalarGridSpec(n...  28.5 us
    pallas_call x1, Pallas kernels, attend(): pl.pallas_call(attend_step, grid_spec=pltpu.PrefetchScalarGridSpec(num_sc...  28.3 us
  transfers between devices with their start and end apart: 90, of which 36 were waited for; matrix products, arithmetic and copies ran while one was open for 19% of the time, Pallas kernels for 31%

profile of v2, /device:TPU:0, one launch (start us, length us, event | category | flops | bytes accessed | tf_op | source)
XLA Modules:
  0.0 787.7 jit_solution(10218418660429282868)
XLA Ops:
  21.9 12.7 %collective-permute-done.refs_3_ = bf16[512,512]{1,0:T(8,128)(2,1)S(1)} collective-permute-done((bf16[512,512]{1,0:T(8,128)(2,1)S(1)}, bf16[512,512]{1,0:T(8,128)(2,1)S(1)}, u32[]{:S(2)}, u32[]{:S(2)}) %collective-permute-start) | collective-permute-done | bytes 524320 | tf_op jit(solution)/shard_map/ppermute | solution.py:324
  34.7 10.0 %collective-permute-done.3.refs_5_ = bf16[512,512]{1,0:T(8,128)(2,1)S(1)} collective-permute-done((bf16[512,512]{1,0:T(8,128)(2,1)S(1)}, bf16[512,512]{1,0:T(8,128)(2,1)S(1)}, u32[]{:S(2)}, u32[]{:S(2)}) %collective-permute-start.3) | collective-permute-done | bytes 524320 | tf_op jit(solution)/shard_map/ppermute | solution.py:324
  49.8 8.9 %collective-permute-done.1.refs_2_ = bf16[512,512]{1,0:T(8,128)(2,1)S(1)} collective-permute-done((bf16[512,512]{1,0:T(8,128)(2,1)S(1)}, bf16[512,512]{1,0:T(8,128)(2,1)S(1)}, u32[]{:S(2)}, u32[]{:S(2)}) %collective-permute-start.1) | collective-permute-done | bytes 524320 | tf_op jit(solution)/shard_map/ppermute | solution.py:324
  58.7 11.1 %collective-permute-done.4.refs_6_ = bf16[512,512]{1,0:T(8,128)(2,1)S(1)} collective-permute-done((bf16[512,512]{1,0:T(8,128)(2,1)S(1)}, bf16[512,512]{1,0:T(8,128)(2,1)S(1)}, u32[]{:S(2)}, u32[]{:S(2)}) %collective-permute-start.4) | collective-permute-done | bytes 524320 | tf_op jit(solution)/shard_map/ppermute | solution.py:324
  72.9 9.4 %collective-permute-done.2.refs_1_ = bf16[512,512]{1,0:T(8,128)(2,1)S(1)} collective-permute-done((bf16[512,512]{1,0:T(8,128)(2,1)S(1)}, bf16[512,512]{1,0:T(8,128)(2,1)S(1)}, u32[]{:S(2)}, u32[]{:S(2)}) %collective-permute-start.2) | collective-permute-done | bytes 524320 | tf_op jit(solution)/shard_map/ppermute | solution.py:324
  82.3 7.8 collective-permute-done.5.refs_7_
  109.5 18.8 %project.1 = (bf16[2048,1024]{1,0:T(8,128)(2,1)}, bf16[2048,256]{1,0:T(8,128)(2,1)}, bf16[2048,128]{1,0:T(8,128)(2,1)}, bf16[2048,128]{1,0:T(8,128)(2,1)}) custom-call(s32[1,2048]{1,0:T(1,128)} %bitcast.237, f32[1,1024]{1,0:T(1,128)} %bitcast.239, bf16[1024,512]{1,0:T(8,128)(2,1)} %slice.809.weight_ref, f32[2048,128]{1,0:T(8,128)} %copy.169.cos_ref, ...), custom_call_target="tpu_custom_call" | custom-call | tf_op jit(solution)/shard_map/project/pallas_call | solution.py:416
  128.3 28.3 %attend.1 = (bf16[2048,256]{1,0:T(8,128)(2,1)}, f32[2048,4]{1,0:T(8,128)}) custom-call(s32[8]{0:T(128)} %and_select_fusion.2.lowest_ref, s32[2048,1]{1,0:T(8,128)} %select_select_fusion.start_ref, bf16[2048,256]{1,0:T(8,128)(2,1)} %get-tuple-element.59.query_ref, bf16[2048,128]{1,0:T(8,128)(2,1)} %get-tuple-element.60.key_ref, ...), custom_call_target="tpu_custom_call" | custom-call | tf_op jit(solution)/shard_map/attend/pallas_call | solution.py:522
  169.1 7.0 collective-permute-done.23.refs_20_
  176.1 7.9 %collective-permute-done.28.refs_26_ = bf16[512,512]{1,0:T(8,128)(2,1)} collective-permute-done((bf16[512,512]{1,0:T(8,128)(2,1)S(1)}, bf16[512,512]{1,0:T(8,128)(2,1)}, u32[]{:S(2)}, u32[]{:S(2)}) %collective-permute-start.28) | collective-permute-done | bytes 524320 | tf_op jit(solution)/shard_map/ppermute | solution.py:39
  187.1 22.8 %all-to-all-done = bf16[4,512,256]{2,1,0:T(8,128)(2,1)} async-done(((bf16[4,512,256]{2,1,0:T(8,128)(2,1)}), bf16[4,512,256]{2,1,0:T(8,128)(2,1)}, u32[]{:S(2)}, u32[]{:S(2)}) %all-to-all-start) | async-done | bytes 1048608 | tf_op jit(solution)/shard_map/all_to_all | solution.py:847
  226.5 17.0 %all-to-all-done.1 = s32[8,4,512]{2,1,0:T(4,128)S(1)} async-done(((s32[8,4,512]{2,1,0:T(4,128)}), s32[8,4,512]{2,1,0:T(4,128)S(1)}, u32[]{:S(2)}, u32[]{:S(2)}) %all-to-all-start.1) | async-done | bytes 65568 | tf_op jit(solution)/shard_map/all_to_all | solution.py:869
  257.4 7.3 collective-permute-done.11.refs_6_
  273.4 27.0 %expert.7 = (bf16[8,192,1024]{2,1,0:T(8,128)(2,1)}, bf16[8,192,1024]{2,1,0:T(8,128)(2,1)}, f32[8,1,512]{2,1,0:T(1,128)}, bf16[4,768,512]{2,1,0:T(8,128)(2,1)}) custom-call(s32[8,1,512]{2,1,0:T(1,128)} %broadcast_in_dim_squeeze.35.slot_ref, f32[8,1,512]{2,1,0:T(1,128)} %get-tuple-element.287.share_ref, bf16[4,768,512]{2,1,0:T(8,128)(2,1)} %bitcast.216, ...), custom_call_target="tpu_custom_call" | custom-call | tf_op jit(solution)/shard_map/expert/pallas_call | solution.py:241
  301.3 27.1 %expert.6 = (bf16[8,192,1024]{2,1,0:T(8,128)(2,1)}, bf16[8,192,1024]{2,1,0:T(8,128)(2,1)}, f32[8,1,512]{2,1,0:T(1,128)}, bf16[4,768,512]{2,1,0:T(8,128)(2,1)}) custom-call(s32[8,1,512]{2,1,0:T(1,128)} %broadcast_in_dim_squeeze.34.slot_ref, f32[8,1,512]{2,1,0:T(1,128)} %get-tuple-element.288.share_ref, bf16[4,768,512]{2,1,0:T(8,128)(2,1)} %bitcast.215, ...), custom_call_target="tpu_custom_call" | custom-call | tf_op jit(solution)/shard_map/expert/pallas_call | solution.py:241
  329.7 27.1 %expert.5 = (bf16[8,192,1024]{2,1,0:T(8,128)(2,1)}, bf16[8,192,1024]{2,1,0:T(8,128)(2,1)}, f32[8,1,512]{2,1,0:T(1,128)}, bf16[4,768,512]{2,1,0:T(8,128)(2,1)}) custom-call(s32[8,1,512]{2,1,0:T(1,128)} %broadcast_in_dim_squeeze.33.slot_ref, f32[8,1,512]{2,1,0:T(1,128)} %get-tuple-element.289.share_ref, bf16[4,768,512]{2,1,0:T(8,128)(2,1)} %bitcast.214, ...), custom_call_target="tpu_custom_call" | custom-call | tf_op jit(solution)/shard_map/expert/pallas_call | solution.py:241
  360.9 27.0 %expert.4 = (bf16[8,192,1024]{2,1,0:T(8,128)(2,1)}, bf16[8,192,1024]{2,1,0:T(8,128)(2,1)}, f32[8,1,512]{2,1,0:T(1,128)}, bf16[4,768,512]{2,1,0:T(8,128)(2,1)}) custom-call(s32[8,1,512]{2,1,0:T(1,128)} %broadcast_in_dim_squeeze.32.slot_ref, f32[8,1,512]{2,1,0:T(1,128)} %get-tuple-element.290.share_ref, bf16[4,768,512]{2,1,0:T(8,128)(2,1)} %bitcast.217, ...), custom_call_target="tpu_custom_call" | custom-call | tf_op jit(solution)/shard_map/expert/pallas_call | solution.py:241
  388.0 9.1 %combine.7 = (bf16[4,512,512]{2,1,0:T(8,128)(2,1)}, bf16[4,512,512]{2,1,0:T(8,128)(2,1)}) custom-call(s32[8,512,4]{2,1,0:T(8,128)} %get-tuple-element.218.slot_ref, bf16[8,192,1024]{2,1,0:T(8,128)(2,1)} %get-tuple-element.76.refs_0_, bf16[8,192,1024]{2,1,0:T(8,128)(2,1)} %get-tuple-element.77.refs_1_, bf16[8,192,1024]{2,1,0:T(8,128)(2,1)} %get-tuple-element.78.refs_2_, ...), custom_call_target="tpu_custom_call" | custom-call | tf_op jit(solution)/shard_map/combine/pallas_call | solution.py:301
  397.6 9.5 %combine.6 = (bf16[4,512,512]{2,1,0:T(8,128)(2,1)}, bf16[4,512,512]{2,1,0:T(8,128)(2,1)}) custom-call(s32[8,512,4]{2,1,0:T(8,128)} %get-tuple-element.218.slot_ref, bf16[8,192,1024]{2,1,0:T(8,128)(2,1)} %get-tuple-element.76.refs_0_, bf16[8,192,1024]{2,1,0:T(8,128)(2,1)} %get-tuple-element.77.refs_1_, bf16[8,192,1024]{2,1,0:T(8,128)(2,1)} %get-tuple-element.78.refs_2_, ...), custom_call_target="tpu_custom_call" | custom-call | tf_op jit(solution)/shard_map/combine/pallas_call | solution.py:301
  422.5 18.8 %all-to-all-done.3 = f32[8,4,512]{2,1,0:T(4,128)S(1)} async-done(((f32[8,4,512]{2,1,0:T(4,128)}), f32[8,4,512]{2,1,0:T(4,128)S(1)}, u32[]{:S(2)}, u32[]{:S(2)}) %all-to-all-start.3) | async-done | bytes 65568 | tf_op jit(solution)/shard_map/all_to_all | solution.py:898
  451.9 7.3 collective-permute-done.36
  498.3 6.3 collective-permute-done.65
  516.6 23.1 %collective-permute-done.67 = bf16[128,640]{1,0:T(8,128)(2,1)S(1)} collective-permute-done((bf16[128,640]{1,0:T(8,128)(2,1)S(1)}, bf16[128,640]{1,0:T(8,128)(2,1)S(1)}, u32[]{:S(2)}, u32[]{:S(2)}) %collective-permute-start.67) | collective-permute-done | bytes 163872 | tf_op jit(solution)/shard_map/ppermute | solution.py:324
  539.7 22.0 %collective-permute-start.68 = (bf16[128,640]{1,0:T(8,128)(2,1)S(1)}, bf16[128,640]{1,0:T(8,128)(2,1)}, u32[]{:S(2)}, u32[]{:S(2)}) collective-permute-start(bf16[128,640]{1,0:T(8,128)(2,1)S(1)} %collective-permute-done.67), channel_id=1, source_target_pairs={{0,1},{1,2},{2,3},{3,0},{4,5},{5,6},{6,7},{7,4},{8,9},{9,10},{10,1... | collective-permute-start | bytes 491528 | tf_op jit(solution)/shard_map/ppermute | solution.py:324
  563.2 9.2 %combine.5 = (bf16[4,512,512]{2,1,0:T(8,128)(2,1)}, bf16[4,512,512]{2,1,0:T(8,128)(2,1)}) custom-call(s32[8,512,4]{2,1,0:T(8,128)} %get-tuple-element.218.slot_ref, bf16[8,192,1024]{2,1,0:T(8,128)(2,1)} %get-tuple-element.66.refs_0_, bf16[8,192,1024]{2,1,0:T(8,128)(2,1)} %get-tuple-element.68.refs_1_, bf16[8,192,1024]{2,1,0:T(8,128)(2,1)} %get-tuple-element.70.refs_2_, ...), custom_call_target="tpu_custom_call" | custom-call | tf_op jit(solution)/shard_map/combine/pallas_call | solution.py:301
  572.4 9.1 %combine.4 = (bf16[4,512,512]{2,1,0:T(8,128)(2,1)}, bf16[4,512,512]{2,1,0:T(8,128)(2,1)}) custom-call(s32[8,512,4]{2,1,0:T(8,128)} %get-tuple-element.218.slot_ref, bf16[8,192,1024]{2,1,0:T(8,128)(2,1)} %get-tuple-element.66.refs_0_, bf16[8,192,1024]{2,1,0:T(8,128)(2,1)} %get-tuple-element.68.refs_1_, bf16[8,192,1024]{2,1,0:T(8,128)(2,1)} %get-tuple-element.70.refs_2_, ...), custom_call_target="tpu_custom_call" | custom-call | tf_op jit(solution)/shard_map/combine/pallas_call | solution.py:301
  588.3 28.5 %attend_back.1 = (f32[2048,256]{1,0:T(8,128)}, f32[2048,128]{1,0:T(8,128)}, f32[2048,128]{1,0:T(8,128)}) custom-call(s32[8]{0:T(128)} %and_select_fusion.2.lowest_ref, s32[2048,1]{1,0:T(8,128)} %select_select_fusion.start_ref, f32[2048,4]{1,0:T(8,128)} %get-tuple-element.91.log_ref, bf16[2048,256]{1,0:T(8,128)(2,1)} %get-tuple-element.59.query_ref, ...), custom_call_target="tpu_custom_call" | custom-call | tf_op jit(solution)/shard_map/attend_back/pallas_call | solution.py:598
  616.8 25.5 %project_back.1 = (bf16[2048,1024]{1,0:T(8,128)(2,1)}, bf16[1024,512]{1,0:T(8,128)(2,1)}, f32[1,1024]{1,0:T(1,128)}) custom-call(s32[1]{0:T(128)} %bitcast.53.own_ref, s32[2048,1]{1,0:T(8,128)} %copy.177.order_ref, f32[1,1024]{1,0:T(1,128)} %bitcast.240, bf16[1024,512]{1,0:T(8,128)(2,1)} %slice.809.weight_ref, f32[2048,128]{1,0:T(8,128)} %copy.169.cos_ref, ...), custom_call_target="tpu_custom_call" | custom-call | tf_op jit(solution)/shard_map/project_back/pallas_call | solution.py:714
  666.6 6.0 collective-permute-done.53
  717.1 6.1 collective-permute-done.50
  748.5 14.7 %collective-permute-done.41 = bf16[2,512,512]{2,1,0:T(8,128)(2,1)S(1)} collective-permute-done((bf16[2,512,512]{2,1,0:T(8,128)(2,1)S(1)}, bf16[2,512,512]{2,1,0:T(8,128)(2,1)S(1)}, u32[]{:S(2)}, u32[]{:S(2)}) %collective-permute-start.41) | collective-permute-done | bytes 1048608 | tf_op jit(solution)/shard_map/ppermute | solution.py:39
  763.8 5.9 collective-permute-done.44
  (472 shorter events, 292.6 us)
Async XLA Ops:
  7.2 98.0 %all-gather.10.cloned.1.call-start = ((), (), s32[]{:S(2)}) async-start(), calls=%async_computation.9 | async-start | bytes 3833856 | tf_op jit(solution)/shard_map/all_gather | solution.py:806
  16.6 256.8 %all-gather.18.cloned.1.call-start = ((), (), s32[]{:S(2)}) async-start(), calls=%async_computation.17 | async-start | bytes 3932160 | tf_op jit(solution)/shard_map/all_gather | solution.py:827
  90.9 210.4 %all-gather.16.cloned.1.call-start = ((), (), s32[]{:S(2)}) async-start(), calls=%async_computation.16 | async-start | bytes 3932160 | tf_op jit(solution)/shard_map/all_gather | solution.py:827
  91.7 238.0 %all-gather.14.cloned.1.call-start = ((), (), s32[]{:S(2)}) async-start(), calls=%async_computation.15 | async-start | bytes 3932160 | tf_op jit(solution)/shard_map/all_gather | solution.py:827
  156.6 53.3 %all-to-all-start = ((bf16[4,512,256]{2,1,0:T(8,128)(2,1)}), bf16[4,512,256]{2,1,0:T(8,128)(2,1)}, u32[]{:S(2)}, u32[]{:S(2)}) async-start(bf16[4,512,256]{2,1,0:T(8,128)(2,1)} %bitcast.211), calls=%async_computation | async-start | bytes 2097152 | tf_op jit(solution)/shard_map/all_to_all | solution.py:847
  161.0 199.9 %all-gather.12.cloned.1.call-start = ((), (), s32[]{:S(2)}) async-start(), calls=%async_computation.14 | async-start | bytes 3932160 | tf_op jit(solution)/shard_map/all_gather | solution.py:827
  163.9 49.6 %collective-permute-start.30 = (bf16[512,512]{1,0:T(8,128)(2,1)S(1)}, bf16[512,512]{1,0:T(8,128)(2,1)}, u32[]{:S(2)}, u32[]{:S(2)}) collective-permute-start(bf16[512,512]{1,0:T(8,128)(2,1)S(1)} %get-tuple-element.241.refs_24_), channel_id=1, source_target_pairs={{0,16},{4,20},{8,24},{12,28},{16,0},{20,4},{24,8},{28,12},{1,17},{... | collective-permute-start | bytes 1572872 | tf_op jit(solution)/shard_map/ppermute | solution.py:39
  165.9 47.7 %collective-permute-start.20 = (bf16[512,512]{1,0:T(8,128)(2,1)S(1)}, bf16[512,512]{1,0:T(8,128)(2,1)S(1)}, u32[]{:S(2)}, u32[]{:S(2)}) collective-permute-start(bf16[512,512]{1,0:T(8,128)(2,1)S(1)} %get-tuple-element.242.refs_16_), channel_id=1, source_target_pairs={{0,4},{4,0},{8,12},{12,8},{16,20},{20,16},{24,28},{28,24},{1,5},{5... | collective-permute-start | bytes 1572872 | tf_op jit(solution)/shard_map/ppermute | solution.py:39
  176.1 38.1 %collective-permute-start.27 = (bf16[512,512]{1,0:T(8,128)(2,1)S(1)}, bf16[512,512]{1,0:T(8,128)(2,1)S(1)}, u32[]{:S(2)}, u32[]{:S(2)}) collective-permute-start(bf16[512,512]{1,0:T(8,128)(2,1)S(1)} %get-tuple-element.241.refs_24_), channel_id=1, source_target_pairs={{0,4},{4,0},{8,12},{12,8},{16,20},{20,16},{24,28},{28,24},{1,5},{5... | collective-permute-start | bytes 1572872 | tf_op jit(solution)/shard_map/ppermute | solution.py:39
  184.0 30.3 %collective-permute-start.25 = (bf16[512,512]{1,0:T(8,128)(2,1)S(1)}, bf16[512,512]{1,0:T(8,128)(2,1)}, u32[]{:S(2)}, u32[]{:S(2)}) collective-permute-start(bf16[512,512]{1,0:T(8,128)(2,1)S(1)} %collective-permute-done.23.refs_20_), channel_id=1, source_target_pairs={{0,8},{4,12},{8,0},{12,4},{16,24},{20,28},{24,16},{28,20},{1,9},{5... | collective-permute-start | bytes 1572872 | tf_op jit(solution)/shard_map/ppermute | solution.py:39
  216.5 33.1 %collective-permute-start.33 = (bf16[512,512]{1,0:T(8,128)(2,1)}, bf16[512,512]{1,0:T(8,128)(2,1)}, u32[]{:S(2)}, u32[]{:S(2)}) collective-permute-start(bf16[512,512]{1,0:T(8,128)(2,1)} %collective-permute-done.32.refs_30_), channel_id=1, source_target_pairs={{0,4},{4,0},{8,12},{12,8},{16,20},{20,16},{24,28},{28,24},{1,5},{5... | collective-permute-start | bytes 1572872 | tf_op jit(solution)/shard_map/ppermute | solution.py:39
  217.2 32.8 %collective-permute-start.14 = (bf16[512,512]{1,0:T(8,128)(2,1)}, bf16[512,512]{1,0:T(8,128)(2,1)}, u32[]{:S(2)}, u32[]{:S(2)}) collective-permute-start(bf16[512,512]{1,0:T(8,128)(2,1)} %get-tuple-element.243.refs_8_), channel_id=1, source_target_pairs={{0,8},{4,12},{8,0},{12,4},{16,24},{20,28},{24,16},{28,20},{1,9},{5... | collective-permute-start | bytes 1572872 | tf_op jit(solution)/shard_map/ppermute | solution.py:39
  217.3 34.5 %collective-permute-start.16 = (bf16[512,512]{1,0:T(8,128)(2,1)}, bf16[512,512]{1,0:T(8,128)(2,1)}, u32[]{:S(2)}, u32[]{:S(2)}) collective-permute-start(bf16[512,512]{1,0:T(8,128)(2,1)} %get-tuple-element.243.refs_8_), channel_id=1, source_target_pairs={{0,16},{4,20},{8,24},{12,28},{16,0},{20,4},{24,8},{28,12},{1,17},{... | collective-permute-start | bytes 1572872 | tf_op jit(solution)/shard_map/ppermute | solution.py:39
  219.6 30.0 %collective-permute-start.9 = (bf16[512,512]{1,0:T(8,128)(2,1)}, bf16[512,512]{1,0:T(8,128)(2,1)}, u32[]{:S(2)}, u32[]{:S(2)}) collective-permute-start(bf16[512,512]{1,0:T(8,128)(2,1)} %get-tuple-element.244.refs_0_), channel_id=1, source_target_pairs={{0,16},{4,20},{8,24},{12,28},{16,0},{20,4},{24,8},{28,12},{1,17},{... | collective-permute-start | bytes 1572872 | tf_op jit(solution)/shard_map/ppermute | solution.py:39
  220.2 31.6 %collective-permute-start.7 = (bf16[512,512]{1,0:T(8,128)(2,1)}, bf16[512,512]{1,0:T(8,128)(2,1)}, u32[]{:S(2)}, u32[]{:S(2)}) collective-permute-start(bf16[512,512]{1,0:T(8,128)(2,1)} %get-tuple-element.244.refs_0_), channel_id=1, source_target_pairs={{0,8},{4,12},{8,0},{12,4},{16,24},{20,28},{24,16},{28,20},{1,9},{5... | collective-permute-start | bytes 1572872 | tf_op jit(solution)/shard_map/ppermute | solution.py:39
  256.7 473.0 %reduce-scatter.11.cloned.1.call-start = ((), (), s32[]{:S(2)}) async-start(), calls=%async_computation.13 | async-start | bytes 3932160 | tf_op jit(solution)/shard_map/reduce_scatter | solution.py:891
  300.4 430.5 %reduce-scatter.9.cloned.1.call-start = ((), (), s32[]{:S(2)}) async-start(), calls=%async_computation.12 | async-start | bytes 3932160 | tf_op jit(solution)/shard_map/reduce_scatter | solution.py:891
  411.4 30.0 %collective-permute-start.35 = (bf16[2,512,512]{2,1,0:T(8,128)(2,1)}, bf16[2,512,512]{2,1,0:T(8,128)(2,1)}, u32[]{:S(2)}, u32[]{:S(2)}) collective-permute-start(bf16[2,512,512]{2,1,0:T(8,128)(2,1)} %get-tuple-element.190), channel_id=1, source_target_pairs={{0,8},{4,12},{8,0},{12,4},{16,24},{20,28},{24,16},{28,20},{1,9},{5... | collective-permute-start | bytes 3145736 | tf_op jit(solution)/shard_map/ppermute | solution.py:39
  415.5 30.9 %collective-permute-start.38 = (bf16[2,512,512]{2,1,0:T(8,128)(2,1)}, bf16[2,512,512]{2,1,0:T(8,128)(2,1)}, u32[]{:S(2)}, u32[]{:S(2)}) collective-permute-start(bf16[2,512,512]{2,1,0:T(8,128)(2,1)} %get-tuple-element.192), channel_id=1, source_target_pairs={{0,16},{4,20},{8,24},{12,28},{16,0},{20,4},{24,8},{28,12},{1,17},{... | collective-permute-start | bytes 3145736 | tf_op jit(solution)/shard_map/ppermute | solution.py:39
  421.7 311.8 %reduce-scatter.7.cloned.1.call-start = ((), (), s32[]{:S(2)}) async-start(), calls=%async_computation.11 | async-start | bytes 3932160 | tf_op jit(solution)/shard_map/reduce_scatter | solution.py:891
  489.2 96.8 %all-to-all-start.4 = ((bf16[4,512,256]{1,2,0:T(8,128)(2,1)}), bf16[4,512,256]{1,2,0:T(8,128)(2,1)}, u32[]{:S(2)}, u32[]{:S(2)}) async-start(bf16[4,512,256]{1,2,0:T(8,128)(2,1)} %fusion.9), calls=%async_computation.4 | async-start | bytes 2097152 | tf_op jit(solution)/shard_map/all_to_all | solution.py:921
  493.4 242.8 %reduce-scatter.5.cloned.1.call-start = ((), (), s32[]{:S(2)}) async-start(), calls=%async_computation.10 | async-start | bytes 3932160 | tf_op jit(solution)/shard_map/reduce_scatter | solution.py:891
  512.9 48.8 %collective-permute-start.73 = (bf16[128,640]{1,0:T(8,128)(2,1)S(1)}, bf16[128,640]{1,0:T(8,128)(2,1)S(1)}, u32[]{:S(2)}, u32[]{:S(2)}) collective-permute-start(bf16[128,640]{1,0:T(8,128)(2,1)S(1)} %fusion.53), channel_id=1, source_target_pairs={{0,3},{1,0},{2,1},{3,2},{4,7},{5,4},{6,5},{7,6},{8,11},{9,8},{10,9... | collective-permute-start | bytes 491528 | tf_op jit(solution)/shard_map/ppermute | solution.py:324
  539.7 41.9 %collective-permute-start.68 = (bf16[128,640]{1,0:T(8,128)(2,1)S(1)}, bf16[128,640]{1,0:T(8,128)(2,1)}, u32[]{:S(2)}, u32[]{:S(2)}) collective-permute-start(bf16[128,640]{1,0:T(8,128)(2,1)S(1)} %collective-permute-done.67), channel_id=1, source_target_pairs={{0,1},{1,2},{2,3},{3,0},{4,5},{5,6},{6,7},{7,4},{8,9},{9,10},{10,1... | collective-permute-start | bytes 491528 | tf_op jit(solution)/shard_map/ppermute | solution.py:324
  581.5 80.3 %collective-permute-start.69 = (bf16[128,640]{1,0:T(8,128)(2,1)}, bf16[128,640]{1,0:T(8,128)(2,1)}, u32[]{:S(2)}, u32[]{:S(2)}) collective-permute-start(bf16[128,640]{1,0:T(8,128)(2,1)} %collective-permute-done.68), channel_id=1, source_target_pairs={{0,1},{1,2},{2,3},{3,0},{4,5},{5,6},{6,7},{7,4},{8,9},{9,10},{10,1... | collective-permute-start | bytes 491528 | tf_op jit(solution)/shard_map/ppermute | solution.py:324
  585.9 72.5 %collective-permute-start.75 = (bf16[128,640]{1,0:T(8,128)(2,1)}, bf16[128,640]{1,0:T(8,128)(2,1)}, u32[]{:S(2)}, u32[]{:S(2)}) collective-permute-start(bf16[128,640]{1,0:T(8,128)(2,1)} %collective-permute-done.74), channel_id=1, source_target_pairs={{0,3},{1,0},{2,1},{3,2},{4,7},{5,4},{6,5},{7,6},{8,11},{9,8},{10,9... | collective-permute-start | bytes 491528 | tf_op jit(solution)/shard_map/ppermute | solution.py:324
  656.2 34.7 %collective-permute-start.46 = (bf16[512,512]{1,0:T(8,128)(2,1)}, bf16[512,512]{1,0:T(8,128)(2,1)S(1)}, u32[]{:S(2)}, u32[]{:S(2)}) collective-permute-start(bf16[512,512]{1,0:T(8,128)(2,1)} %get-tuple-element.199), channel_id=1, source_target_pairs={{0,1},{1,2},{2,3},{3,0},{4,5},{5,6},{6,7},{7,4},{8,9},{9,10},{10,1... | collective-permute-start | bytes 1572872 | tf_op jit(solution)/shard_map/ppermute | solution.py:338
  658.4 39.0 %collective-permute-start.49 = (bf16[512,512]{1,0:T(8,128)(2,1)}, bf16[512,512]{1,0:T(8,128)(2,1)}, u32[]{:S(2)}, u32[]{:S(2)}) collective-permute-start(bf16[512,512]{1,0:T(8,128)(2,1)} %get-tuple-element.200), channel_id=1, source_target_pairs={{0,3},{1,0},{2,1},{3,2},{4,7},{5,4},{6,5},{7,6},{8,11},{9,8},{10,9... | collective-permute-start | bytes 1572872 | tf_op jit(solution)/shard_map/ppermute | solution.py:338
  661.8 75.6 %collective-permute-start.40 = (bf16[4,512,512]{2,1,0:T(8,128)(2,1)}, bf16[4,512,512]{2,1,0:T(8,128)(2,1)}, u32[]{:S(2)}, u32[]{:S(2)}) collective-permute-start(bf16[4,512,512]{2,1,0:T(8,128)(2,1)} %get-tuple-element.88), channel_id=1, source_target_pairs={{0,4},{4,0},{8,12},{12,8},{16,20},{20,16},{24,28},{28,24},{1,5},{5... | collective-permute-start | bytes 6291464 | tf_op jit(solution)/shard_map/ppermute | solution.py:39
  690.9 49.6 %collective-permute-start.43 = (bf16[4,512,512]{2,1,0:T(8,128)(2,1)}, bf16[4,512,512]{2,1,0:T(8,128)(2,1)}, u32[]{:S(2)}, u32[]{:S(2)}) collective-permute-start(bf16[4,512,512]{2,1,0:T(8,128)(2,1)} %get-tuple-element.90), channel_id=1, source_target_pairs={{0,4},{4,0},{8,12},{12,8},{16,20},{20,16},{24,28},{28,24},{1,5},{5... | collective-permute-start | bytes 6291464 | tf_op jit(solution)/shard_map/ppermute | solution.py:39
  725.9 46.4 %collective-permute-start.48 = (bf16[512,512]{1,0:T(8,128)(2,1)}, bf16[512,512]{1,0:T(8,128)(2,1)}, u32[]{:S(2)}, u32[]{:S(2)}) collective-permute-start(bf16[512,512]{1,0:T(8,128)(2,1)} %get-tuple-element.195), channel_id=1, source_target_pairs={{0,1},{1,2},{2,3},{3,0},{4,5},{5,6},{6,7},{7,4},{8,9},{9,10},{10,1... | collective-permute-start | bytes 1572872 | tf_op jit(solution)/shard_map/ppermute | solution.py:338
  726.8 45.4 %collective-permute-start.51 = (bf16[512,512]{1,0:T(8,128)(2,1)}, bf16[512,512]{1,0:T(8,128)(2,1)}, u32[]{:S(2)}, u32[]{:S(2)}) collective-permute-start(bf16[512,512]{1,0:T(8,128)(2,1)} %get-tuple-element.196), channel_id=1, source_target_pairs={{0,3},{1,0},{2,1},{3,2},{4,7},{5,4},{6,5},{7,6},{8,11},{9,8},{10,9... | collective-permute-start | bytes 1572872 | tf_op jit(solution)/shard_map/ppermute | solution.py:338
  (118 other events, 1307.6 us)
Sparse Core Ops, SparseCore 0:
  16.7 36.1 all-gather.9
  91.0 63.5 all-gather.17
  156.2 76.8 all-gather.15
  234.5 62.6 all-gather.13
  298.7 62.1 all-gather.11
  363.1 58.8 reduce-scatter.10
  424.3 60.2 reduce-scatter.8
  486.9 90.8 reduce-scatter.6
  581.7 64.0 reduce-scatter.4

commit v3 on v2

--- a/solution.py
+++ b/solution.py
@@ -46,16 +46,29 @@
     return (high, high[1:2] + high[:1] + high[2:])
 
 
-def gather_pieces(values, axis_name):
+def gather_begin(values):
+    half = values.shape[1] // 2
+    return [{0: values[:, :half]}, {0: values[:, half:]}]
+
+
+def gather_stage(lists, axis_name, stage, gates=()):
     count = lax.axis_size(axis_name)
-    half = values.shape[1] // 2
-    lists = []
-    for order, part in zip(stage_orders(count), (values[:, :half], values[:, half:])):
-        pieces = {0: part}
-        for bit in order:
-            pieces.update({r ^ bit: flip(piece, axis_name, bit) for r, piece in list(pieces.items())})
-        lists.append([pieces[r] for r in range(count)])
-    return lists
+    grown = []
+    for order, pieces in zip(stage_orders(count), lists):
+        keys = list(pieces)
+        held = after([pieces[r] for r in keys], *gates) if gates else [pieces[r] for r in keys]
+        new = dict(zip(keys, held))
+        new.update({r ^ order[stage]: flip(new[r], axis_name, order[stage]) for r in keys})
+        grown.append(new)
+    return grown
+
+
+def gather_end(lists):
+    return [pieces[r] for pieces in lists for r in sorted(pieces)]
+
+
+def newest(lists, stage):
+    return [piece for pieces in lists for piece in list(pieces.values())[1 << stage :]]
 
 
 def chunk_place(index, order):
@@ -65,32 +78,33 @@
     return place
 
 
-def reduce_halves(leave, stay, axis_name):
+def reduce_stage(leave, stay, axis_name, stage):
     count = lax.axis_size(axis_name)
-    sums = []
+    gone_next, kept_next = [], []
     for order, gone, kept in zip(stage_orders(count), leave, stay):
-        for bit in order[::-1]:
-            arrived = flip(gone, axis_name, bit).astype(jnp.float32)
-            middle = kept.shape[0] // 2
-            if middle:
-                gone = (kept[middle:].astype(jnp.float32) + arrived[middle:]).astype(jnp.bfloat16)
-                kept = (kept[:middle].astype(jnp.float32) + arrived[:middle]).astype(jnp.bfloat16)
-            else:
-                kept = kept[0].astype(jnp.float32) + arrived[0]
-        sums.append(kept)
-    return jnp.concatenate(sums, axis=1)
-
-
-def reduce_rows(values, axis_name):
-    count = lax.axis_size(axis_name)
-    half = values.shape[2] // 2
-    leave, stay = [], []
-    for order, part in zip(stage_orders(count), (values[:, :, :half], values[:, :, half:])):
-        later = order[:-1][::-1]
-        evens = sorted(range(count // 2), key=lambda i: chunk_place(i, later))
-        leave.append(jnp.stack([part[2 * i + 1] for i in evens]))
-        stay.append(jnp.stack([part[2 * i] for i in evens]))
-    return reduce_halves(leave, stay, axis_name)
+        arrived = flip(gone, axis_name, order[::-1][stage])
+        middle = kept.shape[0] // 2
+        if middle:
+            total = kept[middle:].astype(jnp.float32) + arrived[middle:].astype(jnp.float32)
+            gone_next.append(total.astype(jnp.bfloat16))
+            total = kept[:middle].astype(jnp.float32) + arrived[:middle].astype(jnp.float32)
+            kept_next.append(total.astype(jnp.bfloat16))
+        else:
+            kept_next.append(kept[0].astype(jnp.float32) + arrived[0].astype(jnp.float32))
+    return gone_next, kept_next
+
+
+def after(values, *others):
+    held = lax.optimization_barrier((*values, *others))
+    return list(held[: len(values)])
+
+
+def shift_pairs(count, by):
+    return [(place, (place + by) % count) for place in range(count)]
+
+
+def exchange_blocks(values, axis_name):
+    return lax.all_to_all(values, axis_name, split_axis=0, concat_axis=0, tiled=True)
 
 
 def pack_expert(gate, up, down):
@@ -214,11 +228,11 @@
     @pl.when(step == steps - 1)
     def _():
         gate_sum = contract(act_rows[...], gate_rows[...], 0, 0).astype(jnp.bfloat16)
-        weight_grad_ref[:, :deep, :] = gate_sum.reshape(shards, deep, hidden_width)
         up_sum = contract(act_rows[...], up_rows[...], 0, 0).astype(jnp.bfloat16)
-        weight_grad_ref[:, deep : 2 * deep, :] = up_sum.reshape(shards, deep, hidden_width)
         for shard in range(shards):
             cols = slice(shard * deep, (shard + 1) * deep)
+            weight_grad_ref[shard, :deep, :] = gate_sum[cols]
+            weight_grad_ref[shard, deep : 2 * deep, :] = up_sum[cols]
             down_sum = contract(hidden_rows[...], down_rows[:, cols], 0, 0).astype(jnp.bfloat16)
             for k in range(hidden_width // deep):
                 weight_grad_ref[shard, 2 * deep :, k * deep : (k + 1) * deep] = down_sum[
@@ -235,7 +249,7 @@
     low = jnp.bfloat16
 
     def by_source(*shape):
-        return pl.BlockSpec((pair,) + shape, lambda s: (s,) + (0,) * len(shape))
+        return pl.BlockSpec((pair,) + shape, lambda s, *_: (s,) + (0,) * len(shape))
 
     anywhere = pl.BlockSpec(memory_space=pl.ANY)
     outs = pl.pallas_call(
@@ -247,13 +261,7 @@
             by_source(CAP, 2 * half),
             by_source(CAP, 2 * half),
             by_source(1, rows),
-            pl.BlockSpec(weights.shape, lambda s: (0, 0, 0)),
-        ],
-        out_shape=[
-            jax.ShapeDtypeStruct((count, CAP, 2 * half), low),
-            jax.ShapeDtypeStruct((count, CAP, 2 * half), low),
-            jax.ShapeDtypeStruct((count, 1, rows), jnp.float32),
-            jax.ShapeDtypeStruct(weights.shape, low),
+            pl.BlockSpec(weights.shape, lambda *_: (0, 0, 0)),
         ],
         scratch_shapes=[
             pltpu.VMEM((2, pair, 2, rows, half), low),
@@ -264,6 +272,12 @@
             pltpu.VMEM((listed, 2 * half), low),
             pltpu.VMEM((listed, hidden_width), low),
             pltpu.VMEM((listed, hidden_width), low),
+        ],
+        out_shape=[
+            jax.ShapeDtypeStruct((count, CAP, 2 * half), low),
+            jax.ShapeDtypeStruct((count, CAP, 2 * half), low),
+            jax.ShapeDtypeStruct((count, 1, rows), jnp.float32),
+            jax.ShapeDtypeStruct(weights.shape, low),
         ],
         compiler_params=pltpu.CompilerParams(
             dimension_semantics=("arbitrary",), vmem_limit_bytes=VMEM_LIMIT
@@ -312,36 +326,40 @@
     )(slots_by_row, *parts)
 
 
-def ring_pieces(values, axis_name):
+def ring_begin(values):
+    half = values.shape[1] // 2
+    return [values[:, :half]], [values[:, half:]]
+
+
+def ring_step(lists, axis_name, gates=()):
     count = lax.axis_size(axis_name)
-    ahead = [(place, (place + 1) % count) for place in range(count)]
-    behind = [(place, (place - 1) % count) for place in range(count)]
-    half = values.shape[1] // 2
-    lists = []
-    for pairs, part in ((ahead, values[:, :half]), (behind, values[:, half:])):
-        pieces = [part]
-        for _ in range(count - 1):
-            pieces.append(lax.ppermute(pieces[-1], axis_name, pairs))
-        lists.append(pieces)
-    return lists
-
-
-def ring_reduce(values, axis_name):
+    moving = [part[-1] for part in lists]
+    if gates:
+        moving = after(moving, *gates)
+    return [
+        part + [lax.ppermute(one, axis_name, shift_pairs(count, by))]
+        for by, part, one in zip((1, -1), lists, moving)
+    ]
+
+
+def reduce_ring_begin(values):
+    half = values.shape[2] // 2
+    parts = (values[:, :, :half], values[:, :, half:])
+    return [part[turn % values.shape[0]] for turn, part in zip((-1, 1), parts)], parts
+
+
+def reduce_ring_step(state, axis_name, step, gates=()):
+    moving, parts = state
     count = lax.axis_size(axis_name)
-    ahead = [(place, (place + 1) % count) for place in range(count)]
-    behind = [(place, (place - 1) % count) for place in range(count)]
-    half = values.shape[2] // 2
-    sums = []
-    for pairs, turn, part in ((ahead, -1, values[:, :, :half]), (behind, 1, values[:, :, half:])):
-        moving = part[turn % count]
-        for step in range(1, count):
-            moving = lax.ppermute(moving, axis_name, pairs)
-            own = part[(turn * (step + 1)) % count]
-            moving = moving.astype(jnp.float32) + own.astype(jnp.float32)
-            if step < count - 1:
-                moving = moving.astype(jnp.bfloat16)
-        sums.append(moving)
-    return jnp.concatenate(sums, axis=1)
+    if gates:
+        moving = after(moving, *gates)
+    made = []
+    for turn, part, one in zip((-1, 1), parts, moving):
+        arrived = lax.ppermute(one, axis_name, shift_pairs(count, -turn))
+        own = part[(turn * (step + 1)) % count]
+        total = arrived.astype(jnp.float32) + own.astype(jnp.float32)
+        made.append(total.astype(jnp.bfloat16) if step < count - 1 else total)
+    return made, parts
 
 
 def sequence_starts(length_row, places):
@@ -641,8 +659,7 @@
     rows_ref,
     residual_ref,
     out_ref,
-    weight_grad_ref,
-    gain_grad_ref,
+    late_ref,
     act_rows,
     grad_rows,
     token_rows,
@@ -685,10 +702,17 @@
 
         @pl.when(block == blocks - 1)
         def _():
-            weight_grad_ref[...] = contract(act_rows[...], grad_rows[...], 0, 0).astype(
-                jnp.bfloat16
-            )
-            gain_grad_ref[...] = gain_sum[...]
+            columns = grad_rows.shape[1]
+            sums = contract(act_rows[...], grad_rows[...], 0, 0)
+            late_ref[:, :columns] = sums.astype(jnp.bfloat16)
+            for first in range(0, width, 128):
+                part = jnp.broadcast_to(gain_sum[:, first : first + 128], (128, 128))
+                row = lax.broadcasted_iota(jnp.int32, (128, 128), 0)
+                lane = lax.broadcasted_iota(jnp.int32, (128, 128), 1)
+                column = jnp.sum(jnp.where(row == lane, part, 0.0), axis=1, keepdims=True)
+                late_ref[first : first + 128, columns:] = jnp.broadcast_to(
+                    column, (128, 128)
+                ).astype(jnp.bfloat16)
 
     @pl.when(phase == 1)
     def _():
@@ -730,8 +754,7 @@
             ],
             out_specs=[
                 late(width),
-                pl.BlockSpec((width, columns), lambda *_: (0, 0)),
-                pl.BlockSpec((1, width), lambda *_: (0, 0)),
+                pl.BlockSpec((width, columns + 128), lambda *_: (0, 0)),
             ],
             scratch_shapes=[
                 pltpu.VMEM((rows, width), low),
@@ -742,8 +765,7 @@
         ),
         out_shape=[
             jax.ShapeDtypeStruct((rows, width), low),
-            jax.ShapeDtypeStruct((width, columns), low),
-            jax.ShapeDtypeStruct((1, width), jnp.float32),
+            jax.ShapeDtypeStruct((width, columns + 128), low),
         ],
         compiler_params=pltpu.CompilerParams(
             dimension_semantics=("arbitrary", "arbitrary"), vmem_limit_bytes=VMEM_LIMIT
@@ -814,17 +836,19 @@
     gain_attend = rest[:, EXPERTS].astype(jnp.float32)[None, :]
     gain_mixer = rest[:, EXPERTS + 1].astype(jnp.float32)[None, :]
 
-    left, right = ring_pieces(tokens, "sp")
-    pieces = [left[-k % sp_count] for k in range(sp_count)] + right
-    expert_parts = [
-        pack_expert(expert_gate[e].astype(low), expert_up[e].astype(low), expert_down[e].astype(low))
-        for e in range(local_experts)
-    ]
-    *expert_parts, routes, _, _ = lax.optimization_barrier(
-        (*expert_parts, routes, left[-1], right[-1])
-    )
-    cot_source, _, _ = lax.optimization_barrier((cotangent, left[1], right[1]))
-    expert_weights = [lax.all_gather(part, "sp", axis=0, tiled=False) for part in expert_parts]
+    expert_range = jnp.arange(EXPERTS, dtype=jnp.int32)
+    member = jnp.any(routes[:, :, None] == expert_range[None, None, :], axis=1)
+    row_range = jnp.arange(token_rows, dtype=jnp.int32)
+    upto = (row_range[:, None] <= row_range[None, :]).astype(low)
+    rank = jnp.dot(member.T.astype(low), upto, preferred_element_type=jnp.float32)
+    slots = jnp.where(member.T, rank.astype(jnp.int32) - 1, -1)
+
+    def to_experts(by_expert):
+        arrived = exchange_blocks(
+            by_expert.reshape(fsdp_count, local_experts, token_rows), "fsdp"
+        )
+        return jnp.swapaxes(jnp.take(arrived, relative, axis=0), 0, 1)
+
     order_row = dealing[0]
     order_here = lax.dynamic_slice_in_dim(
         jnp.concatenate([order_row, order_row]), sp_index * token_rows, group_rows
@@ -839,17 +863,43 @@
     cosine = jnp.tile(jnp.cos(angles), (1, 4))
     sine = jnp.sin(angles)
     sine = jnp.concatenate([-sine, sine, -sine, sine], axis=1)
-
+    slots_here = to_experts(slots)
+    slots_by_row = jnp.transpose(slots_here, (1, 2, 0))
+    expert_parts = [
+        pack_expert(expert_gate[e].astype(low), expert_up[e].astype(low), expert_down[e].astype(low))
+        for e in range(local_experts)
+    ]
+    stages = fsdp_count.bit_length() - 1
+    ring_gates = {
+        1: (cosine, sine, start_column, slots, *expert_parts),
+        2: (qkv_weight, output_full, gain_attend, gain_mixer, slots_by_row, order_here),
+    }
+    with jax.named_scope("tokens_ring"):
+        ring = ring_begin(tokens)
+        for step in range(sp_count - 1):
+            ring = ring_step(ring, "sp", ring_gates.get(step, ()))
+            if step == 0:
+                arrived_first = [part[-1] for part in ring]
+    left, right = ring
+    ring_end = (left[-1], right[-1])
+    with jax.named_scope("cot_gather"):
+        cot_lists = gather_begin(after([cotangent], *arrived_first)[0])
+        cot_lists = gather_stage(cot_lists, "fsdp", 0)
+    pieces = [left[-k % sp_count] for k in range(sp_count)] + right
+    expert_parts = after(expert_parts, *ring_end)
+    with jax.named_scope("weights_queue"):
+        expert_weights = [
+            lax.all_gather(part, "sp", axis=0, tiled=False) for part in expert_parts
+        ]
     rows_initial, query, key, value = project(
         order_here[None, :], gain_attend, qkv_weight, cosine, sine, pieces
     )
+    with jax.named_scope("cot_gather"):
+        for stage in range(1, stages):
+            cot_lists = gather_stage(cot_lists, "fsdp", stage)
     attended, logs = attend(lowest, start_column, query, key, value)
-    attn_back = lax.all_to_all(
-        attended.reshape(sp_count, token_rows, ratio * share),
-        "sp",
-        split_axis=0,
-        concat_axis=0,
-        tiled=True,
+    attn_back = exchange_blocks(
+        attended.reshape(sp_count, token_rows, ratio * share), "sp"
     )
     resid = lax.dynamic_slice_in_dim(rows_initial, sp_index * token_rows, token_rows)
     branch = jnp.einsum("stc,scd->td", attn_back, output_full, preferred_element_type=jnp.float32)
@@ -858,58 +908,51 @@
     normed_two = middle * inv_two
     act_two = (normed_two * gain_mixer).astype(low)
     logits = jnp.dot(act_two, router_full, preferred_element_type=jnp.float32)
-    expert_range = jnp.arange(EXPERTS, dtype=jnp.int32)
-    member = jnp.any(routes[:, :, None] == expert_range[None, None, :], axis=1)
-    row_range = jnp.arange(token_rows, dtype=jnp.int32)
-    upto = (row_range[:, None] <= row_range[None, :]).astype(low)
-    rank = jnp.dot(member.T.astype(low), upto, preferred_element_type=jnp.float32)
-    slots = jnp.where(member.T, rank.astype(jnp.int32) - 1, -1)
-
-    def to_experts(by_expert):
-        arrived = lax.all_to_all(
-            by_expert.reshape(fsdp_count, local_experts, token_rows),
-            "fsdp",
-            split_axis=0,
-            concat_axis=0,
-            tiled=True,
-        )
-        return jnp.swapaxes(jnp.take(arrived, relative, axis=0), 0, 1)
-
-    slots_here = to_experts(slots)
     gate_dense = jax.nn.softmax(jnp.where(member, logits, -jnp.inf), axis=-1)
     gates_here = to_experts(gate_dense.T)
-    cot_left, cot_right = gather_pieces(cot_source, "fsdp")
-    act_left, act_right = gather_pieces(act_two, "fsdp")
+    with jax.named_scope("act_gather"):
+        act_lists = gather_begin(act_two)
+        for stage in range(stages):
+            act_lists = gather_stage(act_lists, "fsdp", stage)
+    act_pieces, cot_pieces = gather_end(act_lists), gather_end(cot_lists)
     mixed_rows, back_rows, gate_grads, expert_sums = [], [], [], []
     for e in range(local_experts):
         mixed, back, gate_grad, weight_grad = run_expert(
-            slots_here[e], gates_here[e], expert_weights[e], act_left + act_right, cot_left + cot_right
+            slots_here[e],
+            gates_here[e],
+            expert_weights[e],
+            act_pieces,
+            cot_pieces,
         )
         mixed_rows.append(mixed)
         back_rows.append(back)
         gate_grads.append(gate_grad)
-        expert_sums.append(lax.psum_scatter(weight_grad, "sp", scatter_dimension=0, tiled=False))
+        with jax.named_scope("grads_queue"):
+            expert_sums.append(
+                lax.psum_scatter(weight_grad, "sp", scatter_dimension=0, tiled=False)
+            )
     gate_grads = jnp.stack(gate_grads, axis=1)
-    slots_by_row = jnp.transpose(slots_here, (1, 2, 0))
-    leave = combine_rows(slots_by_row, back_rows, 1)
-    stay = combine_rows(slots_by_row, back_rows, 0)
-    grad_act_moe = reduce_halves(leave, stay, "fsdp")
+    gate_grad_back = exchange_blocks(jnp.take(gate_grads, relative, axis=0), "fsdp")
+    with jax.named_scope("back_reduce"):
+        leave = combine_rows(slots_by_row, back_rows, 1)
+        leave = after(leave, gate_grad_back)
+        stay = combine_rows(slots_by_row, back_rows, 0)
+        for stage in range(stages):
+            leave, stay = reduce_stage(leave, stay, "fsdp", stage)
+            if stage == 0:
+                mixed_rows = after(mixed_rows, *stay)
+    grad_act_moe = jnp.concatenate(stay, axis=1)
+    with jax.named_scope("mix_reduce"):
+        mix_leave = combine_rows(slots_by_row, mixed_rows, 1)
+        mix_stay = combine_rows(slots_by_row, mixed_rows, 0)
+        mix_leave = after(mix_leave, *stay)
     upstream = cotangent.astype(jnp.float32)
-    gate_grad_back = lax.all_to_all(
-        jnp.take(gate_grads, relative, axis=0),
-        "fsdp",
-        split_axis=0,
-        concat_axis=0,
-        tiled=True,
-    )
     gate_grad = gate_grad_back.reshape(EXPERTS, token_rows).T
     weighted = jnp.sum(gate_dense * gate_grad, axis=1, keepdims=True)
     logit_grad = (gate_dense * (gate_grad - weighted)).astype(low)
-    grad_router_w = jnp.einsum("td,te->de", act_two, logit_grad, preferred_element_type=jnp.float32)
     grad_act_two = grad_act_moe + jnp.dot(
         logit_grad, router_full.T, preferred_element_type=jnp.float32
     )
-    grad_gain_two = jnp.sum(grad_act_two * normed_two, axis=0)
     scaled_two = grad_act_two * gain_mixer
     grad_middle = upstream + inv_two * (
         scaled_two - normed_two * jnp.mean(scaled_two * normed_two, axis=1, keepdims=True)
@@ -918,39 +961,51 @@
     grad_attn = jnp.einsum(
         "td,scd->stc", middle_low, output_full, preferred_element_type=jnp.float32
     ).astype(low)
-    grad_heads = lax.all_to_all(
-        grad_attn, "sp", split_axis=0, concat_axis=0, tiled=True
-    ).reshape(group_rows, ratio * share)
-    leave = combine_rows(slots_by_row, mixed_rows, 1)
-    stay = combine_rows(slots_by_row, mixed_rows, 0)
-    *leave, grad_heads = lax.optimization_barrier((*leave, grad_heads))
-    mixture = reduce_halves(leave, stay, "fsdp")
-    layer_out = (middle + mixture).astype(low)
+    grad_heads = exchange_blocks(grad_attn, "sp").reshape(group_rows, ratio * share)
+    with jax.named_scope("mix_reduce"):
+        mix_leave, mix_stay = reduce_stage(mix_leave, mix_stay, "fsdp", 0)
+    middle_after, *_ = after([middle_low], grad_attn)
     grad_output_w = jnp.einsum(
-        "stc,td->scd", attn_back, middle_low, preferred_element_type=jnp.float32
+        "stc,td->scd", attn_back, middle_after, preferred_element_type=jnp.float32
     ).astype(low)
     grad_output_w = grad_output_w.reshape(sp_count, ratio, kept_heads, HEAD_SIZE, MODEL_WIDTH)
     grad_output_w = jnp.swapaxes(grad_output_w, 1, 2).reshape(MODEL_WIDTH, MODEL_WIDTH)
+    logit_grad_after, grad_act_after = after([logit_grad, grad_act_two], grad_attn)
+    grad_router_w = jnp.einsum(
+        "td,te->de", act_two, logit_grad_after, preferred_element_type=jnp.float32
+    )
+    grad_gain_two = jnp.sum(grad_act_after * normed_two, axis=0)
     early_grads = jnp.concatenate(
         [
             grad_output_w,
             grad_router_w.astype(low),
             grad_gain_two.astype(low)[:, None],
-            jnp.zeros((MODEL_WIDTH, 256 - EXPERTS - 1), low),
+            jnp.zeros((MODEL_WIDTH, 128 - EXPERTS - 1), low),
         ],
         axis=1,
-    ).reshape(fsdp_count, shard_rows, MODEL_WIDTH + 256)
-    early_sum = reduce_rows(jnp.take(early_grads, relative, axis=0), "fsdp").astype(low)
-    early_left, early_right = ring_pieces(early_sum, "sp")
-    early_sum = jnp.concatenate(
-        [sum(part.astype(jnp.float32) for part in parts) for parts in (early_left, early_right)],
-        axis=1,
-    )
-
+    ).reshape(fsdp_count, shard_rows, MODEL_WIDTH + 128)
+    with jax.named_scope("early_fsdp"):
+        early_parts = exchange_blocks(early_grads, "fsdp")
+    grad_heads = after([grad_heads], *mix_leave)[0]
+    with jax.named_scope("mix_reduce"):
+        mix_leave, mix_stay = reduce_stage(mix_leave, mix_stay, "fsdp", 1)
     grad_query, grad_key, grad_value = attend_back(
         lowest, start_column, logs, query, attended, grad_heads, key, value
     )
-    token_grads, grad_qkv, grad_gain_one = project_back(
+    with jax.named_scope("early_fsdp"):
+        early_parts = after([early_parts], grad_query)[0]
+        early_sum = jnp.sum(early_parts.astype(jnp.float32), axis=0).astype(low)
+    with jax.named_scope("early_sp"):
+        early_parts = exchange_blocks(
+            early_sum.reshape(sp_count, shard_rows // sp_count, MODEL_WIDTH + 128), "sp"
+        )
+    grad_query = after([grad_query], *mix_leave, early_sum, *expert_sums[:1])[0]
+    with jax.named_scope("mix_reduce"):
+        mix_leave, mix_stay = reduce_stage(mix_leave, mix_stay, "fsdp", 2) if stages > 2 else (
+            mix_leave,
+            mix_stay,
+        )
+    token_grads, late_grads = project_back(
         sp_index[None],
         order_here[:, None],
         gain_attend,
@@ -963,23 +1018,37 @@
         rows_initial,
         middle_low,
     )
-    tokens_grad = ring_reduce(
-        token_grads.reshape(sp_count, token_rows, MODEL_WIDTH), "sp"
-    ).astype(low)
-    late_grads = jnp.concatenate(
-        [
-            grad_qkv,
-            grad_gain_one.astype(low).T,
-            jnp.zeros((MODEL_WIDTH, 255), low),
-        ],
-        axis=1,
-    ).reshape(fsdp_count, shard_rows, qkv_columns + 256)
-    late_sum = reduce_rows(jnp.take(late_grads, relative, axis=0), "fsdp").astype(low)
-    late_left, late_right = ring_pieces(late_sum, "sp")
-    late_left = [late_left[-k % sp_count] for k in range(sp_count)]
-    late_all = jnp.concatenate([jnp.stack(late_left), jnp.stack(late_right)], axis=2)
-    late_all = jnp.take(late_all, (jnp.arange(sp_count) - sp_index) % sp_count, axis=0)
-    late_all = late_all.astype(jnp.float32)
+    with jax.named_scope("tokens_back"):
+        back_ring = reduce_ring_begin(
+            token_grads.reshape(sp_count, token_rows, MODEL_WIDTH)
+        )
+        for step in range(1, sp_count):
+            back_ring = reduce_ring_step(back_ring, "sp", step)
+            if step == 1:
+                back_first = back_ring[0]
+        tokens_grad = jnp.concatenate(back_ring[0], axis=1).astype(low)
+    expert_sums = after(expert_sums, *back_first)
+    with jax.named_scope("late_fsdp"):
+        late_parts = exchange_blocks(
+            late_grads.reshape(fsdp_count, shard_rows, qkv_columns + 128), "fsdp"
+        )
+    with jax.named_scope("mix_reduce"):
+        mix_stay = after(mix_stay, *back_first)
+        for stage in range(3, stages):
+            mix_leave, mix_stay = reduce_stage(mix_leave, mix_stay, "fsdp", stage)
+    layer_out = (middle + jnp.concatenate(mix_stay, axis=1)).astype(low)
+    with jax.named_scope("early_sp"):
+        early_parts = after([early_parts], *back_first)[0]
+        early_sum = jnp.sum(early_parts.astype(jnp.float32), axis=0).astype(low)
+        early_all = exchange_blocks(
+            jnp.broadcast_to(early_sum[None], (sp_count,) + early_sum.shape), "sp"
+        )
+    early_sum = early_all.reshape(shard_rows, MODEL_WIDTH + 128).astype(jnp.float32)
+    with jax.named_scope("late_sp"):
+        late_sum = jnp.sum(late_parts.astype(jnp.float32), axis=0).astype(low)
+        late_all = exchange_blocks(
+            jnp.broadcast_to(late_sum[None], (sp_count,) + late_sum.shape), "sp"
+        ).astype(jnp.float32)
     query_sum = late_all[:, :, : ratio * share]
     query_sum = query_sum.reshape(sp_count, shard_rows, ratio, kept_heads, HEAD_SIZE)
     query_sum = jnp.transpose(query_sum, (1, 0, 3, 2, 4)).reshape(shard_rows, MODEL_WIDTH)

time: 799 us -> 750 us (0.939)
  starting transfers between devices: 113 us -> 86.6 us
  local copies, waits for them, and re-layouts: 71.2 us -> 55.5 us
    ppermute x24 -> x12, starting transfers between devices: 63.1 us -> 19.2 us  [the longest x6 11.3 us: ring_step(): lax.ppermute(one, axis_name, shift_pairs(count, by))]
    all_gather x4, waiting for transfers between devices: 4.14 us -> 28.5 us  [body(): lax.all_gather(part, 'sp', axis=0, tiled=False)]
    all_to_all x5 -> x10, starting transfers between devices: 18.7 us -> 39.4 us  [exchange_blocks(): lax.all_to_all(values, axis_name, split_axis=0, concat_axis=0, tiled=True)]
    all_to_all x5 -> x10, waiting for transfers between devices: 58.6 us -> 41.6 us  [exchange_blocks(): lax.all_to_all(values, axis_name, split_axis=0, concat_axis=0, tiled=True)]
    gather x3 -> x0, local copies, waits for them, and re-layouts: 8.89 us -> none  [the longest x1 3.96 us: body(): jnp.take(early_grads, relative, axis=0)]
    ppermute x24 -> x12, waiting for transfers between devices: 99.2 us -> 92.1 us  [the longest x6 52.9 us: reduce_ring_step(): arrived = lax.ppermute(one, axis_name, shift_pairs(count, -turn))]
    ppermute x52 -> x40, starting transfers between devices: 29.9 us -> 26.5 us  [flip(): lax.ppermute(values, axis_name, [(place, place ^ bit) for place in range(...]
    convert_element_type x37 -> x13, other arithmetic: 33.7 us -> 30.7 us  [the longest x6 14.7 us: reduce_stage(): gone_next.append(total.astype(jnp.bfloat16))]
  transfers between devices with their start and end apart: 90 -> 71, of which waited for: 36 -> 26; matrix products, arithmetic and copies ran while one was open for 19% -> 18% of each run, Pallas kernels for 31% -> 33%
where the time goes in v3:
time: 750 us; the launch traced here: 742 us
  waiting for transfers between devices  246 us (33%)
  Pallas kernels  246 us (33%)
  starting transfers between devices  86.6 us (12%)
  other arithmetic  82.3 us (11%)
  local copies, waits for them, and re-layouts  55.5 us (7%)
  between operations  16.4 us (2%)
  matrix products  9.95 us (1%)
    pallas_call x4, Pallas kernels, run_expert(): pl.pallas_call(functools.partial(expert_step, count=count), grid=(count /...  108 us
    ppermute x40, waiting for transfers between devices, flip(): lax.ppermute(values, axis_name, [(place, place ^ bit) for place in range(...  82 us
    ppermute x6, waiting for transfers between devices, reduce_ring_step(): arrived = lax.ppermute(one, axis_name, shift_pairs(count, -turn))  52.9 us
    all_to_all x10, waiting for transfers between devices, exchange_blocks(): lax.all_to_all(values, axis_name, split_axis=0, concat_axis=0, tiled=True)  41.6 us
    all_to_all x10, starting transfers between devices, exchange_blocks(): lax.all_to_all(values, axis_name, split_axis=0, concat_axis=0, tiled=True)  39.4 us
    ppermute x6, waiting for transfers between devices, ring_step(): lax.ppermute(one, axis_name, shift_pairs(count, by))  39.2 us
    pallas_call x4, Pallas kernels, combine_rows(): pl.pallas_call(combine_step, grid=(sources // 2,), in_specs=[pl.BlockSpec...  36.7 us
    all_gather x4, waiting for transfers between devices, body(): lax.all_gather(part, 'sp', axis=0, tiled=False)  28.5 us
  transfers between devices with their start and end apart: 71, of which 26 were waited for; matrix products, arithmetic and copies ran while one was open for 18% of the time, Pallas kernels for 33%

profile of v3, /device:TPU:0, one launch (start us, length us, event | category | flops | bytes accessed | tf_op | source)
XLA Modules:
  0.0 742.1 jit_solution(15748247176875815637)
XLA Ops:
  13.9 5.2 all-to-all-start
  42.2 5.8 collective-permute-done.refs_3_
  65.2 9.4 %collective-permute-done.3.refs_6_ = bf16[512,512]{1,0:T(8,128)(2,1)} collective-permute-done((bf16[512,512]{1,0:T(8,128)(2,1)}, bf16[512,512]{1,0:T(8,128)(2,1)}, u32[]{:S(2)}, u32[]{:S(2)}) %collective-permute-start.3) | collective-permute-done | bytes 524320 | tf_op jit(solution)/shard_map/tokens_ring/ppermute | solution.py:340
  78.4 13.0 %collective-permute-done.4.refs_1_ = bf16[512,512]{1,0:T(8,128)(2,1)S(1)} collective-permute-done((bf16[512,512]{1,0:T(8,128)(2,1)}, bf16[512,512]{1,0:T(8,128)(2,1)S(1)}, u32[]{:S(2)}, u32[]{:S(2)}) %collective-permute-start.4) | collective-permute-done | bytes 524320 | tf_op jit(solution)/shard_map/tokens_ring/ppermute | solution.py:340
  91.5 7.8 %collective-permute-done.5.refs_7_ = bf16[512,512]{1,0:T(8,128)(2,1)S(1)} collective-permute-done((bf16[512,512]{1,0:T(8,128)(2,1)}, bf16[512,512]{1,0:T(8,128)(2,1)S(1)}, u32[]{:S(2)}, u32[]{:S(2)}) %collective-permute-start.5) | collective-permute-done | bytes 524320 | tf_op jit(solution)/shard_map/tokens_ring/ppermute | solution.py:340
  103.1 18.8 %project.1 = (bf16[2048,1024]{1,0:T(8,128)(2,1)}, bf16[2048,256]{1,0:T(8,128)(2,1)}, bf16[2048,128]{1,0:T(8,128)(2,1)}, bf16[2048,128]{1,0:T(8,128)(2,1)}) custom-call(s32[1,2048]{1,0:T(1,128)} %bitcast.240, f32[1,1024]{1,0:T(1,128)} %bitcast.242, bf16[1024,512]{1,0:T(8,128)(2,1)} %slice.495.weight_ref, f32[2048,128]{1,0:T(8,128)} %copy.161.cos_ref, ...), custom_call_target="tpu_custom_call" | custom-call | tf_op jit(solution)/shard_map/project/pallas_call | solution.py:434
  121.9 28.5 %attend.1 = (bf16[2048,256]{1,0:T(8,128)(2,1)}, f32[2048,4]{1,0:T(8,128)}) custom-call(s32[8]{0:T(128)} %and_select_fusion.lowest_ref, s32[2048,1]{1,0:T(8,128)} %select_select_fusion.start_ref, bf16[2048,256]{1,0:T(8,128)(2,1)} %get-tuple-element.83.query_ref, bf16[2048,128]{1,0:T(8,128)(2,1)} %get-tuple-element.84.key_ref, ...), custom_call_target="tpu_custom_call" | custom-call | tf_op jit(solution)/shard_map/attend/pallas_call | solution.py:540
  158.9 9.6 %collective-permute-done.30.refs_28_ = bf16[512,512]{1,0:T(8,128)(2,1)S(1)} collective-permute-done((bf16[512,512]{1,0:T(8,128)(2,1)S(1)}, bf16[512,512]{1,0:T(8,128)(2,1)S(1)}, u32[]{:S(2)}, u32[]{:S(2)}) %collective-permute-start.30) | collective-permute-done | bytes 524320 | tf_op jit(solution)/shard_map/cot_gather/ppermute | solution.py:39
  171.9 13.0 %all-to-all-done.1 = bf16[4,512,256]{2,1,0:T(8,128)(2,1)} async-done(((bf16[4,512,256]{2,1,0:T(8,128)(2,1)}), bf16[4,512,256]{2,1,0:T(8,128)(2,1)}, u32[]{:S(2)}, u32[]{:S(2)}) %all-to-all-start.1) | async-done | bytes 1048608 | tf_op jit(solution)/shard_map/all_to_all | solution.py:107
  191.9 11.2 %collective-permute-done.25.refs_22_ = bf16[512,512]{1,0:T(8,128)(2,1)S(1)} collective-permute-done((bf16[512,512]{1,0:T(8,128)(2,1)}, bf16[512,512]{1,0:T(8,128)(2,1)S(1)}, u32[]{:S(2)}, u32[]{:S(2)}) %collective-permute-start.25) | collective-permute-done | bytes 524320 | tf_op jit(solution)/shard_map/cot_gather/ppermute | solution.py:39
  207.5 10.5 %collective-permute-done.16.refs_12_ = bf16[512,512]{1,0:T(8,128)(2,1)} collective-permute-done((bf16[512,512]{1,0:T(8,128)(2,1)S(1)}, bf16[512,512]{1,0:T(8,128)(2,1)}, u32[]{:S(2)}, u32[]{:S(2)}) %collective-permute-start.16) | collective-permute-done | bytes 524320 | tf_op jit(solution)/shard_map/act_gather/ppermute | solution.py:39
  220.2 9.1 %collective-permute-done.9.refs_4_ = bf16[512,512]{1,0:T(8,128)(2,1)} collective-permute-done((bf16[512,512]{1,0:T(8,128)(2,1)}, bf16[512,512]{1,0:T(8,128)(2,1)}, u32[]{:S(2)}, u32[]{:S(2)}) %collective-permute-start.9) | collective-permute-done | bytes 524320 | tf_op jit(solution)/shard_map/act_gather/ppermute | solution.py:39
  243.0 7.9 %slice_reduce_fusion = (s32[8,512]{1,0:T(8,128)S(1)}, s32[8,512]{1,0:T(8,128)S(1)}, s32[8,512]{1,0:T(8,128)S(1)}, s32[8,512]{1,0:T(8,128)S(1)}) fusion(s32[4,8,512]{0,2,1:T(8,128)} %get-tuple-element.239), kind=kLoop, calls=%fused_computation.3 | loop fusion | bytes 131072 | tf_op jit(solution)/shard_map/slice | solution.py:921
  252.9 27.0 %expert.4 = (bf16[8,192,1024]{2,1,0:T(8,128)(2,1)}, bf16[8,192,1024]{2,1,0:T(8,128)(2,1)}, f32[8,1,512]{2,1,0:T(1,128)}, bf16[4,768,512]{2,1,0:T(8,128)(2,1)}) custom-call(s32[8,1,512]{2,1,0:T(1,128)} %broadcast_in_dim_squeeze.32.slot_ref, f32[8,1,512]{2,1,0:T(1,128)} %get-tuple-element.284.share_ref, bf16[4,768,512]{2,1,0:T(8,128)(2,1)} %bitcast.220, ...), custom_call_target="tpu_custom_call" | custom-call | tf_op jit(solution)/shard_map/expert/pallas_call | solution.py:255
  281.1 26.9 %expert.7 = (bf16[8,192,1024]{2,1,0:T(8,128)(2,1)}, bf16[8,192,1024]{2,1,0:T(8,128)(2,1)}, f32[8,1,512]{2,1,0:T(1,128)}, bf16[4,768,512]{2,1,0:T(8,128)(2,1)}) custom-call(s32[8,1,512]{2,1,0:T(1,128)} %broadcast_in_dim_squeeze.35.slot_ref, f32[8,1,512]{2,1,0:T(1,128)} %get-tuple-element.281.share_ref, bf16[4,768,512]{2,1,0:T(8,128)(2,1)} %bitcast.219, ...), custom_call_target="tpu_custom_call" | custom-call | tf_op jit(solution)/shard_map/expert/pallas_call | solution.py:255
  308.9 26.9 %expert.6 = (bf16[8,192,1024]{2,1,0:T(8,128)(2,1)}, bf16[8,192,1024]{2,1,0:T(8,128)(2,1)}, f32[8,1,512]{2,1,0:T(1,128)}, bf16[4,768,512]{2,1,0:T(8,128)(2,1)}) custom-call(s32[8,1,512]{2,1,0:T(1,128)} %broadcast_in_dim_squeeze.34.slot_ref, f32[8,1,512]{2,1,0:T(1,128)} %get-tuple-element.282.share_ref, bf16[4,768,512]{2,1,0:T(8,128)(2,1)} %bitcast.218, ...), custom_call_target="tpu_custom_call" | custom-call | tf_op jit(solution)/shard_map/expert/pallas_call | solution.py:255
  336.5 28.5 %all-gather.14.cloned.1.call-done = bf16[3072,512]{1,0:T(8,128)(2,1)} async-done(((bf16[768,512]{1,0:T(8,128)(2,1)}), bf16[3072,512]{1,0:T(8,128)(2,1)}) %all-gather.14.cloned.1.call-update) | async-done | bytes 3145744 | tf_op jit(solution)/shard_map/weights_queue/all_gather | solution.py:892
  365.0 27.1 %expert.5 = (bf16[8,192,1024]{2,1,0:T(8,128)(2,1)}, bf16[8,192,1024]{2,1,0:T(8,128)(2,1)}, f32[8,1,512]{2,1,0:T(1,128)}, bf16[4,768,512]{2,1,0:T(8,128)(2,1)}) custom-call(s32[8,1,512]{2,1,0:T(1,128)} %broadcast_in_dim_squeeze.33.slot_ref, f32[8,1,512]{2,1,0:T(1,128)} %get-tuple-element.283.share_ref, bf16[4,768,512]{2,1,0:T(8,128)(2,1)} %bitcast.217, ...), custom_call_target="tpu_custom_call" | custom-call | tf_op jit(solution)/shard_map/expert/pallas_call | solution.py:255
  397.9 9.5 %combine.5 = (bf16[4,512,512]{2,1,0:T(8,128)(2,1)}, bf16[4,512,512]{2,1,0:T(8,128)(2,1)}) custom-call(s32[8,512,4]{2,1,0:T(8,128)} %get-tuple-element.240.slot_ref, bf16[8,192,1024]{2,1,0:T(8,128)(2,1)} %get-tuple-element.96.refs_0_, bf16[8,192,1024]{2,1,0:T(8,128)(2,1)} %get-tuple-element.97.refs_1_, bf16[8,192,1024]{2,1,0:T(8,128)(2,1)} %get-tuple-element.98.refs_2_, ...), custom_call_target="tpu_custom_call" | custom-call | tf_op jit(solution)/shard_map/back_reduce/combine/pallas_call | solution.py:315
  408.0 9.0 %combine.4 = (bf16[4,512,512]{2,1,0:T(8,128)(2,1)}, bf16[4,512,512]{2,1,0:T(8,128)(2,1)}) custom-call(s32[8,512,4]{2,1,0:T(8,128)} %get-tuple-element.240.slot_ref, bf16[8,192,1024]{2,1,0:T(8,128)(2,1)} %get-tuple-element.96.refs_0_, bf16[8,192,1024]{2,1,0:T(8,128)(2,1)} %get-tuple-element.97.refs_1_, bf16[8,192,1024]{2,1,0:T(8,128)(2,1)} %get-tuple-element.98.refs_2_, ...), custom_call_target="tpu_custom_call" | custom-call | tf_op jit(solution)/shard_map/back_reduce/combine/pallas_call | solution.py:315
  428.3 18.9 %collective-permute-done.36 = bf16[2,512,512]{2,1,0:T(8,128)(2,1)} collective-permute-done((bf16[2,512,512]{2,1,0:T(8,128)(2,1)}, bf16[2,512,512]{2,1,0:T(8,128)(2,1)}, u32[]{:S(2)}, u32[]{:S(2)}) %collective-permute-start.36) | collective-permute-done | bytes 1048608 | tf_op jit(solution)/shard_map/back_reduce/ppermute | solution.py:39
  454.8 8.4 %collective-permute-done.37 = bf16[1,512,512]{2,1,0:T(8,128)(2,1)S(1)} collective-permute-done((bf16[1,512,512]{2,1,0:T(8,128)(2,1)S(1)}, bf16[1,512,512]{2,1,0:T(8,128)(2,1)S(1)}, u32[]{:S(2)}, u32[]{:S(2)}) %collective-permute-start.37) | collective-permute-done | bytes 524320 | tf_op jit(solution)/shard_map/back_reduce/ppermute | solution.py:39
  477.3 9.1 %combine.7 = (bf16[4,512,512]{2,1,0:T(8,128)(2,1)}, bf16[4,512,512]{2,1,0:T(8,128)(2,1)}) custom-call(s32[8,512,4]{2,1,0:T(8,128)} %get-tuple-element.240.slot_ref, bf16[8,192,1024]{2,1,0:T(8,128)(2,1)} %get-tuple-element.110.refs_0_, bf16[8,192,1024]{2,1,0:T(8,128)(2,1)} %get-tuple-element.111.refs_1_, bf16[8,192,1024]{2,1,0:T(8,128)(2,1)} %get-tuple-element.112.refs_2_, ...), custom_call_target="tpu_custom_call" | custom-call | tf_op jit(solution)/shard_map/mix_reduce/combine/pallas_call | solution.py:315
  499.4 14.4 %all-to-all-done.4 = bf16[4,512,256]{1,2,0:T(8,128)(2,1)} async-done(((bf16[4,512,256]{1,2,0:T(8,128)(2,1)}), bf16[4,512,256]{1,2,0:T(8,128)(2,1)}, u32[]{:S(2)}, u32[]{:S(2)}) %all-to-all-start.4) | async-done | bytes 1048608 | tf_op jit(solution)/shard_map/all_to_all | solution.py:107
  518.3 9.0 %combine.6 = (bf16[4,512,512]{2,1,0:T(8,128)(2,1)}, bf16[4,512,512]{2,1,0:T(8,128)(2,1)}) custom-call(s32[8,512,4]{2,1,0:T(8,128)} %get-tuple-element.240.slot_ref, bf16[8,192,1024]{2,1,0:T(8,128)(2,1)} %get-tuple-element.110.refs_0_, bf16[8,192,1024]{2,1,0:T(8,128)(2,1)} %get-tuple-element.111.refs_1_, bf16[8,192,1024]{2,1,0:T(8,128)(2,1)} %get-tuple-element.112.refs_2_, ...), custom_call_target="tpu_custom_call" | custom-call | tf_op jit(solution)/shard_map/mix_reduce/combine/pallas_call | solution.py:315
  542.0 28.4 %attend_back.1 = (f32[2048,256]{1,0:T(8,128)}, f32[2048,128]{1,0:T(8,128)}, f32[2048,128]{1,0:T(8,128)}) custom-call(s32[8]{0:T(128)} %and_select_fusion.lowest_ref, s32[2048,1]{1,0:T(8,128)} %select_select_fusion.start_ref, f32[2048,4]{1,0:T(8,128)} %get-tuple-element.120.log_ref, bf16[2048,256]{1,0:T(8,128)(2,1)} %get-tuple-element.83.query_ref, ...), custom_call_target="tpu_custom_call" | custom-call | tf_op jit(solution)/shard_map/attend_back/pallas_call | solution.py:616
  577.3 25.5 %project_back.1 = (bf16[2048,1024]{1,0:T(8,128)(2,1)}, bf16[1024,640]{1,0:T(8,128)(2,1)}) custom-call(s32[1]{0:T(128)} %bitcast.49.own_ref, s32[2048,1]{1,0:T(8,128)} %copy.171.order_ref, f32[1,1024]{1,0:T(1,128)} %bitcast.243, bf16[1024,512]{1,0:T(8,128)(2,1)} %slice.495.weight_ref, f32[2048,128]{1,0:T(8,128)} %copy.161.cos_ref, ...), custom_call_target="tpu_custom_call" | custom-call | tf_op jit(solution)/shard_map/project_back/pallas_call | solution.py:738
  611.7 29.8 %collective-permute-done.47 = bf16[512,512]{1,0:T(8,128)(2,1)} collective-permute-done((bf16[512,512]{1,0:T(8,128)(2,1)}, bf16[512,512]{1,0:T(8,128)(2,1)}, u32[]{:S(2)}, u32[]{:S(2)}) %collective-permute-start.47) | collective-permute-done | bytes 524320 | tf_op jit(solution)/shard_map/tokens_back/ppermute | solution.py:358
  641.5 7.0 collective-permute-done.46
  703.9 6.1 collective-permute-done.49
  710.0 10.0 %collective-permute-done.51 = bf16[512,512]{1,0:T(8,128)(2,1)} collective-permute-done((bf16[512,512]{1,0:T(8,128)(2,1)}, bf16[512,512]{1,0:T(8,128)(2,1)}, u32[]{:S(2)}, u32[]{:S(2)}) %collective-permute-start.51) | collective-permute-done | bytes 524320 | tf_op jit(solution)/shard_map/tokens_back/ppermute | solution.py:358
  722.9 9.0 %all-to-all-done.7 = bf16[4,128,640]{1,2,0:T(8,128)(2,1)S(1)} async-done(((bf16[4,128,640]{1,2,0:T(8,128)(2,1)}), bf16[4,128,640]{1,2,0:T(8,128)(2,1)S(1)}, u32[]{:S(2)}, u32[]{:S(2)}) %all-to-all-start.7) | async-done | bytes 655392 | tf_op jit(solution)/shard_map/late_sp/all_to_all | solution.py:107
  (373 shorter events, 245.2 us)
Async XLA Ops:
  7.2 48.6 %all-gather.10.cloned.1.call-start = ((), (), s32[]{:S(2)}) async-start(), calls=%async_computation.14 | async-start | bytes 3833856 | tf_op jit(solution)/shard_map/all_gather | solution.py:828
  13.9 38.1 %all-to-all-start = ((s32[8,4,512]{2,1,0:T(4,128)}), s32[8,4,512]{2,1,0:T(4,128)S(1)}, u32[]{:S(2)}, u32[]{:S(2)}) async-start(s32[8,4,512]{2,1,0:T(4,128)} %reshape.272), calls=%async_computation | async-start | bytes 131072 | tf_op jit(solution)/shard_map/all_to_all | solution.py:107
  19.1 233.8 %all-gather.12.cloned.1.call-start = ((), (), s32[]{:S(2)}) async-start(), calls=%async_computation.19 | async-start | bytes 3932160 | tf_op jit(solution)/shard_map/weights_queue/all_gather | solution.py:892
  49.8 24.8 %collective-permute-start.3 = (bf16[512,512]{1,0:T(8,128)(2,1)}, bf16[512,512]{1,0:T(8,128)(2,1)}, u32[]{:S(2)}, u32[]{:S(2)}) collective-permute-start(bf16[512,512]{1,0:T(8,128)(2,1)} %collective-permute-done.1.refs_5_), channel_id=1, source_target_pairs={{0,3},{1,0},{2,1},{3,2},{4,7},{5,4},{6,5},{7,6},{8,11},{9,8},{10,9... | collective-permute-start | bytes 1572872 | tf_op jit(solution)/shard_map/tokens_ring/ppermute | solution.py:340
  99.3 181.8 %all-gather.18.cloned.1.call-start = ((), (), s32[]{:S(2)}) async-start(), calls=%async_computation.22 | async-start | bytes 3932160 | tf_op jit(solution)/shard_map/weights_queue/all_gather | solution.py:892
  100.1 208.8 %all-gather.16.cloned.1.call-start = ((), (), s32[]{:S(2)}) async-start(), calls=%async_computation.21 | async-start | bytes 3932160 | tf_op jit(solution)/shard_map/weights_queue/all_gather | solution.py:892
  100.7 264.3 %all-gather.14.cloned.1.call-start = ((), (), s32[]{:S(2)}) async-start(), calls=%async_computation.20 | async-start | bytes 3932160 | tf_op jit(solution)/shard_map/weights_queue/all_gather | solution.py:892
  150.4 34.5 %all-to-all-start.1 = ((bf16[4,512,256]{2,1,0:T(8,128)(2,1)}), bf16[4,512,256]{2,1,0:T(8,128)(2,1)}, u32[]{:S(2)}, u32[]{:S(2)}) async-start(bf16[4,512,256]{2,1,0:T(8,128)(2,1)} %bitcast.214), calls=%async_computation.1 | async-start | bytes 2097152 | tf_op jit(solution)/shard_map/all_to_all | solution.py:107
  156.2 32.3 %collective-permute-start.23 = (bf16[512,512]{1,0:T(8,128)(2,1)S(1)}, bf16[512,512]{1,0:T(8,128)(2,1)}, u32[]{:S(2)}, u32[]{:S(2)}) collective-permute-start(bf16[512,512]{1,0:T(8,128)(2,1)S(1)} %get-tuple-element.242.refs_16_), channel_id=1, source_target_pairs={{0,16},{4,20},{8,24},{12,28},{16,0},{20,4},{24,8},{28,12},{1,17},{... | collective-permute-start | bytes 1572872 | tf_op jit(solution)/shard_map/cot_gather/ppermute | solution.py:39
  158.1 30.4 %collective-permute-start.21 = (bf16[512,512]{1,0:T(8,128)(2,1)S(1)}, bf16[512,512]{1,0:T(8,128)(2,1)}, u32[]{:S(2)}, u32[]{:S(2)}) collective-permute-start(bf16[512,512]{1,0:T(8,128)(2,1)S(1)} %get-tuple-element.242.refs_16_), channel_id=1, source_target_pairs={{0,8},{4,12},{8,0},{12,4},{16,24},{20,28},{24,16},{28,20},{1,9},{5... | collective-permute-start | bytes 1572872 | tf_op jit(solution)/shard_map/cot_gather/ppermute | solution.py:39
  206.9 28.7 %collective-permute-start.7 = (bf16[512,512]{1,0:T(8,128)(2,1)}, bf16[512,512]{1,0:T(8,128)(2,1)}, u32[]{:S(2)}, u32[]{:S(2)}) collective-permute-start(bf16[512,512]{1,0:T(8,128)(2,1)} %get-tuple-element.244.refs_0_), channel_id=1, source_target_pairs={{0,8},{4,12},{8,0},{12,4},{16,24},{20,28},{24,16},{28,20},{1,9},{5... | collective-permute-start | bytes 1572872 | tf_op jit(solution)/shard_map/act_gather/ppermute | solution.py:39
  235.3 342.0 %reduce-scatter.5.cloned.1.call-start = ((), (), s32[]{:S(2)}) async-start(), calls=%async_computation.15 | async-start | bytes 3932160 | tf_op jit(solution)/shard_map/grads_queue/reduce_scatter | solution.py:932
  280.0 371.3 %reduce-scatter.11.cloned.1.call-start = ((), (), s32[]{:S(2)}) async-start(), calls=%async_computation.18 | async-start | bytes 3932160 | tf_op jit(solution)/shard_map/grads_queue/reduce_scatter | solution.py:932
  308.0 343.3 %reduce-scatter.9.cloned.1.call-start = ((), (), s32[]{:S(2)}) async-start(), calls=%async_computation.17 | async-start | bytes 3932160 | tf_op jit(solution)/shard_map/grads_queue/reduce_scatter | solution.py:932
  397.9 253.5 %reduce-scatter.7.cloned.1.call-start = ((), (), s32[]{:S(2)}) async-start(), calls=%async_computation.16 | async-start | bytes 3932160 | tf_op jit(solution)/shard_map/grads_queue/reduce_scatter | solution.py:932
  421.4 25.8 %collective-permute-start.36 = (bf16[2,512,512]{2,1,0:T(8,128)(2,1)}, bf16[2,512,512]{2,1,0:T(8,128)(2,1)}, u32[]{:S(2)}, u32[]{:S(2)}) collective-permute-start(bf16[2,512,512]{2,1,0:T(8,128)(2,1)} %get-tuple-element.237), channel_id=1, source_target_pairs={{0,8},{4,12},{8,0},{12,4},{16,24},{20,28},{24,16},{28,20},{1,9},{5... | collective-permute-start | bytes 3145736 | tf_op jit(solution)/shard_map/back_reduce/ppermute | solution.py:39
  426.8 26.4 %collective-permute-start.38 = (bf16[2,512,512]{2,1,0:T(8,128)(2,1)}, bf16[2,512,512]{2,1,0:T(8,128)(2,1)}, u32[]{:S(2)}, u32[]{:S(2)}) collective-permute-start(bf16[2,512,512]{2,1,0:T(8,128)(2,1)} %get-tuple-element.235), channel_id=1, source_target_pairs={{0,16},{4,20},{8,24},{12,28},{16,0},{20,4},{24,8},{28,12},{1,17},{... | collective-permute-start | bytes 3145736 | tf_op jit(solution)/shard_map/back_reduce/ppermute | solution.py:39
  473.0 40.7 %all-to-all-start.4 = ((bf16[4,512,256]{1,2,0:T(8,128)(2,1)}), bf16[4,512,256]{1,2,0:T(8,128)(2,1)}, u32[]{:S(2)}, u32[]{:S(2)}) async-start(bf16[4,512,256]{1,2,0:T(8,128)(2,1)} %fusion.1), calls=%async_computation.4 | async-start | bytes 2097152 | tf_op jit(solution)/shard_map/all_to_all | solution.py:107
  486.4 41.0 %collective-permute-start.40 = (bf16[4,512,512]{2,1,0:T(8,128)(2,1)}, bf16[4,512,512]{2,1,0:T(8,128)(2,1)}, u32[]{:S(2)}, u32[]{:S(2)}) collective-permute-start(bf16[4,512,512]{2,1,0:T(8,128)(2,1)} %get-tuple-element.117), channel_id=1, source_target_pairs={{0,4},{4,0},{8,12},{12,8},{16,20},{20,16},{24,28},{28,24},{1,5},{5... | collective-permute-start | bytes 6291464 | tf_op jit(solution)/shard_map/mix_reduce/ppermute | solution.py:39
  486.4 47.0 %collective-permute-start.43 = (bf16[4,512,512]{2,1,0:T(8,128)(2,1)}, bf16[4,512,512]{2,1,0:T(8,128)(2,1)}, u32[]{:S(2)}, u32[]{:S(2)}) collective-permute-start(bf16[4,512,512]{2,1,0:T(8,128)(2,1)} %get-tuple-element.119), channel_id=1, source_target_pairs={{0,4},{4,0},{8,12},{12,8},{16,20},{20,16},{24,28},{28,24},{1,5},{5... | collective-permute-start | bytes 6291464 | tf_op jit(solution)/shard_map/mix_reduce/ppermute | solution.py:39
  513.8 56.7 %all-to-all-start.5 = ((bf16[8,128,1152]{2,1,0:T(8,128)(2,1)}), bf16[8,128,1152]{2,1,0:T(8,128)(2,1)}, u32[]{:S(2)}, u32[]{:S(2)}) async-start(bf16[8,128,1152]{2,1,0:T(8,128)(2,1)} %concatenate.77), calls=%async_computation.5 | async-start | bytes 4718592 | tf_op jit(solution)/shard_map/early_fsdp/all_to_all | solution.py:107
  531.4 41.8 %collective-permute-start.41 = (bf16[2,512,512]{2,1,0:T(8,128)(2,1)}, bf16[2,512,512]{2,1,0:T(8,128)(2,1)}, u32[]{:S(2)}, u32[]{:S(2)}) collective-permute-start(bf16[2,512,512]{2,1,0:T(8,128)(2,1)} %get-tuple-element.234), channel_id=1, source_target_pairs={{0,8},{4,12},{8,0},{12,4},{16,24},{20,28},{24,16},{28,20},{1,9},{5... | collective-permute-start | bytes 3145736 | tf_op jit(solution)/shard_map/mix_reduce/ppermute | solution.py:39
  536.9 38.3 %collective-permute-start.44 = (bf16[2,512,512]{2,1,0:T(8,128)(2,1)}, bf16[2,512,512]{2,1,0:T(8,128)(2,1)}, u32[]{:S(2)}, u32[]{:S(2)}) collective-permute-start(bf16[2,512,512]{2,1,0:T(8,128)(2,1)} %get-tuple-element.232), channel_id=1, source_target_pairs={{0,16},{4,20},{8,24},{12,28},{16,0},{20,4},{24,8},{28,12},{1,17},{... | collective-permute-start | bytes 3145736 | tf_op jit(solution)/shard_map/mix_reduce/ppermute | solution.py:39
  605.1 36.4 %collective-permute-start.47 = (bf16[512,512]{1,0:T(8,128)(2,1)}, bf16[512,512]{1,0:T(8,128)(2,1)}, u32[]{:S(2)}, u32[]{:S(2)}) collective-permute-start(bf16[512,512]{1,0:T(8,128)(2,1)} %get-tuple-element.229), channel_id=1, source_target_pairs={{0,3},{1,0},{2,1},{3,2},{4,7},{5,4},{6,5},{7,6},{8,11},{9,8},{10,9... | collective-permute-start | bytes 1572872 | tf_op jit(solution)/shard_map/tokens_back/ppermute | solution.py:358
  605.1 43.4 %collective-permute-start.46 = (bf16[512,512]{1,0:T(8,128)(2,1)}, bf16[512,512]{1,0:T(8,128)(2,1)}, u32[]{:S(2)}, u32[]{:S(2)}) collective-permute-start(bf16[512,512]{1,0:T(8,128)(2,1)} %get-tuple-element.230), channel_id=1, source_target_pairs={{0,1},{1,2},{2,3},{3,0},{4,5},{5,6},{6,7},{7,4},{8,9},{9,10},{10,1... | collective-permute-start | bytes 1572872 | tf_op jit(solution)/shard_map/tokens_back/ppermute | solution.py:358
  607.1 53.6 %all-to-all-start.8 = ((bf16[4,32,1152]{2,1,0:T(8,128)(2,1)}), bf16[4,32,1152]{2,1,0:T(8,128)(2,1)S(1)}, u32[]{:S(2)}, u32[]{:S(2)}) async-start(bf16[4,32,1152]{2,1,0:T(8,128)(2,1)} %bitcast.79), calls=%async_computation.9 | async-start | bytes 589824 | tf_op jit(solution)/shard_map/early_sp/all_to_all | solution.py:107
  610.6 57.4 %collective-permute-start.42 = (bf16[1,512,512]{2,1,0:T(8,128)(2,1)}, bf16[1,512,512]{2,1,0:T(8,128)(2,1)}, u32[]{:S(2)}, u32[]{:S(2)}) collective-permute-start(bf16[1,512,512]{2,1,0:T(8,128)(2,1)} %add_convert_fusion.11), channel_id=1, source_target_pairs={{0,16},{4,20},{8,24},{12,28},{16,0},{20,4},{24,8},{28,12},{1,17},{... | collective-permute-start | bytes 1572872 | tf_op jit(solution)/shard_map/mix_reduce/ppermute | solution.py:39
  610.7 59.9 %collective-permute-start.45 = (bf16[1,512,512]{2,1,0:T(8,128)(2,1)}, bf16[1,512,512]{2,1,0:T(8,128)(2,1)}, u32[]{:S(2)}, u32[]{:S(2)}) collective-permute-start(bf16[1,512,512]{2,1,0:T(8,128)(2,1)} %add_convert_fusion.9), channel_id=1, source_target_pairs={{0,8},{4,12},{8,0},{12,4},{16,24},{20,28},{24,16},{28,20},{1,9},{5... | collective-permute-start | bytes 1572872 | tf_op jit(solution)/shard_map/mix_reduce/ppermute | solution.py:39
  654.9 35.3 %collective-permute-start.50 = (bf16[512,512]{1,0:T(8,128)(2,1)}, bf16[512,512]{1,0:T(8,128)(2,1)}, u32[]{:S(2)}, u32[]{:S(2)}) collective-permute-start(bf16[512,512]{1,0:T(8,128)(2,1)} %get-tuple-element.227), channel_id=1, source_target_pairs={{0,3},{1,0},{2,1},{3,2},{4,7},{5,4},{6,5},{7,6},{8,11},{9,8},{10,9... | collective-permute-start | bytes 1572872 | tf_op jit(solution)/shard_map/tokens_back/ppermute | solution.py:358
  654.9 35.3 %collective-permute-start.48 = (bf16[512,512]{1,0:T(8,128)(2,1)}, bf16[512,512]{1,0:T(8,128)(2,1)}, u32[]{:S(2)}, u32[]{:S(2)}) collective-permute-start(bf16[512,512]{1,0:T(8,128)(2,1)} %get-tuple-element.228), channel_id=1, source_target_pairs={{0,1},{1,2},{2,3},{3,0},{4,5},{5,6},{6,7},{7,4},{8,9},{9,10},{10,1... | collective-permute-start | bytes 1572872 | tf_op jit(solution)/shard_map/tokens_back/ppermute | solution.py:358
  695.0 25.0 %collective-permute-start.51 = (bf16[512,512]{1,0:T(8,128)(2,1)}, bf16[512,512]{1,0:T(8,128)(2,1)}, u32[]{:S(2)}, u32[]{:S(2)}) collective-permute-start(bf16[512,512]{1,0:T(8,128)(2,1)} %get-tuple-element.226), channel_id=1, source_target_pairs={{0,3},{1,0},{2,1},{3,2},{4,7},{5,4},{6,5},{7,6},{8,11},{9,8},{10,9... | collective-permute-start | bytes 1572872 | tf_op jit(solution)/shard_map/tokens_back/ppermute | solution.py:358
  698.1 33.8 %all-to-all-start.7 = ((bf16[4,128,640]{1,2,0:T(8,128)(2,1)}), bf16[4,128,640]{1,2,0:T(8,128)(2,1)S(1)}, u32[]{:S(2)}, u32[]{:S(2)}) async-start(bf16[4,128,640]{1,2,0:T(8,128)(2,1)} %broadcast_in_dim.96), calls=%async_computation.8 | async-start | bytes 1310720 | tf_op jit(solution)/shard_map/late_sp/all_to_all | solution.py:107
  (91 other events, 1305.9 us)
Sparse Core Ops, SparseCore 0:
  13.1 36.1 all-gather.9
  99.5 73.8 all-gather.11
  174.9 62.8 all-gather.17
  239.2 62.1 all-gather.15
  302.8 62.1 all-gather.13
  367.1 58.8 reduce-scatter.4
  428.4 68.8 reduce-scatter.10
  499.6 62.5 reduce-scatter.8
  564.4 77.1 reduce-scatter.6

commit v4 on v3

v4 whole, which is shorter than its diff:
```python
import functools
import math

import jax
import jax.numpy as jnp
from jax import lax
from jax.experimental import pallas as pl
from jax.experimental.pallas import tpu as pltpu
from jax.sharding import PartitionSpec as P

MODEL_WIDTH = 1024
QUERY_HEADS = 16
KEY_VALUE_HEADS = 8
HEAD_SIZE = 64
EXPERTS = 32
SPAN = 256
CAP = 192


NORM_EPS = 1e-06
ROPE_BASE = 10000.0
MASKED = -1e30
VMEM_LIMIT = 60 * 1024 * 1024


def contract(left, right, left_dim, right_dim):
    return lax.dot_general(
        left, right, (((left_dim,), (right_dim,)), ((), ())), preferred_element_type=jnp.float32
    )


def axis_bits(count):
    bits = [1 << place for place in range(count.bit_length() - 1)]
    return bits[::-1]


def flip(values, axis_name, bit):
    count = lax.axis_size(axis_name)
    return lax.ppermute(values, axis_name, [(place, place ^ bit) for place in range(count)])


def stage_orders(count):
    high = axis_bits(count)
    if count <= 2:
        return (high, high)
    return (high, high[1:2] + high[:1] + high[2:])


def gather_begin(values):
    half = values.shape[1] // 2
    return [{0: values[:, :half]}, {0: values[:, half:]}]


def gather_stage(lists, axis_name, stage, gates=()):
    count = lax.axis_size(axis_name)
    grown = []
    for order, pieces in zip(stage_orders(count), lists):
        keys = list(pieces)
        held = after([pieces[r] for r in keys], *gates) if gates else [pieces[r] for r in keys]
        new = dict(zip(keys, held))
        new.update({r ^ order[stage]: flip(new[r], axis_name, order[stage]) for r in keys})
        grown.append(new)
    return grown


def gather_end(lists):
    return [pieces[r] for pieces in lists for r in sorted(pieces)]


def newest(lists, stage):
    return [piece for pieces in lists for piece in list(pieces.values())[1 << stage :]]


def chunk_place(index, order):
    place = 0
    for bit in order:
        place = place * 2 + (index * 2 // bit) % 2
    return place


def reduce_stage(leave, stay, axis_name, stage, gates=()):
    count = lax.axis_size(axis_name)
    if gates:
        stay = after(stay, *gates)
    gone_next, kept_next = [], []
    for order, gone, kept in zip(stage_orders(count), leave, stay):
        arrived = flip(gone, axis_name, order[::-1][stage])
        middle = kept.shape[0] // 2
        if middle:
            total = kept[middle:].astype(jnp.float32) + arrived[middle:].astype(jnp.float32)
            gone_next.append(total.astype(jnp.bfloat16))
            total = kept[:middle].astype(jnp.float32) + arrived[:middle].astype(jnp.float32)
            kept_next.append(total.astype(jnp.bfloat16))
        else:
            kept_next.append(kept[0].astype(jnp.float32) + arrived[0].astype(jnp.float32))
    return gone_next, kept_next


def after(values, *others):
    held = lax.optimization_barrier((*values, *others))
    return list(held[: len(values)])


def shift_pairs(count, by):
    return [(place, (place + by) % count) for place in range(count)]


def exchange_blocks(values, axis_name):
    return lax.all_to_all(values, axis_name, split_axis=0, concat_axis=0, tiled=True)


def pack_expert(gate, up, down):
    rows = gate.shape[0]
    blocks = [down[k * rows : (k + 1) * rows] for k in range(down.shape[0] // rows)]
    return jnp.concatenate([gate, up, jnp.concatenate(blocks, axis=1)], axis=0)


def expert_step(own_ref, slot_ref, share_ref, weight_ref, *refs, count, first):
    acts, cots = refs[: 2 * count], refs[2 * count : 4 * count]
    mixed_ref, back_ref, share_grad_ref, weight_grad_ref = refs[4 * count : 4 * count + 4]
    act_buf, cot_buf, arrive, act_rows, hidden_rows, down_rows, gate_rows, up_rows = refs[
        4 * count + 4 :
    ]
    pair, rows = act_buf.shape[1], act_buf.shape[3]
    shards, _, packed_rows, hidden_width = weight_ref.shape
    deep = packed_rows // 3
    width = shards * deep
    tile, tiles = pl.program_id(1), pl.num_programs(1)
    step = pl.program_id(0) * tiles + tile
    steps = pl.num_programs(0) * tiles

    def copies(first, slot):
        made = []
        for source in range(pair):
            for half in range(2):
                lane = 2 * source + half
                index = half * count + first + source
                made.append(
                    pltpu.make_async_copy(
                        acts[index], act_buf.at[slot, source, half], arrive.at[slot, 0, lane]
                    )
                )
                made.append(
                    pltpu.make_async_copy(
                        cots[index], cot_buf.at[slot, source, half], arrive.at[slot, 1, lane]
                    )
                )
        return made

    def fetch(target, slot):
        for known in range(count // pair):

            @pl.when(target == known)
            def _():
                for copy in copies(known * pair, slot):
                    copy.start()

    @pl.when(step == 0)
    def _():
        fetch(0, 0)

    @pl.when(step + 1 < steps)
    def _():
        fetch((step + 1) % tiles, (step + 1) % 2)

    slot = step % 2
    for copy in copies(0, slot):
        copy.wait()

    gate_w = weight_ref[:, 0, :deep, :].reshape(width, hidden_width)
    up_w = weight_ref[:, 0, deep : 2 * deep, :].reshape(width, hidden_width)

    def down_w(shard):
        part = weight_ref[shard, 0, 2 * deep :, :]
        blocks = [part[:, k * deep : (k + 1) * deep] for k in range(hidden_width // deep)]
        return jnp.concatenate(blocks, axis=0)

    picked, cots_here, shares, masks = [], [], [], []
    expert = pl.ds(first + pl.program_id(0), 1)
    for source in range(pair):
        given = source ^ (own_ref[0] % pair)
        mask = lax.broadcasted_iota(jnp.int32, (CAP, rows), 0) == slot_ref[given, expert, :]
        choose = jnp.where(mask, 1.0, 0.0).astype(jnp.bfloat16)
        picked.append(
            jnp.concatenate(
                [contract(choose, act_buf[slot, source, half], 1, 0) for half in range(2)], axis=1
            )
        )
        cots_here.append(
            jnp.concatenate(
                [contract(choose, cot_buf[slot, source, half], 1, 0) for half in range(2)], axis=1
            )
        )
        given_share = share_ref[given, expert, :]
        shares.append(jnp.sum(jnp.where(mask, given_share, 0.0), axis=1, keepdims=True))
        masks.append(mask)
    act = jnp.concatenate(picked, 0).astype(jnp.bfloat16)
    cot = jnp.concatenate(cots_here, 0)
    share = jnp.concatenate(shares, 0)
    gate_pre = contract(act, gate_w, 1, 0)
    up_pre = contract(act, up_w, 1, 0)
    sigmoid = 1.0 / (1.0 + jnp.exp(-gate_pre))
    silu = gate_pre * sigmoid
    hidden = (silu * up_pre).astype(jnp.bfloat16)
    made = jnp.concatenate(
        [contract(hidden, down_w(shard), 1, 0) for shard in range(shards)], axis=1
    )
    made = made.astype(jnp.bfloat16).astype(jnp.float32)
    share_grad = jnp.sum(made * cot, axis=1, keepdims=True)
    mixed = (made * share).astype(jnp.bfloat16)
    made_grad = (share * cot).astype(jnp.bfloat16)
    hidden_grad = sum(
        contract(made_grad[:, shard * deep : (shard + 1) * deep], down_w(shard), 1, 1)
        for shard in range(shards)
    )
    up_grad = (hidden_grad * silu).astype(jnp.bfloat16)
    gate_grad = (
        hidden_grad * up_pre * sigmoid * (1.0 + gate_pre * (1.0 - sigmoid))
    ).astype(jnp.bfloat16)
    back = (contract(gate_grad, gate_w, 1, 1) + contract(up_grad, up_w, 1, 1)).astype(jnp.bfloat16)
    for source in range(pair):
        part = slice(source * CAP, (source + 1) * CAP)
        mixed_ref[0, source] = mixed[part]
        back_ref[0, source] = back[part]
        share_grad_ref[0, source] = jnp.sum(
            jnp.where(masks[source], share_grad[part], 0.0), axis=0, keepdims=True
        )
    here = pl.ds(pl.multiple_of(tile * pair * CAP, pair * CAP), pair * CAP)
    act_rows[here, :] = act
    hidden_rows[here, :] = hidden
    down_rows[here, :] = made_grad
    gate_rows[here, :] = gate_grad
    up_rows[here, :] = up_grad

    @pl.when(tile == tiles - 1)
    def _():
        gate_sum = contract(act_rows[...], gate_rows[...], 0, 0).astype(jnp.bfloat16)
        up_sum = contract(act_rows[...], up_rows[...], 0, 0).astype(jnp.bfloat16)
        for shard in range(shards):
            cols = slice(shard * deep, (shard + 1) * deep)
            weight_grad_ref[shard, 0, :deep, :] = gate_sum[cols]
            weight_grad_ref[shard, 0, deep : 2 * deep, :] = up_sum[cols]
            down_sum = contract(hidden_rows[...], down_rows[:, cols], 0, 0).astype(jnp.bfloat16)
            for k in range(hidden_width // deep):
                weight_grad_ref[shard, 0, 2 * deep :, k * deep : (k + 1) * deep] = down_sum[
                    k * deep : (k + 1) * deep
                ]


def run_experts(own, first, slots, shares, weights, acts, cots):
    count, known, rows = slots.shape
    half = acts[0].shape[1]
    shards, experts, packed_rows, hidden_width = weights.shape
    pair = 2
    listed = count * CAP
    low = jnp.bfloat16

    def by_source(*shape):
        return pl.BlockSpec((1, pair) + shape, lambda e, s, *_: (e, s) + (0,) * len(shape))

    given = pl.BlockSpec((pair, known, rows), lambda e, s, own: (s ^ (own[0] // pair), 0, 0))
    matrices = pl.BlockSpec((shards, 1, packed_rows, hidden_width), lambda e, s, *_: (0, e, 0, 0))
    anywhere = pl.BlockSpec(memory_space=pl.ANY)
    outs = pl.pallas_call(
        functools.partial(expert_step, count=count, first=first),
        grid_spec=pltpu.PrefetchScalarGridSpec(
            num_scalar_prefetch=1,
            grid=(experts, count // pair),
            in_specs=[given, given, matrices] + [anywhere] * (4 * count),
            out_specs=[
                by_source(CAP, 2 * half),
                by_source(CAP, 2 * half),
                by_source(1, rows),
                matrices,
            ],
            scratch_shapes=[
                pltpu.VMEM((2, pair, 2, rows, half), low),
                pltpu.VMEM((2, pair, 2, rows, half), low),
                pltpu.SemaphoreType.DMA((2, 2, 2 * pair)),
                pltpu.VMEM((listed, 2 * half), low),
                pltpu.VMEM((listed, hidden_width), low),
                pltpu.VMEM((listed, 2 * half), low),
                pltpu.VMEM((listed, hidden_width), low),
                pltpu.VMEM((listed, hidden_width), low),
            ],
        ),
        out_shape=[
            jax.ShapeDtypeStruct((experts, count, CAP, 2 * half), low),
            jax.ShapeDtypeStruct((experts, count, CAP, 2 * half), low),
            jax.ShapeDtypeStruct((experts, count, 1, rows), jnp.float32),
            jax.ShapeDtypeStruct(weights.shape, low),
        ],
        compiler_params=pltpu.CompilerParams(
            dimension_semantics=("arbitrary", "arbitrary"), vmem_limit_bytes=VMEM_LIMIT
        ),
        name="experts",
    )(own, slots, shares, weights, *acts, *cots)
    return (outs[0], outs[1], outs[2][:, :, 0], outs[3])


def combine_step(own_ref, slot_ref, *refs):
    parts, (left_ref, right_ref) = refs[:-2], refs[-2:]
    experts = sum(part.shape[0] for part in parts)
    rows, half = left_ref.shape[1:]
    place = lax.broadcasted_iota(jnp.int32, (rows, experts * CAP), 1)
    hit = None
    for expert in range(experts):
        slot = slot_ref[0, :, expert : expert + 1]
        match = place == jnp.where(slot >= 0, slot + expert * CAP, -1)
        hit = match if hit is None else hit | match
    choose = jnp.where(hit, 1.0, 0.0).astype(jnp.bfloat16)
    listed = jnp.concatenate(
        [part[:, 0].reshape(-1, 2 * half) for part in parts], axis=0
    )
    total = contract(choose, listed, 1, 0).astype(jnp.bfloat16)
    left_ref[0] = total[:, :half]
    right_ref[0] = total[:, half:]


def combine_rows(own, slots_by_row, parts, odd):
    sources, rows, experts = slots_by_row.shape
    width = parts[0].shape[3]
    orders = [order[:-1][::-1] for order in stage_orders(sources)]

    def half_of(order):
        return pl.BlockSpec((1, rows, width // 2), lambda i, *_: (chunk_place(i, order), 0, 0))

    return pl.pallas_call(
        combine_step,
        grid_spec=pltpu.PrefetchScalarGridSpec(
            num_scalar_prefetch=1,
            grid=(sources // 2,),
            in_specs=[
                pl.BlockSpec(
                    (1, rows, experts), lambda i, own: (own[0] ^ (2 * i + odd), 0, 0)
                )
            ]
            + [
                pl.BlockSpec((part.shape[0], 1, CAP, width), lambda i, *_: (0, 2 * i + odd, 0, 0))
                for part in parts
            ],
            out_specs=[half_of(order) for order in orders],
        ),
        out_shape=[jax.ShapeDtypeStruct((sources // 2, rows, width // 2), jnp.bfloat16)] * 2,
        compiler_params=pltpu.CompilerParams(
            dimension_semantics=("arbitrary",), vmem_limit_bytes=VMEM_LIMIT
        ),
        name="combine",
    )(own, slots_by_row, *parts)


def ring_begin(values):
    half = values.shape[1] // 2
    return [values[:, :half]], [values[:, half:]]


def ring_step(lists, axis_name, gates=()):
    count = lax.axis_size(axis_name)
    moving = [part[-1] for part in lists]
    if gates:
        moving = after(moving, *gates)
    return [
        part + [lax.ppermute(one, axis_name, shift_pairs(count, by))]
        for by, part, one in zip((1, -1), lists, moving)
    ]


def sequence_starts(length_row, places):
    count = length_row.shape[0]
    ends = [length_row[0]]
    for index in range(1, count):
        ends.append(ends[-1] + length_row[index])
    first = jnp.zeros_like(places)
    for index in range(count - 1):
        first = jnp.where(places >= ends[index], ends[index], first)
    return first


def turn_halves(values, cosine, sine):
    groups = []
    for first in range(0, values.shape[1], 128):
        group = values[:, first : first + 128]
        lane = lax.broadcasted_iota(jnp.int32, group.shape, 1)
        partner = jnp.where(
            lane % HEAD_SIZE < HEAD_SIZE // 2,
            pltpu.roll(group, 128 - HEAD_SIZE // 2, 1),
            pltpu.roll(group, HEAD_SIZE // 2, 1),
        )
        groups.append(group * cosine + partner * sine)
    return jnp.concatenate(groups, axis=1)


def scale_rows(values):
    return lax.rsqrt(jnp.mean(values * values, axis=1, keepdims=True) + NORM_EPS)


def block_state(bounds_ref, block, own_blocks):
    own = (block >= bounds_ref[1]) & (block < bounds_ref[1] + own_blocks)
    needed = (block >= bounds_ref[0]) & (block < bounds_ref[1] + own_blocks)
    return needed, own


def project_step(bounds_ref, order_ref, gain_ref, weight_ref, cos_ref, sin_ref, *refs, own_blocks):
    pieces, (rows_ref, query_ref, key_ref, value_ref) = refs[:-4], refs[-4:]
    count = len(pieces) // 2
    span, width = rows_ref.shape
    token_rows = pieces[0].shape[0]
    queries, keys = query_ref.shape[1], key_ref.shape[1]
    block = pl.program_id(0)
    needed, own = block_state(bounds_ref, block, own_blocks)

    @pl.when(needed)
    def _():
        places = block * span + lax.broadcasted_iota(jnp.int32, (span, token_rows), 0)
        left, right = 0.0, 0.0
        for index in range(count):
            part = order_ref[:, index * token_rows : (index + 1) * token_rows]
            choose = jnp.where(part == places, 1.0, 0.0).astype(jnp.bfloat16)
            left = left + contract(choose, pieces[index][...], 1, 0)
            right = right + contract(choose, pieces[count + index][...], 1, 0)
        values = jnp.concatenate([left, right], axis=1)
        rows_ref[...] = values.astype(jnp.bfloat16)
        act = (values * scale_rows(values) * gain_ref[...]).astype(jnp.bfloat16)
        cosine, sine = cos_ref[...], sin_ref[...]
        made = contract(act, weight_ref[:, queries : queries + keys], 1, 0)
        key_ref[...] = turn_halves(made, cosine, sine).astype(jnp.bfloat16)
        value_ref[...] = contract(act, weight_ref[:, queries + keys :], 1, 0).astype(jnp.bfloat16)

        @pl.when(own)
        def _():
            made = contract(act, weight_ref[:, :queries], 1, 0)
            query_ref[...] = turn_halves(made, cosine, sine).astype(jnp.bfloat16)


def whole_block(array):
    return pl.BlockSpec(
        array.shape, lambda *_: (0,) * array.ndim, pipeline_mode=pl.Buffered(1)
    )


def row_block(width):
    return pl.BlockSpec((SPAN, width), lambda i, *_: (i, 0))


def first_columns(rows, columns):
    return pl.BlockSpec((rows, columns), lambda *_: (0, 0), pipeline_mode=pl.Buffered(1))


def project(bounds, order_row, gain, weight, cosine, sine, pieces):
    rows = order_row.shape[1]
    width = weight.shape[0]
    token_rows = pieces[0].shape[0]
    own_blocks = token_rows // SPAN
    queries, keys = QUERY_HEADS * HEAD_SIZE, KEY_VALUE_HEADS * HEAD_SIZE
    low = jnp.bfloat16
    own_block = pl.BlockSpec(
        (SPAN, queries), lambda i, bounds: (jnp.clip(i - bounds[1], 0, own_blocks - 1), 0)
    )
    return pl.pallas_call(
        functools.partial(project_step, own_blocks=own_blocks),
        grid_spec=pltpu.PrefetchScalarGridSpec(
            num_scalar_prefetch=1,
            grid=(rows // SPAN,),
            in_specs=[
                whole_block(order_row),
                whole_block(gain),
                first_columns(width, queries + 2 * keys),
                row_block(128),
                row_block(128),
            ]
            + [whole_block(piece) for piece in pieces],
            out_specs=[row_block(width), own_block, row_block(keys), row_block(keys)],
        ),
        out_shape=[
            jax.ShapeDtypeStruct((rows, width), low),
            jax.ShapeDtypeStruct((token_rows, queries), low),
            jax.ShapeDtypeStruct((rows, keys), low),
            jax.ShapeDtypeStruct((rows, keys), low),
        ],
        compiler_params=pltpu.CompilerParams(
            dimension_semantics=("arbitrary",), vmem_limit_bytes=VMEM_LIMIT
        ),
        name="project",
    )(bounds, order_row, gain, weight, cosine, sine, *pieces)


def stack_heads(values):
    values = values.astype(jnp.float32)
    lower = lax.broadcasted_iota(jnp.int32, (values.shape[0], 128), 1) < HEAD_SIZE
    first, second = values[:, :128], values[:, 128:]
    first_turned = pltpu.roll(first, HEAD_SIZE, 1)
    second_turned = pltpu.roll(second, HEAD_SIZE, 1)
    return jnp.concatenate(
        [
            jnp.where(lower, first, 0.0),
            jnp.where(lower, first_turned, 0.0),
            jnp.where(lower, 0.0, second_turned),
            jnp.where(lower, 0.0, second),
        ],
        axis=0,
    ).astype(jnp.bfloat16)


def unstack_heads(values):
    span = values.shape[0] // 4
    parts = [values[index * span : (index + 1) * span] for index in range(4)]
    lower = lax.broadcasted_iota(jnp.int32, (span, 128), 1) < HEAD_SIZE
    first = jnp.where(lower, parts[0], pltpu.roll(parts[1], HEAD_SIZE, 1))
    second = jnp.where(lower, pltpu.roll(parts[2], HEAD_SIZE, 1), parts[3])
    return jnp.concatenate([first, second], axis=1)


def allowed_pairs(start_ref, block, key_block, span):
    query_place = block * span + lax.broadcasted_iota(jnp.int32, (span, span), 0)
    key_place = key_block * span + lax.broadcasted_iota(jnp.int32, (span, span), 1)
    return (key_place <= query_place) & (key_place >= start_ref[...])


def mask_scores(scores, allowed):
    span = allowed.shape[0]
    heads = scores.shape[0] // span
    stacked = scores.reshape(heads, span, span)
    return jnp.where(allowed[None], stacked, MASKED).reshape(scores.shape)


def attend_step(
    lowest_ref, first_ref, start_ref, query_ref, key_ref, value_ref, out_ref, log_ref, best, accum
):
    part = pl.program_id(1)
    block = first_ref[0] + part
    span = query_ref.shape[0]
    query = stack_heads(query_ref[...]) * jnp.bfloat16(1.0 / math.sqrt(HEAD_SIZE))
    lowest = lowest_ref[part]

    def scores_of(key_block):
        here = pl.ds(pl.multiple_of(key_block * span, span), span)
        scores = contract(query, key_ref[here, :], 1, 1)
        return mask_scores(scores, allowed_pairs(start_ref, block, key_block, span))

    best[...] = scores_of(block)

    def look(key_block, _):
        best[...] = jnp.maximum(best[...], scores_of(key_block))
        return 0

    lax.fori_loop(lowest, block, look, 0)
    top = jnp.max(best[...], axis=1, keepdims=True)
    accum[...] = jnp.zeros_like(accum)

    def visit(key_block, _):
        here = pl.ds(pl.multiple_of(key_block * span, span), span)
        terms = jnp.exp(scores_of(key_block) - top).astype(jnp.bfloat16)
        values = value_ref[here, :]
        values = jnp.concatenate([values, jnp.ones((span, 128), jnp.bfloat16)], axis=1)
        accum[...] += contract(terms, values, 1, 0)
        return 0

    lax.fori_loop(lowest, block + 1, visit, 0)
    total = accum[:, 128:129]
    out_ref[...] = unstack_heads(accum[:, :128] / total).astype(jnp.bfloat16)
    logs = top + jnp.log(total)
    log_ref[0] = jnp.concatenate(
        [logs[head * span : (head + 1) * span] for head in range(4)], axis=1
    )


def head_specs(rows):
    start = pl.BlockSpec((SPAN, 1), lambda j, i, *_: (i, 0))
    logs = pl.BlockSpec((1, SPAN, 4), lambda j, i, *_: (j, i, 0))
    query = pl.BlockSpec((SPAN, 256), lambda j, i, *_: (i, j))
    key = pl.BlockSpec((rows, 128), lambda j, i, *_: (0, j))
    return start, logs, query, key


def attend(lowest, first, start, query, key, value):
    rows, columns = query.shape
    pairs = key.shape[1] // 128
    start_spec, log_spec, query_spec, key_spec = head_specs(key.shape[0])
    return pl.pallas_call(
        attend_step,
        grid_spec=pltpu.PrefetchScalarGridSpec(
            num_scalar_prefetch=2,
            grid=(pairs, rows // SPAN),
            in_specs=[start_spec, query_spec, key_spec, key_spec],
            out_specs=[query_spec, log_spec],
            scratch_shapes=[
                pltpu.VMEM((4 * SPAN, SPAN), jnp.float32),
                pltpu.VMEM((4 * SPAN, 256), jnp.float32),
            ],
        ),
        out_shape=[
            jax.ShapeDtypeStruct((rows, columns), jnp.bfloat16),
            jax.ShapeDtypeStruct((pairs, rows, 4), jnp.float32),
        ],
        compiler_params=pltpu.CompilerParams(
            dimension_semantics=("arbitrary", "arbitrary"), vmem_limit_bytes=VMEM_LIMIT
        ),
        name="attend",
    )(lowest, first, start, query, key, value)


def attend_back_step(
    lowest_ref,
    first_ref,
    start_ref,
    log_ref,
    query_ref,
    out_ref,
    cot_ref,
    key_ref,
    value_ref,
    query_grad_ref,
    key_grad_ref,
    value_grad_ref,
    accum,
):
    part = pl.program_id(1)
    block = first_ref[0] + part
    span = query_ref.shape[0]
    scale = 1.0 / math.sqrt(HEAD_SIZE)

    @pl.when(part == 0)
    def _():
        key_grad_ref[...] = jnp.zeros_like(key_grad_ref)
        value_grad_ref[...] = jnp.zeros_like(value_grad_ref)

    query = stack_heads(query_ref[...]) * jnp.bfloat16(scale)
    cot = stack_heads(cot_ref[...])
    out = stack_heads(out_ref[...])
    dots = jnp.sum(cot.astype(jnp.float32) * out.astype(jnp.float32), axis=1, keepdims=True)
    logs = jnp.concatenate([log_ref[0, :, head : head + 1] for head in range(4)], axis=0)
    accum[...] = jnp.zeros_like(accum)

    def visit(key_block, _):
        here = pl.ds(pl.multiple_of(key_block * span, span), span)
        keys = key_ref[here, :]
        scores = contract(query, keys, 1, 1)
        scores = mask_scores(scores, allowed_pairs(start_ref, block, key_block, span))
        probs = jnp.exp(scores - logs)
        prob_grad = contract(cot, value_ref[here, :], 1, 1)
        score_grad = (probs * (prob_grad - dots)).astype(jnp.bfloat16)
        accum[...] += contract(score_grad, keys, 1, 0)
        key_grad_ref[here, :] += contract(score_grad, query, 0, 0)
        value_grad_ref[here, :] += contract(probs.astype(jnp.bfloat16), cot, 0, 0)
        return 0

    lax.fori_loop(lowest_ref[part], block + 1, visit, 0)
    query_grad_ref[...] = unstack_heads(accum[...] * scale)


def attend_back(lowest, first, start, logs, query, out, cot, key, value):
    rows, columns = query.shape
    pairs = key.shape[1] // 128
    start_spec, log_spec, query_spec, key_spec = head_specs(key.shape[0])
    return pl.pallas_call(
        attend_back_step,
        grid_spec=pltpu.PrefetchScalarGridSpec(
            num_scalar_prefetch=2,
            grid=(pairs, rows // SPAN),
            in_specs=[
                start_spec,
                log_spec,
                query_spec,
                query_spec,
                query_spec,
                key_spec,
                key_spec,
            ],
            out_specs=[query_spec, key_spec, key_spec],
            scratch_shapes=[pltpu.VMEM((4 * SPAN, 128), jnp.float32)],
        ),
        out_shape=[
            jax.ShapeDtypeStruct((rows, columns), jnp.float32),
            jax.ShapeDtypeStruct(key.shape, jnp.float32),
            jax.ShapeDtypeStruct(key.shape, jnp.float32),
        ],
        compiler_params=pltpu.CompilerParams(
            dimension_semantics=("arbitrary", "arbitrary"), vmem_limit_bytes=VMEM_LIMIT
        ),
        name="attend_back",
    )(lowest, first, start, logs, query, out, cot, key, value)


def weight_back_step(
    bounds_ref,
    gain_ref,
    cos_ref,
    sin_ref,
    query_ref,
    key_ref,
    value_ref,
    rows_ref,
    key_rows,
    query_rows,
    leave_left_ref,
    leave_right_ref,
    stay_left_ref,
    stay_right_ref,
    act_rows,
    left_sums,
    right_sums,
    *,
    orders,
):
    block = pl.program_id(0)
    span, width = rows_ref.shape
    own_rows, queries = query_rows.shape
    here = pl.ds(pl.multiple_of(block * span, span), span)
    needed, own = block_state(bounds_ref, block, own_rows // span)

    @pl.when(jnp.logical_not(needed))
    def _():
        act_rows[here, :] = jnp.zeros((span, width), jnp.bfloat16)
        key_rows[here, :] = jnp.zeros((span, key_rows.shape[1]), jnp.bfloat16)

    @pl.when(needed)
    def _():
        cosine, sine = cos_ref[...], -sin_ref[...]
        key_grads = turn_halves(key_ref[...], cosine, sine)
        key_rows[here, :] = jnp.concatenate([key_grads, value_ref[...]], axis=1).astype(
            jnp.bfloat16
        )
        values = rows_ref[...].astype(jnp.float32)
        act_rows[here, :] = (values * scale_rows(values) * gain_ref[...]).astype(jnp.bfloat16)

        @pl.when(own)
        def _():
            at = pl.ds(pl.multiple_of((block - bounds_ref[1]) * span, span), span)
            query_rows[at, :] = turn_halves(query_ref[...], cosine, sine).astype(jnp.bfloat16)

    @pl.when(block == pl.num_programs(0) - 1)
    def _():
        count, shard = left_sums.shape[:2]
        own_all = pl.ds(pl.multiple_of(bounds_ref[1] * span, span), own_rows)
        sums = contract(act_rows[own_all, :], query_rows[...], 0, 0).astype(jnp.bfloat16)
        left_sums[...] = sums.reshape(left_sums.shape)
        sums = contract(act_rows[...], key_rows[...], 0, 0).astype(jnp.bfloat16)
        right_sums[...] = sums.reshape(right_sums.shape)
        for index in range(count // 2):
            for odd, targets in (
                (1, (leave_left_ref, leave_right_ref)),
                (0, (stay_left_ref, stay_right_ref)),
            ):
                source = bounds_ref[2] ^ (2 * index + odd)
                for order, target, sums in zip(orders, targets, (left_sums, right_sums)):
                    target[chunk_place(index, order)] = sums[source]


def weight_back(bounds, gain, cosine, sine, query_grad, key_grad, value_grad, rows_in, shards):
    rows, width = rows_in.shape
    token_rows, queries = query_grad.shape
    keys = key_grad.shape[1]
    own_blocks = token_rows // SPAN
    shard = width // shards
    low = jnp.bfloat16
    own = pl.BlockSpec(
        (SPAN, queries), lambda i, bounds: (jnp.clip(i - bounds[1], 0, own_blocks - 1), 0)
    )
    widths = (queries, 2 * keys)
    sums = [jax.ShapeDtypeStruct((shards // 2, shard, columns), low) for columns in widths]
    made = [
        jax.ShapeDtypeStruct((rows, 2 * keys), low),
        jax.ShapeDtypeStruct((token_rows, queries), low),
    ]
    return pl.pallas_call(
        functools.partial(
            weight_back_step, orders=[order[:-1][::-1] for order in stage_orders(shards)]
        ),
        grid_spec=pltpu.PrefetchScalarGridSpec(
            num_scalar_prefetch=1,
            grid=(rows // SPAN,),
            in_specs=[
                whole_block(gain),
                row_block(128),
                row_block(128),
                own,
                row_block(keys),
                row_block(keys),
                row_block(width),
            ],
            out_specs=[whole_block(one) for one in made + sums + sums],
            scratch_shapes=[pltpu.VMEM((rows, width), low)]
            + [pltpu.VMEM((shards, shard, columns), low) for columns in widths],
        ),
        out_shape=made + sums + sums,
        compiler_params=pltpu.CompilerParams(
            dimension_semantics=("arbitrary",), vmem_limit_bytes=VMEM_LIMIT
        ),
        name="weight_back",
    )(bounds, gain, cosine, sine, query_grad, key_grad, value_grad, rows_in)


def token_back_step(
    bounds_ref,
    order_ref,
    gain_ref,
    weight_ref,
    query_ref,
    key_ref,
    rows_ref,
    residual_ref,
    out_ref,
    token_rows,
    act_grad,
):
    phase, block = pl.program_id(0), pl.program_id(1)
    span, width = rows_ref.shape
    own_rows, queries = query_ref.shape
    here = pl.ds(pl.multiple_of(block * span, span), span)
    needed, own = block_state(bounds_ref, block, own_rows // span)
    own_at = pl.ds(
        pl.multiple_of(jnp.where(own, block - bounds_ref[1], 0) * span, span), span
    )

    @pl.when((phase == 0) & jnp.logical_not(needed))
    def _():
        token_rows[here, :] = jnp.zeros((span, width), jnp.bfloat16)

    @pl.when((phase == 0) & needed)
    def _():
        act_grad[...] = contract(key_ref[...], weight_ref[:, queries:], 1, 1)

        @pl.when(own)
        def _():
            act_grad[...] += contract(query_ref[own_at, :], weight_ref[:, :queries], 1, 1)

        values = rows_ref[...].astype(jnp.float32)
        scale = scale_rows(values)
        normed = values * scale
        scaled = act_grad[...] * gain_ref[...]
        token_grad = scale * (scaled - normed * jnp.mean(scaled * normed, axis=1, keepdims=True))
        residual = jnp.where(own, residual_ref[own_at, :].astype(jnp.float32), 0.0)
        token_rows[here, :] = (token_grad + residual).astype(jnp.bfloat16)

    @pl.when(phase == 1)
    def _():
        total = token_rows.shape[0]
        places = lax.broadcasted_iota(jnp.int32, (span, total), 1)
        choose = jnp.where(order_ref[...] == places, 1.0, 0.0).astype(jnp.bfloat16)
        out_ref[...] = contract(choose, token_rows[...], 1, 0).astype(jnp.bfloat16)


def token_back(bounds, order_column, gain, weight, query_rows, key_rows, rows_in, residual):
    rows, width = rows_in.shape
    blocks = rows // SPAN
    low = jnp.bfloat16

    def early(columns):
        return pl.BlockSpec((SPAN, columns), lambda p, i, *_: (jnp.where(p == 0, i, blocks - 1), 0))

    def late(columns):
        return pl.BlockSpec((SPAN, columns), lambda p, i, *_: (jnp.where(p == 0, 0, i), 0))

    return pl.pallas_call(
        token_back_step,
        grid_spec=pltpu.PrefetchScalarGridSpec(
            num_scalar_prefetch=1,
            grid=(2, blocks),
            in_specs=[
                late(1),
                whole_block(gain),
                first_columns(width, query_rows.shape[1] + key_rows.shape[1]),
                whole_block(query_rows),
                early(key_rows.shape[1]),
                early(width),
                whole_block(residual),
            ],
            out_specs=late(width),
            scratch_shapes=[
                pltpu.VMEM((rows, width), low),
                pltpu.VMEM((SPAN, width), jnp.float32),
            ],
        ),
        out_shape=jax.ShapeDtypeStruct((rows, width), low),
        compiler_params=pltpu.CompilerParams(
            dimension_semantics=("arbitrary", "arbitrary"), vmem_limit_bytes=VMEM_LIMIT
        ),
        name="token_back",
    )(bounds, order_column, gain, weight, query_rows, key_rows, rows_in, residual)


def body(
    tokens,
    query_weight,
    key_projection_weight,
    value_projection_weight,
    output_weight,
    router_weight,
    first_gain,
    second_gain,
    expert_gate,
    expert_up,
    expert_down,
    routes,
    dealing,
    lengths,
    cotangent,
):
    low = jnp.bfloat16
    token_rows = tokens.shape[0]
    sp_count = lax.axis_size("sp")
    sp_index = lax.axis_index("sp")
    fsdp_count = lax.axis_size("fsdp")
    fsdp_index = lax.axis_index("fsdp")
    group_rows = token_rows * sp_count
    local_experts = EXPERTS // fsdp_count
    shard_rows = query_weight.shape[0]
    relative = fsdp_index ^ jnp.arange(fsdp_count, dtype=jnp.int32)
    packed = jnp.concatenate(
        [
            query_weight.astype(low),
            key_projection_weight.astype(low),
            value_projection_weight.astype(low),
            output_weight.astype(low),
            router_weight.astype(low),
            first_gain.astype(low)[:, None],
            second_gain.astype(low)[:, None],
            jnp.zeros((shard_rows, 128 - EXPERTS - 2), low),
        ],
        axis=1,
    )
    packed_all = lax.all_gather(packed, "fsdp", axis=0, tiled=True)
    query_columns = QUERY_HEADS * HEAD_SIZE
    key_columns = KEY_VALUE_HEADS * HEAD_SIZE
    qkv_columns = query_columns + 2 * key_columns
    output_full = packed_all[:, qkv_columns : qkv_columns + MODEL_WIDTH]
    rest = packed_all[:, qkv_columns + MODEL_WIDTH :]
    router_full = rest[:, :EXPERTS]
    gain_attend = rest[:, EXPERTS].astype(jnp.float32)[None, :]
    gain_mixer = rest[:, EXPERTS + 1].astype(jnp.float32)[None, :]

    expert_range = jnp.arange(EXPERTS, dtype=jnp.int32)
    member = jnp.any(routes[:, :, None] == expert_range[None, None, :], axis=1)
    row_range = jnp.arange(token_rows, dtype=jnp.int32)
    upto = (row_range[:, None] <= row_range[None, :]).astype(low)
    rank = jnp.dot(member.T.astype(low), upto, preferred_element_type=jnp.float32)
    slots = jnp.where(member.T, rank.astype(jnp.int32) - 1, -1)

    def to_experts(by_expert):
        return exchange_blocks(
            by_expert.reshape(fsdp_count, local_experts, token_rows), "fsdp"
        )

    own = fsdp_index.astype(jnp.int32)[None]
    order_row = dealing[0]
    order_here = lax.dynamic_slice_in_dim(
        jnp.concatenate([order_row, order_row]), sp_index * token_rows, group_rows
    )
    places = jnp.arange(group_rows, dtype=jnp.int32)
    starts = sequence_starts(lengths[0], places)
    own_starts = lax.dynamic_slice_in_dim(starts, sp_index * token_rows, token_rows)
    lowest = own_starts[::SPAN] // SPAN
    start_column = own_starts[:, None]
    first_block = sp_index * (token_rows // SPAN)
    bounds = jnp.stack([lowest[0], first_block, fsdp_index]).astype(jnp.int32)
    half_dim = HEAD_SIZE // 2
    frequency = ROPE_BASE ** (-(jnp.arange(half_dim, dtype=jnp.float32) * 2.0 / HEAD_SIZE))
    angles = (places - starts).astype(jnp.float32)[:, None] * frequency[None, :]
    cosine = jnp.tile(jnp.cos(angles), (1, 4))
    sine = jnp.sin(angles)
    sine = jnp.concatenate([-sine, sine, -sine, sine], axis=1)
    slots_here = to_experts(slots)
    slots_by_row = jnp.swapaxes(slots_here, 1, 2)
    merged = max(local_experts // 2, 1)
    groups = [range(first, first + merged) for first in range(0, local_experts, merged)]
    expert_parts = [
        jnp.stack(
            [
                pack_expert(
                    expert_gate[e].astype(low), expert_up[e].astype(low), expert_down[e].astype(low)
                )
                for e in members
            ]
        )
        for members in groups
    ]
    stages = fsdp_count.bit_length() - 1
    ring_gates = {
        2: (cosine, sine, start_column, slots_by_row, order_here, bounds, *expert_parts),
    }
    with jax.named_scope("tokens_ring"):
        ring = ring_begin(tokens)
        for step in range(sp_count - 1):
            ring = ring_step(ring, "sp", ring_gates.get(step, ()))
            if step == 0:
                arrived_first = [part[-1] for part in ring]
    left, right = ring
    ring_end = (left[-1], right[-1])
    with jax.named_scope("cot_gather"):
        cot_lists = gather_begin(after([cotangent], *arrived_first)[0])
        cot_lists = gather_stage(cot_lists, "fsdp", 0)
    pieces = [left[-k % sp_count] for k in range(sp_count)] + right
    expert_parts = after(expert_parts, *ring_end, packed_all)
    with jax.named_scope("weights_queue"):
        expert_weights = [
            lax.all_gather(part, "sp", axis=0, tiled=False) for part in expert_parts
        ]
    rows_initial, query, key, value = project(
        bounds, order_here[None, :], gain_attend, packed_all, cosine, sine, pieces
    )
    with jax.named_scope("cot_gather"):
        for stage in range(1, stages):
            cot_lists = gather_stage(cot_lists, "fsdp", stage)
    attended, logs = attend(lowest, first_block[None], start_column, query, key, value)
    resid = lax.dynamic_slice_in_dim(rows_initial, sp_index * token_rows, token_rows)
    branch = jnp.dot(attended, output_full, preferred_element_type=jnp.float32)
    middle = resid.astype(jnp.float32) + branch
    inv_two = lax.rsqrt(jnp.mean(middle * middle, axis=1, keepdims=True) + NORM_EPS)
    normed_two = middle * inv_two
    act_two = (normed_two * gain_mixer).astype(low)
    logits = jnp.dot(act_two, router_full, preferred_element_type=jnp.float32)
    gate_dense = jax.nn.softmax(jnp.where(member, logits, -jnp.inf), axis=-1)
    gates_here = to_experts(gate_dense.T)
    with jax.named_scope("act_gather"):
        act_lists = gather_begin(act_two)
        for stage in range(stages):
            act_lists = gather_stage(act_lists, "fsdp", stage)
    act_pieces, cot_pieces = gather_end(act_lists), gather_end(cot_lists)
    mixed_rows, back_rows, gate_grads, expert_sums = [], [], [], []
    for members, weights in zip(groups, expert_weights):
        turn = after([own], *mixed_rows[-1:])[0]
        mixed, back, gate_grad, weight_grad = run_experts(
            turn, members[0], slots_here, gates_here, weights, act_pieces, cot_pieces
        )
        mixed_rows.append(mixed)
        back_rows.append(back)
        gate_grads.append(gate_grad)
        with jax.named_scope("grads_queue"):
            expert_sums.append(
                lax.psum_scatter(weight_grad, "sp", scatter_dimension=0, tiled=False)
            )
    gate_grads = jnp.swapaxes(jnp.concatenate(gate_grads, axis=0), 0, 1)
    gate_grad_back = exchange_blocks(jnp.take(gate_grads, relative, axis=0), "fsdp")
    with jax.named_scope("back_reduce"):
        leave = combine_rows(own, slots_by_row, back_rows, 1)
        leave = after(leave, gate_grad_back)
        stay = combine_rows(own, slots_by_row, back_rows, 0)
        for stage in range(stages):
            leave, stay = reduce_stage(leave, stay, "fsdp", stage)
    grad_act_moe = jnp.concatenate(stay, axis=1)
    upstream = cotangent.astype(jnp.float32)
    gate_grad = gate_grad_back.reshape(EXPERTS, token_rows).T
    weighted = jnp.sum(gate_dense * gate_grad, axis=1, keepdims=True)
    logit_grad = (gate_dense * (gate_grad - weighted)).astype(low)
    grad_act_two = grad_act_moe + jnp.dot(
        logit_grad, router_full.T, preferred_element_type=jnp.float32
    )
    scaled_two = grad_act_two * gain_mixer
    grad_middle = upstream + inv_two * (
        scaled_two - normed_two * jnp.mean(scaled_two * normed_two, axis=1, keepdims=True)
    )
    middle_low = grad_middle.astype(low)
    grad_attn = contract(middle_low, output_full, 1, 1).astype(low)
    middle_after, *_ = after([middle_low], grad_attn)
    grad_output_w = contract(attended, middle_after, 0, 0).astype(low)
    logit_grad_after, grad_act_after = after([logit_grad, grad_act_two], grad_attn)
    grad_router_w = jnp.einsum(
        "td,te->de", act_two, logit_grad_after, preferred_element_type=jnp.float32
    )
    grad_gain_two = jnp.sum(grad_act_after * normed_two, axis=0)
    early_grads = jnp.concatenate(
        [
            grad_output_w,
            grad_router_w.astype(low),
            grad_gain_two.astype(low)[:, None],
            jnp.zeros((MODEL_WIDTH, 128 - EXPERTS - 1), low),
        ],
        axis=1,
    ).reshape(fsdp_count, shard_rows, MODEL_WIDTH + 128)
    with jax.named_scope("early_fsdp"):
        early_parts = exchange_blocks(early_grads, "fsdp")
    grad_held = after([grad_attn], expert_sums[0], early_grads)[0]
    grad_query, grad_key, grad_value = attend_back(
        lowest, first_block[None], start_column, logs, query, attended, grad_held, key, value
    )
    key_rows, query_rows, *late_parts = weight_back(
        bounds, gain_attend, cosine, sine, grad_query, grad_key, grad_value, rows_initial, fsdp_count
    )
    token_grads = token_back(
        bounds,
        order_row[:, None],
        gain_attend,
        packed_all,
        after([query_rows], *expert_sums[1:-1])[0],
        key_rows,
        rows_initial,
        middle_low,
    )
    with jax.named_scope("tokens_back"):
        tokens_grad = lax.psum_scatter(token_grads, "sp", scatter_dimension=0, tiled=True)
    with jax.named_scope("early_fsdp"):
        early_parts = after([early_parts], token_grads)[0]
        early_sum = jnp.sum(early_parts.astype(jnp.float32), axis=0).astype(low)
    with jax.named_scope("late_fsdp"):
        late_leave, late_stay = late_parts[:2], late_parts[2:]
        mix_leave, mix_stay = None, None
        for stage in range(stages):
            gates = (token_grads,) if stage == 0 else ()
            late_leave, late_stay = reduce_stage(late_leave, late_stay, "fsdp", stage, gates)
            if stage < 2:
                mixed_held = after(mixed_rows, *late_stay)
                made = combine_rows(own, slots_by_row, mixed_held, 1 - stage)
                if stage == 0:
                    mix_leave = made
                else:
                    mix_stay = made
        late_stay = after(late_stay, *mix_leave, *mix_stay)
        row_sums = jnp.concatenate([early_sum] + [part.astype(low) for part in late_stay], axis=1)
    deep = expert_gate.shape[1]

    def unpack_down(part):
        blocks = [part[:, :, k * deep : (k + 1) * deep] for k in range(part.shape[2] // deep)]
        return jnp.concatenate(blocks, axis=1)

    expert_sums = after(expert_sums, row_sums)
    expert_grads = [
        jnp.concatenate([part[:, :deep] for part in expert_sums]).astype(jnp.float32),
        jnp.concatenate([part[:, deep : 2 * deep] for part in expert_sums]).astype(jnp.float32),
        jnp.concatenate([unpack_down(part[:, 2 * deep :]) for part in expert_sums]).astype(
            jnp.float32
        ),
    ]
    with jax.named_scope("mix_reduce"):
        for stage in range(stages):
            mix_leave, mix_stay = reduce_stage(mix_leave, mix_stay, "fsdp", stage)
            if stage == 0:
                mix_leave = after(mix_leave, *expert_grads)
    layer_out = (middle + jnp.concatenate(mix_stay, axis=1)).astype(low)
    with jax.named_scope("sums_sp"):
        row_sums = exchange_blocks(
            row_sums.reshape(sp_count, shard_rows // sp_count, row_sums.shape[1]), "sp"
        )
        row_sums = jnp.sum(row_sums.astype(jnp.float32), axis=0).astype(low)
        row_sums = exchange_blocks(
            jnp.broadcast_to(row_sums[None], (sp_count,) + row_sums.shape), "sp"
        )
    row_sums = row_sums.reshape(shard_rows, -1).astype(jnp.float32)
    early_sum = row_sums[:, : MODEL_WIDTH + 128]
    late_all = row_sums[:, MODEL_WIDTH + 128 :]
    return (
        layer_out,
        tokens_grad,
        late_all[:, :query_columns],
        late_all[:, query_columns : query_columns + key_columns],
        late_all[:, query_columns + key_columns : qkv_columns],
        early_sum[:, :MODEL_WIDTH],
        early_sum[:, MODEL_WIDTH : MODEL_WIDTH + EXPERTS],
        jnp.sum(late_all * packed[:, :qkv_columns].astype(jnp.float32), axis=1)
        / first_gain.astype(low).astype(jnp.float32),
        early_sum[:, MODEL_WIDTH + EXPERTS],
        *expert_grads,
    )


def solution(mesh):
    return jax.shard_map(
        body,
        mesh=mesh,
        in_specs=(
            P(("fsdp", "sp"), None),
            P("fsdp", None),
            P("fsdp", None),
            P("fsdp", None),
            P("fsdp", None),
            P("fsdp", None),
            P("fsdp"),
            P("fsdp"),
            P("fsdp", "sp", None),
            P("fsdp", "sp", None),
            P("fsdp", None, "sp"),
            P(("fsdp", "sp"), None),
            P("fsdp", None),
            P("fsdp", None),
            P(("fsdp", "sp"), None),
        ),
        out_specs=(
            P(("fsdp", "sp"), None),
            P(("fsdp", "sp"), None),
            P("fsdp", None),
            P("fsdp", None),
            P("fsdp", None),
            P("fsdp", None),
            P("fsdp", None),
            P("fsdp"),
            P("fsdp"),
            P("fsdp", "sp", None),
            P("fsdp", "sp", None),
            P("fsdp", None, "sp"),
        ),
        check_vma=False,
    )
```

time: 750 us -> 702 us (0.936)
  local copies, waits for them, and re-layouts: 55.5 us -> 36 us
  Pallas kernels: 246 us -> 230 us
  other arithmetic: 82.3 us -> 68.4 us
    ppermute x6 -> x0, waiting for transfers between devices: 52.9 us -> none  [reduce_ring_step(): arrived = lax.ppermute(one, axis_name, shift_pairs(count, -turn))]
    all_gather x4 -> x2, waiting for transfers between devices: 28.5 us -> 70.2 us  [body(): lax.all_gather(part, 'sp', axis=0, tiled=False)]
    pallas_call x1, Pallas kernels: 28.5 us -> 18.6 us  [attend(): pl.pallas_call(attend_step, grid_spec=pltpu.PrefetchScalarGridSpec(num_sc...]
    slice x11 -> x6, local copies, waits for them, and re-layouts: 11.7 us -> 3.51 us  [the longest x2 1.46 us: body(): part[:, deep:2 * deep]]
    pallas_call x1, Pallas kernels: 28.4 us -> 20.2 us  [attend_back(): pl.pallas_call(attend_back_step, grid_spec=pltpu.PrefetchScalarGridSpec(n...]
    ppermute x6 -> x0, starting transfers between devices: 7.88 us -> none  [reduce_ring_step(): arrived = lax.ppermute(one, axis_name, shift_pairs(count, -turn))]
    ppermute x40 -> x46, starting transfers between devices: 26.5 us -> 33.6 us  [flip(): lax.ppermute(values, axis_name, [(place, place ^ bit) for place in range(...]
    pallas_call x10 -> x9, Pallas kernels: 189 us -> 191 us  [the longest x2 95.8 us: run_experts(): pl.pallas_call(functools.partial(expert_step, count=count, first=first),...]
  transfers between devices with their start and end apart: 71 -> 64, of which waited for: 26 -> 24; matrix products, arithmetic and copies ran while one was open for 18% -> 16% of each run, Pallas kernels for 33% -> 33%
where the time goes in v4:
time: 702 us; the launch traced here: 693 us
  waiting for transfers between devices  239 us (34%)
  Pallas kernels  230 us (33%)
  starting transfers between devices  86.8 us (12%)
  other arithmetic  68.4 us (10%)
  local copies, waits for them, and re-layouts  36 us (5%)
  between operations  16.9 us (2%)
  matrix products  15.8 us (2%)
    pallas_call x2, Pallas kernels, run_experts(): pl.pallas_call(functools.partial(expert_step, count=count, first=first),...  95.8 us
    ppermute x46, waiting for transfers between devices, flip(): lax.ppermute(values, axis_name, [(place, place ^ bit) for place in range(...  80.8 us
    all_gather x2, waiting for transfers between devices, body(): lax.all_gather(part, 'sp', axis=0, tiled=False)  70.2 us
    ppermute x6, waiting for transfers between devices, ring_step(): lax.ppermute(one, axis_name, shift_pairs(count, by))  44.3 us
    all_to_all x6, waiting for transfers between devices, exchange_blocks(): lax.all_to_all(values, axis_name, split_axis=0, concat_axis=0, tiled=True)  43.3 us
    all_to_all x6, starting transfers between devices, exchange_blocks(): lax.all_to_all(values, axis_name, split_axis=0, concat_axis=0, tiled=True)  41.8 us
    pallas_call x4, Pallas kernels, combine_rows(): pl.pallas_call(combine_step, grid_spec=pltpu.PrefetchScalarGridSpec(num_s...  36.4 us
    ppermute x46, starting transfers between devices, flip(): lax.ppermute(values, axis_name, [(place, place ^ bit) for place in range(...  33.6 us
  transfers between devices with their start and end apart: 64, of which 24 were waited for; matrix products, arithmetic and copies ran while one was open for 16% of the time, Pallas kernels for 33%

profile of v4, /device:TPU:0, one launch (start us, length us, event | category | flops | bytes accessed | tf_op | source)
XLA Modules:
  0.0 693.2 jit_solution(8804619675143123273)
XLA Ops:
  14.0 5.2 all-to-all-start
  38.3 10.3 %collective-permute-done.2.refs_5_ = bf16[512,512]{1,0:T(8,128)(2,1)} collective-permute-done((bf16[512,512]{1,0:T(8,128)(2,1)}, bf16[512,512]{1,0:T(8,128)(2,1)}, u32[]{:S(2)}, u32[]{:S(2)}) %collective-permute-start.2) | collective-permute-done | bytes 524320 | tf_op jit(solution)/shard_map/tokens_ring/ppermute | solution.py:363
  63.8 7.8 %collective-permute-done.3.refs_6_ = bf16[512,512]{1,0:T(8,128)(2,1)} collective-permute-done((bf16[512,512]{1,0:T(8,128)(2,1)}, bf16[512,512]{1,0:T(8,128)(2,1)}, u32[]{:S(2)}, u32[]{:S(2)}) %collective-permute-start.3) | collective-permute-done | bytes 524320 | tf_op jit(solution)/shard_map/tokens_ring/ppermute | solution.py:363
  75.6 13.1 %collective-permute-done.4.refs_1_ = bf16[512,512]{1,0:T(8,128)(2,1)} collective-permute-done((bf16[512,512]{1,0:T(8,128)(2,1)}, bf16[512,512]{1,0:T(8,128)(2,1)}, u32[]{:S(2)}, u32[]{:S(2)}) %collective-permute-start.4) | collective-permute-done | bytes 524320 | tf_op jit(solution)/shard_map/tokens_ring/ppermute | solution.py:363
  88.8 8.7 %collective-permute-done.5.refs_7_ = bf16[512,512]{1,0:T(8,128)(2,1)} collective-permute-done((bf16[512,512]{1,0:T(8,128)(2,1)}, bf16[512,512]{1,0:T(8,128)(2,1)}, u32[]{:S(2)}, u32[]{:S(2)}) %collective-permute-start.5) | collective-permute-done | bytes 524320 | tf_op jit(solution)/shard_map/tokens_ring/ppermute | solution.py:363
  106.8 15.7 %project.1 = (bf16[2048,1024]{1,0:T(8,128)(2,1)}, bf16[512,1024]{1,0:T(8,128)(2,1)}, bf16[2048,512]{1,0:T(8,128)(2,1)}, bf16[2048,512]{1,0:T(8,128)(2,1)}) custom-call(s32[3]{0:T(128)} %pad_add_fusion.bounds_ref, s32[1,2048]{1,0:T(1,128)} %bitcast.143, f32[1,1024]{1,0:T(1,128)} %bitcast.138, bf16[1024,3200]{1,0:T(8,128)(2,1)} %all-gather.6.cloned.1.call-done.weight_ref, ...), custom_call_target="tpu_custom_call" | custom-call | tf_op jit(solution)/shard_map/project/pallas_call | solution.py:459
  122.5 18.6 %attend.1 = (bf16[512,1024]{1,0:T(8,128)(2,1)}, f32[4,512,4]{2,1,0:T(8,128)}) custom-call(s32[2]{0:T(128)} %copy-done.67, s32[1]{0:T(128)} %bitcast.2.first_ref, s32[512,1]{1,0:T(8,128)} %copy.88.start_ref, bf16[512,1024]{1,0:T(8,128)(2,1)} %get-tuple-element.71.query_ref, bf16[2048,512]{1,0:T(8,128)(2,1)} %get-tuple-element.72.key_ref, ...), custom_call_target="tpu_custom_call" | custom-call | tf_op jit(solution)/shard_map/attend/pallas_call | solution.py:579
  149.2 6.6 collective-permute-done.25.refs_22_
  162.3 10.6 %collective-permute-done.9.refs_4_ = bf16[512,512]{1,0:T(8,128)(2,1)S(1)} collective-permute-done((bf16[512,512]{1,0:T(8,128)(2,1)S(1)}, bf16[512,512]{1,0:T(8,128)(2,1)S(1)}, u32[]{:S(2)}, u32[]{:S(2)}) %collective-permute-start.9) | collective-permute-done | bytes 524320 | tf_op jit(solution)/shard_map/act_gather/ppermute | solution.py:39
  175.1 8.5 %collective-permute-done.16.refs_12_ = bf16[512,512]{1,0:T(8,128)(2,1)} collective-permute-done((bf16[512,512]{1,0:T(8,128)(2,1)S(1)}, bf16[512,512]{1,0:T(8,128)(2,1)}, u32[]{:S(2)}, u32[]{:S(2)}) %collective-permute-start.16) | collective-permute-done | bytes 524320 | tf_op jit(solution)/shard_map/act_gather/ppermute | solution.py:39
  186.5 9.6 %collective-permute-done.11.refs_6_ = bf16[512,512]{1,0:T(8,128)(2,1)} collective-permute-done((bf16[512,512]{1,0:T(8,128)(2,1)S(1)}, bf16[512,512]{1,0:T(8,128)(2,1)}, u32[]{:S(2)}, u32[]{:S(2)}) %collective-permute-start.11) | collective-permute-done | bytes 524320 | tf_op jit(solution)/shard_map/act_gather/ppermute | solution.py:39
  204.8 4.6 all-to-all-done.1.share_ref
  212.9 47.9 %experts.2 = (bf16[2,8,192,1024]{3,2,1,0:T(8,128)(2,1)}, bf16[2,8,192,1024]{3,2,1,0:T(8,128)(2,1)}, f32[2,8,1,512]{3,2,1,0:T(1,128)}, bf16[4,2,768,512]{3,2,1,0:T(8,128)(2,1)}) custom-call(s32[1]{0:T(128)} %bitcast.3.own_ref, s32[8,4,512]{2,1,0:T(4,128)} %copy-done.39, f32[8,4,512]{2,1,0:T(4,128)} %copy-done.43, bf16[4,2,768,512]{3,2,1,0:T(8,128)(2,1)} %bitcast.128, ...), custom_call_target="tpu_custom_call" | custom-call | tf_op jit(solution)/shard_map/experts/pallas_call | solution.py:264
  261.4 66.7 %all-gather.10.cloned.1.call-done = bf16[8,768,512]{2,1,0:T(8,128)(2,1)} async-done(((bf16[2,768,512]{2,1,0:T(8,128)(2,1)}), bf16[8,768,512]{2,1,0:T(8,128)(2,1)}) %all-gather.10.cloned.1.call-update) | async-done | bytes 6291472 | tf_op jit(solution)/shard_map/weights_queue/all_gather | solution.py:996
  328.1 47.9 %experts.3 = (bf16[2,8,192,1024]{3,2,1,0:T(8,128)(2,1)}, bf16[2,8,192,1024]{3,2,1,0:T(8,128)(2,1)}, f32[2,8,1,512]{3,2,1,0:T(1,128)}, bf16[4,2,768,512]{3,2,1,0:T(8,128)(2,1)}) custom-call(s32[1]{0:T(128)} %bitcast.3.own_ref, s32[8,4,512]{2,1,0:T(4,128)} %copy-done.39, f32[8,4,512]{2,1,0:T(4,128)} %copy-done.43, bf16[4,2,768,512]{3,2,1,0:T(8,128)(2,1)} %bitcast.127, ...), custom_call_target="tpu_custom_call" | custom-call | tf_op jit(solution)/shard_map/experts/pallas_call | solution.py:264
  384.7 9.1 %combine.5 = (bf16[4,512,512]{2,1,0:T(8,128)(2,1)}, bf16[4,512,512]{2,1,0:T(8,128)(2,1)}) custom-call(s32[1]{0:T(128)} %bitcast.3.own_ref, s32[8,512,4]{2,1,0:T(8,128)} %bitcast.119, bf16[2,8,192,1024]{3,2,1,0:T(8,128)(2,1)} %get-tuple-element.82.refs_0_, bf16[2,8,192,1024]{3,2,1,0:T(8,128)(2,1)} %get-tuple-element.83.refs_1_), custom_call_target="tpu_custom_call" | custom-call | tf_op jit(solution)/shard_map/back_reduce/combine/pallas_call | solution.py:328
  394.5 9.1 %combine.4 = (bf16[4,512,512]{2,1,0:T(8,128)(2,1)}, bf16[4,512,512]{2,1,0:T(8,128)(2,1)}) custom-call(s32[1]{0:T(128)} %bitcast.3.own_ref, s32[8,512,4]{2,1,0:T(8,128)} %bitcast.120, bf16[2,8,192,1024]{3,2,1,0:T(8,128)(2,1)} %get-tuple-element.82.refs_0_, bf16[2,8,192,1024]{3,2,1,0:T(8,128)(2,1)} %get-tuple-element.83.refs_1_), custom_call_target="tpu_custom_call" | custom-call | tf_op jit(solution)/shard_map/back_reduce/combine/pallas_call | solution.py:328
  403.6 4.3 add_convert_fusion.8
  415.7 18.1 %collective-permute-done.35 = bf16[2,512,512]{2,1,0:T(8,128)(2,1)} collective-permute-done((bf16[2,512,512]{2,1,0:T(8,128)(2,1)}, bf16[2,512,512]{2,1,0:T(8,128)(2,1)}, u32[]{:S(2)}, u32[]{:S(2)}) %collective-permute-start.35) | collective-permute-done | bytes 1048608 | tf_op jit(solution)/shard_map/back_reduce/ppermute | solution.py:39
  441.3 8.4 %collective-permute-done.36 = bf16[1,512,512]{2,1,0:T(8,128)(2,1)S(1)} collective-permute-done((bf16[1,512,512]{2,1,0:T(8,128)(2,1)S(1)}, bf16[1,512,512]{2,1,0:T(8,128)(2,1)S(1)}, u32[]{:S(2)}, u32[]{:S(2)}) %collective-permute-start.36) | collective-permute-done | bytes 524320 | tf_op jit(solution)/shard_map/back_reduce/ppermute | solution.py:39
  456.7 4.4 fusion.7.cot_ref
  467.0 5.1 concatenate.86
  472.0 20.2 %attend_back.1 = (f32[512,1024]{1,0:T(8,128)}, f32[2048,512]{1,0:T(8,128)}, f32[2048,512]{1,0:T(8,128)}) custom-call(s32[2]{0:T(128)} %copy-done.67, s32[1]{0:T(128)} %bitcast.2.first_ref, s32[512,1]{1,0:T(8,128)} %copy.88.start_ref, f32[4,512,4]{2,1,0:T(8,128)} %get-tuple-element.81.log_ref, bf16[512,1024]{1,0:T(8,128)(2,1)} %get-tuple-element.71.query_ref, ...), custom_call_target="tpu_custom_call" | custom-call | tf_op jit(solution)/shard_map/attend_back/pallas_call | solution.py:655
  492.2 19.7 %weight_back.1 = (bf16[2048,1024]{1,0:T(8,128)(2,1)}, bf16[512,1024]{1,0:T(8,128)(2,1)}, bf16[4,128,1024]{2,1,0:T(8,128)(2,1)}, bf16[4,128,1024]{2,1,0:T(8,128)(...) custom-call(s32[3]{0:T(128)} %pad_add_fusion.bounds_ref, f32[1,1024]{1,0:T(1,128)} %bitcast.139, ...), custom_call_target="tpu_custom_call" | custom-call | tf_op jit(solution)/shard_map/weight_back/pallas_call | solution.py:765
  512.4 4.4 all-to-all-start.3
  518.2 23.8 %token_back.1 = bf16[2048,1024]{1,0:T(8,128)(2,1)} custom-call(s32[3]{0:T(128)} %pad_add_fusion.bounds_ref, s32[2048,1]{1,0:T(8,128)} %copy.94.order_ref, f32[1,1024]{1,0:T(1,128)} %bitcast.140, bf16[1024,3200]{1,0:T(8,128)(2,1)} %all-gather.6.cloned.1.call-done.weight_ref, bf16[512,1024]{1,0:T(8,128)(2,1)} %get-tuple-element.102.query_ref, ...), custom_call_target="tpu_custom_call" | custom-call | tf_op jit(solution)/shard_map/token_back/pallas_call | solution.py:854
  549.1 9.2 %collective-permute-done.43 = bf16[2,128,1024]{2,1,0:T(8,128)(2,1)S(1)} collective-permute-done((bf16[2,128,1024]{2,1,0:T(8,128)(2,1)S(1)}, bf16[2,128,1024]{2,1,0:T(8,128)(2,1)S(1)}, u32[]{:S(2)}, u32[]{:S(2)}) %collective-permute-start.43) | collective-permute-done | bytes 524320 | tf_op jit(solution)/shard_map/late_fsdp/ppermute | solution.py:39
  567.3 9.1 %combine.7 = (bf16[4,512,512]{2,1,0:T(8,128)(2,1)}, bf16[4,512,512]{2,1,0:T(8,128)(2,1)}) custom-call(s32[1]{0:T(128)} %bitcast.3.own_ref, s32[8,512,4]{2,1,0:T(8,128)} %bitcast.121, bf16[2,8,192,1024]{3,2,1,0:T(8,128)(2,1)} %get-tuple-element.108.refs_0_, bf16[2,8,192,1024]{3,2,1,0:T(8,128)(2,1)} %get-tuple-element.109.refs_1_), custom_call_target="tpu_custom_call" | custom-call | tf_op jit(solution)/shard_map/late_fsdp/combine/pallas_call | solution.py:328
  579.3 9.1 %combine.6 = (bf16[4,512,512]{2,1,0:T(8,128)(2,1)}, bf16[4,512,512]{2,1,0:T(8,128)(2,1)}) custom-call(s32[1]{0:T(128)} %bitcast.3.own_ref, s32[8,512,4]{2,1,0:T(8,128)} %bitcast.122, bf16[2,8,192,1024]{3,2,1,0:T(8,128)(2,1)} %get-tuple-element.108.refs_0_, bf16[2,8,192,1024]{3,2,1,0:T(8,128)(2,1)} %get-tuple-element.109.refs_1_), custom_call_target="tpu_custom_call" | custom-call | tf_op jit(solution)/shard_map/late_fsdp/combine/pallas_call | solution.py:328
  589.4 21.5 %all-to-all-start.4 = ((bf16[4,32,3200]{2,1,0:T(8,128)(2,1)}), bf16[4,32,3200]{2,1,0:T(8,128)(2,1)S(1)}, u32[]{:S(2)}, u32[]{:S(2)}) async-start(bf16[4,32,3200]{2,1,0:T(8,128)(2,1)} %bitcast.50), calls=%async_computation.7 | async-start | bytes 1638400 | tf_op jit(solution)/shard_map/sums_sp/all_to_all | solution.py:109
  628.0 24.7 %all-to-all-done.4 = bf16[4,32,3200]{2,1,0:T(8,128)(2,1)S(1)} async-done(((bf16[4,32,3200]{2,1,0:T(8,128)(2,1)}), bf16[4,32,3200]{2,1,0:T(8,128)(2,1)S(1)}, u32[]{:S(2)}, u32[]{:S(2)}) %all-to-all-start.4) | async-done | bytes 819232 | tf_op jit(solution)/shard_map/sums_sp/all_to_all | solution.py:109
  663.7 13.9 %all-to-all-done.5 = bf16[4,32,3200]{2,1,0:T(8,128)(2,1)S(1)} async-done(((bf16[4,32,3200]{2,1,0:T(8,128)(2,1)}), bf16[4,32,3200]{2,1,0:T(8,128)(2,1)S(1)}, u32[]{:S(2)}, u32[]{:S(2)}) %all-to-all-start.5) | async-done | bytes 819232 | tf_op jit(solution)/shard_map/sums_sp/all_to_all | solution.py:109
  (370 shorter events, 180.4 us)
Async XLA Ops:
  7.2 90.3 %all-gather.6.cloned.1.call-start = ((), (), s32[]{:S(2)}) async-start(), calls=%async_computation.9 | async-start | bytes 7372800 | tf_op jit(solution)/shard_map/all_gather | solution.py:922
  14.0 44.0 %all-to-all-start = ((s32[8,4,512]{2,1,0:T(4,128)}), s32[8,4,512]{2,1,0:T(4,128)S(1)}, u32[]{:S(2)}, u32[]{:S(2)}) async-start(s32[8,4,512]{2,1,0:T(4,128)} %reshape.202), calls=%async_computation | async-start | bytes 131072 | tf_op jit(solution)/shard_map/all_to_all | solution.py:109
  19.2 193.8 %all-gather.8.cloned.1.call-start = ((), (), s32[]{:S(2)}) async-start(), calls=%async_computation.13 | async-start | bytes 7864320 | tf_op jit(solution)/shard_map/weights_queue/all_gather | solution.py:996
  23.0 25.6 %collective-permute-start.2 = (bf16[512,512]{1,0:T(8,128)(2,1)}, bf16[512,512]{1,0:T(8,128)(2,1)}, u32[]{:S(2)}, u32[]{:S(2)}) collective-permute-start(bf16[512,512]{1,0:T(8,128)(2,1)} %get-tuple-element.230.refs_4_), channel_id=1, source_target_pairs={{0,3},{1,0},{2,1},{3,2},{4,7},{5,4},{6,5},{7,6},{8,11},{9,8},{10,9... | collective-permute-start | bytes 1572872 | tf_op jit(solution)/shard_map/tokens_ring/ppermute | solution.py:363
  38.3 25.5 %collective-permute-start.1 = (bf16[512,512]{1,0:T(8,128)(2,1)}, bf16[512,512]{1,0:T(8,128)(2,1)}, u32[]{:S(2)}, u32[]{:S(2)}) collective-permute-start(bf16[512,512]{1,0:T(8,128)(2,1)} %collective-permute-done.refs_3_), channel_id=1, source_target_pairs={{0,1},{1,2},{2,3},{3,0},{4,5},{5,6},{6,7},{7,4},{8,9},{9,10},{10,1... | collective-permute-start | bytes 1572872 | tf_op jit(solution)/shard_map/tokens_ring/ppermute | solution.py:363
  48.6 23.1 %collective-permute-start.3 = (bf16[512,512]{1,0:T(8,128)(2,1)}, bf16[512,512]{1,0:T(8,128)(2,1)}, u32[]{:S(2)}, u32[]{:S(2)}) collective-permute-start(bf16[512,512]{1,0:T(8,128)(2,1)} %collective-permute-done.2.refs_5_), channel_id=1, source_target_pairs={{0,3},{1,0},{2,1},{3,2},{4,7},{5,4},{6,5},{7,6},{8,11},{9,8},{10,9... | collective-permute-start | bytes 1572872 | tf_op jit(solution)/shard_map/tokens_ring/ppermute | solution.py:363
  72.4 25.1 %collective-permute-start.5 = (bf16[512,512]{1,0:T(8,128)(2,1)}, bf16[512,512]{1,0:T(8,128)(2,1)}, u32[]{:S(2)}, u32[]{:S(2)}) collective-permute-start(bf16[512,512]{1,0:T(8,128)(2,1)} %collective-permute-done.3.refs_6_), channel_id=1, source_target_pairs={{0,3},{1,0},{2,1},{3,2},{4,7},{5,4},{6,5},{7,6},{8,11},{9,8},{10,9... | collective-permute-start | bytes 1572872 | tf_op jit(solution)/shard_map/tokens_ring/ppermute | solution.py:363
  97.5 230.6 %all-gather.10.cloned.1.call-start = ((), (), s32[]{:S(2)}) async-start(), calls=%async_computation.14 | async-start | bytes 7864320 | tf_op jit(solution)/shard_map/weights_queue/all_gather | solution.py:996
  98.4 42.7 %collective-permute-start.23 = (bf16[512,512]{1,0:T(8,128)(2,1)S(1)}, bf16[512,512]{1,0:T(8,128)(2,1)}, u32[]{:S(2)}, u32[]{:S(2)}) collective-permute-start(bf16[512,512]{1,0:T(8,128)(2,1)S(1)} %get-tuple-element.211.refs_16_), channel_id=1, source_target_pairs={{0,16},{4,20},{8,24},{12,28},{16,0},{20,4},{24,8},{28,12},{1,17},{... | collective-permute-start | bytes 1572872 | tf_op jit(solution)/shard_map/cot_gather/ppermute | solution.py:39
  100.1 41.5 %collective-permute-start.28 = (bf16[512,512]{1,0:T(8,128)(2,1)S(1)}, bf16[512,512]{1,0:T(8,128)(2,1)}, u32[]{:S(2)}, u32[]{:S(2)}) collective-permute-start(bf16[512,512]{1,0:T(8,128)(2,1)S(1)} %get-tuple-element.210.refs_24_), channel_id=1, source_target_pairs={{0,8},{4,12},{8,0},{12,4},{16,24},{20,28},{24,16},{28,20},{1,9},{5... | collective-permute-start | bytes 1572872 | tf_op jit(solution)/shard_map/cot_gather/ppermute | solution.py:39
  101.6 41.7 %collective-permute-start.21 = (bf16[512,512]{1,0:T(8,128)(2,1)S(1)}, bf16[512,512]{1,0:T(8,128)(2,1)S(1)}, u32[]{:S(2)}, u32[]{:S(2)}) collective-permute-start(bf16[512,512]{1,0:T(8,128)(2,1)S(1)} %get-tuple-element.211.refs_16_), channel_id=1, source_target_pairs={{0,8},{4,12},{8,0},{12,4},{16,24},{20,28},{24,16},{28,20},{1,9},{5... | collective-permute-start | bytes 1572872 | tf_op jit(solution)/shard_map/cot_gather/ppermute | solution.py:39
  104.3 44.1 %collective-permute-start.30 = (bf16[512,512]{1,0:T(8,128)(2,1)S(1)}, bf16[512,512]{1,0:T(8,128)(2,1)S(1)}, u32[]{:S(2)}, u32[]{:S(2)}) collective-permute-start(bf16[512,512]{1,0:T(8,128)(2,1)S(1)} %get-tuple-element.210.refs_24_), channel_id=1, source_target_pairs={{0,16},{4,20},{8,24},{12,28},{16,0},{20,4},{24,8},{28,12},{1,17},{... | collective-permute-start | bytes 1572872 | tf_op jit(solution)/shard_map/cot_gather/ppermute | solution.py:39
  104.7 43.9 %collective-permute-start.20 = (bf16[512,512]{1,0:T(8,128)(2,1)S(1)}, bf16[512,512]{1,0:T(8,128)(2,1)}, u32[]{:S(2)}, u32[]{:S(2)}) collective-permute-start(bf16[512,512]{1,0:T(8,128)(2,1)S(1)} %get-tuple-element.211.refs_16_), channel_id=1, source_target_pairs={{0,4},{4,0},{8,12},{12,8},{16,20},{20,16},{24,28},{28,24},{1,5},{5... | collective-permute-start | bytes 1572872 | tf_op jit(solution)/shard_map/cot_gather/ppermute | solution.py:39
  160.2 23.4 %collective-permute-start.16 = (bf16[512,512]{1,0:T(8,128)(2,1)S(1)}, bf16[512,512]{1,0:T(8,128)(2,1)}, u32[]{:S(2)}, u32[]{:S(2)}) collective-permute-start(bf16[512,512]{1,0:T(8,128)(2,1)S(1)} %get-tuple-element.212.refs_8_), channel_id=1, source_target_pairs={{0,16},{4,20},{8,24},{12,28},{16,0},{20,4},{24,8},{28,12},{1,17},{... | collective-permute-start | bytes 1572872 | tf_op jit(solution)/shard_map/act_gather/ppermute | solution.py:39
  160.8 25.0 %collective-permute-start.7 = (bf16[512,512]{1,0:T(8,128)(2,1)S(1)}, bf16[512,512]{1,0:T(8,128)(2,1)}, u32[]{:S(2)}, u32[]{:S(2)}) collective-permute-start(bf16[512,512]{1,0:T(8,128)(2,1)S(1)} %get-tuple-element.213.refs_0_), channel_id=1, source_target_pairs={{0,8},{4,12},{8,0},{12,4},{16,24},{20,28},{24,16},{28,20},{1,9},{5... | collective-permute-start | bytes 1572872 | tf_op jit(solution)/shard_map/act_gather/ppermute | solution.py:39
  162.3 23.5 %collective-permute-start.13 = (bf16[512,512]{1,0:T(8,128)(2,1)S(1)}, bf16[512,512]{1,0:T(8,128)(2,1)S(1)}, u32[]{:S(2)}, u32[]{:S(2)}) collective-permute-start(bf16[512,512]{1,0:T(8,128)(2,1)S(1)} %get-tuple-element.212.refs_8_), channel_id=1, source_target_pairs={{0,4},{4,0},{8,12},{12,8},{16,20},{20,16},{24,28},{28,24},{1,5},{5... | collective-permute-start | bytes 1572872 | tf_op jit(solution)/shard_map/act_gather/ppermute | solution.py:39
  185.8 23.6 %collective-permute-start.15 = (bf16[512,512]{1,0:T(8,128)(2,1)}, bf16[512,512]{1,0:T(8,128)(2,1)}, u32[]{:S(2)}, u32[]{:S(2)}) collective-permute-start(bf16[512,512]{1,0:T(8,128)(2,1)} %collective-permute-done.14.refs_10_), channel_id=1, source_target_pairs={{0,4},{4,0},{8,12},{12,8},{16,20},{20,16},{24,28},{28,24},{1,5},{5... | collective-permute-start | bytes 1572872 | tf_op jit(solution)/shard_map/act_gather/ppermute | solution.py:39
  186.4 23.1 %collective-permute-start.17 = (bf16[512,512]{1,0:T(8,128)(2,1)}, bf16[512,512]{1,0:T(8,128)(2,1)}, u32[]{:S(2)}, u32[]{:S(2)}) collective-permute-start(bf16[512,512]{1,0:T(8,128)(2,1)} %collective-permute-done.16.refs_12_), channel_id=1, source_target_pairs={{0,4},{4,0},{8,12},{12,8},{16,20},{20,16},{24,28},{28,24},{1,5},{5... | collective-permute-start | bytes 1572872 | tf_op jit(solution)/shard_map/act_gather/ppermute | solution.py:39
  204.5 267.5 %reduce-scatter.4.cloned.1.call-start = ((), (), s32[]{:S(2)}) async-start(), calls=%async_computation.10 | async-start | bytes 7864320 | tf_op jit(solution)/shard_map/grads_queue/reduce_scatter | solution.py:1030
  260.9 328.5 %reduce-scatter.6.cloned.1.call-start = ((), (), s32[]{:S(2)}) async-start(), calls=%async_computation.11 | async-start | bytes 7864320 | tf_op jit(solution)/shard_map/grads_queue/reduce_scatter | solution.py:1030
  407.9 25.8 %collective-permute-start.35 = (bf16[2,512,512]{2,1,0:T(8,128)(2,1)}, bf16[2,512,512]{2,1,0:T(8,128)(2,1)}, u32[]{:S(2)}, u32[]{:S(2)}) collective-permute-start(bf16[2,512,512]{2,1,0:T(8,128)(2,1)} %get-tuple-element.195), channel_id=1, source_target_pairs={{0,8},{4,12},{8,0},{12,4},{16,24},{20,28},{24,16},{28,20},{1,9},{5... | collective-permute-start | bytes 3145736 | tf_op jit(solution)/shard_map/back_reduce/ppermute | solution.py:39
  413.3 26.4 %collective-permute-start.38 = (bf16[2,512,512]{2,1,0:T(8,128)(2,1)}, bf16[2,512,512]{2,1,0:T(8,128)(2,1)}, u32[]{:S(2)}, u32[]{:S(2)}) collective-permute-start(bf16[2,512,512]{2,1,0:T(8,128)(2,1)} %get-tuple-element.197), channel_id=1, source_target_pairs={{0,16},{4,20},{8,24},{12,28},{16,0},{20,4},{24,8},{28,12},{1,17},{... | collective-permute-start | bytes 3145736 | tf_op jit(solution)/shard_map/back_reduce/ppermute | solution.py:39
  511.9 30.1 %collective-permute-start.42 = (bf16[4,128,1024]{2,1,0:T(8,128)(2,1)}, bf16[4,128,1024]{2,1,0:T(8,128)(2,1)}, u32[]{:S(2)}, u32[]{:S(2)}) collective-permute-start(bf16[4,128,1024]{2,1,0:T(8,128)(2,1)} %get-tuple-element.107), channel_id=1, source_target_pairs={{0,4},{4,0},{8,12},{12,8},{16,20},{20,16},{24,28},{28,24},{1,5},{5... | collective-permute-start | bytes 3145736 | tf_op jit(solution)/shard_map/late_fsdp/ppermute | solution.py:39
  511.9 34.0 %collective-permute-start.40 = (bf16[4,128,1024]{2,1,0:T(8,128)(2,1)}, bf16[4,128,1024]{2,1,0:T(8,128)(2,1)}, u32[]{:S(2)}, u32[]{:S(2)}) collective-permute-start(bf16[4,128,1024]{2,1,0:T(8,128)(2,1)} %get-tuple-element.105), channel_id=1, source_target_pairs={{0,4},{4,0},{8,12},{12,8},{16,20},{20,16},{24,28},{28,24},{1,5},{5... | collective-permute-start | bytes 3145736 | tf_op jit(solution)/shard_map/late_fsdp/ppermute | solution.py:39
  512.4 52.2 %all-to-all-start.3 = ((bf16[8,128,1152]{2,1,0:T(8,128)(2,1)}), bf16[8,128,1152]{2,1,0:T(8,128)(2,1)}, u32[]{:S(2)}, u32[]{:S(2)}) async-start(bf16[8,128,1152]{2,1,0:T(8,128)(2,1)} %concatenate.86), calls=%async_computation.5 | async-start | bytes 4718592 | tf_op jit(solution)/shard_map/early_fsdp/all_to_all | solution.py:109
  516.8 169.2 %reduce-scatter.8.cloned.1.call-start = ((), (), s32[]{:S(2)}) async-start(), calls=%async_computation.12 | async-start | bytes 5242880 | tf_op jit(solution)/shard_map/tokens_back/reduce_scatter | solution.py:1090
  576.4 41.8 %collective-permute-start.45 = (bf16[4,512,512]{2,1,0:T(8,128)(2,1)}, bf16[4,512,512]{2,1,0:T(8,128)(2,1)}, u32[]{:S(2)}, u32[]{:S(2)}) collective-permute-start(bf16[4,512,512]{2,1,0:T(8,128)(2,1)} %get-tuple-element.115), channel_id=1, source_target_pairs={{0,4},{4,0},{8,12},{12,8},{16,20},{20,16},{24,28},{28,24},{1,5},{5... | collective-permute-start | bytes 6291464 | tf_op jit(solution)/shard_map/mix_reduce/ppermute | solution.py:39
  576.4 46.2 %collective-permute-start.44 = (bf16[4,512,512]{2,1,0:T(8,128)(2,1)}, bf16[4,512,512]{2,1,0:T(8,128)(2,1)}, u32[]{:S(2)}, u32[]{:S(2)}) collective-permute-start(bf16[4,512,512]{2,1,0:T(8,128)(2,1)} %get-tuple-element.113), channel_id=1, source_target_pairs={{0,4},{4,0},{8,12},{12,8},{16,20},{20,16},{24,28},{28,24},{1,5},{5... | collective-permute-start | bytes 6291464 | tf_op jit(solution)/shard_map/mix_reduce/ppermute | solution.py:39
  589.4 63.4 %all-to-all-start.4 = ((bf16[4,32,3200]{2,1,0:T(8,128)(2,1)}), bf16[4,32,3200]{2,1,0:T(8,128)(2,1)S(1)}, u32[]{:S(2)}, u32[]{:S(2)}) async-start(bf16[4,32,3200]{2,1,0:T(8,128)(2,1)} %bitcast.50), calls=%async_computation.7 | async-start | bytes 1638400 | tf_op jit(solution)/shard_map/sums_sp/all_to_all | solution.py:109
  626.1 31.3 %collective-permute-start.48 = (bf16[2,512,512]{2,1,0:T(8,128)(2,1)}, bf16[2,512,512]{2,1,0:T(8,128)(2,1)}, u32[]{:S(2)}, u32[]{:S(2)}) collective-permute-start(bf16[2,512,512]{2,1,0:T(8,128)(2,1)} %get-tuple-element.122), channel_id=1, source_target_pairs={{0,8},{4,12},{8,0},{12,4},{16,24},{20,28},{24,16},{28,20},{1,9},{5... | collective-permute-start | bytes 3145736 | tf_op jit(solution)/shard_map/mix_reduce/ppermute | solution.py:39
  626.4 33.8 %collective-permute-start.50 = (bf16[2,512,512]{2,1,0:T(8,128)(2,1)}, bf16[2,512,512]{2,1,0:T(8,128)(2,1)}, u32[]{:S(2)}, u32[]{:S(2)}) collective-permute-start(bf16[2,512,512]{2,1,0:T(8,128)(2,1)} %get-tuple-element.123), channel_id=1, source_target_pairs={{0,16},{4,20},{8,24},{12,28},{16,0},{20,4},{24,8},{28,12},{1,17},{... | collective-permute-start | bytes 3145736 | tf_op jit(solution)/shard_map/mix_reduce/ppermute | solution.py:39
  653.9 23.8 %all-to-all-start.5 = ((bf16[4,32,3200]{2,1,0:T(8,128)(2,1)}), bf16[4,32,3200]{2,1,0:T(8,128)(2,1)S(1)}, u32[]{:S(2)}, u32[]{:S(2)}) async-start(bf16[4,32,3200]{2,1,0:T(8,128)(2,1)} %broadcast_in_dim.76), calls=%async_computation.8 | async-start | bytes 1638400 | tf_op jit(solution)/shard_map/sums_sp/all_to_all | solution.py:109
  (104 other events, 1288.7 us)
Sparse Core Ops, SparseCore 0:
  13.2 49.3 all-gather.5
  97.6 115.2 all-gather.7
  214.5 113.5 all-gather.9
  330.3 108.9 reduce-scatter.3
  441.4 111.2 reduce-scatter.5
  555.5 94.5 reduce-scatter.7

commit v5 on v4

--- a/solution.py
+++ b/solution.py
@@ -350,8 +350,9 @@
 
 
 def ring_begin(values):
-    half = values.shape[1] // 2
-    return [values[:, :half]], [values[:, half:]]
+    rows, half = values.shape[0] // 2, values.shape[1] // 2
+    parts = [values[:, :half], values[:, half:]]
+    return [[part[first : first + rows]] for part in parts for first in (0, rows)]
 
 
 def ring_step(lists, axis_name, gates=()):
@@ -361,7 +362,7 @@
         moving = after(moving, *gates)
     return [
         part + [lax.ppermute(one, axis_name, shift_pairs(count, by))]
-        for by, part, one in zip((1, -1), lists, moving)
+        for by, part, one in zip((1, 1, -1, -1), lists, moving)
     ]
 
 
@@ -446,10 +447,9 @@
     return pl.BlockSpec((rows, columns), lambda *_: (0, 0), pipeline_mode=pl.Buffered(1))
 
 
-def project(bounds, order_row, gain, weight, cosine, sine, pieces):
+def project(bounds, order_row, gain, weight, cosine, sine, pieces, token_rows):
     rows = order_row.shape[1]
     width = weight.shape[0]
-    token_rows = pieces[0].shape[0]
     own_blocks = token_rows // SPAN
     queries, keys = QUERY_HEADS * HEAD_SIZE, KEY_VALUE_HEADS * HEAD_SIZE
     low = jnp.bfloat16
@@ -906,12 +906,17 @@
     local_experts = EXPERTS // fsdp_count
     shard_rows = query_weight.shape[0]
     relative = fsdp_index ^ jnp.arange(fsdp_count, dtype=jnp.int32)
+    ring = ring_begin(tokens)
+    held = after(
+        [query_weight, key_projection_weight, value_projection_weight, output_weight],
+        *[part[0] for part in ring],
+    )
     packed = jnp.concatenate(
         [
-            query_weight.astype(low),
-            key_projection_weight.astype(low),
-            value_projection_weight.astype(low),
-            output_weight.astype(low),
+            held[0].astype(low),
+            held[1].astype(low),
+            held[2].astype(low),
+            held[3].astype(low),
             router_weight.astype(low),
             first_gain.astype(low)[:, None],
             second_gain.astype(low)[:, None],
@@ -959,8 +964,6 @@
     cosine = jnp.tile(jnp.cos(angles), (1, 4))
     sine = jnp.sin(angles)
     sine = jnp.concatenate([-sine, sine, -sine, sine], axis=1)
-    slots_here = to_experts(slots)
-    slots_by_row = jnp.swapaxes(slots_here, 1, 2)
     merged = max(local_experts // 2, 1)
     groups = [range(first, first + merged) for first in range(0, local_experts, merged)]
     expert_parts = [
@@ -975,28 +978,30 @@
         for members in groups
     ]
     stages = fsdp_count.bit_length() - 1
+    with jax.named_scope("tokens_ring"):
+        ring = ring_step(ring, "sp")
+    arrived_first = [part[-1] for part in ring]
+    slots_here = to_experts(after([slots], *arrived_first)[0])
+    slots_by_row = jnp.swapaxes(slots_here, 1, 2)
     ring_gates = {
         2: (cosine, sine, start_column, slots_by_row, order_here, bounds, *expert_parts),
     }
     with jax.named_scope("tokens_ring"):
-        ring = ring_begin(tokens)
-        for step in range(sp_count - 1):
+        for step in range(1, sp_count - 1):
             ring = ring_step(ring, "sp", ring_gates.get(step, ()))
-            if step == 0:
-                arrived_first = [part[-1] for part in ring]
-    left, right = ring
-    ring_end = (left[-1], right[-1])
+    ring_end = [part[-1] for part in ring]
     with jax.named_scope("cot_gather"):
         cot_lists = gather_begin(after([cotangent], *arrived_first)[0])
         cot_lists = gather_stage(cot_lists, "fsdp", 0)
-    pieces = [left[-k % sp_count] for k in range(sp_count)] + right
+    pieces = [part[-k % sp_count] for k in range(sp_count) for part in ring[:2]]
+    pieces += [part[k] for k in range(sp_count) for part in ring[2:]]
     expert_parts = after(expert_parts, *ring_end, packed_all)
     with jax.named_scope("weights_queue"):
         expert_weights = [
             lax.all_gather(part, "sp", axis=0, tiled=False) for part in expert_parts
         ]
     rows_initial, query, key, value = project(
-        bounds, order_here[None, :], gain_attend, packed_all, cosine, sine, pieces
+        bounds, order_here[None, :], gain_attend, packed_all, cosine, sine, pieces, token_rows
     )
     with jax.named_scope("cot_gather"):
         for stage in range(1, stages):

time: 702 us -> 695 us (0.990)
  waiting for transfers between devices: 239 us -> 228 us
    ppermute x6 -> x12, waiting for transfers between devices: 44.3 us -> 26.1 us  [ring_step(): lax.ppermute(one, axis_name, shift_pairs(count, by))]
    ppermute x6 -> x12, starting transfers between devices: 10.3 us -> 17.3 us  [ring_step(): lax.ppermute(one, axis_name, shift_pairs(count, by))]
  transfers between devices with their start and end apart: 64 -> 70, of which waited for: 24 -> 24; matrix products, arithmetic and copies ran while one was open for 16% -> 16% of each run, Pallas kernels for 33% -> 34%
where the time goes in v5:
time: 695 us; the launch traced here: 686 us
  Pallas kernels  231 us (33%)
  waiting for transfers between devices  228 us (33%)
  starting transfers between devices  92.1 us (13%)
  other arithmetic  65.3 us (9%)
  local copies, waits for them, and re-layouts  38 us (5%)
  between operations  17 us (2%)
  matrix products  15.7 us (2%)
    pallas_call x2, Pallas kernels, run_experts(): pl.pallas_call(functools.partial(expert_step, count=count, first=first),...  95.8 us
    ppermute x46, waiting for transfers between devices, flip(): lax.ppermute(values, axis_name, [(place, place ^ bit) for place in range(...  82.7 us
    all_gather x2, waiting for transfers between devices, body(): lax.all_gather(part, 'sp', axis=0, tiled=False)  69.7 us
    all_to_all x6, waiting for transfers between devices, exchange_blocks(): lax.all_to_all(values, axis_name, split_axis=0, concat_axis=0, tiled=True)  48.6 us
    all_to_all x6, starting transfers between devices, exchange_blocks(): lax.all_to_all(values, axis_name, split_axis=0, concat_axis=0, tiled=True)  41.3 us
    pallas_call x4, Pallas kernels, combine_rows(): pl.pallas_call(combine_step, grid_spec=pltpu.PrefetchScalarGridSpec(num_s...  36.8 us
    ppermute x46, starting transfers between devices, flip(): lax.ppermute(values, axis_name, [(place, place ^ bit) for place in range(...  32.4 us
    ppermute x12, waiting for transfers between devices, ring_step(): lax.ppermute(one, axis_name, shift_pairs(count, by))  26.1 us
  transfers between devices with their start and end apart: 70, of which 24 were waited for; matrix products, arithmetic and copies ran while one was open for 16% of the time, Pallas kernels for 34%

profile of v5, /device:TPU:0, one launch (start us, length us, event | category | flops | bytes accessed | tf_op | source)
XLA Modules:
  0.0 686.4 jit_solution(2220951614095141059)
XLA Ops:
  29.7 4.4 fusion.14
  50.1 5.2 all-to-all-done.slot_ref
  58.4 4.8 collective-permute-done.7.refs_13_
  68.2 5.2 collective-permute-done.10.refs_14_
  73.4 5.7 collective-permute-done.11.refs_15_
  79.1 6.2 collective-permute-done.8.refs_2_
  98.3 15.8 %project.1 = (bf16[2048,1024]{1,0:T(8,128)(2,1)}, bf16[512,1024]{1,0:T(8,128)(2,1)}, bf16[2048,512]{1,0:T(8,128)(2,1)}, bf16[2048,512]{1,0:T(8,128)(2,1)}) custom-call(s32[3]{0:T(128)} %pad_add_fusion.bounds_ref, s32[1,2048]{1,0:T(1,128)} %bitcast.143, f32[1,1024]{1,0:T(1,128)} %bitcast.138, bf16[1024,3200]{1,0:T(8,128)(2,1)} %all-gather.6.cloned.1.call-done.weight_ref, ...), custom_call_target="tpu_custom_call" | custom-call | tf_op jit(solution)/shard_map/project/pallas_call | solution.py:459
  114.1 18.6 %attend.1 = (bf16[512,1024]{1,0:T(8,128)(2,1)}, f32[4,512,4]{2,1,0:T(8,128)}) custom-call(s32[2]{0:T(128)} %and_select_fusion.lowest_ref, s32[1]{0:T(128)} %bitcast.2.first_ref, s32[512,1]{1,0:T(8,128)} %copy.88.start_ref, bf16[512,1024]{1,0:T(8,128)(2,1)} %get-tuple-element.85.query_ref, bf16[2048,512]{1,0:T(8,128)(2,1)} %get-tuple-element.86.key_ref, ...), custom_call_target="tpu_custom_call" | custom-call | tf_op jit(solution)/shard_map/attend/pallas_call | solution.py:579
  140.7 6.7 collective-permute-done.31.refs_22_
  153.7 10.8 %collective-permute-done.15.refs_4_ = bf16[512,512]{1,0:T(8,128)(2,1)} collective-permute-done((bf16[512,512]{1,0:T(8,128)(2,1)S(1)}, bf16[512,512]{1,0:T(8,128)(2,1)}, u32[]{:S(2)}, u32[]{:S(2)}) %collective-permute-start.15) | collective-permute-done | bytes 524320 | tf_op jit(solution)/shard_map/act_gather/ppermute | solution.py:39
  166.7 10.5 %collective-permute-done.13.refs_2_ = bf16[512,512]{1,0:T(8,128)(2,1)S(1)} collective-permute-done((bf16[512,512]{1,0:T(8,128)(2,1)S(1)}, bf16[512,512]{1,0:T(8,128)(2,1)S(1)}, u32[]{:S(2)}, u32[]{:S(2)}) %collective-permute-start.13) | collective-permute-done | bytes 524320 | tf_op jit(solution)/shard_map/act_gather/ppermute | solution.py:39
  178.4 9.3 %collective-permute-done.17.refs_6_ = bf16[512,512]{1,0:T(8,128)(2,1)} collective-permute-done((bf16[512,512]{1,0:T(8,128)(2,1)}, bf16[512,512]{1,0:T(8,128)(2,1)}, u32[]{:S(2)}, u32[]{:S(2)}) %collective-permute-start.17) | collective-permute-done | bytes 524320 | tf_op jit(solution)/shard_map/act_gather/ppermute | solution.py:39
  197.3 4.6 all-to-all-done.1.share_ref
  204.9 47.9 %experts.2 = (bf16[2,8,192,1024]{3,2,1,0:T(8,128)(2,1)}, bf16[2,8,192,1024]{3,2,1,0:T(8,128)(2,1)}, f32[2,8,1,512]{3,2,1,0:T(1,128)}, bf16[4,2,768,512]{3,2,1,0:T(8,128)(2,1)}) custom-call(s32[1]{0:T(128)} %bitcast.3.own_ref, s32[8,4,512]{2,1,0:T(4,128)} %copy-done.41, f32[8,4,512]{2,1,0:T(4,128)} %copy-done.45, bf16[4,2,768,512]{3,2,1,0:T(8,128)(2,1)} %bitcast.128, ...), custom_call_target="tpu_custom_call" | custom-call | tf_op jit(solution)/shard_map/experts/pallas_call | solution.py:264
  253.4 66.7 %all-gather.10.cloned.1.call-done = bf16[8,768,512]{2,1,0:T(8,128)(2,1)} async-done(((bf16[2,768,512]{2,1,0:T(8,128)(2,1)}), bf16[8,768,512]{2,1,0:T(8,128)(2,1)}) %all-gather.10.cloned.1.call-update) | async-done | bytes 6291472 | tf_op jit(solution)/shard_map/weights_queue/all_gather | solution.py:1001
  320.1 47.9 %experts.3 = (bf16[2,8,192,1024]{3,2,1,0:T(8,128)(2,1)}, bf16[2,8,192,1024]{3,2,1,0:T(8,128)(2,1)}, f32[2,8,1,512]{3,2,1,0:T(1,128)}, bf16[4,2,768,512]{3,2,1,0:T(8,128)(2,1)}) custom-call(s32[1]{0:T(128)} %bitcast.3.own_ref, s32[8,4,512]{2,1,0:T(4,128)} %copy-done.41, f32[8,4,512]{2,1,0:T(4,128)} %copy-done.45, bf16[4,2,768,512]{3,2,1,0:T(8,128)(2,1)} %bitcast.127, ...), custom_call_target="tpu_custom_call" | custom-call | tf_op jit(solution)/shard_map/experts/pallas_call | solution.py:264
  376.7 9.1 %combine.5 = (bf16[4,512,512]{2,1,0:T(8,128)(2,1)}, bf16[4,512,512]{2,1,0:T(8,128)(2,1)}) custom-call(s32[1]{0:T(128)} %bitcast.3.own_ref, s32[8,512,4]{2,1,0:T(8,128)} %bitcast.119, bf16[2,8,192,1024]{3,2,1,0:T(8,128)(2,1)} %get-tuple-element.96.refs_0_, bf16[2,8,192,1024]{3,2,1,0:T(8,128)(2,1)} %get-tuple-element.97.refs_1_), custom_call_target="tpu_custom_call" | custom-call | tf_op jit(solution)/shard_map/back_reduce/combine/pallas_call | solution.py:328
  386.5 9.1 %combine.4 = (bf16[4,512,512]{2,1,0:T(8,128)(2,1)}, bf16[4,512,512]{2,1,0:T(8,128)(2,1)}) custom-call(s32[1]{0:T(128)} %bitcast.3.own_ref, s32[8,512,4]{2,1,0:T(8,128)} %bitcast.120, bf16[2,8,192,1024]{3,2,1,0:T(8,128)(2,1)} %get-tuple-element.96.refs_0_, bf16[2,8,192,1024]{3,2,1,0:T(8,128)(2,1)} %get-tuple-element.97.refs_1_), custom_call_target="tpu_custom_call" | custom-call | tf_op jit(solution)/shard_map/back_reduce/combine/pallas_call | solution.py:328
  407.7 18.1 %collective-permute-done.41 = bf16[2,512,512]{2,1,0:T(8,128)(2,1)} collective-permute-done((bf16[2,512,512]{2,1,0:T(8,128)(2,1)}, bf16[2,512,512]{2,1,0:T(8,128)(2,1)}, u32[]{:S(2)}, u32[]{:S(2)}) %collective-permute-start.41) | collective-permute-done | bytes 1048608 | tf_op jit(solution)/shard_map/back_reduce/ppermute | solution.py:39
  433.3 8.4 %collective-permute-done.42 = bf16[1,512,512]{2,1,0:T(8,128)(2,1)S(1)} collective-permute-done((bf16[1,512,512]{2,1,0:T(8,128)(2,1)S(1)}, bf16[1,512,512]{2,1,0:T(8,128)(2,1)S(1)}, u32[]{:S(2)}, u32[]{:S(2)}) %collective-permute-start.42) | collective-permute-done | bytes 524320 | tf_op jit(solution)/shard_map/back_reduce/ppermute | solution.py:39
  448.6 4.3 fusion.7.cot_ref
  458.9 5.0 concatenate.86
  463.9 20.3 %attend_back.1 = (f32[512,1024]{1,0:T(8,128)}, f32[2048,512]{1,0:T(8,128)}, f32[2048,512]{1,0:T(8,128)}) custom-call(s32[2]{0:T(128)} %and_select_fusion.lowest_ref, s32[1]{0:T(128)} %bitcast.2.first_ref, s32[512,1]{1,0:T(8,128)} %copy.88.start_ref, f32[4,512,4]{2,1,0:T(8,128)} %get-tuple-element.95.log_ref, bf16[512,1024]{1,0:T(8,128)(2,1)} %get-tuple-element.85.query_ref, ...), custom_call_target="tpu_custom_call" | custom-call | tf_op jit(solution)/shard_map/attend_back/pallas_call | solution.py:655
  484.2 19.6 %weight_back.1 = (bf16[2048,1024]{1,0:T(8,128)(2,1)}, bf16[512,1024]{1,0:T(8,128)(2,1)}, bf16[4,128,1024]{2,1,0:T(8,128)(2,1)}, bf16[4,128,1024]{2,1,0:T(8,128)(...) custom-call(s32[3]{0:T(128)} %pad_add_fusion.bounds_ref, f32[1,1024]{1,0:T(1,128)} %bitcast.139, ...), custom_call_target="tpu_custom_call" | custom-call | tf_op jit(solution)/shard_map/weight_back/pallas_call | solution.py:765
  504.3 4.4 all-to-all-start.3
  510.1 23.7 %token_back.1 = bf16[2048,1024]{1,0:T(8,128)(2,1)} custom-call(s32[3]{0:T(128)} %pad_add_fusion.bounds_ref, s32[2048,1]{1,0:T(8,128)} %copy.94.order_ref, f32[1,1024]{1,0:T(1,128)} %bitcast.140, bf16[1024,3200]{1,0:T(8,128)(2,1)} %all-gather.6.cloned.1.call-done.weight_ref, bf16[512,1024]{1,0:T(8,128)(2,1)} %get-tuple-element.116.query_ref, ...), custom_call_target="tpu_custom_call" | custom-call | tf_op jit(solution)/shard_map/token_back/pallas_call | solution.py:854
  541.0 9.1 %collective-permute-done.49 = bf16[2,128,1024]{2,1,0:T(8,128)(2,1)S(1)} collective-permute-done((bf16[2,128,1024]{2,1,0:T(8,128)(2,1)S(1)}, bf16[2,128,1024]{2,1,0:T(8,128)(2,1)S(1)}, u32[]{:S(2)}, u32[]{:S(2)}) %collective-permute-start.49) | collective-permute-done | bytes 524320 | tf_op jit(solution)/shard_map/late_fsdp/ppermute | solution.py:39
  559.2 9.5 %combine.7 = (bf16[4,512,512]{2,1,0:T(8,128)(2,1)}, bf16[4,512,512]{2,1,0:T(8,128)(2,1)}) custom-call(s32[1]{0:T(128)} %bitcast.3.own_ref, s32[8,512,4]{2,1,0:T(8,128)} %bitcast.121, bf16[2,8,192,1024]{3,2,1,0:T(8,128)(2,1)} %get-tuple-element.122.refs_0_, bf16[2,8,192,1024]{3,2,1,0:T(8,128)(2,1)} %get-tuple-element.123.refs_1_), custom_call_target="tpu_custom_call" | custom-call | tf_op jit(solution)/shard_map/late_fsdp/combine/pallas_call | solution.py:328
  571.6 9.1 %combine.6 = (bf16[4,512,512]{2,1,0:T(8,128)(2,1)}, bf16[4,512,512]{2,1,0:T(8,128)(2,1)}) custom-call(s32[1]{0:T(128)} %bitcast.3.own_ref, s32[8,512,4]{2,1,0:T(8,128)} %bitcast.122, bf16[2,8,192,1024]{3,2,1,0:T(8,128)(2,1)} %get-tuple-element.122.refs_0_, bf16[2,8,192,1024]{3,2,1,0:T(8,128)(2,1)} %get-tuple-element.123.refs_1_), custom_call_target="tpu_custom_call" | custom-call | tf_op jit(solution)/shard_map/late_fsdp/combine/pallas_call | solution.py:328
  581.7 22.5 %all-to-all-start.4 = ((bf16[4,32,3200]{2,1,0:T(8,128)(2,1)}), bf16[4,32,3200]{2,1,0:T(8,128)(2,1)S(1)}, u32[]{:S(2)}, u32[]{:S(2)}) async-start(bf16[4,32,3200]{2,1,0:T(8,128)(2,1)} %bitcast.50), calls=%async_computation.7 | async-start | bytes 1638400 | tf_op jit(solution)/shard_map/sums_sp/all_to_all | solution.py:109
  621.2 24.7 %all-to-all-done.4 = bf16[4,32,3200]{2,1,0:T(8,128)(2,1)S(1)} async-done(((bf16[4,32,3200]{2,1,0:T(8,128)(2,1)}), bf16[4,32,3200]{2,1,0:T(8,128)(2,1)S(1)}, u32[]{:S(2)}, u32[]{:S(2)}) %all-to-all-start.4) | async-done | bytes 819232 | tf_op jit(solution)/shard_map/sums_sp/all_to_all | solution.py:109
  656.9 14.0 %all-to-all-done.5 = bf16[4,32,3200]{2,1,0:T(8,128)(2,1)S(1)} async-done(((bf16[4,32,3200]{2,1,0:T(8,128)(2,1)}), bf16[4,32,3200]{2,1,0:T(8,128)(2,1)S(1)}, u32[]{:S(2)}, u32[]{:S(2)}) %all-to-all-start.5) | async-done | bytes 819232 | tf_op jit(solution)/shard_map/sums_sp/all_to_all | solution.py:109
  (412 shorter events, 188.0 us)
Async XLA Ops:
  7.2 81.8 %all-gather.6.cloned.1.call-start = ((), (), s32[]{:S(2)}) async-start(), calls=%async_computation.9 | async-start | bytes 7372800 | tf_op jit(solution)/shard_map/all_gather | solution.py:927
  11.3 26.4 %collective-permute-start = (bf16[256,512]{1,0:T(8,128)(2,1)}, bf16[256,512]{1,0:T(8,128)(2,1)}, u32[]{:S(2)}, u32[]{:S(2)}) collective-permute-start(bf16[256,512]{1,0:T(8,128)(2,1)} %get-tuple-element.246.refs_0_), channel_id=1, source_target_pairs={{0,1},{1,2},{2,3},{3,0},{4,5},{5,6},{6,7},{7,4},{8,9},{9,10},{10,1... | collective-permute-start | bytes 786440 | tf_op jit(solution)/shard_map/tokens_ring/ppermute | solution.py:364
  14.4 25.1 %collective-permute-start.2 = (bf16[256,512]{1,0:T(8,128)(2,1)}, bf16[256,512]{1,0:T(8,128)(2,1)}, u32[]{:S(2)}, u32[]{:S(2)}) collective-permute-start(bf16[256,512]{1,0:T(8,128)(2,1)} %get-tuple-element.245.refs_1_), channel_id=1, source_target_pairs={{0,1},{1,2},{2,3},{3,0},{4,5},{5,6},{6,7},{7,4},{8,9},{9,10},{10,1... | collective-permute-start | bytes 786440 | tf_op jit(solution)/shard_map/tokens_ring/ppermute | solution.py:364
  16.0 23.6 %collective-permute-start.4 = (bf16[256,512]{1,0:T(8,128)(2,1)}, bf16[256,512]{1,0:T(8,128)(2,1)}, u32[]{:S(2)}, u32[]{:S(2)}) collective-permute-start(bf16[256,512]{1,0:T(8,128)(2,1)} %get-tuple-element.247.refs_8_), channel_id=1, source_target_pairs={{0,3},{1,0},{2,1},{3,2},{4,7},{5,4},{6,5},{7,6},{8,11},{9,8},{10,9... | collective-permute-start | bytes 786440 | tf_op jit(solution)/shard_map/tokens_ring/ppermute | solution.py:364
  18.2 25.1 %collective-permute-start.6 = (bf16[256,512]{1,0:T(8,128)(2,1)}, bf16[256,512]{1,0:T(8,128)(2,1)}, u32[]{:S(2)}, u32[]{:S(2)}) collective-permute-start(bf16[256,512]{1,0:T(8,128)(2,1)} %get-tuple-element.244.refs_9_), channel_id=1, source_target_pairs={{0,3},{1,0},{2,1},{3,2},{4,7},{5,4},{6,5},{7,6},{8,11},{9,8},{10,9... | collective-permute-start | bytes 786440 | tf_op jit(solution)/shard_map/tokens_ring/ppermute | solution.py:364
  49.4 155.5 %all-gather.8.cloned.1.call-start = ((), (), s32[]{:S(2)}) async-start(), calls=%async_computation.13 | async-start | bytes 7864320 | tf_op jit(solution)/shard_map/weights_queue/all_gather | solution.py:1001
  89.1 231.0 %all-gather.10.cloned.1.call-start = ((), (), s32[]{:S(2)}) async-start(), calls=%async_computation.14 | async-start | bytes 7864320 | tf_op jit(solution)/shard_map/weights_queue/all_gather | solution.py:1001
  90.0 42.8 %collective-permute-start.29 = (bf16[512,512]{1,0:T(8,128)(2,1)S(1)}, bf16[512,512]{1,0:T(8,128)(2,1)}, u32[]{:S(2)}, u32[]{:S(2)}) collective-permute-start(bf16[512,512]{1,0:T(8,128)(2,1)S(1)} %get-tuple-element.225.refs_16_), channel_id=1, source_target_pairs={{0,16},{4,20},{8,24},{12,28},{16,0},{20,4},{24,8},{28,12},{1,17},{... | collective-permute-start | bytes 1572872 | tf_op jit(solution)/shard_map/cot_gather/ppermute | solution.py:39
  91.5 41.8 %collective-permute-start.34 = (bf16[512,512]{1,0:T(8,128)(2,1)S(1)}, bf16[512,512]{1,0:T(8,128)(2,1)}, u32[]{:S(2)}, u32[]{:S(2)}) collective-permute-start(bf16[512,512]{1,0:T(8,128)(2,1)S(1)} %get-tuple-element.224.refs_24_), channel_id=1, source_target_pairs={{0,8},{4,12},{8,0},{12,4},{16,24},{20,28},{24,16},{28,20},{1,9},{5... | collective-permute-start | bytes 1572872 | tf_op jit(solution)/shard_map/cot_gather/ppermute | solution.py:39
  93.0 41.8 %collective-permute-start.27 = (bf16[512,512]{1,0:T(8,128)(2,1)S(1)}, bf16[512,512]{1,0:T(8,128)(2,1)S(1)}, u32[]{:S(2)}, u32[]{:S(2)}) collective-permute-start(bf16[512,512]{1,0:T(8,128)(2,1)S(1)} %get-tuple-element.225.refs_16_), channel_id=1, source_target_pairs={{0,8},{4,12},{8,0},{12,4},{16,24},{20,28},{24,16},{28,20},{1,9},{5... | collective-permute-start | bytes 1572872 | tf_op jit(solution)/shard_map/cot_gather/ppermute | solution.py:39
  95.7 44.2 %collective-permute-start.36 = (bf16[512,512]{1,0:T(8,128)(2,1)S(1)}, bf16[512,512]{1,0:T(8,128)(2,1)S(1)}, u32[]{:S(2)}, u32[]{:S(2)}) collective-permute-start(bf16[512,512]{1,0:T(8,128)(2,1)S(1)} %get-tuple-element.224.refs_24_), channel_id=1, source_target_pairs={{0,16},{4,20},{8,24},{12,28},{16,0},{20,4},{24,8},{28,12},{1,17},{... | collective-permute-start | bytes 1572872 | tf_op jit(solution)/shard_map/cot_gather/ppermute | solution.py:39
  96.2 43.8 %collective-permute-start.26 = (bf16[512,512]{1,0:T(8,128)(2,1)S(1)}, bf16[512,512]{1,0:T(8,128)(2,1)}, u32[]{:S(2)}, u32[]{:S(2)}) collective-permute-start(bf16[512,512]{1,0:T(8,128)(2,1)S(1)} %get-tuple-element.225.refs_16_), channel_id=1, source_target_pairs={{0,4},{4,0},{8,12},{12,8},{16,20},{20,16},{24,28},{28,24},{1,5},{5... | collective-permute-start | bytes 1572872 | tf_op jit(solution)/shard_map/cot_gather/ppermute | solution.py:39
  151.8 25.4 %collective-permute-start.13 = (bf16[512,512]{1,0:T(8,128)(2,1)S(1)}, bf16[512,512]{1,0:T(8,128)(2,1)S(1)}, u32[]{:S(2)}, u32[]{:S(2)}) collective-permute-start(bf16[512,512]{1,0:T(8,128)(2,1)S(1)} %get-tuple-element.227.refs_0_), channel_id=1, source_target_pairs={{0,8},{4,12},{8,0},{12,4},{16,24},{20,28},{24,16},{28,20},{1,9},{5... | collective-permute-start | bytes 1572872 | tf_op jit(solution)/shard_map/act_gather/ppermute | solution.py:39
  153.2 24.5 %collective-permute-start.22 = (bf16[512,512]{1,0:T(8,128)(2,1)S(1)}, bf16[512,512]{1,0:T(8,128)(2,1)}, u32[]{:S(2)}, u32[]{:S(2)}) collective-permute-start(bf16[512,512]{1,0:T(8,128)(2,1)S(1)} %get-tuple-element.226.refs_8_), channel_id=1, source_target_pairs={{0,16},{4,20},{8,24},{12,28},{16,0},{20,4},{24,8},{28,12},{1,17},{... | collective-permute-start | bytes 1572872 | tf_op jit(solution)/shard_map/act_gather/ppermute | solution.py:39
  153.7 24.0 %collective-permute-start.12 = (bf16[512,512]{1,0:T(8,128)(2,1)S(1)}, bf16[512,512]{1,0:T(8,128)(2,1)S(1)}, u32[]{:S(2)}, u32[]{:S(2)}) collective-permute-start(bf16[512,512]{1,0:T(8,128)(2,1)S(1)} %get-tuple-element.227.refs_0_), channel_id=1, source_target_pairs={{0,4},{4,0},{8,12},{12,8},{16,20},{20,16},{24,28},{28,24},{1,5},{5... | collective-permute-start | bytes 1572872 | tf_op jit(solution)/shard_map/act_gather/ppermute | solution.py:39
  177.7 24.2 %collective-permute-start.16 = (bf16[512,512]{1,0:T(8,128)(2,1)}, bf16[512,512]{1,0:T(8,128)(2,1)}, u32[]{:S(2)}, u32[]{:S(2)}) collective-permute-start(bf16[512,512]{1,0:T(8,128)(2,1)} %collective-permute-done.15.refs_4_), channel_id=1, source_target_pairs={{0,4},{4,0},{8,12},{12,8},{16,20},{20,16},{24,28},{28,24},{1,5},{5... | collective-permute-start | bytes 1572872 | tf_op jit(solution)/shard_map/act_gather/ppermute | solution.py:39
  178.2 23.7 %collective-permute-start.21 = (bf16[512,512]{1,0:T(8,128)(2,1)}, bf16[512,512]{1,0:T(8,128)(2,1)}, u32[]{:S(2)}, u32[]{:S(2)}) collective-permute-start(bf16[512,512]{1,0:T(8,128)(2,1)} %collective-permute-done.20.refs_10_), channel_id=1, source_target_pairs={{0,4},{4,0},{8,12},{12,8},{16,20},{20,16},{24,28},{28,24},{1,5},{5... | collective-permute-start | bytes 1572872 | tf_op jit(solution)/shard_map/act_gather/ppermute | solution.py:39
  196.9 267.0 %reduce-scatter.4.cloned.1.call-start = ((), (), s32[]{:S(2)}) async-start(), calls=%async_computation.10 | async-start | bytes 7864320 | tf_op jit(solution)/shard_map/grads_queue/reduce_scatter | solution.py:1035
  252.9 328.8 %reduce-scatter.6.cloned.1.call-start = ((), (), s32[]{:S(2)}) async-start(), calls=%async_computation.11 | async-start | bytes 7864320 | tf_op jit(solution)/shard_map/grads_queue/reduce_scatter | solution.py:1035
  399.9 25.8 %collective-permute-start.41 = (bf16[2,512,512]{2,1,0:T(8,128)(2,1)}, bf16[2,512,512]{2,1,0:T(8,128)(2,1)}, u32[]{:S(2)}, u32[]{:S(2)}) collective-permute-start(bf16[2,512,512]{2,1,0:T(8,128)(2,1)} %get-tuple-element.209), channel_id=1, source_target_pairs={{0,8},{4,12},{8,0},{12,4},{16,24},{20,28},{24,16},{28,20},{1,9},{5... | collective-permute-start | bytes 3145736 | tf_op jit(solution)/shard_map/back_reduce/ppermute | solution.py:39
  405.3 26.4 %collective-permute-start.44 = (bf16[2,512,512]{2,1,0:T(8,128)(2,1)}, bf16[2,512,512]{2,1,0:T(8,128)(2,1)}, u32[]{:S(2)}, u32[]{:S(2)}) collective-permute-start(bf16[2,512,512]{2,1,0:T(8,128)(2,1)} %get-tuple-element.211), channel_id=1, source_target_pairs={{0,16},{4,20},{8,24},{12,28},{16,0},{20,4},{24,8},{28,12},{1,17},{... | collective-permute-start | bytes 3145736 | tf_op jit(solution)/shard_map/back_reduce/ppermute | solution.py:39
  503.8 30.1 %collective-permute-start.48 = (bf16[4,128,1024]{2,1,0:T(8,128)(2,1)}, bf16[4,128,1024]{2,1,0:T(8,128)(2,1)}, u32[]{:S(2)}, u32[]{:S(2)}) collective-permute-start(bf16[4,128,1024]{2,1,0:T(8,128)(2,1)} %get-tuple-element.121), channel_id=1, source_target_pairs={{0,4},{4,0},{8,12},{12,8},{16,20},{20,16},{24,28},{28,24},{1,5},{5... | collective-permute-start | bytes 3145736 | tf_op jit(solution)/shard_map/late_fsdp/ppermute | solution.py:39
  503.8 34.0 %collective-permute-start.46 = (bf16[4,128,1024]{2,1,0:T(8,128)(2,1)}, bf16[4,128,1024]{2,1,0:T(8,128)(2,1)}, u32[]{:S(2)}, u32[]{:S(2)}) collective-permute-start(bf16[4,128,1024]{2,1,0:T(8,128)(2,1)} %get-tuple-element.119), channel_id=1, source_target_pairs={{0,4},{4,0},{8,12},{12,8},{16,20},{20,16},{24,28},{28,24},{1,5},{5... | collective-permute-start | bytes 3145736 | tf_op jit(solution)/shard_map/late_fsdp/ppermute | solution.py:39
  504.3 52.1 %all-to-all-start.3 = ((bf16[8,128,1152]{2,1,0:T(8,128)(2,1)}), bf16[8,128,1152]{2,1,0:T(8,128)(2,1)}, u32[]{:S(2)}, u32[]{:S(2)}) async-start(bf16[8,128,1152]{2,1,0:T(8,128)(2,1)} %concatenate.86), calls=%async_computation.5 | async-start | bytes 4718592 | tf_op jit(solution)/shard_map/early_fsdp/all_to_all | solution.py:109
  508.7 170.5 %reduce-scatter.8.cloned.1.call-start = ((), (), s32[]{:S(2)}) async-start(), calls=%async_computation.12 | async-start | bytes 5242880 | tf_op jit(solution)/shard_map/tokens_back/reduce_scatter | solution.py:1095
  568.7 42.8 %collective-permute-start.51 = (bf16[4,512,512]{2,1,0:T(8,128)(2,1)}, bf16[4,512,512]{2,1,0:T(8,128)(2,1)}, u32[]{:S(2)}, u32[]{:S(2)}) collective-permute-start(bf16[4,512,512]{2,1,0:T(8,128)(2,1)} %get-tuple-element.129), channel_id=1, source_target_pairs={{0,4},{4,0},{8,12},{12,8},{16,20},{20,16},{24,28},{28,24},{1,5},{5... | collective-permute-start | bytes 6291464 | tf_op jit(solution)/shard_map/mix_reduce/ppermute | solution.py:39
  568.7 47.1 %collective-permute-start.50 = (bf16[4,512,512]{2,1,0:T(8,128)(2,1)}, bf16[4,512,512]{2,1,0:T(8,128)(2,1)}, u32[]{:S(2)}, u32[]{:S(2)}) collective-permute-start(bf16[4,512,512]{2,1,0:T(8,128)(2,1)} %get-tuple-element.127), channel_id=1, source_target_pairs={{0,4},{4,0},{8,12},{12,8},{16,20},{20,16},{24,28},{28,24},{1,5},{5... | collective-permute-start | bytes 6291464 | tf_op jit(solution)/shard_map/mix_reduce/ppermute | solution.py:39
  581.7 64.2 %all-to-all-start.4 = ((bf16[4,32,3200]{2,1,0:T(8,128)(2,1)}), bf16[4,32,3200]{2,1,0:T(8,128)(2,1)S(1)}, u32[]{:S(2)}, u32[]{:S(2)}) async-start(bf16[4,32,3200]{2,1,0:T(8,128)(2,1)} %bitcast.50), calls=%async_computation.7 | async-start | bytes 1638400 | tf_op jit(solution)/shard_map/sums_sp/all_to_all | solution.py:109
  619.3 31.2 %collective-permute-start.54 = (bf16[2,512,512]{2,1,0:T(8,128)(2,1)}, bf16[2,512,512]{2,1,0:T(8,128)(2,1)}, u32[]{:S(2)}, u32[]{:S(2)}) collective-permute-start(bf16[2,512,512]{2,1,0:T(8,128)(2,1)} %get-tuple-element.136), channel_id=1, source_target_pairs={{0,8},{4,12},{8,0},{12,4},{16,24},{20,28},{24,16},{28,20},{1,9},{5... | collective-permute-start | bytes 3145736 | tf_op jit(solution)/shard_map/mix_reduce/ppermute | solution.py:39
  620.2 33.2 %collective-permute-start.56 = (bf16[2,512,512]{2,1,0:T(8,128)(2,1)}, bf16[2,512,512]{2,1,0:T(8,128)(2,1)}, u32[]{:S(2)}, u32[]{:S(2)}) collective-permute-start(bf16[2,512,512]{2,1,0:T(8,128)(2,1)} %get-tuple-element.137), channel_id=1, source_target_pairs={{0,16},{4,20},{8,24},{12,28},{16,0},{20,4},{24,8},{28,12},{1,17},{... | collective-permute-start | bytes 3145736 | tf_op jit(solution)/shard_map/mix_reduce/ppermute | solution.py:39
  647.0 23.9 %all-to-all-start.5 = ((bf16[4,32,3200]{2,1,0:T(8,128)(2,1)}), bf16[4,32,3200]{2,1,0:T(8,128)(2,1)S(1)}, u32[]{:S(2)}, u32[]{:S(2)}) async-start(bf16[4,32,3200]{2,1,0:T(8,128)(2,1)} %broadcast_in_dim.76), calls=%async_computation.8 | async-start | bytes 1638400 | tf_op jit(solution)/shard_map/sums_sp/all_to_all | solution.py:109
  652.7 22.4 %collective-permute-start.55 = (bf16[1,512,512]{2,1,0:T(8,128)(2,1)}, bf16[1,512,512]{2,1,0:T(8,128)(2,1)}, u32[]{:S(2)}, u32[]{:S(2)}) collective-permute-start(bf16[1,512,512]{2,1,0:T(8,128)(2,1)} %add_convert_fusion.11), channel_id=1, source_target_pairs={{0,16},{4,20},{8,24},{12,28},{16,0},{20,4},{24,8},{28,12},{1,17},{... | collective-permute-start | bytes 1572872 | tf_op jit(solution)/shard_map/mix_reduce/ppermute | solution.py:39
  (125 other events, 1515.8 us)
Sparse Core Ops, SparseCore 0:
  11.4 50.0 all-gather.5
  89.2 115.6 all-gather.7
  206.5 113.5 all-gather.9
  322.2 108.9 reduce-scatter.3
  433.4 111.2 reduce-scatter.5
  547.4 95.7 reduce-scatter.7

commit v6 on v5

--- a/solution.py
+++ b/solution.py
@@ -1109,7 +1109,7 @@
                     mix_leave = made
                 else:
                     mix_stay = made
-        late_stay = after(late_stay, *mix_leave, *mix_stay)
+        late_stay = after(late_stay, *mix_leave)
         row_sums = jnp.concatenate([early_sum] + [part.astype(low) for part in late_stay], axis=1)
     deep = expert_gate.shape[1]
 

time: 695 us -> 686 us (0.987)
  waiting for transfers between devices: 228 us -> 221 us
    all_to_all x6, waiting for transfers between devices: 48.6 us -> 40 us  [exchange_blocks(): lax.all_to_all(values, axis_name, split_axis=0, concat_axis=0, tiled=True)]
  transfers between devices with their start and end apart: 70 -> 70, of which waited for: 24 -> 25; matrix products, arithmetic and copies ran while one was open for 16% -> 16% of each run, Pallas kernels for 34% -> 34%
where the time goes in v6:
time: 686 us; the launch traced here: 675 us
  Pallas kernels  230 us (34%)
  waiting for transfers between devices  221 us (32%)
  starting transfers between devices  86.9 us (13%)
  other arithmetic  66.4 us (10%)
  local copies, waits for them, and re-layouts  38 us (6%)
  between operations  17 us (2%)
  matrix products  15.7 us (2%)
    pallas_call x2, Pallas kernels, run_experts(): pl.pallas_call(functools.partial(expert_step, count=count, first=first),...  95.8 us
    ppermute x46, waiting for transfers between devices, flip(): lax.ppermute(values, axis_name, [(place, place ^ bit) for place in range(...  84.9 us
    all_gather x2, waiting for transfers between devices, body(): lax.all_gather(part, 'sp', axis=0, tiled=False)  69.7 us
    all_to_all x6, waiting for transfers between devices, exchange_blocks(): lax.all_to_all(values, axis_name, split_axis=0, concat_axis=0, tiled=True)  40 us
    all_to_all x6, starting transfers between devices, exchange_blocks(): lax.all_to_all(values, axis_name, split_axis=0, concat_axis=0, tiled=True)  36.8 us
    pallas_call x4, Pallas kernels, combine_rows(): pl.pallas_call(combine_step, grid_spec=pltpu.PrefetchScalarGridSpec(num_s...  36.4 us
    ppermute x46, starting transfers between devices, flip(): lax.ppermute(values, axis_name, [(place, place ^ bit) for place in range(...  31.6 us
    ppermute x12, waiting for transfers between devices, ring_step(): lax.ppermute(one, axis_name, shift_pairs(count, by))  26.1 us
  transfers between devices with their start and end apart: 70, of which 25 were waited for; matrix products, arithmetic and copies ran while one was open for 16% of the time, Pallas kernels for 34%

profile of v6, /device:TPU:0, one launch (start us, length us, event | category | flops | bytes accessed | tf_op | source)
XLA Modules:
  0.0 675.3 jit_solution(1317040947284755015)
XLA Ops:
  29.7 4.4 fusion.14
  50.0 5.2 all-to-all-done.slot_ref
  58.3 4.8 collective-permute-done.7.refs_13_
  68.1 5.2 collective-permute-done.10.refs_14_
  73.3 5.7 collective-permute-done.11.refs_15_
  79.0 6.2 collective-permute-done.8.refs_2_
  98.2 15.8 %project.1 = (bf16[2048,1024]{1,0:T(8,128)(2,1)}, bf16[512,1024]{1,0:T(8,128)(2,1)}, bf16[2048,512]{1,0:T(8,128)(2,1)}, bf16[2048,512]{1,0:T(8,128)(2,1)}) custom-call(s32[3]{0:T(128)} %pad_add_fusion.bounds_ref, s32[1,2048]{1,0:T(1,128)} %bitcast.143, f32[1,1024]{1,0:T(1,128)} %bitcast.138, bf16[1024,3200]{1,0:T(8,128)(2,1)} %all-gather.6.cloned.1.call-done.weight_ref, ...), custom_call_target="tpu_custom_call" | custom-call | tf_op jit(solution)/shard_map/project/pallas_call | solution.py:459
  114.0 18.6 %attend.1 = (bf16[512,1024]{1,0:T(8,128)(2,1)}, f32[4,512,4]{2,1,0:T(8,128)}) custom-call(s32[2]{0:T(128)} %and_select_fusion.lowest_ref, s32[1]{0:T(128)} %bitcast.2.first_ref, s32[512,1]{1,0:T(8,128)} %copy.88.start_ref, bf16[512,1024]{1,0:T(8,128)(2,1)} %get-tuple-element.85.query_ref, bf16[2048,512]{1,0:T(8,128)(2,1)} %get-tuple-element.86.key_ref, ...), custom_call_target="tpu_custom_call" | custom-call | tf_op jit(solution)/shard_map/attend/pallas_call | solution.py:579
  140.6 6.7 collective-permute-done.31.refs_22_
  153.7 10.8 %collective-permute-done.15.refs_4_ = bf16[512,512]{1,0:T(8,128)(2,1)} collective-permute-done((bf16[512,512]{1,0:T(8,128)(2,1)S(1)}, bf16[512,512]{1,0:T(8,128)(2,1)}, u32[]{:S(2)}, u32[]{:S(2)}) %collective-permute-start.15) | collective-permute-done | bytes 524320 | tf_op jit(solution)/shard_map/act_gather/ppermute | solution.py:39
  166.6 10.5 %collective-permute-done.13.refs_2_ = bf16[512,512]{1,0:T(8,128)(2,1)S(1)} collective-permute-done((bf16[512,512]{1,0:T(8,128)(2,1)S(1)}, bf16[512,512]{1,0:T(8,128)(2,1)S(1)}, u32[]{:S(2)}, u32[]{:S(2)}) %collective-permute-start.13) | collective-permute-done | bytes 524320 | tf_op jit(solution)/shard_map/act_gather/ppermute | solution.py:39
  178.3 9.2 %collective-permute-done.17.refs_6_ = bf16[512,512]{1,0:T(8,128)(2,1)} collective-permute-done((bf16[512,512]{1,0:T(8,128)(2,1)}, bf16[512,512]{1,0:T(8,128)(2,1)}, u32[]{:S(2)}, u32[]{:S(2)}) %collective-permute-start.17) | collective-permute-done | bytes 524320 | tf_op jit(solution)/shard_map/act_gather/ppermute | solution.py:39
  197.2 4.6 all-to-all-done.1.share_ref
  204.8 47.9 %experts.2 = (bf16[2,8,192,1024]{3,2,1,0:T(8,128)(2,1)}, bf16[2,8,192,1024]{3,2,1,0:T(8,128)(2,1)}, f32[2,8,1,512]{3,2,1,0:T(1,128)}, bf16[4,2,768,512]{3,2,1,0:T(8,128)(2,1)}) custom-call(s32[1]{0:T(128)} %bitcast.3.own_ref, s32[8,4,512]{2,1,0:T(4,128)} %copy-done.41, f32[8,4,512]{2,1,0:T(4,128)} %copy-done.45, bf16[4,2,768,512]{3,2,1,0:T(8,128)(2,1)} %bitcast.128, ...), custom_call_target="tpu_custom_call" | custom-call | tf_op jit(solution)/shard_map/experts/pallas_call | solution.py:264
  253.3 66.7 %all-gather.10.cloned.1.call-done = bf16[8,768,512]{2,1,0:T(8,128)(2,1)} async-done(((bf16[2,768,512]{2,1,0:T(8,128)(2,1)}), bf16[8,768,512]{2,1,0:T(8,128)(2,1)}) %all-gather.10.cloned.1.call-update) | async-done | bytes 6291472 | tf_op jit(solution)/shard_map/weights_queue/all_gather | solution.py:1001
  320.0 47.9 %experts.3 = (bf16[2,8,192,1024]{3,2,1,0:T(8,128)(2,1)}, bf16[2,8,192,1024]{3,2,1,0:T(8,128)(2,1)}, f32[2,8,1,512]{3,2,1,0:T(1,128)}, bf16[4,2,768,512]{3,2,1,0:T(8,128)(2,1)}) custom-call(s32[1]{0:T(128)} %bitcast.3.own_ref, s32[8,4,512]{2,1,0:T(4,128)} %copy-done.41, f32[8,4,512]{2,1,0:T(4,128)} %copy-done.45, bf16[4,2,768,512]{3,2,1,0:T(8,128)(2,1)} %bitcast.127, ...), custom_call_target="tpu_custom_call" | custom-call | tf_op jit(solution)/shard_map/experts/pallas_call | solution.py:264
  376.6 9.1 %combine.5 = (bf16[4,512,512]{2,1,0:T(8,128)(2,1)}, bf16[4,512,512]{2,1,0:T(8,128)(2,1)}) custom-call(s32[1]{0:T(128)} %bitcast.3.own_ref, s32[8,512,4]{2,1,0:T(8,128)} %bitcast.119, bf16[2,8,192,1024]{3,2,1,0:T(8,128)(2,1)} %get-tuple-element.96.refs_0_, bf16[2,8,192,1024]{3,2,1,0:T(8,128)(2,1)} %get-tuple-element.97.refs_1_), custom_call_target="tpu_custom_call" | custom-call | tf_op jit(solution)/shard_map/back_reduce/combine/pallas_call | solution.py:328
  386.5 9.1 %combine.4 = (bf16[4,512,512]{2,1,0:T(8,128)(2,1)}, bf16[4,512,512]{2,1,0:T(8,128)(2,1)}) custom-call(s32[1]{0:T(128)} %bitcast.3.own_ref, s32[8,512,4]{2,1,0:T(8,128)} %bitcast.120, bf16[2,8,192,1024]{3,2,1,0:T(8,128)(2,1)} %get-tuple-element.96.refs_0_, bf16[2,8,192,1024]{3,2,1,0:T(8,128)(2,1)} %get-tuple-element.97.refs_1_), custom_call_target="tpu_custom_call" | custom-call | tf_op jit(solution)/shard_map/back_reduce/combine/pallas_call | solution.py:328
  407.6 18.1 %collective-permute-done.41 = bf16[2,512,512]{2,1,0:T(8,128)(2,1)} collective-permute-done((bf16[2,512,512]{2,1,0:T(8,128)(2,1)}, bf16[2,512,512]{2,1,0:T(8,128)(2,1)}, u32[]{:S(2)}, u32[]{:S(2)}) %collective-permute-start.41) | collective-permute-done | bytes 1048608 | tf_op jit(solution)/shard_map/back_reduce/ppermute | solution.py:39
  433.2 8.4 %collective-permute-done.42 = bf16[1,512,512]{2,1,0:T(8,128)(2,1)S(1)} collective-permute-done((bf16[1,512,512]{2,1,0:T(8,128)(2,1)S(1)}, bf16[1,512,512]{2,1,0:T(8,128)(2,1)S(1)}, u32[]{:S(2)}, u32[]{:S(2)}) %collective-permute-start.42) | collective-permute-done | bytes 524320 | tf_op jit(solution)/shard_map/back_reduce/ppermute | solution.py:39
  448.5 4.3 fusion.7.cot_ref
  458.8 5.0 concatenate.86
  463.8 20.2 %attend_back.1 = (f32[512,1024]{1,0:T(8,128)}, f32[2048,512]{1,0:T(8,128)}, f32[2048,512]{1,0:T(8,128)}) custom-call(s32[2]{0:T(128)} %and_select_fusion.lowest_ref, s32[1]{0:T(128)} %bitcast.2.first_ref, s32[512,1]{1,0:T(8,128)} %copy.88.start_ref, f32[4,512,4]{2,1,0:T(8,128)} %get-tuple-element.95.log_ref, bf16[512,1024]{1,0:T(8,128)(2,1)} %get-tuple-element.85.query_ref, ...), custom_call_target="tpu_custom_call" | custom-call | tf_op jit(solution)/shard_map/attend_back/pallas_call | solution.py:655
  484.0 19.6 %weight_back.1 = (bf16[2048,1024]{1,0:T(8,128)(2,1)}, bf16[512,1024]{1,0:T(8,128)(2,1)}, bf16[4,128,1024]{2,1,0:T(8,128)(2,1)}, bf16[4,128,1024]{2,1,0:T(8,128)(...) custom-call(s32[3]{0:T(128)} %pad_add_fusion.bounds_ref, f32[1,1024]{1,0:T(1,128)} %bitcast.139, ...), custom_call_target="tpu_custom_call" | custom-call | tf_op jit(solution)/shard_map/weight_back/pallas_call | solution.py:765
  504.1 4.4 all-to-all-start.3
  509.9 23.8 %token_back.1 = bf16[2048,1024]{1,0:T(8,128)(2,1)} custom-call(s32[3]{0:T(128)} %pad_add_fusion.bounds_ref, s32[2048,1]{1,0:T(8,128)} %copy.94.order_ref, f32[1,1024]{1,0:T(1,128)} %bitcast.140, bf16[1024,3200]{1,0:T(8,128)(2,1)} %all-gather.6.cloned.1.call-done.weight_ref, bf16[512,1024]{1,0:T(8,128)(2,1)} %get-tuple-element.116.query_ref, ...), custom_call_target="tpu_custom_call" | custom-call | tf_op jit(solution)/shard_map/token_back/pallas_call | solution.py:854
  540.8 9.2 %collective-permute-done.49 = bf16[2,128,1024]{2,1,0:T(8,128)(2,1)S(1)} collective-permute-done((bf16[2,128,1024]{2,1,0:T(8,128)(2,1)S(1)}, bf16[2,128,1024]{2,1,0:T(8,128)(2,1)S(1)}, u32[]{:S(2)}, u32[]{:S(2)}) %collective-permute-start.49) | collective-permute-done | bytes 524320 | tf_op jit(solution)/shard_map/late_fsdp/ppermute | solution.py:39
  559.1 9.1 %combine.7 = (bf16[4,512,512]{2,1,0:T(8,128)(2,1)}, bf16[4,512,512]{2,1,0:T(8,128)(2,1)}) custom-call(s32[1]{0:T(128)} %bitcast.3.own_ref, s32[8,512,4]{2,1,0:T(8,128)} %bitcast.121, bf16[2,8,192,1024]{3,2,1,0:T(8,128)(2,1)} %get-tuple-element.122.refs_0_, bf16[2,8,192,1024]{3,2,1,0:T(8,128)(2,1)} %get-tuple-element.123.refs_1_), custom_call_target="tpu_custom_call" | custom-call | tf_op jit(solution)/shard_map/late_fsdp/combine/pallas_call | solution.py:328
  572.0 17.4 %all-to-all-start.4 = ((bf16[4,32,3200]{2,1,0:T(8,128)(2,1)}), bf16[4,32,3200]{2,1,0:T(8,128)(2,1)S(1)}, u32[]{:S(2)}, u32[]{:S(2)}) async-start(bf16[4,32,3200]{2,1,0:T(8,128)(2,1)} %bitcast.50), calls=%async_computation.7 | async-start | bytes 1638400 | tf_op jit(solution)/shard_map/sums_sp/all_to_all | solution.py:109
  596.0 9.1 %combine.6 = (bf16[4,512,512]{2,1,0:T(8,128)(2,1)}, bf16[4,512,512]{2,1,0:T(8,128)(2,1)}) custom-call(s32[1]{0:T(128)} %bitcast.3.own_ref, s32[8,512,4]{2,1,0:T(8,128)} %bitcast.122, bf16[2,8,192,1024]{3,2,1,0:T(8,128)(2,1)} %get-tuple-element.122.refs_0_, bf16[2,8,192,1024]{3,2,1,0:T(8,128)(2,1)} %get-tuple-element.123.refs_1_), custom_call_target="tpu_custom_call" | custom-call | tf_op jit(solution)/shard_map/late_fsdp/combine/pallas_call | solution.py:328
  616.4 16.3 %all-to-all-done.4 = bf16[4,32,3200]{2,1,0:T(8,128)(2,1)S(1)} async-done(((bf16[4,32,3200]{2,1,0:T(8,128)(2,1)}), bf16[4,32,3200]{2,1,0:T(8,128)(2,1)S(1)}, u32[]{:S(2)}, u32[]{:S(2)}) %all-to-all-start.4) | async-done | bytes 819232 | tf_op jit(solution)/shard_map/sums_sp/all_to_all | solution.py:109
  645.9 13.8 %all-to-all-done.5 = bf16[4,32,3200]{2,1,0:T(8,128)(2,1)S(1)} async-done(((bf16[4,32,3200]{2,1,0:T(8,128)(2,1)}), bf16[4,32,3200]{2,1,0:T(8,128)(2,1)S(1)}, u32[]{:S(2)}, u32[]{:S(2)}) %all-to-all-start.5) | async-done | bytes 819232 | tf_op jit(solution)/shard_map/sums_sp/all_to_all | solution.py:109
  (414 shorter events, 191.1 us)
Async XLA Ops:
  7.2 81.7 %all-gather.6.cloned.1.call-start = ((), (), s32[]{:S(2)}) async-start(), calls=%async_computation.9 | async-start | bytes 7372800 | tf_op jit(solution)/shard_map/all_gather | solution.py:927
  11.3 26.4 %collective-permute-start = (bf16[256,512]{1,0:T(8,128)(2,1)}, bf16[256,512]{1,0:T(8,128)(2,1)}, u32[]{:S(2)}, u32[]{:S(2)}) collective-permute-start(bf16[256,512]{1,0:T(8,128)(2,1)} %get-tuple-element.246.refs_0_), channel_id=1, source_target_pairs={{0,1},{1,2},{2,3},{3,0},{4,5},{5,6},{6,7},{7,4},{8,9},{9,10},{10,1... | collective-permute-start | bytes 786440 | tf_op jit(solution)/shard_map/tokens_ring/ppermute | solution.py:364
  14.4 25.0 %collective-permute-start.2 = (bf16[256,512]{1,0:T(8,128)(2,1)}, bf16[256,512]{1,0:T(8,128)(2,1)}, u32[]{:S(2)}, u32[]{:S(2)}) collective-permute-start(bf16[256,512]{1,0:T(8,128)(2,1)} %get-tuple-element.245.refs_1_), channel_id=1, source_target_pairs={{0,1},{1,2},{2,3},{3,0},{4,5},{5,6},{6,7},{7,4},{8,9},{9,10},{10,1... | collective-permute-start | bytes 786440 | tf_op jit(solution)/shard_map/tokens_ring/ppermute | solution.py:364
  16.0 23.5 %collective-permute-start.4 = (bf16[256,512]{1,0:T(8,128)(2,1)}, bf16[256,512]{1,0:T(8,128)(2,1)}, u32[]{:S(2)}, u32[]{:S(2)}) collective-permute-start(bf16[256,512]{1,0:T(8,128)(2,1)} %get-tuple-element.247.refs_8_), channel_id=1, source_target_pairs={{0,3},{1,0},{2,1},{3,2},{4,7},{5,4},{6,5},{7,6},{8,11},{9,8},{10,9... | collective-permute-start | bytes 786440 | tf_op jit(solution)/shard_map/tokens_ring/ppermute | solution.py:364
  18.2 25.0 %collective-permute-start.6 = (bf16[256,512]{1,0:T(8,128)(2,1)}, bf16[256,512]{1,0:T(8,128)(2,1)}, u32[]{:S(2)}, u32[]{:S(2)}) collective-permute-start(bf16[256,512]{1,0:T(8,128)(2,1)} %get-tuple-element.244.refs_9_), channel_id=1, source_target_pairs={{0,3},{1,0},{2,1},{3,2},{4,7},{5,4},{6,5},{7,6},{8,11},{9,8},{10,9... | collective-permute-start | bytes 786440 | tf_op jit(solution)/shard_map/tokens_ring/ppermute | solution.py:364
  49.3 155.5 %all-gather.8.cloned.1.call-start = ((), (), s32[]{:S(2)}) async-start(), calls=%async_computation.13 | async-start | bytes 7864320 | tf_op jit(solution)/shard_map/weights_queue/all_gather | solution.py:1001
  89.0 231.0 %all-gather.10.cloned.1.call-start = ((), (), s32[]{:S(2)}) async-start(), calls=%async_computation.14 | async-start | bytes 7864320 | tf_op jit(solution)/shard_map/weights_queue/all_gather | solution.py:1001
  89.9 42.8 %collective-permute-start.29 = (bf16[512,512]{1,0:T(8,128)(2,1)S(1)}, bf16[512,512]{1,0:T(8,128)(2,1)}, u32[]{:S(2)}, u32[]{:S(2)}) collective-permute-start(bf16[512,512]{1,0:T(8,128)(2,1)S(1)} %get-tuple-element.225.refs_16_), channel_id=1, source_target_pairs={{0,16},{4,20},{8,24},{12,28},{16,0},{20,4},{24,8},{28,12},{1,17},{... | collective-permute-start | bytes 1572872 | tf_op jit(solution)/shard_map/cot_gather/ppermute | solution.py:39
  91.5 41.8 %collective-permute-start.34 = (bf16[512,512]{1,0:T(8,128)(2,1)S(1)}, bf16[512,512]{1,0:T(8,128)(2,1)}, u32[]{:S(2)}, u32[]{:S(2)}) collective-permute-start(bf16[512,512]{1,0:T(8,128)(2,1)S(1)} %get-tuple-element.224.refs_24_), channel_id=1, source_target_pairs={{0,8},{4,12},{8,0},{12,4},{16,24},{20,28},{24,16},{28,20},{1,9},{5... | collective-permute-start | bytes 1572872 | tf_op jit(solution)/shard_map/cot_gather/ppermute | solution.py:39
  93.0 41.8 %collective-permute-start.27 = (bf16[512,512]{1,0:T(8,128)(2,1)S(1)}, bf16[512,512]{1,0:T(8,128)(2,1)S(1)}, u32[]{:S(2)}, u32[]{:S(2)}) collective-permute-start(bf16[512,512]{1,0:T(8,128)(2,1)S(1)} %get-tuple-element.225.refs_16_), channel_id=1, source_target_pairs={{0,8},{4,12},{8,0},{12,4},{16,24},{20,28},{24,16},{28,20},{1,9},{5... | collective-permute-start | bytes 1572872 | tf_op jit(solution)/shard_map/cot_gather/ppermute | solution.py:39
  95.7 44.2 %collective-permute-start.36 = (bf16[512,512]{1,0:T(8,128)(2,1)S(1)}, bf16[512,512]{1,0:T(8,128)(2,1)S(1)}, u32[]{:S(2)}, u32[]{:S(2)}) collective-permute-start(bf16[512,512]{1,0:T(8,128)(2,1)S(1)} %get-tuple-element.224.refs_24_), channel_id=1, source_target_pairs={{0,16},{4,20},{8,24},{12,28},{16,0},{20,4},{24,8},{28,12},{1,17},{... | collective-permute-start | bytes 1572872 | tf_op jit(solution)/shard_map/cot_gather/ppermute | solution.py:39
  96.2 43.8 %collective-permute-start.26 = (bf16[512,512]{1,0:T(8,128)(2,1)S(1)}, bf16[512,512]{1,0:T(8,128)(2,1)}, u32[]{:S(2)}, u32[]{:S(2)}) collective-permute-start(bf16[512,512]{1,0:T(8,128)(2,1)S(1)} %get-tuple-element.225.refs_16_), channel_id=1, source_target_pairs={{0,4},{4,0},{8,12},{12,8},{16,20},{20,16},{24,28},{28,24},{1,5},{5... | collective-permute-start | bytes 1572872 | tf_op jit(solution)/shard_map/cot_gather/ppermute | solution.py:39
  151.7 25.4 %collective-permute-start.13 = (bf16[512,512]{1,0:T(8,128)(2,1)S(1)}, bf16[512,512]{1,0:T(8,128)(2,1)S(1)}, u32[]{:S(2)}, u32[]{:S(2)}) collective-permute-start(bf16[512,512]{1,0:T(8,128)(2,1)S(1)} %get-tuple-element.227.refs_0_), channel_id=1, source_target_pairs={{0,8},{4,12},{8,0},{12,4},{16,24},{20,28},{24,16},{28,20},{1,9},{5... | collective-permute-start | bytes 1572872 | tf_op jit(solution)/shard_map/act_gather/ppermute | solution.py:39
  153.1 24.5 %collective-permute-start.22 = (bf16[512,512]{1,0:T(8,128)(2,1)S(1)}, bf16[512,512]{1,0:T(8,128)(2,1)}, u32[]{:S(2)}, u32[]{:S(2)}) collective-permute-start(bf16[512,512]{1,0:T(8,128)(2,1)S(1)} %get-tuple-element.226.refs_8_), channel_id=1, source_target_pairs={{0,16},{4,20},{8,24},{12,28},{16,0},{20,4},{24,8},{28,12},{1,17},{... | collective-permute-start | bytes 1572872 | tf_op jit(solution)/shard_map/act_gather/ppermute | solution.py:39
  153.7 24.0 %collective-permute-start.12 = (bf16[512,512]{1,0:T(8,128)(2,1)S(1)}, bf16[512,512]{1,0:T(8,128)(2,1)S(1)}, u32[]{:S(2)}, u32[]{:S(2)}) collective-permute-start(bf16[512,512]{1,0:T(8,128)(2,1)S(1)} %get-tuple-element.227.refs_0_), channel_id=1, source_target_pairs={{0,4},{4,0},{8,12},{12,8},{16,20},{20,16},{24,28},{28,24},{1,5},{5... | collective-permute-start | bytes 1572872 | tf_op jit(solution)/shard_map/act_gather/ppermute | solution.py:39
  177.7 24.2 %collective-permute-start.16 = (bf16[512,512]{1,0:T(8,128)(2,1)}, bf16[512,512]{1,0:T(8,128)(2,1)}, u32[]{:S(2)}, u32[]{:S(2)}) collective-permute-start(bf16[512,512]{1,0:T(8,128)(2,1)} %collective-permute-done.15.refs_4_), channel_id=1, source_target_pairs={{0,4},{4,0},{8,12},{12,8},{16,20},{20,16},{24,28},{28,24},{1,5},{5... | collective-permute-start | bytes 1572872 | tf_op jit(solution)/shard_map/act_gather/ppermute | solution.py:39
  178.2 23.7 %collective-permute-start.21 = (bf16[512,512]{1,0:T(8,128)(2,1)}, bf16[512,512]{1,0:T(8,128)(2,1)}, u32[]{:S(2)}, u32[]{:S(2)}) collective-permute-start(bf16[512,512]{1,0:T(8,128)(2,1)} %collective-permute-done.20.refs_10_), channel_id=1, source_target_pairs={{0,4},{4,0},{8,12},{12,8},{16,20},{20,16},{24,28},{28,24},{1,5},{5... | collective-permute-start | bytes 1572872 | tf_op jit(solution)/shard_map/act_gather/ppermute | solution.py:39
  196.9 266.9 %reduce-scatter.4.cloned.1.call-start = ((), (), s32[]{:S(2)}) async-start(), calls=%async_computation.10 | async-start | bytes 7864320 | tf_op jit(solution)/shard_map/grads_queue/reduce_scatter | solution.py:1035
  252.8 319.2 %reduce-scatter.6.cloned.1.call-start = ((), (), s32[]{:S(2)}) async-start(), calls=%async_computation.11 | async-start | bytes 7864320 | tf_op jit(solution)/shard_map/grads_queue/reduce_scatter | solution.py:1035
  399.8 25.8 %collective-permute-start.41 = (bf16[2,512,512]{2,1,0:T(8,128)(2,1)}, bf16[2,512,512]{2,1,0:T(8,128)(2,1)}, u32[]{:S(2)}, u32[]{:S(2)}) collective-permute-start(bf16[2,512,512]{2,1,0:T(8,128)(2,1)} %get-tuple-element.209), channel_id=1, source_target_pairs={{0,8},{4,12},{8,0},{12,4},{16,24},{20,28},{24,16},{28,20},{1,9},{5... | collective-permute-start | bytes 3145736 | tf_op jit(solution)/shard_map/back_reduce/ppermute | solution.py:39
  405.2 26.4 %collective-permute-start.44 = (bf16[2,512,512]{2,1,0:T(8,128)(2,1)}, bf16[2,512,512]{2,1,0:T(8,128)(2,1)}, u32[]{:S(2)}, u32[]{:S(2)}) collective-permute-start(bf16[2,512,512]{2,1,0:T(8,128)(2,1)} %get-tuple-element.211), channel_id=1, source_target_pairs={{0,16},{4,20},{8,24},{12,28},{16,0},{20,4},{24,8},{28,12},{1,17},{... | collective-permute-start | bytes 3145736 | tf_op jit(solution)/shard_map/back_reduce/ppermute | solution.py:39
  503.6 30.2 %collective-permute-start.48 = (bf16[4,128,1024]{2,1,0:T(8,128)(2,1)}, bf16[4,128,1024]{2,1,0:T(8,128)(2,1)}, u32[]{:S(2)}, u32[]{:S(2)}) collective-permute-start(bf16[4,128,1024]{2,1,0:T(8,128)(2,1)} %get-tuple-element.121), channel_id=1, source_target_pairs={{0,4},{4,0},{8,12},{12,8},{16,20},{20,16},{24,28},{28,24},{1,5},{5... | collective-permute-start | bytes 3145736 | tf_op jit(solution)/shard_map/late_fsdp/ppermute | solution.py:39
  503.6 34.1 %collective-permute-start.46 = (bf16[4,128,1024]{2,1,0:T(8,128)(2,1)}, bf16[4,128,1024]{2,1,0:T(8,128)(2,1)}, u32[]{:S(2)}, u32[]{:S(2)}) collective-permute-start(bf16[4,128,1024]{2,1,0:T(8,128)(2,1)} %get-tuple-element.119), channel_id=1, source_target_pairs={{0,4},{4,0},{8,12},{12,8},{16,20},{20,16},{24,28},{28,24},{1,5},{5... | collective-permute-start | bytes 3145736 | tf_op jit(solution)/shard_map/late_fsdp/ppermute | solution.py:39
  504.1 52.2 %all-to-all-start.3 = ((bf16[8,128,1152]{2,1,0:T(8,128)(2,1)}), bf16[8,128,1152]{2,1,0:T(8,128)(2,1)}, u32[]{:S(2)}, u32[]{:S(2)}) async-start(bf16[8,128,1152]{2,1,0:T(8,128)(2,1)} %concatenate.86), calls=%async_computation.5 | async-start | bytes 4718592 | tf_op jit(solution)/shard_map/early_fsdp/all_to_all | solution.py:109
  508.5 159.6 %reduce-scatter.8.cloned.1.call-start = ((), (), s32[]{:S(2)}) async-start(), calls=%async_computation.12 | async-start | bytes 5242880 | tf_op jit(solution)/shard_map/tokens_back/reduce_scatter | solution.py:1095
  568.2 39.5 %collective-permute-start.51 = (bf16[4,512,512]{2,1,0:T(8,128)(2,1)}, bf16[4,512,512]{2,1,0:T(8,128)(2,1)}, u32[]{:S(2)}, u32[]{:S(2)}) collective-permute-start(bf16[4,512,512]{2,1,0:T(8,128)(2,1)} %get-tuple-element.129), channel_id=1, source_target_pairs={{0,4},{4,0},{8,12},{12,8},{16,20},{20,16},{24,28},{28,24},{1,5},{5... | collective-permute-start | bytes 6291464 | tf_op jit(solution)/shard_map/mix_reduce/ppermute | solution.py:39
  568.2 43.2 %collective-permute-start.50 = (bf16[4,512,512]{2,1,0:T(8,128)(2,1)}, bf16[4,512,512]{2,1,0:T(8,128)(2,1)}, u32[]{:S(2)}, u32[]{:S(2)}) collective-permute-start(bf16[4,512,512]{2,1,0:T(8,128)(2,1)} %get-tuple-element.127), channel_id=1, source_target_pairs={{0,4},{4,0},{8,12},{12,8},{16,20},{20,16},{24,28},{28,24},{1,5},{5... | collective-permute-start | bytes 6291464 | tf_op jit(solution)/shard_map/mix_reduce/ppermute | solution.py:39
  572.0 60.8 %all-to-all-start.4 = ((bf16[4,32,3200]{2,1,0:T(8,128)(2,1)}), bf16[4,32,3200]{2,1,0:T(8,128)(2,1)S(1)}, u32[]{:S(2)}, u32[]{:S(2)}) async-start(bf16[4,32,3200]{2,1,0:T(8,128)(2,1)} %bitcast.50), calls=%async_computation.7 | async-start | bytes 1638400 | tf_op jit(solution)/shard_map/sums_sp/all_to_all | solution.py:109
  614.9 25.2 %collective-permute-start.54 = (bf16[2,512,512]{2,1,0:T(8,128)(2,1)}, bf16[2,512,512]{2,1,0:T(8,128)(2,1)}, u32[]{:S(2)}, u32[]{:S(2)}) collective-permute-start(bf16[2,512,512]{2,1,0:T(8,128)(2,1)} %get-tuple-element.136), channel_id=1, source_target_pairs={{0,8},{4,12},{8,0},{12,4},{16,24},{20,28},{24,16},{28,20},{1,9},{5... | collective-permute-start | bytes 3145736 | tf_op jit(solution)/shard_map/mix_reduce/ppermute | solution.py:39
  615.6 27.1 %collective-permute-start.56 = (bf16[2,512,512]{2,1,0:T(8,128)(2,1)}, bf16[2,512,512]{2,1,0:T(8,128)(2,1)}, u32[]{:S(2)}, u32[]{:S(2)}) collective-permute-start(bf16[2,512,512]{2,1,0:T(8,128)(2,1)} %get-tuple-element.137), channel_id=1, source_target_pairs={{0,16},{4,20},{8,24},{12,28},{16,0},{20,4},{24,8},{28,12},{1,17},{... | collective-permute-start | bytes 3145736 | tf_op jit(solution)/shard_map/mix_reduce/ppermute | solution.py:39
  633.9 25.9 %all-to-all-start.5 = ((bf16[4,32,3200]{2,1,0:T(8,128)(2,1)}), bf16[4,32,3200]{2,1,0:T(8,128)(2,1)S(1)}, u32[]{:S(2)}, u32[]{:S(2)}) async-start(bf16[4,32,3200]{2,1,0:T(8,128)(2,1)} %broadcast_in_dim.76), calls=%async_computation.8 | async-start | bytes 1638400 | tf_op jit(solution)/shard_map/sums_sp/all_to_all | solution.py:109
  642.2 21.7 %collective-permute-start.55 = (bf16[1,512,512]{2,1,0:T(8,128)(2,1)}, bf16[1,512,512]{2,1,0:T(8,128)(2,1)}, u32[]{:S(2)}, u32[]{:S(2)}) collective-permute-start(bf16[1,512,512]{2,1,0:T(8,128)(2,1)} %add_convert_fusion.11), channel_id=1, source_target_pairs={{0,16},{4,20},{8,24},{12,28},{16,0},{20,4},{24,8},{28,12},{1,17},{... | collective-permute-start | bytes 1572872 | tf_op jit(solution)/shard_map/mix_reduce/ppermute | solution.py:39
  (126 other events, 1515.6 us)
Sparse Core Ops, SparseCore 0:
  11.4 50.0 all-gather.5
  89.1 115.6 all-gather.7
  206.4 113.5 all-gather.9
  322.2 108.9 reduce-scatter.3
  433.3 111.2 reduce-scatter.5
  547.4 90.8 reduce-scatter.7
